TPU v7x, 32 devices: a whole 2x2x4 slice. The times are simulated.
32 devices in a mesh: pair: 2 (over x), batch: 16 (over z, y, core).
Axes of the slice: x: 2, y: 2, z: 4, core: 2. Of those that a mesh axis runs over, the one named last changes fastest.
Arguments:
- frames: bfloat16 [2, 3584, 4, 84, 84], P('pair', 'batch'), may hold values from -4 to 4
- kernel_first: bfloat16 [2, 8, 8, 4, 32], P('pair'), may hold values from -0.5 to 0.5
- bias_first: bfloat16 [2, 32], P('pair'), may hold values from -1.5 to 1.5
- kernel_second: bfloat16 [2, 4, 4, 32, 64], P('pair'), may hold values from -0.375 to 0.375
- bias_second: bfloat16 [2, 64], P('pair'), may hold values from -1.5 to 1.5
- kernel_third: bfloat16 [2, 3, 3, 64, 64], P('pair'), may hold values from -0.375 to 0.375
- bias_third: bfloat16 [2, 64], P('pair'), may hold values from -1.5 to 1.5
- dense_weight: bfloat16 [2, 3136, 512], P('pair'), may hold values from -0.15625 to 0.15625
- dense_bias: bfloat16 [2, 512], P('pair'), may hold values from -1.5 to 1.5
- head_weight: bfloat16 [2, 512, 918], P('pair'), may hold values from -0.375 to 0.375
- head_bias: bfloat16 [2, 918], P('pair'), may hold values from -2.5 to 2.5
- taken_actions: int32 [3584], P('batch'), may hold values from 0 to 17
- greedy_actions: int32 [3584], P('batch'), may hold values from 0 to 17
- done_flags: int32 [3584], P('batch'), may hold values 0 or 1
- bin_lower: int32 [3584, 51], P('batch'), may hold values from 0 to 49
- bin_fraction: float32 [3584, 51], P('batch'), may hold values from 0 to 1
- owner_shard: int32 [3584, 1], P('batch'), may hold values from 0 to 15; in each aligned block of 224 rows (0 to 223, 224 to 447, ...) at most 28 rows name the same one
Outputs:
- first_kernel_grad: float32 [8, 8, 4, 32], P('pair')
- first_bias_grad: float32 [32], P('pair')
- second_kernel_grad: float32 [4, 4, 32, 64], P('pair')
- second_bias_grad: float32 [64], P('pair')
- third_kernel_grad: float32 [3, 3, 64, 64], P(None, None, None, 'pair')
- third_bias_grad: float32 [64], P('pair')
- dense_weight_grad: float32 [3136, 512], P(None, 'pair')
- dense_bias_grad: float32 [512], P('pair')
- head_weight_grad: float32 [512, 918], P('pair')
- head_bias_grad: float32 [918], P('pair')
- frame_grad: bfloat16 [3584, 4, 84, 84], P('batch', 'pair')
- priorities: float32 [16, 16, 28], P('batch', None, 'pair')
Inputs may be any that keep to these rules, and one draw needn't show every extreme that they name: `owner_shard`: among the 224 rows of one index of batch (aligned blocks), at most 28 name the same shard, and in every draw some shard is named by exactly 28 of them.
All inputs are finite; a program needn't handle non-finite values. No bound on the sum of `done_flags` on one device may be relied on, other than what follows from the above.
Results may differ from a plain program's by a relative error of at most 0.013.
Values may be sent and summed in bfloat16 or wider, within the bound.
No kernel may reach another device: no remote copies, remote signals or barrier semaphores. Data moves between devices by JAX's collectives and lax.ppermute only.
A program may use at most 704 MiB of HBM per device.

v0:
```python
import jax
import jax.numpy as jnp
from jax import lax
from jax.sharding import PartitionSpec as P

ACT = 18
ATOMS = 51
LOSS_SCALE = 256


HIGHEST_PRECISION = lax.Precision.HIGHEST
SPLIT_DIMS = (0, 0, 0, 0, 3, 0, 1, 0, 0, 0)


def shifted(block, axis, distance):
    devices = range(lax.axis_size(axis))
    route = [(i - distance, i) for i in devices if i - distance in devices]
    return lax.ppermute(block, axis, route)


def kernel_matrix(kernel, stride):
    kernel_side, in_chan, out_chan = (kernel.shape[0], kernel.shape[2], kernel.shape[3])
    kernel_reach = kernel_side // stride
    shaped = kernel.reshape(kernel_reach, stride, kernel_reach, stride, in_chan, out_chan)
    shaped = shaped.transpose(0, 2, 1, 3, 4, 5)
    return shaped.reshape(kernel_reach * kernel_reach * stride * stride * in_chan, out_chan)


def kernel_back(matrix, stride, kernel_side, in_chan):
    kernel_reach = kernel_side // stride
    out_chan = matrix.shape[1]
    shaped = matrix.reshape(kernel_reach, kernel_reach, stride, stride, in_chan, out_chan)
    shaped = shaped.transpose(0, 2, 1, 3, 4, 5)
    return shaped.reshape(kernel_side, kernel_side, in_chan, out_chan)


def to_cells(values, stride):
    batch_rows, height, channels = (values.shape[0], values.shape[1], values.shape[3])
    cell_side = height // stride
    shaped = values.reshape(batch_rows, cell_side, stride, cell_side, stride, channels)
    return shaped.transpose(0, 1, 3, 2, 4, 5).reshape(
        batch_rows, cell_side, cell_side, stride * stride * channels
    )


def from_cells(values, stride, channels):
    batch_rows, cell_side = (values.shape[0], values.shape[1])
    shaped = values.reshape(batch_rows, cell_side, cell_side, stride, stride, channels)
    return shaped.transpose(0, 1, 3, 2, 4, 5).reshape(
        batch_rows, cell_side * stride, cell_side * stride, channels
    )


def frames_to_cells(frame_rows):
    batch_rows, channels, side_len = (frame_rows.shape[0], frame_rows.shape[1], frame_rows.shape[2])
    cell_side = side_len // 4
    shaped = frame_rows.reshape(batch_rows, channels, cell_side, 4, cell_side, 4)
    return shaped.transpose(0, 2, 4, 3, 5, 1).reshape(
        batch_rows, cell_side, cell_side, 16 * channels
    )


def cells_to_frames(values, channels):
    batch_rows, cell_side = (values.shape[0], values.shape[1])
    shaped = values.reshape(batch_rows, cell_side, cell_side, 4, 4, channels)
    return shaped.transpose(0, 5, 1, 3, 2, 4).reshape(
        batch_rows, channels, cell_side * 4, cell_side * 4
    )


def gather_cells(cells_in, kernel_reach, out_side):
    batch_rows, features = (cells_in.shape[0], cells_in.shape[3])
    windows = [
        cells_in[:, row_off : row_off + out_side, col_off : col_off + out_side, :]
        for row_off in range(kernel_reach)
        for col_off in range(kernel_reach)
    ]
    return jnp.stack(windows, axis=3).reshape(
        batch_rows * out_side * out_side, kernel_reach * kernel_reach * features
    )


def spread_cells(columns, kernel_reach, out_side, cell_side, batch_rows):
    features = columns.shape[1] // (kernel_reach * kernel_reach)
    shaped = columns.reshape(batch_rows, out_side, out_side, kernel_reach * kernel_reach, features)
    summed = jnp.zeros((batch_rows, cell_side, cell_side, features), jnp.float32)
    for row_off in range(kernel_reach):
        for col_off in range(kernel_reach):
            portion = shaped[:, :, :, row_off * kernel_reach + col_off, :]
            padding = (
                (0, 0, 0),
                (row_off, cell_side - out_side - row_off, 0),
                (col_off, cell_side - out_side - col_off, 0),
                (0, 0, 0),
            )
            summed = summed + lax.pad(portion, jnp.float32(0), padding)
    return summed


def dot_first(left_arr, right_arr):
    return lax.dot_general(
        left_arr, right_arr, (((0,), (0,)), ((), ())), preferred_element_type=jnp.float32
    )


def dot_last(left_arr, right_arr):
    return lax.dot_general(
        left_arr, right_arr, (((1,), (1,)), ((), ())), preferred_element_type=jnp.float32
    )


def silu_slope(pre_values):
    sigmoid_val = jax.nn.sigmoid(pre_values)
    return sigmoid_val * (1.0 + pre_values * (1.0 - sigmoid_val))


def activate(pre_values):
    return jax.nn.silu(pre_values).astype(jnp.bfloat16)


def dense_pre(inputs, matrix, bias_vec):
    return jnp.dot(inputs, matrix, preferred_element_type=jnp.float32) + bias_vec.astype(
        jnp.float32
    )


def forward_block(frame_rows, weights, matrices):
    batch_rows = frame_rows.shape[0]
    cells_first = frames_to_cells(frame_rows)
    side_first = cells_first.shape[1] - 1
    patch_first = gather_cells(cells_first, 2, side_first)
    pre_first = dense_pre(patch_first, matrices[0], weights[1]).reshape(
        batch_rows, side_first, side_first, -1
    )
    act_first = activate(pre_first)
    cells_second = to_cells(act_first, 2)
    side_second = cells_second.shape[1] - 1
    patch_second = gather_cells(cells_second, 2, side_second)
    pre_second = dense_pre(patch_second, matrices[1], weights[3]).reshape(
        batch_rows, side_second, side_second, -1
    )
    act_second = activate(pre_second)
    side_third = side_second - 2
    patch_third = gather_cells(act_second, 3, side_third)
    pre_third = dense_pre(patch_third, matrices[2], weights[5]).reshape(
        batch_rows, side_third, side_third, -1
    )
    act_third = activate(pre_third)
    pre_dense = dense_pre(act_third.reshape(batch_rows, -1), weights[6], weights[7])
    act_dense = activate(pre_dense)
    logits = jnp.dot(act_dense, weights[8], preferred_element_type=jnp.float32) + weights[9].astype(
        jnp.float32
    )
    return ((pre_first, pre_second, pre_third, pre_dense), logits.reshape(batch_rows, ACT, ATOMS))


def backward_block(frame_rows, kept, diff_logit, matrices, weights):
    pre_first, pre_second, pre_third, pre_dense = kept
    act_first = activate(pre_first)
    act_second = activate(pre_second)
    act_third = activate(pre_third)
    act_dense = activate(pre_dense)
    batch_rows, channels = (frame_rows.shape[0], frame_rows.shape[1])
    cells_first = frames_to_cells(frame_rows)
    side_first = cells_first.shape[1] - 1
    patch_first = gather_cells(cells_first, 2, side_first)
    cells_second = to_cells(act_first, 2)
    side_second = cells_second.shape[1] - 1
    patch_second = gather_cells(cells_second, 2, side_second)
    side_third = side_second - 2
    patch_third = gather_cells(act_second, 3, side_third)
    diff_head = diff_logit.reshape(batch_rows, -1)
    head_bias_grad = jnp.sum(diff_head, axis=0)
    round_head = diff_head.astype(jnp.bfloat16)
    head_weight_grad = dot_first(act_dense, round_head)
    diff_dense = dot_last(round_head, weights[8]) * silu_slope(pre_dense)
    dense_bias_grad = jnp.sum(diff_dense, axis=0)
    round_dense = diff_dense.astype(jnp.bfloat16)
    dense_weight_grad = dot_first(act_third.reshape(batch_rows, -1), round_dense)
    diff_third = dot_last(round_dense, weights[6]).reshape(pre_third.shape) * silu_slope(pre_third)
    third_bias_grad = jnp.sum(diff_third, axis=(0, 1, 2))
    round_third = diff_third.reshape(-1, diff_third.shape[3]).astype(jnp.bfloat16)
    third_kernel_grad = kernel_back(dot_first(patch_third, round_third), 1, 3, act_second.shape[3])
    diff_second = spread_cells(
        dot_last(round_third, matrices[2]), 3, side_third, side_second, batch_rows
    )
    diff_second = diff_second * silu_slope(pre_second)
    second_bias_grad = jnp.sum(diff_second, axis=(0, 1, 2))
    round_second = diff_second.reshape(-1, diff_second.shape[3]).astype(jnp.bfloat16)
    second_kernel_grad = kernel_back(
        dot_first(patch_second, round_second), 2, 4, act_first.shape[3]
    )
    diff_cells = spread_cells(
        dot_last(round_second, matrices[1]), 2, side_second, side_second + 1, batch_rows
    )
    diff_first = from_cells(diff_cells, 2, act_first.shape[3]) * silu_slope(pre_first)
    first_bias_grad = jnp.sum(diff_first, axis=(0, 1, 2))
    round_first = diff_first.reshape(-1, diff_first.shape[3]).astype(jnp.bfloat16)
    first_kernel_grad = kernel_back(dot_first(patch_first, round_first), 4, 8, channels)
    frame_cells = spread_cells(
        dot_last(round_first, matrices[0]), 2, side_first, side_first + 1, batch_rows
    )
    frame_diff = cells_to_frames(frame_cells, channels).astype(jnp.bfloat16)
    gradients_out = (
        first_kernel_grad,
        first_bias_grad,
        second_kernel_grad,
        second_bias_grad,
        third_kernel_grad,
        third_bias_grad,
        dense_weight_grad,
        dense_bias_grad,
        head_weight_grad,
        head_bias_grad,
    )
    return (gradients_out, frame_diff)


def project_mass(chosen, done_rows, lower_bins, fractions):
    atom_ids = jnp.arange(ATOMS, dtype=jnp.int32)
    first_atom = (atom_ids == 0).astype(jnp.float32)
    finished = done_rows.astype(jnp.float32)[:, None]
    atom_mass = (1.0 - finished) * chosen + finished * first_atom[None, :]
    lower_hot = (lower_bins[:, :, None] == atom_ids[None, None, :]).astype(jnp.float32)
    upper_hot = ((lower_bins + 1)[:, :, None] == atom_ids[None, None, :]).astype(jnp.float32)
    spread_table = (1.0 - fractions)[:, :, None] * lower_hot + fractions[:, :, None] * upper_hot
    return jnp.einsum("ri,rij->rj", atom_mass, spread_table, precision=HIGHEST_PRECISION)


def split_half(gradient, axis_dim):
    length = gradient.shape[axis_dim] // 2
    return (
        lax.slice_in_dim(gradient, 0, length, axis=axis_dim),
        lax.slice_in_dim(gradient, length, 2 * length, axis=axis_dim),
    )


def local(
    frames,
    kernel_first,
    bias_first,
    kernel_second,
    bias_second,
    kernel_third,
    bias_third,
    dense_weight,
    dense_bias,
    head_weight,
    head_bias,
    taken_actions,
    greedy_actions,
    done_flags,
    bin_lower,
    bin_fraction,
    owner_shard,
):
    online_side = lax.axis_index("pair") == 0
    weights = tuple(
        (
            tensor[0]
            for tensor in (
                kernel_first,
                bias_first,
                kernel_second,
                bias_second,
                kernel_third,
                bias_third,
                dense_weight,
                dense_bias,
                head_weight,
                head_bias,
            )
        )
    )
    matrices = (
        kernel_matrix(weights[0], 4),
        kernel_matrix(weights[2], 2),
        kernel_matrix(weights[4], 1),
    )
    own_frames = frames[0]
    row_count = own_frames.shape[0]
    block_rows = max((divisor for divisor in range(1, 65) if row_count % divisor == 0))
    block_count = row_count // block_rows
    frame_blocks = own_frames.reshape((block_count, block_rows) + own_frames.shape[1:])
    kept, logits = lax.map(lambda rows_in: forward_block(rows_in, weights, matrices), frame_blocks)
    logits = logits.reshape(row_count, ACT, ATOMS)
    action_ids = jnp.arange(ACT, dtype=jnp.int32)
    greedy_hot = (greedy_actions[:, None] == action_ids[None, :]).astype(jnp.float32)
    picked = jnp.einsum("rak,ra->rk", logits, greedy_hot, precision=HIGHEST_PRECISION)
    chosen = jax.nn.softmax(picked, axis=-1).astype(jnp.bfloat16)
    arrived = shifted(chosen, "pair", -1)
    projected = project_mass(arrived.astype(jnp.float32), done_flags, bin_lower, bin_fraction)
    taken_hot = (taken_actions[:, None] == action_ids[None, :]).astype(jnp.float32)
    taken_row = jnp.einsum("rak,ra->rk", logits, taken_hot, precision=HIGHEST_PRECISION)
    log_probs = jax.nn.log_softmax(taken_row, axis=-1)
    row_loss = -jnp.sum(projected * log_probs, axis=-1)
    diff_taken = (
        jnp.sum(projected, axis=-1, keepdims=True) * jnp.exp(log_probs) - projected
    ) * LOSS_SCALE
    diff_logit = taken_hot[:, :, None] * diff_taken[:, None, :]
    diff_blocks = diff_logit.reshape(block_count, block_rows, ACT, ATOMS)

    def run_backward(operands):

        def one_block(summed, scan_item):
            block_grads, frame_diff = backward_block(
                scan_item[0], scan_item[1], scan_item[2], matrices, weights
            )
            return (
                tuple((acc_val + new_val for acc_val, new_val in zip(summed, block_grads))),
                frame_diff,
            )

        initial = tuple((jnp.zeros(tensor.shape, jnp.float32) for tensor in weights))
        return lax.scan(one_block, initial, operands)

    def skip_backward(operands):
        initial = tuple((jnp.zeros(tensor.shape, jnp.float32) for tensor in weights))
        return (initial, jnp.zeros(operands[0].shape, jnp.bfloat16))

    local_grads, frame_diffs = lax.cond(
        online_side, run_backward, skip_backward, (frame_blocks, kept, diff_blocks)
    )
    frame_diff = frame_diffs.reshape(own_frames.shape)
    channels_half = own_frames.shape[1] // 2
    handed_frames = shifted(frame_diff[:, channels_half:], "pair", 1)
    frame_out = jnp.where(online_side, frame_diff[:, :channels_half], handed_frames)
    shard_count = lax.axis_size("batch")
    capacity = 2 * ((row_count + shard_count - 1) // shard_count)
    owner_ids = owner_shard[:, 0]
    owner_hot = (owner_ids[:, None] == jnp.arange(shard_count, dtype=jnp.int32)[None, :]).astype(
        jnp.int32
    )
    slot_ids = jnp.sum(jnp.cumsum(owner_hot, axis=0) * owner_hot, axis=1) - 1
    outgoing = jnp.zeros((shard_count, capacity), jnp.float32).at[owner_ids, slot_ids].set(row_loss)
    incoming = lax.all_to_all(outgoing, "batch", split_axis=0, concat_axis=0, tiled=True)
    half_cap = capacity // 2
    own_prio = incoming[:, :half_cap]
    far_prio = incoming[:, half_cap:]
    summed = lax.psum(
        (
            local_grads[0],
            local_grads[1],
            local_grads[2],
            local_grads[3],
            local_grads[4],
            local_grads[5],
            local_grads[6],
            local_grads[7],
            local_grads[8],
            local_grads[9],
        ),
        "batch",
    )
    summed = tuple((gradient / LOSS_SCALE for gradient in summed))
    lower_parts = [
        split_half(gradient, axis_dim)[0] for gradient, axis_dim in zip(summed, SPLIT_DIMS)
    ]
    upper_parts = [
        split_half(gradient, axis_dim)[1] for gradient, axis_dim in zip(summed, SPLIT_DIMS)
    ]
    handed = (
        shifted(upper_parts[0].astype(jnp.bfloat16), "pair", 1).astype(jnp.float32),
        shifted(upper_parts[1].astype(jnp.bfloat16), "pair", 1).astype(jnp.float32),
        shifted(upper_parts[2].astype(jnp.bfloat16), "pair", 1).astype(jnp.float32),
        shifted(upper_parts[3].astype(jnp.bfloat16), "pair", 1).astype(jnp.float32),
        shifted(upper_parts[4].astype(jnp.bfloat16), "pair", 1).astype(jnp.float32),
        shifted(upper_parts[5].astype(jnp.bfloat16), "pair", 1).astype(jnp.float32),
        shifted(upper_parts[6].astype(jnp.bfloat16), "pair", 1).astype(jnp.float32),
        shifted(upper_parts[7].astype(jnp.bfloat16), "pair", 1).astype(jnp.float32),
        shifted(upper_parts[8].astype(jnp.bfloat16), "pair", 1).astype(jnp.float32),
        shifted(upper_parts[9].astype(jnp.bfloat16), "pair", 1).astype(jnp.float32),
        shifted(far_prio.astype(jnp.bfloat16), "pair", 1).astype(far_prio.dtype),
    )
    finals = tuple(
        (
            jnp.where(online_side, lower_part, handed_part)
            for lower_part, handed_part in zip(lower_parts, handed[:10])
        )
    )
    prio_out = jnp.where(online_side, own_prio, handed[10])
    return (
        finals[0],
        finals[1],
        finals[2],
        finals[3],
        finals[4],
        finals[5],
        finals[6],
        finals[7],
        finals[8],
        finals[9],
        frame_out,
        prio_out[None],
    )


def solution(mesh):
    return jax.shard_map(
        local,
        mesh=mesh,
        in_specs=(
            P("pair", "batch", None, None, None),
            P("pair", None, None, None, None),
            P("pair", None),
            P("pair", None, None, None, None),
            P("pair", None),
            P("pair", None, None, None, None),
            P("pair", None),
            P("pair", None, None),
            P("pair", None),
            P("pair", None, None),
            P("pair", None),
            P("batch"),
            P("batch"),
            P("batch"),
            P("batch", None),
            P("batch", None),
            P("batch", None),
        ),
        out_specs=(
            P("pair", None, None, None),
            P("pair"),
            P("pair", None, None, None),
            P("pair"),
            P(None, None, None, "pair"),
            P("pair"),
            P(None, "pair"),
            P("pair"),
            P("pair", None),
            P("pair"),
            P("batch", "pair", None, None),
            P("batch", None, "pair"),
        ),
        check_vma=False,
    )
```

profile of v0, /device:TPU:0, one launch (start us, length us, event | category | flops | bytes accessed | tf_op | source)
XLA Modules:
  0.0 3498.2 jit_solution(12374082922648154968)
XLA Ops:
  7.4 28.9 copy.398
  38.4 1211.9 %while.62 = (s32[]{:T(128)}, f32[4,56,20,20,32]{3,2,1,4,0:T(8,128)}, f32[4,56,9,9,64]{4,3,2,1,0:T(8,128)}, f32[4,56,7,7,64]{4,3,2,1,0:T(8,128)}, f32[4,56,512]{2...) while((s32[]{:T(128)}, ...), condition=%wide.region_1.2_spmd, body=%wide.region_0.1_spmd.sunk | while | flops 1130547072 | bytes 288557120 | solution.py:285
  65.4 16.1 slice_bitcast_fusion.58
  81.5 16.0 pad_maximum_fusion.8
  97.4 48.4 %copy.512 = bf16[56,20,20,4,64]{4,3,2,1,0:T(4,128)(2,1)} copy(bf16[56,20,20,4,64]{0,4,2,1,3:T(8,128)(2,1)} %pad_maximum_fusion.8) | data formatting | bytes 22937600 | tf_op jit(solution)/shard_map/while/body/eval_jaxpr/stack | solution.py:78
  145.8 32.7 reshape.324
  186.3 20.2 broadcast_in_dim.83
  206.4 15.9 constant_dynamic-update-slice_fusion.10
  228.7 15.7 copy.514
  366.4 16.1 slice_bitcast_fusion.58
  382.5 16.0 pad_maximum_fusion.8
  398.5 48.4 %copy.512 = bf16[56,20,20,4,64]{4,3,2,1,0:T(4,128)(2,1)} copy(bf16[56,20,20,4,64]{0,4,2,1,3:T(8,128)(2,1)} %pad_maximum_fusion.8) | data formatting | bytes 22937600 | tf_op jit(solution)/shard_map/while/body/eval_jaxpr/stack | solution.py:78
  446.8 32.7 reshape.324
  487.3 20.2 broadcast_in_dim.83
  507.4 15.9 constant_dynamic-update-slice_fusion.10
  529.6 15.7 copy.514
  667.3 16.1 slice_bitcast_fusion.58
  683.4 16.0 pad_maximum_fusion.8
  699.4 48.4 %copy.512 = bf16[56,20,20,4,64]{4,3,2,1,0:T(4,128)(2,1)} copy(bf16[56,20,20,4,64]{0,4,2,1,3:T(8,128)(2,1)} %pad_maximum_fusion.8) | data formatting | bytes 22937600 | tf_op jit(solution)/shard_map/while/body/eval_jaxpr/stack | solution.py:78
  747.8 32.7 reshape.324
  788.2 20.2 broadcast_in_dim.83
  808.4 15.8 constant_dynamic-update-slice_fusion.10
  830.5 15.7 copy.514
  968.4 16.1 slice_bitcast_fusion.58
  984.4 16.0 pad_maximum_fusion.8
  1000.4 48.4 %copy.512 = bf16[56,20,20,4,64]{4,3,2,1,0:T(4,128)(2,1)} copy(bf16[56,20,20,4,64]{0,4,2,1,3:T(8,128)(2,1)} %pad_maximum_fusion.8) | data formatting | bytes 22937600 | tf_op jit(solution)/shard_map/while/body/eval_jaxpr/stack | solution.py:78
  1048.8 32.7 reshape.324
  1089.2 20.2 broadcast_in_dim.83
  1109.4 15.8 constant_dynamic-update-slice_fusion.10
  1262.9 1811.2 %conditional.1 = (f32[8,8,4,32]{3,1,2,0:T(8,128)}, f32[32]{0:T(128)}, f32[4,4,32,64]{3,2,1,0:T(8,128)}, f32[64]{0:T(128)}, f32[3,3,64,64]{3,2,1,0:T(8,128)}, /*i...) conditional(s32[]{:T(128)} %convert_element_type.200, () %tuple.30, ...), branch_computations={%region_6.7_spmd, %region_7.17_spmd} | conditional | flops 2252836352 | bytes 572928384 | solution.py:321
  1278.3 61.1 %copy.405 = f32[4,56,20,20,32]{1,4,3,2,0:T(8,128)} copy(f32[4,56,20,20,32]{3,2,1,4,0:T(8,128)} %get-tuple-element.617) | data formatting | bytes 22937600 | tf_op jit(solution)/shard_map
  1339.4 1728.3 %while.61 = (s32[]{:T(128)}, f32[8,8,4,32]{3,1,2,0:T(8,128)}, f32[32]{0:T(128)}, f32[4,4,32,64]{3,2,1,0:T(8,128)}, f32[64]{0:T(128)}, /*index=5*/f32[3,3,64,64]{...) while((s32[]{:T(128)}, f32[8,8,4,32]{3,1,2,0:T(8,128)}, ...), condition=%wide.region_16.16_spmd.clone, body=%wide.region_9.15_spmd.clone.sunk | while | flops 2252585216 | bytes 539369664 | solution.py:315
  1366.6 16.1 slice_bitcast_fusion.60
  1382.7 16.0 pad_maximum_fusion.10
  1398.6 48.4 %copy.523 = bf16[56,20,20,4,64]{4,3,2,1,0:T(4,128)(2,1)} copy(bf16[56,20,20,4,64]{0,4,2,1,3:T(8,128)(2,1)} %pad_maximum_fusion.10) | data formatting | bytes 22937600 | tf_op jit(solution)/shard_map/cond/branch_1_fun/while/body/eval_jaxpr/stack | solution.py:78
  1447.0 32.7 reshape.328
  1676.9 19.7 fusion.208
  1696.6 26.8 slice_bitcast_fusion.64
  1793.2 16.1 slice_bitcast_fusion.60
  1809.3 16.0 pad_maximum_fusion.10
  1825.2 48.4 %copy.523 = bf16[56,20,20,4,64]{4,3,2,1,0:T(4,128)(2,1)} copy(bf16[56,20,20,4,64]{0,4,2,1,3:T(8,128)(2,1)} %pad_maximum_fusion.10) | data formatting | bytes 22937600 | tf_op jit(solution)/shard_map/cond/branch_1_fun/while/body/eval_jaxpr/stack | solution.py:78
  1873.6 32.7 reshape.328
  2110.6 19.7 fusion.208
  2130.3 26.8 slice_bitcast_fusion.64
  2227.0 16.1 slice_bitcast_fusion.60
  2243.0 16.0 pad_maximum_fusion.10
  2259.0 48.4 %copy.523 = bf16[56,20,20,4,64]{4,3,2,1,0:T(4,128)(2,1)} copy(bf16[56,20,20,4,64]{0,4,2,1,3:T(8,128)(2,1)} %pad_maximum_fusion.10) | data formatting | bytes 22937600 | tf_op jit(solution)/shard_map/cond/branch_1_fun/while/body/eval_jaxpr/stack | solution.py:78
  2307.4 32.7 reshape.328
  2544.3 19.7 fusion.208
  2564.1 26.8 slice_bitcast_fusion.64
  2660.4 16.1 slice_bitcast_fusion.60
  2676.5 16.0 pad_maximum_fusion.10
  2692.4 48.4 %copy.523 = bf16[56,20,20,4,64]{4,3,2,1,0:T(4,128)(2,1)} copy(bf16[56,20,20,4,64]{0,4,2,1,3:T(8,128)(2,1)} %pad_maximum_fusion.10) | data formatting | bytes 22937600 | tf_op jit(solution)/shard_map/cond/branch_1_fun/while/body/eval_jaxpr/stack | solution.py:78
  2740.8 32.7 reshape.328
  2977.9 19.7 fusion.208
  2997.6 26.8 slice_bitcast_fusion.64
  3077.9 70.4 %all-reduce.18 = (f32[8,8,4,32]{3,2,1,0:T(4,128)S(1)}, f32[32]{0:T(128)S(1)}, f32[64]{0:T(128)S(1)}, f32[64]{0:T(128)S(1)}, f32[512]{0:T(512)S(1)}, /*index=5*/f32[918]{0:T(1024)S(1)}) all-reduce(f32[8,8,4,32]{3,2,1,0:T(4,128)S(1)} %copy.406, f32[32]{0:T(128)} %get-tuple-element.331, ...), channel_id=1, replica_groups=mesh['pair'=2,'batch'=16] {'batch'}, use_global_device_ids=true, to_apply=%region_17.18 | all-reduce | flops 9782 | bytes 78256 | tf_op jit(solution)/shard_map/psum | solution.py:340
  3149.6 44.1 %copy.408 = bf16[4,56,4,84,84]{4,1,0,3,2:T(8,128)(2,1)} copy(bf16[4,56,4,84,84]{1,2,4,3,0:T(4,128)(2,1)} %get-tuple-element.340) | data formatting | bytes 25288704 | tf_op jit(solution)/shard_map/cond | solution.py:321
  3203.2 20.0 copy.409
  3232.2 31.5 scatter_fusion
  3267.2 108.7 %collective-permute-done.2 = bf16[16]{0:T(256)(128)(2,1)S(1)} collective-permute-done((bf16[16]{0:T(256)(128)(2,1)S(1)}, bf16[16]{0:T(256)(128)(2,1)S(1)}, u32[]{:S(2)}, u32[]{:S(2)}) %collective-permute-start.2) | collective-permute-done | bytes 64 | tf_op jit(solution)/shard_map/ppermute | solution.py:18
  3401.7 30.1 collective-permute-done.3
  3441.7 19.7 copy.410
  3470.8 19.9 copy.414
  (736 shorter events, 1748.2 us)
Async XLA Ops:
  7.2 3381.2 %all-reduce.22.cloned.1.call-start = ((), (), s32[]{:S(2)}) async-start(), calls=%async_computation.1 | async-start | bytes 17727488 | tf_op jit(solution)/shard_map/psum | solution.py:340
  7.3 29.0 copy-start.28
  7.3 29.0 copy-start.27
  7.3 29.7 copy-start.22
  7.3 31.0 copy-start.34
  7.3 31.0 copy-start.33
  7.3 31.0 copy-start.36
  7.3 31.0 copy-start.37
  7.4 31.0 copy-start.38
  38.3 1211.9 %copy-start.35 = (s32[224]{0:T(256)S(1)}, s32[224]{0:T(256)}, u32[]{:S(2)}) copy-start(s32[224]{0:T(256)} %param.35) | copy-start | bytes 2692
  38.4 1216.9 %copy-start.31 = (s32[224]{0:T(256)S(1)}, s32[224]{0:T(256)}, u32[]{:S(2)}) copy-start(s32[224]{0:T(256)} %param.34) | copy-start | bytes 2692
  38.4 1217.1 %copy-start.32 = (s32[224]{0:T(256)S(1)}, s32[224]{0:T(256)}, u32[]{:S(2)}) copy-start(s32[224]{0:T(256)} %param.36) | copy-start | bytes 2692
  38.4 140.2 %copy-start.16 = (bf16[256,32]{1,0:T(8,128)(2,1)}, bf16[256,32]{1,0:T(8,128)(2,1)S(1)}, u32[]{:S(2)}) copy-start(bf16[256,32]{1,0:T(8,128)(2,1)S(1)} %get-tuple-element.1250) | copy-start | bytes 49156 | tf_op jit(solution)/shard_map/while
  260.8 13.2 copy-start.10
  339.4 140.2 %copy-start.16 = (bf16[256,32]{1,0:T(8,128)(2,1)}, bf16[256,32]{1,0:T(8,128)(2,1)S(1)}, u32[]{:S(2)}) copy-start(bf16[256,32]{1,0:T(8,128)(2,1)S(1)} %get-tuple-element.1250) | copy-start | bytes 49156 | tf_op jit(solution)/shard_map/while
  561.8 13.2 copy-start.10
  640.3 140.2 %copy-start.16 = (bf16[256,32]{1,0:T(8,128)(2,1)}, bf16[256,32]{1,0:T(8,128)(2,1)S(1)}, u32[]{:S(2)}) copy-start(bf16[256,32]{1,0:T(8,128)(2,1)S(1)} %get-tuple-element.1250) | copy-start | bytes 49156 | tf_op jit(solution)/shard_map/while
  862.7 13.2 copy-start.10
  941.4 140.2 %copy-start.16 = (bf16[256,32]{1,0:T(8,128)(2,1)}, bf16[256,32]{1,0:T(8,128)(2,1)S(1)}, u32[]{:S(2)}) copy-start(bf16[256,32]{1,0:T(8,128)(2,1)S(1)} %get-tuple-element.1250) | copy-start | bytes 49156 | tf_op jit(solution)/shard_map/while
  1163.7 13.2 copy-start.10
  1250.3 12.6 copy-start.18
  1250.3 10.6 copy-start.25
  1250.3 10.6 copy-start.26
  1254.0 6.9 collective-permute-start
  1278.3 61.1 %copy-start.11 = (bf16[512,64]{1,0:T(8,128)(2,1)S(1)}, bf16[512,64]{1,0:T(8,128)(2,1)}, u32[]{:S(2)}) copy-start(bf16[512,64]{1,0:T(8,128)(2,1)} %get-tuple-element.1149) | copy-start | bytes 196612 | tf_op jit(solution)/shard_map/cond
  1511.2 6.9 copy-start.13
  1618.8 7.7 copy-start
  1668.8 8.1 copy-start.19
  1757.5 8.5 copy-start.12
  1937.6 6.9 copy-start.13
  2046.9 9.2 copy-start
  2093.9 8.1 copy-start.15
  2100.6 7.2 copy-start.1
  2100.6 10.0 copy-start.19
  2191.0 8.6 copy-start.12
  2371.3 6.9 copy-start.13
  2480.5 9.4 copy-start
  2527.7 8.1 copy-start.15
  2534.3 7.2 copy-start.1
  2534.3 10.0 copy-start.19
  2624.7 8.4 copy-start.12
  2804.8 6.9 copy-start.13
  2914.2 9.2 copy-start
  2961.2 8.1 copy-start.15
  2967.9 7.2 copy-start.1
  2967.9 10.0 copy-start.19
  3058.3 8.5 copy-start.12
  3148.3 248.4 %collective-permute-start.1 = (bf16[4,8,4,32]{3,2,1,0:T(4,128)(2,1)S(1)}, bf16[4,8,4,32]{3,2,1,0:T(4,128)(2,1)S(1)}, u32[]{:S(2)}, u32[]{:S(2)}) collective-permute-start(bf16[4,8,4,32]{3,2,1,0:T(4,128)(2,1)S(1)} %slice.490), channel_id=1, source_target_pairs={{0,16},{1,17},{2,18},{3,19},{4,20},{5,21},{6,22},{7,23},{8,24},{9,... | collective-permute-start | bytes 24584 | tf_op jit(solution)/shard_map/ppermute | solution.py:18
  3203.2 28.4 copy-start.30
  3223.2 218.5 %collective-permute-start.11 = (bf16[224,2,84,84]{0,1,3,2:T(2,128)(2,1)}, bf16[224,2,84,84]{0,1,3,2:T(2,128)(2,1)}, u32[]{:S(2)}, u32[]{:S(2)}) collective-permute-start(bf16[224,2,84,84]{0,1,3,2:T(2,128)(2,1)} %copy.409), channel_id=1, source_target_pairs={{0,16},{1,17},{2,18},{3,19},{4,20},{5,21},{6,22},{7,23},{8,24},{9,... | collective-permute-start | bytes 18966536 | tf_op jit(solution)/shard_map/ppermute | solution.py:18
  3227.5 148.5 %collective-permute-start.2 = (bf16[16]{0:T(256)(128)(2,1)S(1)}, bf16[16]{0:T(256)(128)(2,1)S(1)}, u32[]{:S(2)}, u32[]{:S(2)}) collective-permute-start(bf16[16]{0:T(256)(128)(2,1)S(1)} %slice.248), channel_id=1, source_target_pairs={{0,16},{1,17},{2,18},{3,19},{4,20},{5,21},{6,22},{7,23},{8,24},{9,... | collective-permute-start | bytes 104 | tf_op jit(solution)/shard_map/ppermute | solution.py:18
  3228.9 152.0 %collective-permute-start.4 = (bf16[32]{0:T(256)(128)(2,1)S(1)}, bf16[32]{0:T(256)(128)(2,1)S(1)}, u32[]{:S(2)}, u32[]{:S(2)}) collective-permute-start(bf16[32]{0:T(256)(128)(2,1)S(1)} %slice.252), channel_id=1, source_target_pairs={{0,16},{1,17},{2,18},{3,19},{4,20},{5,21},{6,22},{7,23},{8,24},{9,... | collective-permute-start | bytes 200 | tf_op jit(solution)/shard_map/ppermute | solution.py:18
  3230.2 152.5 %collective-permute-start.6 = (bf16[32]{0:T(256)(128)(2,1)S(1)}, bf16[32]{0:T(256)(128)(2,1)S(1)}, u32[]{:S(2)}, u32[]{:S(2)}) collective-permute-start(bf16[32]{0:T(256)(128)(2,1)S(1)} %slice.256), channel_id=1, source_target_pairs={{0,16},{1,17},{2,18},{3,19},{4,20},{5,21},{6,22},{7,23},{8,24},{9,... | collective-permute-start | bytes 200 | tf_op jit(solution)/shard_map/ppermute | solution.py:18
  3263.8 120.0 %all-to-all-start = ((f32[16,1,28]{2,1,0:T(1,128)}), f32[16,1,28]{2,1,0:T(1,128)S(1)}, u32[]{:S(2)}, u32[]{:S(2)}) async-start(f32[16,1,28]{2,1,0:T(1,128)} %bitcast.52), calls=%async_computation | async-start | bytes 16384 | tf_op jit(solution)/shard_map/all_to_all | solution.py:336
  3376.0 7.2 collective-permute-start.8
  3380.9 5.6 collective-permute-start.10
  3383.8 3.9 collective-permute-start.12
  3388.4 9.0 copy-start.24
  3388.4 10.3 copy-start.20
  3392.2 8.2 copy-start.23
  3392.4 47.0 %collective-permute-start.7 = (bf16[3136,256]{1,0:T(8,128)(2,1)S(1)}, bf16[3136,256]{1,0:T(8,128)(2,1)S(1)}, u32[]{:S(2)}, u32[]{:S(2)}) collective-permute-start(bf16[3136,256]{1,0:T(8,128)(2,1)S(1)} %slice.486), channel_id=1, source_target_pairs={{0,16},{1,17},{2,18},{3,19},{4,20},{5,21},{6,22},{7,23},{8,24},{9,... | collective-permute-start | bytes 4816904 | tf_op jit(solution)/shard_map/ppermute | solution.py:18
  3397.4 34.4 collective-permute-start.3
  3399.0 39.3 %collective-permute-start.9 = (bf16[256,918]{0,1:T(8,128)(2,1)S(1)}, bf16[256,918]{0,1:T(8,128)(2,1)S(1)}, u32[]{:S(2)}, u32[]{:S(2)}) collective-permute-start(bf16[256,918]{0,1:T(8,128)(2,1)S(1)} %slice.487), channel_id=1, source_target_pairs={{0,16},{1,17},{2,18},{3,19},{4,20},{5,21},{6,22},{7,23},{8,24},{9,... | collective-permute-start | bytes 1410056 | tf_op jit(solution)/shard_map/ppermute | solution.py:18
  3400.4 37.2 %collective-permute-start.5 = (bf16[3,3,64,32]{2,3,1,0:T(8,128)(2,1)S(1)}, bf16[3,3,64,32]{2,3,1,0:T(8,128)(2,1)S(1)}, u32[]{:S(2)}, u32[]{:S(2)}) collective-permute-start(bf16[3,3,64,32]{2,3,1,0:T(8,128)(2,1)S(1)} %slice.488), channel_id=1, source_target_pairs={{0,16},{1,17},{2,18},{3,19},{4,20},{5,21},{6,22},{7,23},{8,24},{9,... | collective-permute-start | bytes 110600 | tf_op jit(solution)/shard_map/ppermute | solution.py:18
  (47 other events, 208.9 us)
Sparse Core Ops, SparseCore 0:
  3076.1 181.2 all-reduce.21
where the time goes:
time: 3570 us; the launch traced here: 3500 us
  local copies, waits for them, and re-layouts  2520 us (71%)
  other arithmetic  387 us (11%)
  matrix products  317 us (9%)
  waiting for transfers between devices  145 us (4%)
  blocking collectives  70.4 us (2%)
    another operation x48, local copies, waits for them, and re-layouts, gather_cells(): jnp.stack(windows, axis=3)  755 us
    reshape x16, local copies, waits for them, and re-layouts, gather_cells(): jnp.stack(windows, axis=3)  358 us
    another operation x16, other arithmetic, gather_cells(): jnp.stack(windows, axis=3)  174 us
    dot_general x16, local copies, waits for them, and re-layouts, dot_first(): lax.dot_general(left_arr, right_arr, (((0,), (0,)), ((), ())), preferred_...  158 us
    squeeze x12, local copies, waits for them, and re-layouts, spread_cells(): portion = shaped[:, :, :, row_off * kernel_reach + col_off, :]  149 us
    ppermute x13, waiting for transfers between devices, shifted(): return lax.ppermute(block, axis, route)  145 us
    dynamic_slice x16, local copies, waits for them, and re-layouts, local(): lax.map(lambda rows_in: forward_block(rows_in, weights, matrices), frame_...  136 us
    dot_general x20, matrix products, dot_last(): lax.dot_general(left_arr, right_arr, (((1,), (1,)), ((), ())), preferred_...  128 us
  transfers between devices with their start and end apart: 15, of which 4 were waited for; matrix products, arithmetic and copies ran while one was open for 4% of the time, Pallas kernels for 0%

commit v1 on v0

v1 whole, which is shorter than its diff:
```python
import functools

import jax
import jax.numpy as jnp
from jax import lax
from jax.experimental import pallas as pl
from jax.experimental.pallas import tpu as pltpu
from jax.sharding import PartitionSpec as P

ACT = 18
ATOMS = 51
LOGITS = ACT * ATOMS
LOSS_SCALE = 256
LANES = 256
BF = jnp.bfloat16
F32 = jnp.float32
VMEM_BIG = 60 << 20


def call(kernel, out, ins, outs, grid=None, scratch=(), flops=0, nbytes=0):
    return pl.pallas_call(
        kernel,
        out_shape=out,
        grid=() if grid is None else grid,
        in_specs=ins,
        out_specs=outs,
        scratch_shapes=list(scratch),
        compiler_params=pltpu.CompilerParams(vmem_limit_bytes=VMEM_BIG),
        cost_estimate=pl.CostEstimate(flops=flops, bytes_accessed=nbytes, transcendentals=0),
    )


def whole(shape):
    return pl.BlockSpec(shape, lambda *_: (0,) * len(shape))


def sds(shape, dtype):
    return jax.ShapeDtypeStruct(shape, dtype)


def dot(left, right):
    return jnp.dot(left, right, preferred_element_type=F32)


def dot_nt(left, right):
    return lax.dot_general(left, right, (((1,), (1,)), ((), ())), preferred_element_type=F32)


def act_slope(half):
    tan = jnp.tanh(half)
    up = 1.0 + tan
    act = half * up
    return act, up + act * (1.0 - tan)


def bands_kernel(k1t, b1c, k2t, k3t, b3c, k2n, k3n, k1h, t1, t2, t3, t3b, t2b, t1b, w1, w2, w3, w3b, w2b, w1b):
    for ref in (w1, w2, w3, w3b, w2b, w1b):
        ref[...] = jnp.zeros_like(ref)
    for jj in range(10):
        for dy in range(8):
            w1[32 * jj : 32 * jj + 32, 176 * dy + 16 * jj : 176 * dy + 16 * jj + 32] = k1t[:, 32 * dy : 32 * dy + 32]
        w1[32 * jj : 32 * jj + 32, 1408:1409] = b1c[...]
    for jj in range(3):
        for u in range(4):
            w2[64 * jj : 64 * jj + 64, 256 * u + 64 * jj : 256 * u + 64 * jj + 128] = k2t[:, 128 * u : 128 * u + 128]
    for j in range(7):
        for u in range(3):
            w3[64 * j : 64 * j + 64, 576 * u + 64 * j : 576 * u + 64 * j + 192] = k3t[:, 192 * u : 192 * u + 192]
            w3b[64 * j : 64 * j + 192, 448 * (2 - u) + 64 * j : 448 * (2 - u) + 64 * j + 64] = k3n[192 * u : 192 * u + 192, :]
        w3[64 * j : 64 * j + 64, 1728:1729] = b3c[...]
    for e in range(2):
        for t in range(2):
            u = 2 * t + e
            for j in range(6):
                lo = max(0, 2 * j - 2)
                hi = min(10, 2 * j + 2)
                v0 = lo - (2 * j - 2)
                w2b[320 * e + 32 * lo : 320 * e + 32 * hi, 384 * t + 64 * j : 384 * t + 64 * j + 64] = k2n[
                    128 * u + 32 * v0 : 128 * u + 32 * (v0 + hi - lo), :
                ]
    for dy in range(8):
        t, row = divmod(dy, 4)
        for j in range(8):
            lo = max(0, 4 * j - 4)
            hi = min(28, 4 * j + 4)
            d0 = lo - (4 * j - 4)
            w1b[56 * row + 2 * lo : 56 * row + 2 * hi, 256 * t + 32 * j : 256 * t + 32 * j + 32] = k1h[
                dy, 2 * d0 : 2 * (d0 + hi - lo), :
            ]
    t1[...] = (0.5 * w1[...]).astype(BF)
    t2[...] = (0.5 * w2[...]).astype(BF)
    t3[...] = (0.5 * w3[...]).astype(BF)
    t3b[...] = (0.5 * w3b[...]).astype(BF)
    t2b[...] = (0.5 * w2b[...]).astype(BF)
    t1b[...] = w1b[...].astype(BF)


def bands(k1, b1, k2, k3, b3, k1_half):
    f = lambda a: a.astype(F32)
    ins = (
        f(k1).transpose(3, 0, 1, 2).reshape(32, 256),
        f(b1)[:, None],
        f(k2).transpose(3, 0, 1, 2).reshape(64, 512),
        f(k3).transpose(3, 0, 1, 2).reshape(64, 576),
        f(b3)[:, None],
        f(k2).reshape(512, 64),
        f(k3).reshape(576, 64),
        f(k1_half).reshape(8, 16, 32),
    )
    shapes = ((320, 1424), (192, 1024), (448, 1744), (576, 1344), (640, 768), (224, 512))
    return call(
        bands_kernel,
        tuple(sds(s, BF) for s in shapes),
        [whole(a.shape) for a in ins],
        [whole(s) for s in shapes],
        scratch=[pltpu.VMEM(s, F32) for s in shapes],
        nbytes=6_000_000,
    )(*ins)


def conv1_kernel(rows, x_ref, t1_ref, ones_ref, a_ref, s_ref, xt_ref, cells):
    c = pl.program_id(0)
    slot = lax.rem(c, 2)

    @pl.when(c == 0)
    def _():
        cells[...] = jnp.zeros_like(cells)

    for dy in range(4):
        flat = x_ref[dy].reshape(336, rows)
        cells[slot, dy, :, :rows] = flat
        xt_ref[dy, :, :] = cells[slot, dy]

    @pl.when(c > 0)
    def _():
        for g in range(2):
            window = pl.ds(160 * g, 176)
            parts = [cells[1 - slot, dy, window, :] for dy in range(4)]
            parts += [cells[slot, dy, window, :] for dy in range(4)]
            half = dot(t1_ref[...], jnp.concatenate(parts + [ones_ref[...]], axis=0))
            act, slope = act_slope(half)
            a_ref[0, 320 * g : 320 * g + 320, :] = act.astype(BF)
            s_ref[0, 320 * g : 320 * g + 320, :] = slope.astype(BF)


def conv1(xv, t1, ones):
    rows = xv.shape[3]

    def out_map(c):
        i = jnp.maximum(c - 1, 0)
        return (lax.rem(i, 2), 0, i // 2)

    out = pl.BlockSpec((1, 640, LANES), out_map)
    return call(
        functools.partial(conv1_kernel, rows),
        (sds((2, 640, 10 * LANES), BF), sds((2, 640, 10 * LANES), BF), sds((4, 336, 21 * LANES), BF)),
        [pl.BlockSpec((4, 84, 4, rows), lambda c: (c, 0, 0, 0)), whole((320, 1424)), whole((16, LANES))],
        [out, out, pl.BlockSpec((4, 336, LANES), lambda c: (0, 0, c))],
        grid=(21,),
        scratch=[pltpu.VMEM((2, 4, 336, LANES), BF)],
        flops=2 * 40 * 320 * 1424 * LANES,
        nbytes=42_000_000,
    )(xv, t1, ones)


def conv2_kernel(r0_ref, r1_ref, t2_ref, b2_ref, a_ref, s_ref):
    for g in range(3):
        window = pl.ds(192 * g, 256)
        parts = [r0_ref[0, window, :], r0_ref[1, window, :], r1_ref[0, window, :], r1_ref[1, window, :]]
        half = dot(t2_ref[...], jnp.concatenate(parts, axis=0)) + b2_ref[...]
        act, slope = act_slope(half)
        a_ref[192 * g : 192 * g + 192, :] = act.astype(BF)
        s_ref[192 * g : 192 * g + 192, :] = slope.astype(BF)


def conv2(a1, t2, b2):
    out = pl.BlockSpec((576, LANES), lambda i: (0, i))
    return call(
        conv2_kernel,
        (sds((576, 9 * LANES), BF), sds((576, 9 * LANES), BF)),
        [
            pl.BlockSpec((2, 640, LANES), lambda i: (0, 0, i)),
            pl.BlockSpec((2, 640, LANES), lambda i: (0, 0, i + 1)),
            whole((192, 1024)),
            whole((192, 1)),
        ],
        [out, out],
        grid=(9,),
        flops=2 * 27 * 192 * 1024 * LANES,
        nbytes=18_000_000,
    )(a1, a1, t2, b2)


def conv3_kernel(r0_ref, r1_ref, r2_ref, t3_ref, ones_ref, a_ref, s_ref):
    half = dot(t3_ref[...], jnp.concatenate([r0_ref[...], r1_ref[...], r2_ref[...], ones_ref[...]], axis=0))
    act, slope = act_slope(half)
    a_ref[...] = act.astype(BF)
    s_ref[...] = slope.astype(BF)


def conv3(a2, t3, ones):
    out = pl.BlockSpec((448, LANES), lambda i: (i, 0))
    return call(
        conv3_kernel,
        (sds((3136, LANES), BF), sds((3136, LANES), BF)),
        [pl.BlockSpec((576, LANES), lambda i, u=u: (0, i + u)) for u in range(3)]
        + [whole((448, 1744)), whole((16, LANES))],
        [out, out],
        grid=(7,),
        flops=2 * 7 * 448 * 1744 * LANES,
        nbytes=8_000_000,
    )(a2, a2, a2, t3, ones)


def head_kernel(rows, pd_ref, bd_ref, wh_ref, bh_ref, sel_ref, act_ref, slope_ref, lp_ref, cho_ref, lg_ref):
    act, slope = act_slope((pd_ref[...] + bd_ref[...]) * 0.5)
    act_ref[...] = act.astype(BF)
    slope_ref[...] = slope.astype(BF)
    lg_ref[...] = dot(wh_ref[...], act_ref[...]) + bh_ref[...]
    sel = sel_ref[...]
    pick = jnp.zeros((ATOMS, rows), F32)
    for a in range(ACT):
        pick = jnp.where(sel == a, lg_ref[ATOMS * a : ATOMS * a + ATOMS, :rows], pick)
    shifted = pick - jnp.max(pick, axis=0, keepdims=True)
    grown = jnp.exp(shifted)
    total = jnp.sum(grown, axis=0, keepdims=True)
    cho_ref[...] = (grown / total).astype(BF)
    lp_ref[...] = shifted - jnp.log(total)


def head(pd, bd, wht, bh, sel):
    rows = sel.shape[1]
    ins = (pd, bd, wht, bh, sel)
    outs = (((512, LANES), BF), ((512, LANES), BF), ((ATOMS, rows), F32), ((ATOMS, rows), BF))
    return call(
        functools.partial(head_kernel, rows),
        tuple(sds(*o) for o in outs),
        [whole(a.shape) for a in ins],
        [whole(o[0]) for o in outs],
        scratch=[pltpu.VMEM((LOGITS, LANES), F32)],
        flops=2 * LOGITS * 512 * LANES,
        nbytes=2_000_000,
    )(*ins)


def loss_kernel(rows, cho_ref, done_ref, low_ref, frac_ref, lp_ref, taken_ref, loss_ref, rh_ref, hb_ref, d_ref):
    atoms = lax.broadcasted_iota(jnp.int32, (ATOMS, rows), 0)
    done = done_ref[...].astype(F32)
    mass = (1.0 - done) * cho_ref[...].astype(F32) + done * (atoms == 0).astype(F32)
    frac = frac_ref[...]
    stay = mass * (1.0 - frac)
    move = mass * frac
    low = low_ref[...]
    proj = jnp.zeros((ATOMS, rows), F32)
    for i in range(ATOMS):
        gap = atoms - low[i : i + 1, :]
        proj = proj + jnp.where(gap == 0, stay[i : i + 1, :], jnp.where(gap == 1, move[i : i + 1, :], 0.0))
    lp = lp_ref[...]
    loss_ref[...] = -jnp.sum(proj * lp, axis=0, keepdims=True)
    diff = (jnp.sum(proj, axis=0, keepdims=True) * jnp.exp(lp) - proj) * LOSS_SCALE
    taken = taken_ref[...]
    for a in range(ACT):
        d_ref[ATOMS * a : ATOMS * a + ATOMS, :] = jnp.where(taken == a, diff, 0.0)
    rh_ref[...] = jnp.zeros_like(rh_ref)
    rh_ref[:, :rows] = d_ref[...].astype(BF)
    hb_ref[...] = jnp.sum(d_ref[...], axis=1, keepdims=True) * (1.0 / LOSS_SCALE)


def loss(cho, done, low, frac, lp, taken):
    rows = taken.shape[1]
    ins = (cho, done, low, frac, lp, taken)
    outs = (((1, rows), F32), ((LOGITS, LANES), BF), ((LOGITS, 1), F32))
    return call(
        functools.partial(loss_kernel, rows),
        tuple(sds(*o) for o in outs),
        [whole(a.shape) for a in ins],
        [whole(o[0]) for o in outs],
        scratch=[pltpu.VMEM((LOGITS, rows), F32)],
        nbytes=1_000_000,
    )(*ins)


def dflat_kernel(w_ref, rd_ref, s_ref, r_ref, b_ref):
    @pl.when(pl.program_id(0) == 0)
    def _():
        b_ref[...] = jnp.zeros_like(b_ref)

    diff = dot(w_ref[...], rd_ref[...]) * (0.5 * s_ref[...].astype(F32))
    r_ref[...] = diff.astype(BF)
    b_ref[...] += jnp.sum(diff.reshape(7, 64, LANES), axis=0)


def dflat(wd, rd, s3):
    block = pl.BlockSpec((448, LANES), lambda i: (i, 0))
    return call(
        dflat_kernel,
        (sds((3136, LANES), BF), sds((64, LANES), F32)),
        [pl.BlockSpec((448, 512), lambda i: (i, 0)), whole((512, LANES)), block],
        [block, whole((64, LANES))],
        grid=(7,),
        flops=2 * 3136 * 512 * LANES,
        nbytes=6_500_000,
    )(wd, rd, s3)


def dconv3_kernel(r3_ref, t_ref, s_ref, r_ref, b_ref, pad):
    p = pl.program_id(0)

    @pl.when(p == 0)
    def _():
        b_ref[...] = jnp.zeros_like(b_ref)
        pad[:896, :] = jnp.zeros((896, LANES), BF)
        pad[896:4032, :] = r3_ref[...]
        pad[4032:, :] = jnp.zeros((896, LANES), BF)

    window = pl.ds(pl.multiple_of(448 * p, 64), 1344)
    diff = dot(t_ref[...], pad[window, :]) * s_ref[...].astype(F32)
    r_ref[...] = diff.astype(BF)
    b_ref[...] += jnp.sum(diff.reshape(9, 64, LANES), axis=0)


def dconv3(r3, t3b, s2):
    block = pl.BlockSpec((576, LANES), lambda p: (0, p))
    return call(
        dconv3_kernel,
        (sds((576, 9 * LANES), BF), sds((64, LANES), F32)),
        [whole((3136, LANES)), whole((576, 1344)), block],
        [block, whole((64, LANES))],
        grid=(9,),
        scratch=[pltpu.VMEM((4928, LANES), BF)],
        flops=2 * 9 * 576 * 1344 * LANES,
        nbytes=9_000_000,
    )(r3, t3b, s2)


def dconv2_kernel(cur_ref, prev_ref, t_ref, s_ref, r_ref, b_ref):
    m = pl.program_id(0)

    @pl.when(m == 0)
    def _():
        b_ref[...] = jnp.zeros_like(b_ref)

    none = jnp.zeros((64, LANES), BF)
    cur = jnp.where(m < 9, cur_ref[...], jnp.zeros((576, LANES), BF))
    prev = jnp.where(m > 0, prev_ref[...], jnp.zeros((576, LANES), BF))
    for h in range(2):
        if h == 0:
            parts = [none, cur[:320], none, prev[:320]]
        else:
            parts = [cur[256:], none, prev[256:], none]
        diff = dot(t_ref[...], jnp.concatenate(parts, axis=0))
        for e in range(2):
            rows = slice(320 * h, 320 * h + 320)
            part = diff[320 * e : 320 * e + 320] * s_ref[e, rows, :].astype(F32)
            r_ref[e, rows, :] = part.astype(BF)
            b_ref[...] += jnp.sum(part.reshape(10, 32, LANES), axis=0)


def dconv2(r2, t2b, s1):
    block = pl.BlockSpec((2, 640, LANES), lambda m: (0, 0, m))
    return call(
        dconv2_kernel,
        (sds((2, 640, 10 * LANES), BF), sds((32, LANES), F32)),
        [
            pl.BlockSpec((576, LANES), lambda m: (0, jnp.minimum(m, 8))),
            pl.BlockSpec((576, LANES), lambda m: (0, jnp.maximum(m - 1, 0))),
            whole((640, 768)),
            block,
        ],
        [block, whole((32, LANES))],
        grid=(10,),
        flops=2 * 20 * 640 * 768 * LANES,
        nbytes=16_000_000,
    )(r2, r2, t2b, s1)


def dframes_kernel(rows, flag_ref, own0_ref, own1_ref, got0_ref, got1_ref, t_ref, o_ref):
    c = pl.program_id(0)
    own = flag_ref[0] == 1
    zero = jnp.zeros((640, LANES), BF)
    r0 = jnp.where(c < 20, jnp.where(own, own0_ref[0], got0_ref[0]), zero)
    r1 = jnp.where(c > 0, jnp.where(own, own1_ref[0], got1_ref[0]), zero)
    none = jnp.zeros((32, LANES), BF)
    for g in range(3):
        if g == 0:
            parts = [none, r0[:224], none, r1[:224]]
        elif g == 1:
            parts = [r0[192:448], r1[192:448]]
        else:
            parts = [r0[416:], none, r1[416:], none]
        out = dot(t_ref[...], jnp.concatenate(parts, axis=0)).astype(BF)
        for dy in range(4):
            o_ref[dy, 28 * g : 28 * g + 28, :, :] = out[56 * dy : 56 * dy + 56, :rows].reshape(28, 2, rows)


def dframes(flag, own, got, t1b, rows):
    def place(i):
        return (lax.rem(i, 2), 0, i // 2)

    now = pl.BlockSpec((1, 640, LANES), lambda c, *_: place(jnp.minimum(c, 19)))
    before = pl.BlockSpec((1, 640, LANES), lambda c, *_: place(jnp.maximum(c - 1, 0)))
    return pl.pallas_call(
        functools.partial(dframes_kernel, rows),
        out_shape=sds((84, 84, 2, rows), BF),
        grid_spec=pltpu.PrefetchScalarGridSpec(
            num_scalar_prefetch=1,
            grid=(21,),
            in_specs=[now, before, now, before, pl.BlockSpec((224, 512), lambda c, *_: (0, 0))],
            out_specs=pl.BlockSpec((4, 84, 2, rows), lambda c, *_: (c, 0, 0, 0)),
        ),
        compiler_params=pltpu.CompilerParams(vmem_limit_bytes=VMEM_BIG),
        cost_estimate=pl.CostEstimate(flops=2 * 63 * 224 * 512 * LANES, bytes_accessed=33_000_000, transcendentals=0),
    )(flag, own, own, got, got, t1b)


def wdense_kernel(a_ref, rd_ref, g_ref):
    grad = (dot_nt(a_ref[...], rd_ref[...]) * (1.0 / LOSS_SCALE)).astype(BF)
    for half in range(2):
        for lane in range(2):
            g_ref[0, lane, half] = grad[:, 256 * half + 128 * lane : 256 * half + 128 * lane + 128]


def wdense(a, rd, block):
    return call(
        wdense_kernel,
        sds((8, 2, 2, block, 128), BF),
        [pl.BlockSpec((block, LANES), lambda i: (i, 0)), whole((512, LANES))],
        pl.BlockSpec((1, 2, 2, block, 128), lambda i: (i, 0, 0, 0, 0)),
        grid=(8,),
        flops=2 * 8 * block * 512 * LANES,
        nbytes=5_000_000,
    )(a, rd)


def wconv3_kernel(a_ref, r_ref, g_ref):
    acc = jnp.zeros((576, 64), F32)
    for j in range(7):
        left = jnp.concatenate(
            [a_ref[64 * j : 64 * j + 192, LANES * u : LANES * (u + 7)] for u in range(3)], axis=0
        )
        right = jnp.concatenate([r_ref[448 * i + 64 * j : 448 * i + 64 * j + 64, :] for i in range(7)], axis=1)
        acc = acc + dot_nt(left, right)
    g_ref[...] = acc * (1.0 / LOSS_SCALE)


def wconv3(a2, r3):
    return call(
        wconv3_kernel,
        sds((576, 64), F32),
        [whole(a2.shape), whole(r3.shape)],
        whole((576, 64)),
        flops=2 * 49 * 576 * 64 * LANES,
        nbytes=4_500_000,
    )(a2, r3)


def wconv2_kernel(a_ref, r_ref, g_ref):
    g_ref[...] = jnp.zeros_like(g_ref)

    def body(j, _):
        window = pl.ds(pl.multiple_of(64 * j, 64), 128)
        left = jnp.concatenate(
            [a_ref[e, window, LANES * t : LANES * (t + 9)] for t in range(2) for e in range(2)], axis=0
        )
        g_ref[...] += dot_nt(left, r_ref[pl.ds(pl.multiple_of(64 * j, 64), 64), :])
        return 0

    lax.fori_loop(0, 9, body, 0)
    g_ref[...] = g_ref[...] * (1.0 / LOSS_SCALE)


def wconv2(a1, r2):
    return call(
        wconv2_kernel,
        sds((512, 64), F32),
        [whole(a1.shape), whole(r2.shape)],
        whole((512, 64)),
        flops=2 * 81 * 512 * 64 * LANES,
        nbytes=9_500_000,
    )(a1, r2)


def wconv1_kernel(x_ref, n_ref, r_ref, g_ref, acc):
    step = pl.program_id(0)

    @pl.when(step == 0)
    def _():
        acc[...] = jnp.zeros_like(acc)

    def column(dy, rows, c):
        if c < 4:
            return x_ref[dy, rows, LANES * c : LANES * (c + 1)]
        return n_ref[dy, rows, :]

    total = acc[...]
    for g in range(5):
        rows = slice(64 * g, 64 * g + 80)
        left = jnp.concatenate(
            [
                jnp.concatenate([column(dy, rows, ii + t) for ii in range(4)], axis=1)
                for t in range(2)
                for dy in range(4)
            ],
            axis=0,
        )
        right = jnp.concatenate(
            [r_ref[ii % 2, 128 * g : 128 * g + 128, LANES * (ii // 2) : LANES * (ii // 2 + 1)] for ii in range(4)],
            axis=1,
        )
        total = total + dot_nt(left, right)
    acc[...] = total

    @pl.when(step == 4)
    def _():
        for dy in range(8):
            part = jnp.zeros((32, 32), F32)
            for jj in range(4):
                part = part + acc[80 * dy + 16 * jj : 80 * dy + 16 * jj + 32, 32 * jj : 32 * jj + 32]
            g_ref[32 * dy : 32 * dy + 32, :] = part * (1.0 / LOSS_SCALE)


def wconv1(xt, r1):
    return call(
        wconv1_kernel,
        sds((256, 32), F32),
        [
            pl.BlockSpec((4, 336, 4 * LANES), lambda s: (0, 0, s)),
            pl.BlockSpec((4, 336, LANES), lambda s: (0, 0, 4 * s + 4)),
            pl.BlockSpec((2, 640, 2 * LANES), lambda s: (0, 0, s)),
        ],
        whole((256, 32)),
        grid=(5,),
        scratch=[pltpu.VMEM((640, 128), F32)],
        flops=2 * 100 * 640 * 128 * LANES,
        nbytes=21_000_000,
    )(xt, xt, r1)


def to_chunks(grad, devices):
    split = devices // 16
    n = grad.shape[3] // split
    parts = grad.reshape(8, 2, 2, split, n, 128).transpose(0, 3, 1, 2, 4, 5)
    return parts.reshape(devices, 2, n, 128)


def from_chunks(parts):
    devices, n = parts.shape[0], parts.shape[1]
    return parts.reshape(devices // 2, 2, n, 128).transpose(0, 2, 1, 3).reshape(devices // 2 * n, 256)


def hand(value):
    return lax.ppermute(value, "pair", [(0, 1)])


def local(
    frames,
    kernel_first,
    bias_first,
    kernel_second,
    bias_second,
    kernel_third,
    bias_third,
    dense_weight,
    dense_bias,
    head_weight,
    head_bias,
    taken_actions,
    greedy_actions,
    done_flags,
    bin_lower,
    bin_fraction,
    owner_shard,
):
    online = lax.axis_index("pair") == 0
    shard_count = lax.axis_size("batch")
    rows = frames.shape[1]
    xv = frames[0].transpose(2, 3, 1, 0)
    k1, k2, k3 = kernel_first[0], kernel_second[0], kernel_third[0]
    k1_half = jnp.where(online, k1[:, :, :2], hand(k1[:, :, 2:]))
    ones = jnp.zeros((16, LANES), BF).at[0].set(1)
    t1, t2, t3, t3b, t2b, t1b = bands(k1, bias_first[0], k2, k3, bias_third[0], k1_half)

    a1, s1, xt = conv1(xv, t1, ones)
    b2 = jnp.tile(bias_second[0].astype(F32) * 0.5, 3)[:, None]
    a2, s2 = conv2(a1, t2, b2)
    a3, s3 = conv3(a2, t3, ones)
    wd = dense_weight[0]
    wht = head_weight[0].T
    pd = lax.dot_general(wd, a3, (((0,), (0,)), ((), ())), preferred_element_type=F32)
    taken = taken_actions[None, :]
    sel = jnp.where(online, taken, greedy_actions[None, :])
    h, sd, lp, cho = head(pd, dense_bias[0].astype(F32)[:, None], wht, head_bias[0].astype(F32)[:, None], sel)
    cho = lax.ppermute(cho, "pair", [(1, 0)])
    row_loss, rh, hb = loss(cho, done_flags[None, :], bin_lower.T, bin_fraction.T, lp, taken)

    diff_dense = lax.dot_general(wht, rh, (((0,), (0,)), ((), ())), preferred_element_type=F32)
    diff_dense = diff_dense * (0.5 * sd.astype(F32))
    rd = diff_dense.astype(BF)
    dense_bias_grad = jnp.sum(diff_dense, axis=1) * (1.0 / LOSS_SCALE)

    g_dense = wdense(a3, rd, 392)
    g_head = wdense(rh, h, 120)
    chunks = jnp.concatenate([to_chunks(g_dense, shard_count), to_chunks(g_head, shard_count)], axis=2)
    cut = g_dense.shape[3] * 16 // shard_count
    summed = lax.psum_scatter(chunks, "batch", scatter_dimension=0, tiled=False)
    mine = jnp.where(online, summed[0], hand(summed[1]))
    gathered = lax.all_gather(mine, "batch", axis=0, tiled=False)

    r3, b3g = dflat(wd, rd, s3)
    r2, b2g = dconv3(r3, t3b, s2)
    r1, b1g = dconv2(r2, t2b, s1)
    got = hand(r1)
    g3 = wconv3(a2, r3)
    g2 = wconv2(a1, r2)
    g1 = wconv1(xt, r1)
    scale = 1.0 / LOSS_SCALE
    small = (
        g1,
        jnp.sum(b1g, axis=1) * scale,
        g2,
        jnp.sum(b2g, axis=1) * scale,
        g3,
        jnp.sum(b3g, axis=1) * scale,
        dense_bias_grad,
        hb[:, 0],
    )
    small = lax.psum(small, "batch")
    small = [
        small[0].reshape(8, 8, 4, 32),
        small[1],
        small[2].reshape(4, 4, 32, 64),
        small[3],
        small[4].reshape(3, 3, 64, 64),
        small[5],
        small[6],
        small[7],
    ]
    dims = (0, 0, 0, 0, 3, 0, 0, 0)
    lower = [lax.slice_in_dim(v, 0, v.shape[d] // 2, axis=d) for v, d in zip(small, dims)]
    upper = [lax.slice_in_dim(v, v.shape[d] // 2, v.shape[d], axis=d) for v, d in zip(small, dims)]

    owner = owner_shard[:, 0]
    capacity = 2 * ((rows + shard_count - 1) // shard_count)
    earlier = jnp.arange(rows)[:, None] < jnp.arange(rows)[None, :]
    slot = jnp.sum(((owner[:, None] == owner[None, :]) & earlier).astype(jnp.int32), axis=0)
    owner_hot = (jnp.arange(shard_count)[:, None] == owner[None, :]).astype(F32)
    slot_hot = (slot[:, None] == jnp.arange(capacity)[None, :]).astype(F32)
    outgoing = jnp.dot(owner_hot * row_loss, slot_hot, precision=lax.Precision.HIGHEST)
    incoming = lax.all_to_all(outgoing, "batch", split_axis=0, concat_axis=0, tiled=True)
    upper.append(incoming[:, capacity // 2 :])
    lower.append(incoming[:, : capacity // 2])

    flat = hand(jnp.concatenate([v.astype(BF).reshape(-1) for v in upper]))
    finals = []
    start = 0
    for low_part in lower:
        size = low_part.size
        far = flat[start : start + size].reshape(low_part.shape).astype(F32)
        finals.append(jnp.where(online, low_part, far))
        start += size

    flag = online.astype(jnp.int32)[None]
    frame_out = dframes(flag, r1, got, t1b, rows).transpose(3, 2, 0, 1)
    dense_out = from_chunks(gathered[:, :cut]).astype(F32)
    head_out = from_chunks(gathered[:, cut:])[:LOGITS].astype(F32).T
    return (
        finals[0],
        finals[1],
        finals[2],
        finals[3],
        finals[4],
        finals[5],
        dense_out,
        finals[6],
        head_out,
        finals[7],
        frame_out,
        finals[8][None],
    )


def solution(mesh):
    return jax.shard_map(
        local,
        mesh=mesh,
        in_specs=(
            P("pair", "batch", None, None, None),
            P("pair", None, None, None, None),
            P("pair", None),
            P("pair", None, None, None, None),
            P("pair", None),
            P("pair", None, None, None, None),
            P("pair", None),
            P("pair", None, None),
            P("pair", None),
            P("pair", None, None),
            P("pair", None),
            P("batch"),
            P("batch"),
            P("batch"),
            P("batch", None),
            P("batch", None),
            P("batch", None),
        ),
        out_specs=(
            P("pair", None, None, None),
            P("pair"),
            P("pair", None, None, None),
            P("pair"),
            P(None, None, None, "pair"),
            P("pair"),
            P(None, "pair"),
            P("pair"),
            P("pair", None),
            P("pair"),
            P("batch", "pair", None, None),
            P("batch", None, "pair"),
        ),
        check_vma=False,
    )
```

time: 3570 us -> 412 us (0.12); the launches traced: 3500 us -> 409 us
  local copies, waits for them, and re-layouts: 2520 us -> 21 us
  other arithmetic: 387 us -> 22.5 us
  matrix products: 317 us -> 7.07 us
  Pallas kernels: 0 us -> 156 us
  waiting for transfers between devices: 145 us -> 103 us
    another operation x53 -> x2, local copies, waits for them, and re-layouts: 830 us -> 0.78 us  [local(): b2 = jnp.tile(bias_second[0].astype(F32) * 0.5, 3)[:, None]]
    reshape x28 -> x5, local copies, waits for them, and re-layouts: 431 us -> 2.48 us  [the longest x1 0.8 us: bands(): f(k3).transpose(3, 0, 1, 2).reshape(64, 576)]
    dot_general x62 -> x3, matrix products: 317 us -> 7.07 us  [the longest x1 3.61 us: local(): lax.dot_general(wd, a3, (((0,), (0,)), ((), ())), preferred_element_type=...]
    another operation x21 -> x6, other arithmetic: 175 us -> 0.67 us  [the longest x1 0.66 us: local(): b2 = jnp.tile(bias_second[0].astype(F32) * 0.5, 3)[:, None]]
    convert_element_type x40 -> x11, local copies, waits for them, and re-layouts: 165 us -> 5.45 us  [the longest x1 1.65 us: local(): dense_out = from_chunks(gathered[:, :cut]).astype(F32)]
    dot_general x18 -> x0, local copies, waits for them, and re-layouts: 159 us -> none  [the longest x16 158 us: dot_first(): lax.dot_general(left_arr, right_arr, (((0,), (0,)), ((), ())), preferred_...]
    dynamic_slice x24 -> x0, local copies, waits for them, and re-layouts: 158 us -> none  [the longest x16 136 us: local(): lax.map(lambda rows_in: forward_block(rows_in, weights, matrices), frame_...]
    pallas_call x0 -> x15, Pallas kernels: none -> 156 us  [the longest x1 28 us: conv1(): call(functools.partial(conv1_kernel, rows), (sds((2, 640, 10 * LANES), BF...]
  transfers between devices with their start and end apart: 15 -> 9, of which waited for: 4 -> 3; matrix products, arithmetic and copies ran while one was open for 4% -> 7% of each run, Pallas kernels for 0% -> 20%
where the time goes in v1:
time: 412 us; the launch traced here: 409 us
  Pallas kernels  156 us (38%)
  waiting for transfers between devices  103 us (25%)
  blocking collectives  62.1 us (15%)
  starting transfers between devices  22.7 us (6%)
  other arithmetic  22.5 us (5%)
  local copies, waits for them, and re-layouts  21 us (5%)
  between operations  14.1 us (3%)
  matrix products  7.07 us (2%)
    ppermute x4, waiting for transfers between devices, hand(): return lax.ppermute(value, 'pair', [(0, 1)])  98.1 us
    psum x1, blocking collectives, local(): small = lax.psum(small, 'batch')  62.1 us
    pallas_call x1, Pallas kernels, conv1(): call(functools.partial(conv1_kernel, rows), (sds((2, 640, 10 * LANES), BF...  28 us
    pallas_call x1, Pallas kernels, dframes(): pl.pallas_call(functools.partial(dframes_kernel, rows), out_shape=sds((84...  21 us
    ppermute x4, starting transfers between devices, hand(): return lax.ppermute(value, 'pair', [(0, 1)])  15.3 us
    pallas_call x1, Pallas kernels, wconv1(): call(wconv1_kernel, sds((256, 32), F32), [pl.BlockSpec((4, 336, 4 * LANES...  13.8 us
    pallas_call x1, Pallas kernels, dconv2(): call(dconv2_kernel, (sds((2, 640, 10 * LANES), BF), sds((32, LANES), F32)...  13.3 us
    pallas_call x2, Pallas kernels, wdense(): call(wdense_kernel, sds((8, 2, 2, block, 128), BF), [pl.BlockSpec((block,...  12.7 us
  transfers between devices with their start and end apart: 9, of which 3 were waited for; matrix products, arithmetic and copies ran while one was open for 7% of the time, Pallas kernels for 20%

profile of v1, /device:TPU:0, one launch (start us, length us, event | category | flops | bytes accessed | tf_op | source)
XLA Modules:
  0.0 408.6 jit_solution(15255089563038058192)
XLA Ops:
  7.2 0.9 slice.172
  8.1 4.8 %collective-permute-start = (bf16[8,8,2,32]{3,2,1,0:T(2,128)(2,1)S(1)}, bf16[8,8,2,32]{3,2,1,0:T(2,128)(2,1)S(1)}, u32[]{:S(2)}, u32[]{:S(2)}) collective-permute-start(bf16[8,8,2,32]{3,2,1,0:T(2,128)(2,1)S(1)} %slice.172), channel_id=1, source_target_pairs={{0,16},{1,17},{2,18},{3,19},{4,20},{5,21},{6,22},{7,23},{8,24},{9,... | collective-permute-start | bytes 24584 | tf_op jit(solution)/shard_map/ppermute | solution.py:552
  13.0 0.9 bitcast_convert_fusion.4
  13.8 0.7 bitcast_convert_fusion.3
  14.5 0.7 multiply_bitcast_fusion
  15.1 0.7 bitcast_convert_fusion.1
  15.8 0.7 bitcast_convert_fusion
  16.5 1.2 broadcast_select_fusion.6
  17.8 0.7 bitcast_convert_fusion.2
  18.4 0.7 copy.80.b1c
  19.1 0.7 copy.83.b3c
  19.8 0.8 broadcast_in_dim_tile.4.b2_ref
  20.6 0.7 copy.79.k1t
  21.3 0.8 copy.86.bd_ref
  22.1 0.9 reshape.216
  23.0 0.8 copy.81.k2t
  23.8 0.9 reshape.218
  24.8 0.8 copy.82.k3t
  25.6 1.0 copy.87.bh_ref
  26.6 0.9 broadcast_select_fusion.1
  28.1 5.5 %shard_map.256 = (bf16[320,1424]{1,0:T(8,128)(2,1)}, bf16[192,1024]{1,0:T(8,128)(2,1)}, bf16[448,1744]{1,0:T(8,128)(2,1)}, bf16[576,1344]{1,0:T(8,128)(2,1)}, bf...) custom-call(f32[32,256]{1,0:T(8,128)} %copy.79.k1t, f32[32,1]{1,0:T(8,128)} %copy.80.b1c, f32[64,512]{1,0:T(8,128)} %copy.81.k2t, ...), custom_call_target="tpu_custom_call" | custom-call | bytes 6000000 | tf_op jit(solution)/shard_map/pallas_call | solution.py:111
  33.6 28.0 %shard_map.257 = (bf16[2,640,2560]{2,1,0:T(8,128)(2,1)}, bf16[2,640,2560]{2,1,0:T(8,128)(2,1)}, bf16[4,336,5376]{2,1,0:T(8,128)(2,1)}) custom-call(bf16[84,84,4,224]{3,2,1,0:T(4,128)(2,1)} %bitcast.140, bf16[320,1424]{1,0:T(8,128)(2,1)} %get-tuple-element.50.t1_ref, bf16[16,256]{1,0:T(8,128)(2,1)} %constant.45.clone.1.ones_ref), custom_call_target="tpu_custom_call" | custom-call | flops 9332326400 | bytes 42000000 | tf_op jit(solution)/shard_map/pallas_call | solution.py:154
  61.7 11.3 %shard_map.258 = (bf16[576,2304]{1,0:T(8,128)(2,1)}, bf16[576,2304]{1,0:T(8,128)(2,1)}) custom-call(bf16[2,640,2560]{2,1,0:T(8,128)(2,1)} %get-tuple-element.52.r0_ref.r1_ref.a_ref, bf16[2,640,2560]{2,1,0:T(8,128)(2,1)} %get-tuple-element.52.r0_ref.r1_ref.a_ref, bf16[192,1024]{1,0:T(8,128)(2,1)} %get-tuple-element.53.t2_ref, ...), custom_call_target="tpu_custom_call" | custom-call | flops 2717908992 | bytes 18000000 | tf_op jit(solution)/shard_map/pallas_call | solution.py:178
  73.0 9.2 %shard_map.259 = (bf16[3136,256]{1,0:T(8,128)(2,1)}, bf16[3136,256]{1,0:T(8,128)(2,1)}) custom-call(bf16[576,2304]{1,0:T(8,128)(2,1)} %get-tuple-element.54.r0_ref.r1_ref.r2_ref.a_ref, bf16[576,2304]{1,0:T(8,128)(2,1)} %get-tuple-element.54.r0_ref.r1_ref.r2_ref.a_ref, bf16[576,2304]{1,0:T(8,128)(2,1)} %get-tuple-element.54.r0_ref.r1_ref.r2_ref.a_ref, ...), custom_call_target="tpu_custom_call" | custom-call | flops 2800222208 | bytes 8000000 | tf_op jit(solution)/shard_map/pallas_call | solution.py:203
  82.2 3.6 convolution_bitcast_fusion.1.pd_ref
  85.8 2.9 shard_map.260
  88.7 1.3 collective-permute-start.1
  90.0 4.7 %collective-permute-done.1.cho_ref = bf16[51,224]{1,0:T(8,128)(2,1)S(1)} collective-permute-done((bf16[51,224]{1,0:T(8,128)(2,1)}, bf16[51,224]{1,0:T(8,128)(2,1)S(1)}, u32[]{:S(2)}, u32[]{:S(2)}) %collective-permute-start.1) | collective-permute-done | bytes 22880 | tf_op jit(solution)/shard_map/ppermute | solution.py:593
  95.3 2.8 shard_map.261
  98.1 2.6 fusion.13
  100.7 5.8 %shard_map.269 = bf16[8,2,2,120,128]{4,3,2,1,0:T(8,128)(2,1)} custom-call(bf16[918,256]{1,0:T(8,128)(2,1)} %get-tuple-element.59.a_ref, bf16[512,256]{1,0:T(8,128)(2,1)} %get-tuple-element.74.rd_ref), custom_call_target="tpu_custom_call" | custom-call | flops 251658240 | bytes 5000000 | tf_op jit(solution)/shard_map/pallas_call | solution.py:424
  106.5 7.0 %shard_map.268 = bf16[8,2,2,392,128]{4,3,2,1,0:T(8,128)(2,1)} custom-call(bf16[3136,256]{1,0:T(8,128)(2,1)} %get-tuple-element.56.a_ref, bf16[512,256]{1,0:T(8,128)(2,1)} %get-tuple-element.145.rd_ref), custom_call_target="tpu_custom_call" | custom-call | flops 822083584 | bytes 5000000 | tf_op jit(solution)/shard_map/pallas_call | solution.py:424
  113.5 4.5 %pad_maximum_fusion = bf16[16,2,512,128]{3,2,1,0:T(8,128)(2,1)} fusion(bf16[16,2,120,128]{3,2,1,0:T(8,128)(2,1)S(1)} %bitcast.109, bf16[16,2,392,128]{3,2,1,0:T(8,128)(2,1)} %bitcast.106), kind=kLoop, calls=%fused_computation | loop fusion | flops 8388608 | bytes 8388608 | tf_op jit(solution)/shard_map/concatenate | solution.py:603
  118.0 6.8 %shard_map.262 = (bf16[3136,256]{1,0:T(8,128)(2,1)}, f32[64,256]{1,0:T(8,128)}) custom-call(bf16[3136,512]{1,0:T(8,128)(2,1)} %bitcast.110, bf16[512,256]{1,0:T(8,128)(2,1)} %get-tuple-element.145.rd_ref, bf16[3136,256]{1,0:T(8,128)(2,1)} %get-tuple-element.61.s_ref), custom_call_target="tpu_custom_call" | custom-call | flops 822083584 | bytes 6500000 | tf_op jit(solution)/shard_map/pallas_call | solution.py:295
  124.7 10.8 %shard_map.263 = (bf16[576,2304]{1,0:T(8,128)(2,1)}, f32[64,256]{1,0:T(8,128)}) custom-call(bf16[3136,256]{1,0:T(8,128)(2,1)} %get-tuple-element.62.r3_ref.r_ref, bf16[576,1344]{1,0:T(8,128)(2,1)} %get-tuple-element.63.t_ref, bf16[576,2304]{1,0:T(8,128)(2,1)} %get-tuple-element.64.s_ref), custom_call_target="tpu_custom_call" | custom-call | flops 3567255552 | bytes 9000000 | tf_op jit(solution)/shard_map/pallas_call | solution.py:324
  135.5 13.3 %shard_map.264 = (bf16[2,640,2560]{2,1,0:T(8,128)(2,1)}, f32[32,256]{1,0:T(8,128)}) custom-call(bf16[576,2304]{1,0:T(8,128)(2,1)} %get-tuple-element.65.cur_ref.prev_ref.r_ref, bf16[576,2304]{1,0:T(8,128)(2,1)} %get-tuple-element.65.cur_ref.prev_ref.r_ref, bf16[640,768]{1,0:T(8,128)(2,1)} %get-tuple-element.66.t_ref, ...), custom_call_target="tpu_custom_call" | custom-call | flops 5033164800 | bytes 16000000 | tf_op jit(solution)/shard_map/pallas_call | solution.py:361
  148.8 4.4 %collective-permute-start.4 = (bf16[2,640,2560]{2,1,0:T(8,128)(2,1)}, bf16[2,640,2560]{2,1,0:T(8,128)(2,1)}, u32[]{:S(2)}, u32[]{:S(2)}) collective-permute-start(bf16[2,640,2560]{2,1,0:T(8,128)(2,1)} %get-tuple-element.68.r_ref.own0_ref.own1_ref), channel_id=1, source_target_pairs={{0,16},{1,17},{2,18},{3,19},{4,20},{5,21},{6,22},{7,23},{8,24},{9,... | collective-permute-start | bytes 19660808 | tf_op jit(solution)/shard_map/ppermute | solution.py:552
  153.3 0.8 fusion.4
  154.1 5.8 %all-to-all-start = ((f32[16,1,28]{2,1,0:T(1,128)}), f32[16,1,28]{2,1,0:T(1,128)S(1)}, u32[]{:S(2)}, u32[]{:S(2)}) async-start(f32[16,1,28]{2,1,0:T(1,128)} %bitcast.34), calls=%async_computation | async-start | bytes 16384 | tf_op jit(solution)/shard_map/all_to_all | solution.py:649
  160.4 0.9 reduce_sum.45
  161.3 6.9 %shard_map.267 = f32[576,64]{1,0:T(8,128)} custom-call(bf16[576,2304]{1,0:T(8,128)(2,1)} %get-tuple-element.54.r0_ref.r1_ref.r2_ref.a_ref, bf16[3136,256]{1,0:T(8,128)(2,1)} %get-tuple-element.62.r3_ref.r_ref), custom_call_target="tpu_custom_call" | custom-call | flops 924844032 | bytes 4500000 | tf_op jit(solution)/shard_map/pallas_call | solution.py:447
  168.2 11.3 %shard_map.266 = f32[512,64]{1,0:T(8,128)} custom-call(bf16[2,640,2560]{2,1,0:T(8,128)(2,1)} %get-tuple-element.52.r0_ref.r1_ref.a_ref, bf16[576,2304]{1,0:T(8,128)(2,1)} %get-tuple-element.65.cur_ref.prev_ref.r_ref), custom_call_target="tpu_custom_call" | custom-call | flops 1358954496 | bytes 9500000 | tf_op jit(solution)/shard_map/pallas_call | solution.py:473
  179.6 13.8 %shard_map.265 = f32[256,32]{1,0:T(8,128)} custom-call(bf16[4,336,5376]{2,1,0:T(8,128)(2,1)} %get-tuple-element.51.x_ref.n_ref, bf16[4,336,5376]{2,1,0:T(8,128)(2,1)} %get-tuple-element.51.x_ref.n_ref, bf16[2,640,2560]{2,1,0:T(8,128)(2,1)} %get-tuple-element.68.r_ref.own0_ref.own1_ref), custom_call_target="tpu_custom_call" | custom-call | flops 4194304000 | bytes 21000000 | tf_op jit(solution)/shard_map/pallas_call | solution.py:523
  193.3 0.9 slice_bitcast_fusion
  194.2 1.3 collective-permute-start.3
  195.6 97.0 %collective-permute-done.3 = bf16[512,128]{1,0:T(8,128)(2,1)S(1)} collective-permute-done((bf16[512,128]{1,0:T(8,128)(2,1)S(1)}, bf16[512,128]{1,0:T(8,128)(2,1)S(1)}, u32[]{:S(2)}, u32[]{:S(2)}) %collective-permute-start.3) | collective-permute-done | bytes 131104 | tf_op jit(solution)/shard_map/ppermute | solution.py:552
  292.6 1.6 fusion.3
  294.4 62.1 %all-reduce = (f32[256,32]{1,0:T(8,128)S(1)}, f32[32]{0:T(128)S(1)}, f32[64]{0:T(128)S(1)}, f32[64]{0:T(128)S(1)}, f32[512]{0:T(512)S(1)}, /*index=5*/f32[918]{0:T(1024)S(1)}) all-reduce(f32[256,32]{1,0:T(8,128)} %shard_map.265, f32[32]{0:T(128)S(1)} %broadcast_multiply_fusion.3, ...), channel_id=1, replica_groups=mesh['pair'=2,'batch'=16] {'batch'}, use_global_device_ids=true, to_apply=%region_0.1 | all-reduce | flops 9782 | bytes 78256 | tf_op jit(solution)/shard_map/psum | solution.py:627
  357.2 0.9 slice.230
  358.2 1.1 slice.229
  359.6 4.8 %collective-permute-start.2 = (bf16[39931]{0:T(1024)(128)(2,1)S(1)}, bf16[39931]{0:T(1024)(128)(2,1)S(1)}, u32[]{:S(2)}, u32[]{:S(2)}) collective-permute-start(bf16[39931]{0:T(1024)(128)(2,1)S(1)} %concatenate.8), channel_id=1, source_target_pairs={{0,16},{1,17},{2,18},{3,19},{4,20},{5,21},{6,22},{7,23},{8,24},{9,... | collective-permute-start | bytes 239594 | tf_op jit(solution)/shard_map/ppermute | solution.py:552
  364.4 0.9 slice.180
  365.3 1.1 collective-permute-done.2
  366.6 0.7 copy.93
  367.7 1.0 slice_select_fusion
  368.7 0.8 copy.92
  371.3 0.7 convert_select_fusion
  372.6 0.7 broadcast_select_fusion
  373.2 21.0 %shard_map.270 = bf16[84,84,2,224]{3,2,1,0:T(2,128)(2,1)} custom-call(s32[1]{0:T(128)} %bitcast.47.flag_ref, bf16[2,640,2560]{2,1,0:T(8,128)(2,1)} %get-tuple-element.68.r_ref.own0_ref.own1_ref, bf16[2,640,2560]{2,1,0:T(8,128)(2,1)} %get-tuple-element.68.r_ref.own0_ref.own1_ref, bf16[2,640,2560]{2,1,0:T(8,128)(2,1)} %collective-permute-done.4.got0_ref.got1_ref, ...), custom_call_target="tpu_custom_call" | custom-call | flops 3699376128 | bytes 33000000 | tf_op jit(solution)/shard_map/pallas_call | solution.py:402
  394.2 1.1 slice.190
  395.3 1.5 slice.188
  397.3 1.0 convert_bitcast_fusion.1
  398.5 1.7 copy.90
  400.2 1.9 copy.100
  (75 shorter events, 6.9 us)
Async XLA Ops:
  7.2 186.1 %reduce-scatter.2.cloned.1.call-start = ((), (), s32[]{:S(2)}) async-start(), calls=%async_computation.2 | async-start | bytes 4456448 | tf_op jit(solution)/shard_map/reduce_scatter | solution.py:605
  8.1 18.5 %collective-permute-start = (bf16[8,8,2,32]{3,2,1,0:T(2,128)(2,1)S(1)}, bf16[8,8,2,32]{3,2,1,0:T(2,128)(2,1)S(1)}, u32[]{:S(2)}, u32[]{:S(2)}) collective-permute-start(bf16[8,8,2,32]{3,2,1,0:T(2,128)(2,1)S(1)} %slice.172), channel_id=1, source_target_pairs={{0,16},{1,17},{2,18},{3,19},{4,20},{5,21},{6,22},{7,23},{8,24},{9,... | collective-permute-start | bytes 24584 | tf_op jit(solution)/shard_map/ppermute | solution.py:552
  23.0 5.1 %copy-start.3 = (f32[1,4,4,32,64]{4,3,2,1,0:T(8,128)}, f32[1,4,4,32,64]{4,3,2,1,0:T(8,128)S(1)}, u32[]{:S(2)}) copy-start(f32[1,4,4,32,64]{4,3,2,1,0:T(8,128)S(1)} %reshape.216) | copy-start | bytes 393220
  24.7 3.4 copy-start.2
  73.0 9.2 %copy-start.1 = (bf16[1,3136,512]{2,1,0:T(8,128)(2,1)S(1)}, bf16[1,3136,512]{2,1,0:T(8,128)(2,1)}, u32[]{:S(2)}) copy-start(bf16[1,3136,512]{2,1,0:T(8,128)(2,1)} %param.26) | copy-start | bytes 9633796
  88.7 6.0 %collective-permute-start.1 = (bf16[51,224]{1,0:T(8,128)(2,1)}, bf16[51,224]{1,0:T(8,128)(2,1)S(1)}, u32[]{:S(2)}, u32[]{:S(2)}) collective-permute-start(bf16[51,224]{1,0:T(8,128)(2,1)} %get-tuple-element.57), channel_id=1, source_target_pairs={{16,0},{17,1},{18,2},{19,3},{20,4},{21,5},{22,6},{23,7},{24,8},{25... | collective-permute-start | bytes 68552 | tf_op jit(solution)/shard_map/ppermute | solution.py:593
  94.7 0.6 copy-start.7
  106.5 7.0 %copy-start = (bf16[8,2,2,120,128]{4,3,2,1,0:T(8,128)(2,1)S(1)}, bf16[8,2,2,120,128]{4,3,2,1,0:T(8,128)(2,1)}, u32[]{:S(2)}) copy-start(bf16[8,2,2,120,128]{4,3,2,1,0:T(8,128)(2,1)} %shard_map.269) | copy-start | bytes 2949124
  135.5 17.7 %copy-start.8 = (s32[224,1]{0,1:T(1,128)S(1)}, s32[224,1]{0,1:T(1,128)}, u32[]{:S(2)}) copy-start(s32[224,1]{0,1:T(1,128)} %param.35) | copy-start | bytes 2692
  135.5 17.8 %copy-start.9 = (f32[1,224]{1,0:T(1,128)S(1)}, f32[1,224]{1,0:T(1,128)}, u32[]{:S(2)}) copy-start(f32[1,224]{1,0:T(1,128)} %get-tuple-element.73) | copy-start | bytes 2692
  135.5 24.7 %copy-start.5 = (f32[64,256]{1,0:T(8,128)S(1)}, f32[64,256]{1,0:T(8,128)}, u32[]{:S(2)}) copy-start(f32[64,256]{1,0:T(8,128)} %get-tuple-element.71) | copy-start | bytes 196612
  135.5 24.8 %copy-start.6 = (f32[64,256]{1,0:T(8,128)S(1)}, f32[64,256]{1,0:T(8,128)}, u32[]{:S(2)}) copy-start(f32[64,256]{1,0:T(8,128)} %get-tuple-element.70) | copy-start | bytes 196612
  148.8 224.4 %collective-permute-start.4 = (bf16[2,640,2560]{2,1,0:T(8,128)(2,1)}, bf16[2,640,2560]{2,1,0:T(8,128)(2,1)}, u32[]{:S(2)}, u32[]{:S(2)}) collective-permute-start(bf16[2,640,2560]{2,1,0:T(8,128)(2,1)} %get-tuple-element.68.r_ref.own0_ref.own1_ref), channel_id=1, source_target_pairs={{0,16},{1,17},{2,18},{3,19},{4,20},{5,21},{6,22},{7,23},{8,24},{9,... | collective-permute-start | bytes 19660808 | tf_op jit(solution)/shard_map/ppermute | solution.py:552
  154.1 202.9 %all-to-all-start = ((f32[16,1,28]{2,1,0:T(1,128)}), f32[16,1,28]{2,1,0:T(1,128)S(1)}, u32[]{:S(2)}, u32[]{:S(2)}) async-start(f32[16,1,28]{2,1,0:T(1,128)} %bitcast.34), calls=%async_computation | async-start | bytes 16384 | tf_op jit(solution)/shard_map/all_to_all | solution.py:649
  160.0 197.2 %all-reduce.4.cloned.1.call-start = ((), (), s32[]{:S(2)}) async-start(), calls=%async_computation.4 | async-start | bytes 1114112 | tf_op jit(solution)/shard_map/psum | solution.py:627
  179.5 214.8 %all-gather.3.cloned.1.call-start = ((), (), s32[]{:S(2)}) async-start(), calls=%async_computation.3 | async-start | bytes 2228224 | tf_op jit(solution)/shard_map/all_gather | solution.py:607
  179.5 114.7 %copy-start.4 = (f32[918,1]{1,0:T(8,128)S(1)}, f32[918,1]{1,0:T(8,128)}, u32[]{:S(2)}) copy-start(f32[918,1]{1,0:T(8,128)} %get-tuple-element.72) | copy-start | bytes 11020
  194.2 98.3 %collective-permute-start.3 = (bf16[512,128]{1,0:T(8,128)(2,1)S(1)}, bf16[512,128]{1,0:T(8,128)(2,1)S(1)}, u32[]{:S(2)}, u32[]{:S(2)}) collective-permute-start(bf16[512,128]{1,0:T(8,128)(2,1)S(1)} %slice_bitcast_fusion), channel_id=1, source_target_pairs={{0,16},{1,17},{2,18},{3,19},{4,20},{5,21},{6,22},{7,23},{8,24},{9,... | collective-permute-start | bytes 393224 | tf_op jit(solution)/shard_map/ppermute | solution.py:552
  359.6 6.8 %collective-permute-start.2 = (bf16[39931]{0:T(1024)(128)(2,1)S(1)}, bf16[39931]{0:T(1024)(128)(2,1)S(1)}, u32[]{:S(2)}, u32[]{:S(2)}) collective-permute-start(bf16[39931]{0:T(1024)(128)(2,1)S(1)} %concatenate.8), channel_id=1, source_target_pairs={{0,16},{1,17},{2,18},{3,19},{4,20},{5,21},{6,22},{7,23},{8,24},{9,... | collective-permute-start | bytes 239594 | tf_op jit(solution)/shard_map/ppermute | solution.py:552
Sparse Core Ops, SparseCore 0:
  118.1 73.0 reduce-scatter.1
  195.6 89.9 all-reduce.3
  294.3 44.3 all-gather.2

commit v2 on v1

v2 whole, which is shorter than its diff:
```python
import functools

import jax
import jax.numpy as jnp
from jax import lax
from jax.experimental import pallas as pl
from jax.experimental.pallas import tpu as pltpu
from jax.sharding import PartitionSpec as P

ACT = 18
ATOMS = 51
LOGITS = ACT * ATOMS
LOSS_SCALE = 256
LANES = 256
BF = jnp.bfloat16
F32 = jnp.float32
VMEM_BIG = 60 << 20
FAR = 6
EARLY = 4
NEAR = ((6, 2), (8, 2))


def cost(us):
    return pl.CostEstimate(flops=int(us * 0.5e9), bytes_accessed=0, transcendentals=0)


def call(kernel, out, ins, outs, us, grid=None, scratch=()):
    return pl.pallas_call(
        kernel,
        out_shape=out,
        grid=() if grid is None else grid,
        in_specs=ins,
        out_specs=outs,
        scratch_shapes=list(scratch),
        compiler_params=pltpu.CompilerParams(vmem_limit_bytes=VMEM_BIG),
        cost_estimate=cost(us),
    )


def whole(shape):
    return pl.BlockSpec(shape, lambda *_: (0,) * len(shape))


def sds(shape, dtype):
    return jax.ShapeDtypeStruct(shape, dtype)


def dot(left, right):
    return jnp.dot(left, right, preferred_element_type=F32)


def dot_nt(left, right):
    return lax.dot_general(left, right, (((1,), (1,)), ((), ())), preferred_element_type=F32)


def act_slope(half):
    tan = jnp.tanh(half)
    up = 1.0 + tan
    act = half * up
    return act, up + act * (1.0 - tan)


def second_bands(k2n, w2b):
    for e in range(2):
        for t in range(2):
            u = 2 * t + e
            for j in range(6):
                lo = max(0, 2 * j - 2)
                hi = min(10, 2 * j + 2)
                v0 = lo - (2 * j - 2)
                w2b[320 * e + 32 * lo : 320 * e + 32 * hi, 384 * t + 64 * j : 384 * t + 64 * j + 64] = k2n[
                    128 * u + 32 * v0 : 128 * u + 32 * (v0 + hi - lo), :
                ]


def bands_kernel(k1, b1, k2, b2, k3, b3, t1, t2, t3, t3b, t2b, b2c, w1, w2, w3, w3b, w2b):
    for ref in (w1, w2, w3, w3b, w2b):
        ref[...] = jnp.zeros_like(ref)

    def turned(kernel, bias):
        flat = kernel[...].astype(F32)
        flat = flat.reshape(-1, flat.shape[-1])
        bias = jnp.broadcast_to(bias[...].astype(F32), (8, flat.shape[1]))
        return flat, flat.T, bias.T[:, :1]

    _, k1t, b1c = turned(k1, b1)
    k2n, k2t, b2t = turned(k2, b2)
    k3n, k3t, b3c = turned(k3, b3)
    for jj in range(10):
        for dy in range(8):
            w1[32 * jj : 32 * jj + 32, 176 * dy + 16 * jj : 176 * dy + 16 * jj + 32] = k1t[:, 32 * dy : 32 * dy + 32]
        w1[32 * jj : 32 * jj + 32, 1408:1409] = b1c
    for jj in range(3):
        for u in range(4):
            w2[64 * jj : 64 * jj + 64, 256 * u + 64 * jj : 256 * u + 64 * jj + 128] = k2t[:, 128 * u : 128 * u + 128]
        b2c[64 * jj : 64 * jj + 64, :] = 0.5 * b2t
    for j in range(7):
        for u in range(3):
            w3[64 * j : 64 * j + 64, 576 * u + 64 * j : 576 * u + 64 * j + 192] = k3t[:, 192 * u : 192 * u + 192]
            w3b[64 * j : 64 * j + 192, 448 * (2 - u) + 64 * j : 448 * (2 - u) + 64 * j + 64] = k3n[192 * u : 192 * u + 192, :]
        w3[64 * j : 64 * j + 64, 1728:1729] = b3c
    second_bands(k2n, w2b)
    t1[...] = (0.5 * w1[...]).astype(BF)
    t2[...] = (0.5 * w2[...]).astype(BF)
    t3[...] = (0.5 * w3[...]).astype(BF)
    t3b[...] = (0.5 * w3b[...]).astype(BF)
    t2b[...] = (0.5 * w2b[...]).astype(BF)


def bands(*ins):
    shapes = ((320, 1424), (192, 1024), (448, 1744), (576, 1344), (640, 768))
    return call(
        bands_kernel,
        tuple(sds(s, BF) for s in shapes) + (sds((192, 1), F32),),
        [whole(a.shape) for a in ins],
        [whole(s) for s in shapes] + [whole((192, 1))],
        scratch=[pltpu.VMEM(s, F32) for s in shapes],
        us=5,
    )(*ins)


def band_frames_kernel(flag_ref, k1, k1_got, k2, k2_got, t1b, t2b, w1b, w2b):
    own = flag_ref[0] == 1
    w1b[...] = jnp.zeros_like(w1b)
    w2b[...] = jnp.zeros_like(w2b)
    half = jnp.where(own, k1[:, :, :2, :].astype(F32), k1_got[...].astype(F32)).reshape(8, 16, 32)
    for dy in range(8):
        t, row = divmod(dy, 4)
        for j in range(8):
            lo = max(0, 4 * j - 4)
            hi = min(28, 4 * j + 4)
            d0 = lo - (4 * j - 4)
            w1b[56 * row + 2 * lo : 56 * row + 2 * hi, 256 * t + 32 * j : 256 * t + 32 * j + 32] = half[
                dy, 2 * d0 : 2 * (d0 + hi - lo), :
            ]
    second_bands(jnp.where(own, k2[...].astype(F32), k2_got[...].astype(F32)).reshape(512, 64), w2b)
    t1b[...] = w1b[...].astype(BF)
    t2b[...] = (0.5 * w2b[...]).astype(BF)


def band_frames(flag, *ins):
    shapes = ((224, 512), (640, 768))
    return call(
        band_frames_kernel,
        tuple(sds(s, BF) for s in shapes),
        [pl.BlockSpec(memory_space=pltpu.SMEM)] + [whole(a.shape) for a in ins],
        [whole(s) for s in shapes],
        scratch=[pltpu.VMEM(s, F32) for s in shapes],
        us=3,
    )(flag, *ins)


def pack_rows(part, n):
    lane = lax.broadcasted_iota(jnp.int32, (n // 4, 128), 1)
    tail = [part[n // 4 * k : n // 4 * (k + 1), 128:] for k in range(4)]
    packed = [jnp.where(lane < 96, tail[k], pltpu.roll(tail[3], 96 - 32 * k, 1)) for k in range(3)]
    return jnp.concatenate([part[:, :128]] + packed, axis=0)


def unpack_rows(packed, n):
    lane = lax.broadcasted_iota(jnp.int32, (n // 4, 128), 1)
    tail = [packed[n + n // 4 * k : n + n // 4 * (k + 1)] for k in range(3)]
    last = pltpu.roll(tail[0], 32, 1)
    last = jnp.where(lane < 32, last, jnp.where(lane < 64, pltpu.roll(tail[1], 64, 1), pltpu.roll(tail[2], 96, 1)))
    return jnp.concatenate([packed[:n], jnp.concatenate(tail + [last], axis=0)], axis=1)


def conv1_kernel(rows, start, packs, x_ref, t1_ref, ones_ref, *rest):
    cells = rest[-1]
    a_ref, s_ref, xt_ref, p_ref = rest[-5:-1]
    c = pl.program_id(0) + start
    slot = lax.rem(c, 2)

    @pl.when(c == start)
    def _():
        cells[...] = jnp.zeros_like(cells)

    for dy in range(4):
        flat = x_ref[dy].reshape(336, rows)
        cells[slot, dy, :, :rows] = flat
        xt_ref[dy, :, :] = cells[slot, dy]

    @pl.when(c > start)
    def _():
        slopes = []
        for g in range(2):
            window = pl.ds(160 * g, 176)
            parts = [cells[1 - slot, dy, window, :] for dy in range(4)]
            parts += [cells[slot, dy, window, :] for dy in range(4)]
            half = dot(t1_ref[...], jnp.concatenate(parts + [ones_ref[...]], axis=0))
            act, slope = act_slope(half)
            a_ref[0, 320 * g : 320 * g + 320, :] = act.astype(BF)
            s_ref[0, 320 * g : 320 * g + 320, :] = slope.astype(BF)
            slopes.append(slope)
        @pl.when(c <= packs)
        def _():
            p_ref[0, 0] = pack_rows(jnp.concatenate(slopes, axis=0), 640).astype(BF)


def conv1(xv, t1, ones, start, stop, before):
    rows = xv.shape[3]
    packs = min(stop, 2 * FAR)

    def place(c):
        i = jnp.maximum(c - 1 + start, start)
        return (lax.rem(i, 2), i // 2)

    out = pl.BlockSpec((1, 640, LANES), lambda c: (place(c)[0], 0, place(c)[1]))
    outs = [out, out, pl.BlockSpec((4, 336, LANES), lambda c: (0, 0, c + start))]
    shapes = [sds((2, 640, 10 * LANES), BF), sds((2, 640, 10 * LANES), BF), sds((4, 336, 21 * LANES), BF)]
    def packed_place(c):
        i = jnp.clip(c - 1, 0, packs - start - 1)
        return (i // 2, lax.rem(i, 2), 0, 0)

    outs.append(pl.BlockSpec((1, 1, 1120, 128), packed_place))
    shapes.append(sds(((packs - start) // 2, 2, 1120, 128), BF))
    return pl.pallas_call(
        functools.partial(conv1_kernel, rows, start, packs),
        out_shape=tuple(shapes),
        grid=(stop - start + 1,),
        in_specs=[pl.BlockSpec((4, 84, 4, rows), lambda c: (c + start, 0, 0, 0)), whole((320, 1424)), whole((16, LANES))]
        + [pl.BlockSpec(memory_space=pl.ANY)] * len(before),
        out_specs=outs,
        scratch_shapes=[pltpu.VMEM((2, 4, 336, LANES), BF)],
        input_output_aliases={3 + n: n for n in range(len(before))},
        compiler_params=pltpu.CompilerParams(vmem_limit_bytes=VMEM_BIG),
        cost_estimate=cost(0.1 * (stop - start)),
    )(xv, t1, ones, *before)


def conv2_kernel(r0_ref, r1_ref, t2_ref, b2_ref, a_ref, s_ref):
    for g in range(3):
        window = pl.ds(192 * g, 256)
        parts = [r0_ref[0, window, :], r0_ref[1, window, :], r1_ref[0, window, :], r1_ref[1, window, :]]
        half = dot(t2_ref[...], jnp.concatenate(parts, axis=0)) + b2_ref[...]
        act, slope = act_slope(half)
        a_ref[192 * g : 192 * g + 192, :] = act.astype(BF)
        s_ref[192 * g : 192 * g + 192, :] = slope.astype(BF)


def conv2(a1, t2, b2):
    out = pl.BlockSpec((576, LANES), lambda i: (0, i))
    return call(
        conv2_kernel,
        (sds((576, 9 * LANES), BF), sds((576, 9 * LANES), BF)),
        [
            pl.BlockSpec((2, 640, LANES), lambda i: (0, 0, i)),
            pl.BlockSpec((2, 640, LANES), lambda i: (0, 0, i + 1)),
            whole((192, 1024)),
            whole((192, 1)),
        ],
        [out, out],
        grid=(9,),
        us=1,
    )(a1, a1, t2, b2)


def conv3_kernel(r0_ref, r1_ref, r2_ref, t3_ref, ones_ref, a_ref, s_ref):
    half = dot(t3_ref[...], jnp.concatenate([r0_ref[...], r1_ref[...], r2_ref[...], ones_ref[...]], axis=0))
    act, slope = act_slope(half)
    a_ref[...] = act.astype(BF)
    s_ref[...] = slope.astype(BF)


def conv3(a2, t3, ones):
    out = pl.BlockSpec((448, LANES), lambda i: (i, 0))
    return call(
        conv3_kernel,
        (sds((3136, LANES), BF), sds((3136, LANES), BF)),
        [pl.BlockSpec((576, LANES), lambda i, u=u: (0, i + u)) for u in range(3)]
        + [whole((448, 1744)), whole((16, LANES))],
        [out, out],
        grid=(7,),
        us=1,
    )(a2, a2, a2, t3, ones)


def head_kernel(rows, pd_ref, bd_ref, wh_ref, bh_ref, sel_ref, act_ref, slope_ref, lp_ref, cho_ref, lg_ref):
    bd = jnp.broadcast_to(bd_ref[...].astype(F32), (8, 512)).T[:, :1]
    bh = jnp.broadcast_to(bh_ref[...].astype(F32), (8, LOGITS)).T[:, :1]
    act, slope = act_slope((pd_ref[...] + bd) * 0.5)
    act_ref[...] = act.astype(BF)
    slope_ref[...] = slope.astype(BF)
    lg_ref[...] = dot(wh_ref[...], act_ref[...]) + bh
    sel = sel_ref[...]
    pick = jnp.zeros((ATOMS, rows), F32)
    for a in range(ACT):
        pick = jnp.where(sel == a, lg_ref[ATOMS * a : ATOMS * a + ATOMS, :rows], pick)
    shifted = pick - jnp.max(pick, axis=0, keepdims=True)
    grown = jnp.exp(shifted)
    total = jnp.sum(grown, axis=0, keepdims=True)
    cho_ref[...] = (grown / total).astype(BF)
    lp_ref[...] = shifted - jnp.log(total)


def head(pd, bd, wht, bh, sel):
    rows = sel.shape[1]
    ins = (pd, bd, wht, bh, sel)
    outs = (((512, LANES), BF), ((512, LANES), BF), ((ATOMS, rows), F32), ((ATOMS, rows), BF))
    return call(
        functools.partial(head_kernel, rows),
        tuple(sds(*o) for o in outs),
        [whole(a.shape) for a in ins],
        [whole(o[0]) for o in outs],
        scratch=[pltpu.VMEM((LOGITS, LANES), F32)],
        us=0.5,
    )(*ins)


def loss_kernel(rows, cho_ref, done_ref, low_ref, frac_ref, lp_ref, taken_ref, loss_ref, rh_ref, hb_ref, d_ref):
    atoms = lax.broadcasted_iota(jnp.int32, (ATOMS, rows), 0)
    done = done_ref[...].astype(F32)
    mass = (1.0 - done) * cho_ref[...].astype(F32) + done * (atoms == 0).astype(F32)
    frac = frac_ref[...]
    stay = mass * (1.0 - frac)
    move = mass * frac
    low = low_ref[...]
    proj = jnp.zeros((ATOMS, rows), F32)
    for i in range(ATOMS):
        gap = atoms - low[i : i + 1, :]
        proj = proj + jnp.where(gap == 0, stay[i : i + 1, :], jnp.where(gap == 1, move[i : i + 1, :], 0.0))
    lp = lp_ref[...]
    loss_ref[...] = -jnp.sum(proj * lp, axis=0, keepdims=True)
    diff = (jnp.sum(proj, axis=0, keepdims=True) * jnp.exp(lp) - proj) * LOSS_SCALE
    taken = taken_ref[...]
    for a in range(ACT):
        d_ref[ATOMS * a : ATOMS * a + ATOMS, :] = jnp.where(taken == a, diff, 0.0)
    rh_ref[...] = jnp.zeros_like(rh_ref)
    rh_ref[:, :rows] = d_ref[...].astype(BF)
    hb_ref[...] = jnp.sum(d_ref[...], axis=1, keepdims=True) * (1.0 / LOSS_SCALE)


def loss(cho, done, low, frac, lp, taken):
    rows = taken.shape[1]
    ins = (cho, done, low, frac, lp, taken)
    outs = (((1, rows), F32), ((LOGITS, LANES), BF), ((LOGITS, 1), F32))
    return call(
        functools.partial(loss_kernel, rows),
        tuple(sds(*o) for o in outs),
        [whole(a.shape) for a in ins],
        [whole(o[0]) for o in outs],
        scratch=[pltpu.VMEM((LOGITS, rows), F32)],
        us=0.5,
    )(*ins)


def dflat_kernel(w_ref, rd_ref, s_ref, r_ref, b_ref):
    @pl.when(pl.program_id(0) == 0)
    def _():
        b_ref[...] = jnp.zeros_like(b_ref)

    diff = dot(w_ref[...], rd_ref[...]) * (0.5 * s_ref[...].astype(F32))
    r_ref[...] = diff.astype(BF)
    b_ref[...] += jnp.sum(diff.reshape(7, 64, LANES), axis=0)


def dflat(wd, rd, s3):
    block = pl.BlockSpec((448, LANES), lambda i: (i, 0))
    return call(
        dflat_kernel,
        (sds((3136, LANES), BF), sds((64, LANES), F32)),
        [pl.BlockSpec((448, 512), lambda i: (i, 0)), whole((512, LANES)), block],
        [block, whole((64, LANES))],
        grid=(7,),
        us=2,
    )(wd, rd, s3)


def dconv3_kernel(r3_ref, t_ref, s_ref, r_ref, p_ref, b_ref, pad):
    p = pl.program_id(0)

    @pl.when(p == 0)
    def _():
        b_ref[...] = jnp.zeros_like(b_ref)
        pad[:896, :] = jnp.zeros((896, LANES), BF)
        pad[896:4032, :] = r3_ref[...]
        pad[4032:, :] = jnp.zeros((896, LANES), BF)

    window = pl.ds(pl.multiple_of(448 * p, 64), 1344)
    diff = dot(t_ref[...], pad[window, :]) * s_ref[...].astype(F32)
    r_ref[...] = diff.astype(BF)
    b_ref[...] += jnp.sum(diff.reshape(9, 64, LANES), axis=0)

    @pl.when(p < FAR)
    def _():
        p_ref[0] = pack_rows(diff, 576).astype(BF)


def dconv3(r3, t3b, s2):
    block = pl.BlockSpec((576, LANES), lambda p: (0, p))
    return call(
        dconv3_kernel,
        (sds((576, 9 * LANES), BF), sds((FAR, 1008, 128), BF), sds((64, LANES), F32)),
        [whole((3136, LANES)), whole((576, 1344)), block],
        [block, pl.BlockSpec((1, 1008, 128), lambda p: (jnp.minimum(p, FAR - 1), 0, 0)), whole((64, LANES))],
        grid=(9,),
        scratch=[pltpu.VMEM((4928, LANES), BF)],
        us=11,
    )(r3, t3b, s2)


def first_diffs(t, cur, prev):
    none = jnp.zeros((64, LANES), BF)
    halves = []
    for h in range(2):
        if h == 0:
            parts = [none, cur[:320], none, prev[:320]]
        else:
            parts = [cur[256:], none, prev[256:], none]
        halves.append(dot(t, jnp.concatenate(parts, axis=0)))
    return [jnp.concatenate([half[320 * e : 320 * e + 320] for half in halves], axis=0) for e in range(2)]


def dconv2_kernel(first, packs, cur_ref, prev_ref, t_ref, s_ref, *rest):
    r_ref, b_ref = (rest[-3], rest[-1]) if packs else rest[-2:]
    m = pl.program_id(0) + first

    @pl.when(pl.program_id(0) == 0)
    def _():
        b_ref[...] = jnp.zeros_like(b_ref)

    cur = jnp.where(m < 9, cur_ref[...], jnp.zeros((576, LANES), BF))
    prev = jnp.where(m > 0, prev_ref[...], jnp.zeros((576, LANES), BF))
    for e, part in enumerate(first_diffs(t_ref[...], cur, prev)):
        part = part * s_ref[e].astype(F32)
        r_ref[e] = part.astype(BF)
        if packs:
            rest[-2][0, e] = pack_rows(part, 640).astype(BF)
        b_ref[...] += jnp.sum(part.reshape(20, 32, LANES), axis=0)


def dconv2(r2, t2b, s1, first, count, packs, r1):
    block = pl.BlockSpec((2, 640, LANES), lambda m: (0, 0, m + first))
    ins = [r2, r2, t2b, s1]
    in_specs = [
        pl.BlockSpec((576, LANES), lambda m: (0, jnp.minimum(m + first, 8))),
        pl.BlockSpec((576, LANES), lambda m: (0, jnp.maximum(m + first - 1, 0))),
        whole((640, 768)),
        block,
    ]
    aliases = {}
    if r1 is not None:
        ins.append(r1)
        in_specs.append(pl.BlockSpec(memory_space=pl.ANY))
        aliases = {4: 0}
    shapes = [sds((2, 640, 10 * LANES), BF), sds((count, 2, 1120, 128), BF), sds((32, LANES), F32)]
    outs = [block, pl.BlockSpec((1, 2, 1120, 128), lambda m: (m, 0, 0, 0)), whole((32, LANES))]
    if not packs:
        del shapes[1], outs[1]
    return pl.pallas_call(
        functools.partial(dconv2_kernel, first, packs),
        out_shape=tuple(shapes),
        grid=(count,),
        in_specs=in_specs,
        out_specs=outs,
        input_output_aliases=aliases,
        compiler_params=pltpu.CompilerParams(vmem_limit_bytes=VMEM_BIG),
        cost_estimate=cost(2 * count),
    )(*ins)


def frame_rows(r0, r1, t1b, o_ref, at, rows):
    none = jnp.zeros((32, LANES), BF)
    for g in range(3):
        if g == 0:
            parts = [none, r0[:224], none, r1[:224]]
        elif g == 1:
            parts = [r0[192:448], r1[192:448]]
        else:
            parts = [r0[416:], none, r1[416:], none]
        out = dot(t1b, jnp.concatenate(parts, axis=0)).astype(BF)
        for dy in range(4):
            o_ref[at + dy, 28 * g : 28 * g + 28, :, :] = out[56 * dy : 56 * dy + 56, :rows].reshape(28, 2, rows)


def dframes_kernel(rows, first, last, far, flag_ref, own_ref, *rest):
    edge_ref, pair = rest[-2:]
    o_ref = rest[-3]
    own = flag_ref[0] == 1
    m = pl.program_id(0)
    t1b = rest[4] if far else rest[1]

    @pl.when(m == 0)
    def _():
        edge_ref[...] = jnp.zeros_like(edge_ref) if first == 0 else rest[5 if far else 2][...]

    @pl.when(own)
    def _():
        for e in range(2):
            pair[e] = own_ref[e]

    @pl.when(jnp.logical_not(own))
    def _():
        if far:
            cur = unpack_rows(rest[0][0].astype(F32), 576).astype(BF)
            prev = unpack_rows(rest[1][0].astype(F32), 576).astype(BF)
            prev = jnp.where(m + first > 0, prev, jnp.zeros_like(prev))
            for e, part in enumerate(first_diffs(rest[3][...], cur, prev)):
                pair[e] = (part * unpack_rows(rest[2][0, e].astype(F32), 640)).astype(BF)
        else:
            for e in range(2):
                pair[e] = unpack_rows(rest[0][0, e].astype(F32), 640).astype(BF)

    if last:
        inside = m < pl.num_programs(0) - 1
        for e in range(2):
            pair[e] = jnp.where(inside, pair[e], jnp.zeros((640, LANES), BF))
    frame_rows(pair[0], edge_ref[...], t1b[...], o_ref, 0, rows)
    if last:

        @pl.when(inside)
        def _():
            frame_rows(pair[1], pair[0], t1b[...], o_ref, 4, rows)

    else:
        frame_rows(pair[1], pair[0], t1b[...], o_ref, 4, rows)
    edge_ref[...] = pair[1]


def dframes(flag, own, got, t1b, rows, first, count, edge, out):
    far = len(got) > 1
    last = first + count == 10
    at = lambda m: jnp.minimum(m, count - 1)
    fixed = lambda shape: pl.BlockSpec(shape, lambda *_: (0,) * len(shape))
    ins = [flag, own]
    in_specs = [pl.BlockSpec((2, 640, LANES), lambda m, *_: (0, 0, at(m) + first))]
    if far:
        r2p, s1p, t2b = got
        ins += [r2p, r2p, s1p, t2b]
        in_specs += [
            pl.BlockSpec((1, 1008, 128), lambda m, *_: (m + first, 0, 0)),
            pl.BlockSpec((1, 1008, 128), lambda m, *_: (jnp.maximum(m + first - 1, 0), 0, 0)),
            pl.BlockSpec((1, 2, 1120, 128), lambda m, *_: (m, 0, 0, 0)),
            fixed((640, 768)),
        ]
    else:
        ins.append(got[0])
        in_specs.append(pl.BlockSpec((1, 2, 1120, 128), lambda m, *_: (at(m), 0, 0, 0)))
    ins.append(t1b)
    in_specs.append(fixed((224, 512)))
    aliases = {}
    if first:
        ins += [edge, out]
        in_specs += [fixed((640, LANES)), pl.BlockSpec(memory_space=pl.ANY)]
        aliases = {len(ins) - 1: 0}
    return pl.pallas_call(
        functools.partial(dframes_kernel, rows, first, last, far),
        out_shape=(sds((84, 84, 2, rows), BF), sds((640, LANES), BF)),
        grid_spec=pltpu.PrefetchScalarGridSpec(
            num_scalar_prefetch=1,
            grid=(count + 1 if last else count,),
            in_specs=in_specs,
            out_specs=[pl.BlockSpec((8, 84, 2, rows), lambda m, *_: (m + first, 0, 0, 0)), fixed((640, LANES))],
            scratch_shapes=[pltpu.VMEM((2, 640, LANES), BF)],
        ),
        input_output_aliases=aliases,
        compiler_params=pltpu.CompilerParams(vmem_limit_bytes=VMEM_BIG),
        cost_estimate=cost(3 * count),
    )(*ins)


def wdense_kernel(flag_ref, a_ref, rd_ref, rh_ref, h_ref, keep_ref, send_ref):
    core = flag_ref[1]
    grads = []
    for left, right in ((a_ref, rd_ref), (rh_ref, h_ref)):
        grads.append((dot_nt(left[...], right[...]) * (1.0 / LOSS_SCALE)).astype(BF))
    start = 0
    for grad in grads:
        size = grad.shape[0]
        for half in range(2):
            tile0 = grad[:, 256 * half : 256 * half + 128]
            tile1 = grad[:, 256 * half + 128 : 256 * half + 256]
            keep_ref[0, half, start : start + size, :] = jnp.where(core == 0, tile0, tile1)
            send_ref[0, half, start : start + size, :] = jnp.where(core == 0, tile1, tile0)
        start += size


def wdense(flag, a3, rd, rh, h):
    out = pl.BlockSpec((1, 2, 512, 128), lambda i, *_: (i, 0, 0, 0))
    return pl.pallas_call(
        wdense_kernel,
        out_shape=(sds((8, 2, 512, 128), BF), sds((8, 2, 512, 128), BF)),
        grid_spec=pltpu.PrefetchScalarGridSpec(
            num_scalar_prefetch=1,
            grid=(8,),
            in_specs=[
                pl.BlockSpec((392, LANES), lambda i, *_: (i, 0)),
                whole((512, LANES)),
                pl.BlockSpec((120, LANES), lambda i, *_: (i, 0)),
                whole((512, LANES)),
            ],
            out_specs=[out, out],
        ),
        compiler_params=pltpu.CompilerParams(vmem_limit_bytes=VMEM_BIG),
        cost_estimate=cost(1),
    )(flag, a3, rd, rh, h)


def wconv3_kernel(a_ref, r_ref, g_ref):
    acc = jnp.zeros((64, 576), F32)
    for j in range(7):
        left = jnp.concatenate(
            [a_ref[64 * j : 64 * j + 192, LANES * u : LANES * (u + 7)] for u in range(3)], axis=0
        )
        right = jnp.concatenate([r_ref[448 * i + 64 * j : 448 * i + 64 * j + 64, :] for i in range(7)], axis=1)
        acc = acc + dot_nt(right, left)
    g_ref[...] = acc * (1.0 / LOSS_SCALE)


def wconv3(a2, r3):
    return call(
        wconv3_kernel,
        sds((64, 576), F32),
        [whole(a2.shape), whole(r3.shape)],
        whole((64, 576)),
        us=7,
    )(a2, r3)


def wconv2_kernel(a_ref, r_ref, g_ref):
    g_ref[...] = jnp.zeros_like(g_ref)

    def body(j, _):
        window = pl.ds(pl.multiple_of(64 * j, 64), 128)
        left = jnp.concatenate(
            [a_ref[e, window, LANES * t : LANES * (t + 9)] for t in range(2) for e in range(2)], axis=0
        )
        g_ref[...] += dot_nt(left, r_ref[pl.ds(pl.multiple_of(64 * j, 64), 64), :])
        return 0

    lax.fori_loop(0, 9, body, 0)
    g_ref[...] = g_ref[...] * (1.0 / LOSS_SCALE)


def wconv2(a1, r2):
    return call(
        wconv2_kernel,
        sds((512, 64), F32),
        [whole(a1.shape), whole(r2.shape)],
        whole((512, 64)),
        us=11,
    )(a1, r2)


def wconv1_kernel(x_ref, n_ref, r_ref, g_ref, acc):
    step = pl.program_id(0)

    @pl.when(step == 0)
    def _():
        acc[...] = jnp.zeros_like(acc)

    def column(dy, rows, c):
        if c < 4:
            return x_ref[dy, rows, LANES * c : LANES * (c + 1)]
        return n_ref[dy, rows, :]

    total = acc[...]
    for g in range(5):
        rows = slice(64 * g, 64 * g + 80)
        left = jnp.concatenate(
            [
                jnp.concatenate([column(dy, rows, ii + t) for ii in range(4)], axis=1)
                for t in range(2)
                for dy in range(4)
            ],
            axis=0,
        )
        right = jnp.concatenate(
            [r_ref[ii % 2, 128 * g : 128 * g + 128, LANES * (ii // 2) : LANES * (ii // 2 + 1)] for ii in range(4)],
            axis=1,
        )
        total = total + dot_nt(left, right)
    acc[...] = total

    @pl.when(step == 4)
    def _():
        for dy in range(8):
            part = jnp.zeros((32, 32), F32)
            for jj in range(4):
                part = part + acc[80 * dy + 16 * jj : 80 * dy + 16 * jj + 32, 32 * jj : 32 * jj + 32]
            g_ref[32 * dy : 32 * dy + 32, :] = part * (1.0 / LOSS_SCALE)


def wconv1(xt, r1):
    return call(
        wconv1_kernel,
        sds((256, 32), F32),
        [
            pl.BlockSpec((4, 336, 4 * LANES), lambda s: (0, 0, s)),
            pl.BlockSpec((4, 336, LANES), lambda s: (0, 0, 4 * s + 4)),
            pl.BlockSpec((2, 640, 2 * LANES), lambda s: (0, 0, s)),
        ],
        whole((256, 32)),
        grid=(5,),
        scratch=[pltpu.VMEM((640, 128), F32)],
        us=14,
    )(xt, xt, r1)


SMALL_ROWS = 704


def lanes_of(shards):
    return max(1, 128 // shards)


def slot_rows(capacity):
    return (capacity + 7) // 8 * 8


def pack_kernel(shards, capacity, flag_ref, *refs):
    b1_refs, (b2_ref, b3_ref, g1_ref, g2_ref, g3_ref, db_ref, hb_ref, loss_ref, owner_ref, p_ref, w) = refs[:-11], refs[-11:]
    scale = 1.0 / LOSS_SCALE
    w[...] = jnp.zeros_like(w)
    for k in range(4):
        w[64 * k : 64 * k + 64, :] = g3_ref[:, 128 * k : 128 * k + 128]
    w[256:320, :64] = g3_ref[:, 512:]
    w[320:576, :64] = g2_ref[:256, :]
    w[320:576, 64:] = g2_ref[256:, :]
    w[576:704, :32] = g1_ref[:128, :]
    w[576:704, 32:64] = g1_ref[128:, :]
    total = b1_refs[0][...]
    for ref in b1_refs[1:]:
        total = total + ref[...]
    for column, value in ((64, total), (65, b2_ref[...]), (66, b3_ref[...])):
        w[576 : 576 + value.shape[0], column : column + 1] = jnp.sum(value, axis=1, keepdims=True) * scale
    for k in range(4):
        w[576:704, 67 + k : 68 + k] = db_ref[128 * k : 128 * k + 128, :] * scale
    for half in range(2):
        for k in range(4):
            start = 459 * half + 128 * k
            size = min(128, 459 * (half + 1) - start)
            w[576 : 576 + size, 71 + 4 * half + k : 72 + 4 * half + k] = hb_ref[start : start + size, :]

    owner = owner_ref[...]
    rows = owner.shape[1]
    owner_f = owner.astype(F32)
    down = jnp.broadcast_to(owner_f, (8, rows)).T[:, :1]
    same = (down == owner_f) & (
        lax.broadcasted_iota(jnp.int32, (rows, rows), 0) < lax.broadcasted_iota(jnp.int32, (rows, rows), 1)
    )
    slot = jnp.sum(same.astype(F32), axis=0, keepdims=True)
    group, height = lanes_of(shards), slot_rows(capacity)
    place = lax.broadcasted_iota(jnp.int32, (height, rows), 0).astype(F32)
    spread = jnp.where(place == slot, loss_ref[...], 0.0).astype(BF)
    lane = lax.broadcasted_iota(jnp.int32, (128, rows), 0)
    here = shards * lax.rem(owner, group) + flag_ref[2]
    for g in range(shards // group):
        hot = ((lane == here) & (owner // group == g)).astype(BF)
        w[SMALL_ROWS + height * g : SMALL_ROWS + height * g + height, :] = dot_nt(spread, hot)
    p_ref[...] = w[...].astype(BF)


def pack(flag, b1s, shards, capacity, *ins):
    total = SMALL_ROWS + shards // lanes_of(shards) * slot_rows(capacity)
    ins = tuple(b1s) + ins
    return call(
        functools.partial(pack_kernel, shards, capacity),
        sds((total, 128), BF),
        [pl.BlockSpec(memory_space=pltpu.SMEM)] + [whole(a.shape) for a in ins],
        whole((total, 128)),
        scratch=[pltpu.VMEM((total, 128), F32)],
        us=3,
    )(flag, *ins)


def split_kernel(shards, capacity, flag_ref, own_ref, got_ref, k1, b1, k2, b2, k3, b3, db, hb, prio, w):
    own = flag_ref[0] == 1
    w[...] = jnp.where(own, own_ref[...].astype(F32), got_ref[...].astype(F32))

    def pick(low, high):
        return jnp.where(own, low, high)

    k1[...] = pick(w[576:704, :32], w[576:704, 32:64])
    k2[...] = pick(w[320:576, :64], w[320:576, 64:])
    for n in range(9):
        rows = slice(64 * (n // 2), 64 * (n // 2) + 64)
        part = w[rows, 64 * (n % 2) : 64 * (n % 2) + 64]
        k3[n] = pick(part[:32], part[32:])
    columns = w[576:704, :].T
    b1[...] = pick(columns[64:65, :16], columns[64:65, 16:32])
    for ref, at in ((b2, 65), (b3, 66)):
        ref[...] = pick(columns[at : at + 1, :32], columns[at : at + 1, 32:64])
    for k in range(2):
        db[:, 128 * k : 128 * k + 128] = pick(columns[67 + k : 68 + k], columns[69 + k : 70 + k])
    for k in range(4):
        size = min(128, 459 - 128 * k)
        hb[:, 128 * k : 128 * k + size] = pick(columns[71 + k : 72 + k, :size], columns[75 + k : 76 + k, :size])
    group, height = lanes_of(shards), slot_rows(capacity)
    me = flag_ref[2]
    block = w[pl.ds(pl.multiple_of(SMALL_ROWS + height * (me // group), 8), height), :]
    if group > 1:
        block = pltpu.roll(block, lax.rem(128 - shards * lax.rem(me, group), 128), 1)
    half = capacity // 2
    prio[:, 0, :] = pick(block[:half, :shards], block[half : 2 * half, :shards])


def split(flag, own, got, shards, capacity):
    shapes = (
        (128, 32),
        (1, 16),
        (256, 64),
        (1, 32),
        (9, 32, 64),
        (1, 32),
        (1, 256),
        (1, 459),
        (capacity // 2, 1, shards),
    )
    return call(
        functools.partial(split_kernel, shards, capacity),
        tuple(sds(s, F32) for s in shapes),
        [pl.BlockSpec(memory_space=pltpu.SMEM), whole(own.shape), whole(got.shape)],
        [whole(s) for s in shapes],
        scratch=[pltpu.VMEM(own.shape, F32)],
        us=2,
    )(flag, own, got)


def unchunk_kernel(flag_ref, cur_ref, other_ref, d_ref, h_ref):
    core = flag_ref[1]
    cur, other = cur_ref[0].astype(F32), other_ref[0].astype(F32)
    tile0 = jnp.where(core == 0, cur, other)
    tile1 = jnp.where(core == 0, other, cur)
    d_ref[:, :128] = tile0[:392]
    d_ref[:, 128:] = tile1[:392]
    h_ref[:, :128] = tile0[392:]
    h_ref[:, 128:] = tile1[392:]


def unchunk(flag, cur, other):
    part = pl.BlockSpec((1, 512, 128), lambda i, f: (i ^ f[3], 0, 0))
    return pl.pallas_call(
        unchunk_kernel,
        out_shape=(sds((3136, 256), F32), sds((LOGITS, 256), F32)),
        grid_spec=pltpu.PrefetchScalarGridSpec(
            num_scalar_prefetch=1,
            grid=(8,),
            in_specs=[part, part],
            out_specs=[
                pl.BlockSpec((392, 256), lambda i, *_: (i, 0)),
                pl.BlockSpec((120, 256), lambda i, *_: (i, 0)),
            ],
        ),
        compiler_params=pltpu.CompilerParams(vmem_limit_bytes=VMEM_BIG),
        cost_estimate=cost(7),
    )(flag, cur, other)


def after(value, *others):
    return lax.optimization_barrier((value,) + others)[0]


def hand(value):
    return lax.ppermute(value, "pair", [(0, 1)])


def swap(value, bit):
    devices = lax.axis_size("batch")
    return lax.ppermute(value, "batch", [(i, i ^ bit) for i in range(devices)])


def add(left, right):
    return (left.astype(F32) + right.astype(F32)).astype(BF)


def reduce_chunks(keep, send, me):
    devices = lax.axis_size("batch")
    got = swap(send, 1)
    cur = add(keep, got)
    blocks, spread = devices // 2, devices // 16
    if spread > 1:
        cur = cur.reshape(8, 2, spread, 512 // spread, 128).transpose(0, 2, 1, 3, 4)
        cur = cur.reshape(blocks, 2, 512 // spread, 128)
    bit = 2
    arrived = [got]
    while bit < devices:
        mine = (me // bit) % 2
        pairs = cur.reshape((cur.shape[0] // 2, 2) + cur.shape[1:])
        send = lax.dynamic_index_in_dim(pairs, 1 - mine, axis=1, keepdims=False)
        keep = lax.dynamic_index_in_dim(pairs, mine, axis=1, keepdims=False)
        got = swap(send, bit)
        arrived.append(got)
        cur = add(keep, got)
        bit *= 2
    return cur[0], arrived


def unmix(blocks, code):
    bit = 1
    while bit < blocks.shape[0]:
        pairs = blocks.reshape((-1, 2, bit) + blocks.shape[1:])
        blocks = jnp.where((code // bit) % 2 == 1, pairs[:, ::-1], pairs).reshape(blocks.shape)
        bit *= 2
    return blocks


def gather_chunks(mine, me, late):
    devices = lax.axis_size("batch")
    cur = mine[None]
    bit = devices // 2
    while bit > 1:
        if bit == 2:
            cur = after(cur, late)
        other = swap(cur, bit)
        cur = jnp.stack([cur, other], axis=1).reshape((2 * cur.shape[0],) + cur.shape[1:])
        bit //= 2
    other = swap(cur, 1)
    return cur, other


def local(
    frames,
    kernel_first,
    bias_first,
    kernel_second,
    bias_second,
    kernel_third,
    bias_third,
    dense_weight,
    dense_bias,
    head_weight,
    head_bias,
    taken_actions,
    greedy_actions,
    done_flags,
    bin_lower,
    bin_fraction,
    owner_shard,
):
    online = lax.axis_index("pair") == 0
    me = lax.axis_index("batch")
    shards = lax.axis_size("batch")
    rows = frames.shape[1]
    capacity = 2 * ((rows + shards - 1) // shards)
    block = me // 2 if shards == 16 else me * 0
    flag = jnp.stack([online.astype(jnp.int32), me % 2, me, block]).astype(jnp.int32)
    xv = frames[0].transpose(2, 3, 1, 0)
    k1, k2, k3 = kernel_first[0], kernel_second[0], kernel_third[0]
    ones = jnp.zeros((16, LANES), BF).at[0].set(1)
    t1, t2, t3, t3b, t2b, b2 = bands(k1, bias_first, k2, bias_second, k3, bias_third)

    k1_got, k2_got = hand(after(k1[:, :, 2:], t1)), hand(after(k2, t1))
    a1, s1, xt, early = conv1(xv, t1, ones, 0, 2 * EARLY, ())
    early = hand(after(early, k1_got, k2_got))
    a1, s1, xt, late = conv1(xv, t1, ones, 2 * EARLY, 20, (a1, s1, xt))
    late = hand(late)
    a2, s2 = conv2(a1, t2, b2)
    a3, s3 = conv3(a2, t3, ones)
    wd = dense_weight[0]
    wht = head_weight[0].T
    pd = lax.dot_general(wd, a3, (((0,), (0,)), ((), ())), preferred_element_type=F32)
    taken = taken_actions[None, :]
    sel = jnp.where(online, taken, greedy_actions[None, :])
    h, sd, lp, cho = head(pd, dense_bias, wht, head_bias, sel)
    cho = lax.ppermute(cho, "pair", [(1, 0)])
    row_loss, rh, hb = loss(cho, done_flags[None, :], bin_lower.T, bin_fraction.T, lp, taken)

    diff_dense = lax.dot_general(wht, rh, (((0,), (0,)), ((), ())), preferred_element_type=F32)
    diff_dense = diff_dense * (0.5 * sd.astype(F32))
    rd = diff_dense.astype(BF)
    db = jnp.sum(diff_dense, axis=1, keepdims=True)

    keep, send = wdense(flag, a3, after(rd, early), rh, h)
    chunk, arrived = reduce_chunks(keep, send, me)

    r3, b3g = dflat(wd, rd, s3)
    r2, r2p, b2g = dconv3(after(r3, arrived[0]), t3b, s2)
    r2p = hand(r2p)
    r1, packed, b1s = None, [], []
    for first, count in NEAR:
        r1, part, b1g = dconv2(after(r2, late), t2b, s1, first, count, True, r1)
        packed.append(part)
        b1s.append(b1g)
    r1, b1g = dconv2(r2, t2b, s1, 0, FAR, False, r1)
    b1s.append(b1g)
    gots = [hand(after(packed[0], r2p))]
    g3 = wconv3(a2, after(r3, arrived[1]))
    g2 = wconv2(a1, after(r2, arrived[1]))
    g1 = wconv1(xt, after(r1, arrived[2]))
    small = pack(flag, b1s, shards, capacity, b2g, b3g, g1, g2, g3, db, hb, row_loss, owner_shard.T)
    t1b, t2b_online = band_frames(flag, k1, k1_got, k2, k2_got)
    far_chunk = hand(chunk[1])
    gots.append(hand(after(packed[1], arrived[-1], gots[0])))
    out, edge, outs = None, None, []
    for first, s1p in ((0, early), (EARLY, late)):
        out, edge = dframes(flag, r1, (r2p, s1p, t2b_online), t1b, rows, first, s1p.shape[0], edge, out)
        outs.append(edge)
    for (first, count), got in zip(NEAR, gots):
        out, edge = dframes(flag, r1, (got,), t1b, rows, first, count, edge, out)
        outs.append(edge)
    small = after(small, gots[0])
    bit, n = 1, -2
    while bit < shards:
        if 0 <= n < 3:
            small = after(small, outs[n])
        small = add(small, swap(small, bit))
        bit, n = 2 * bit, n + 1
    far_small = hand(small)
    mine = jnp.where(online, chunk[0], far_chunk)
    cur, other = gather_chunks(mine, me, gots[1])
    if shards != 16:
        cur, other = (unmix(v, me // 2).reshape(8, 512, 128) for v in (cur, other))
    dense_out, head_out = unchunk(flag, cur, other)
    o = split(flag, small, far_small, shards, capacity)
    return (
        o[0].reshape(4, 8, 4, 32),
        o[1].reshape(16),
        o[2].reshape(2, 4, 32, 64),
        o[3].reshape(32),
        o[4].reshape(3, 3, 32, 64).transpose(0, 1, 3, 2),
        o[5].reshape(32),
        dense_out,
        o[6].reshape(256),
        head_out.T,
        o[7].reshape(459),
        out.transpose(3, 2, 0, 1),
        o[8].transpose(1, 2, 0),
    )


def solution(mesh):
    return jax.shard_map(
        local,
        mesh=mesh,
        in_specs=(
            P("pair", "batch", None, None, None),
            P("pair", None, None, None, None),
            P("pair", None),
            P("pair", None, None, None, None),
            P("pair", None),
            P("pair", None, None, None, None),
            P("pair", None),
            P("pair", None, None),
            P("pair", None),
            P("pair", None, None),
            P("pair", None),
            P("batch"),
            P("batch"),
            P("batch"),
            P("batch", None),
            P("batch", None),
            P("batch", None),
        ),
        out_specs=(
            P("pair", None, None, None),
            P("pair"),
            P("pair", None, None, None),
            P("pair"),
            P(None, None, None, "pair"),
            P("pair"),
            P(None, "pair"),
            P("pair"),
            P("pair", None),
            P("pair"),
            P("batch", "pair", None, None),
            P("batch", None, "pair"),
        ),
        check_vma=False,
    )
```

time: 412 us -> 269 us (0.65)
  waiting for transfers between devices: 103 us -> 28.8 us
  blocking collectives: 62.1 us -> 0 us
  starting transfers between devices: 22.7 us -> 43.4 us
  Pallas kernels: 156 us -> 174 us
  other arithmetic: 22.5 us -> 6.14 us
  local copies, waits for them, and re-layouts: 21 us -> 7.32 us
  between operations: 14.1 us -> 1.03 us
    ppermute x4 -> x9, waiting for transfers between devices: 98.1 us -> 16.4 us  [hand(): return lax.ppermute(value, 'pair', [(0, 1)])]
    psum x1 -> x0, blocking collectives: 62.1 us -> none  [local(): small = lax.psum(small, 'batch')]
    pallas_call x8 -> x17, Pallas kernels: 98.2 us -> 116 us  [the longest x2 31.5 us: conv1(): pl.pallas_call(functools.partial(conv1_kernel, rows, start, packs), out_s...]
    ppermute x4 -> x9, starting transfers between devices: 15.3 us -> 28.9 us  [hand(): return lax.ppermute(value, 'pair', [(0, 1)])]
    ppermute x0 -> x12, starting transfers between devices: none -> 13.1 us  [swap(): return lax.ppermute(value, 'batch', [(i, i ^ bit) for i in range(devices)])]
    ppermute x0 -> x12, waiting for transfers between devices: none -> 8.44 us  [swap(): return lax.ppermute(value, 'batch', [(i, i ^ bit) for i in range(devices)])]
    select_n x9 -> x0, other arithmetic: 7.16 us -> none  [the longest x7 4.7 us: local(): finals.append(jnp.where(online, low_part, far))]
    slice x14 -> x1, local copies, waits for them, and re-layouts: 6.77 us -> 0.04 us  [local(): k1_got, k2_got = (hand(after(k1[:, :, 2:], t1)), hand(after(k2, t1)))]
  transfers between devices with their start and end apart: 9 -> 22, of which waited for: 3 -> 6; matrix products, arithmetic and copies ran while one was open for 7% -> 5% of each run, Pallas kernels for 20% -> 58%
where the time goes in v2:
time: 269 us; the launch traced here: 266 us
  Pallas kernels  174 us (65%)
  starting transfers between devices  43.4 us (16%)
  waiting for transfers between devices  28.8 us (11%)
  local copies, waits for them, and re-layouts  7.32 us (3%)
  other arithmetic  6.14 us (2%)
  matrix products  5.94 us (2%)
    pallas_call x2, Pallas kernels, conv1(): pl.pallas_call(functools.partial(conv1_kernel, rows, start, packs), out_s...  31.5 us
    ppermute x9, starting transfers between devices, hand(): return lax.ppermute(value, 'pair', [(0, 1)])  28.9 us
    pallas_call x4, Pallas kernels, dframes(): pl.pallas_call(functools.partial(dframes_kernel, rows, first, last, far),...  21.9 us
    pallas_call x3, Pallas kernels, dconv2(): pl.pallas_call(functools.partial(dconv2_kernel, first, packs), out_shape=...  17.6 us
    ppermute x9, waiting for transfers between devices, hand(): return lax.ppermute(value, 'pair', [(0, 1)])  16.4 us
    pallas_call x1, Pallas kernels, wconv1(): call(wconv1_kernel, sds((256, 32), F32), [pl.BlockSpec((4, 336, 4 * LANES...  13.6 us
    ppermute x12, starting transfers between devices, swap(): return lax.ppermute(value, 'batch', [(i, i ^ bit) for i in range(devices)])  13.1 us
    pallas_call x1, Pallas kernels, conv2(): call(conv2_kernel, (sds((576, 9 * LANES), BF), sds((576, 9 * LANES), BF))...  11.3 us
  transfers between devices with their start and end apart: 22, of which 6 were waited for; matrix products, arithmetic and copies ran while one was open for 5% of the time, Pallas kernels for 58%

profile of v2, /device:TPU:0, one launch (start us, length us, event | category | flops | bytes accessed | tf_op | source)
XLA Modules:
  0.0 266.3 jit_solution(9375173076922007352)
XLA Ops:
  0.7 4.7 %shard_map.256 = (bf16[320,1424]{1,0:T(8,128)(2,1)}, bf16[192,1024]{1,0:T(8,128)(2,1)}, bf16[448,1744]{1,0:T(8,128)(2,1)}, bf16[576,1344]{1,0:T(8,128)(2,1)}, bf...) custom-call(bf16[8,8,4,32]{3,2,1,0:T(4,128)(2,1)} %bitcast.106, bf16[1,32]{1,0:T(2,128)(2,1)} %b1.1, ...), custom_call_target="tpu_custom_call" | custom-call | flops 2500000000 | tf_op jit(solution)/shard_map/pallas_call | solution.py:112
  5.3 4.8 %collective-permute-start.2 = (bf16[4,4,32,64]{3,2,1,0:T(8,128)(2,1)S(1)}, bf16[4,4,32,64]{3,2,1,0:T(8,128)(2,1)S(1)}, u32[]{:S(2)}, u32[]{:S(2)}) collective-permute-start(bf16[4,4,32,64]{3,2,1,0:T(8,128)(2,1)S(1)} %bitcast.115), channel_id=1, source_target_pairs={{0,16},{1,17},{2,18},{3,19},{4,20},{5,21},{6,22},{7,23},{8,24},{9,... | collective-permute-start | bytes 196616 | tf_op jit(solution)/shard_map/ppermute | solution.py:855
  10.2 1.3 collective-permute-start.1
  11.5 13.4 %shard_map.257 = (bf16[2,640,2560]{2,1,0:T(8,128)(2,1)}, bf16[2,640,2560]{2,1,0:T(8,128)(2,1)}, bf16[4,336,5376]{2,1,0:T(8,128)(2,1)}, bf16[4,2,1120,128]{3,2,1,0:T(8,128)(2,1)}) custom-call(bf16[84,84,4,224]{3,2,1,0:T(4,128)(2,1)} %bitcast.91, bf16[320,1424]{1,0:T(8,128)(2,1)} %get-tuple-element.99.t1_ref, bf16[16,256]{1,0:T(8,128)(2,1)} %constant.120.clone.1.ones_ref), custom_call_target="tpu_custom_call" | custom-call | flops 400000000 | tf_op jit(solution)/shard_map/pallas_call | solution.py:217
  25.0 0.6 copy-done.17
  25.7 2.7 collective-permute-start.3
  28.3 18.1 %shard_map.258 = (bf16[2,640,2560]{2,1,0:T(8,128)(2,1)}, bf16[2,640,2560]{2,1,0:T(8,128)(2,1)}, bf16[4,336,5376]{2,1,0:T(8,128)(2,1)}, bf16[2,2,1120,128]{3,2,1,0:T(8,128)(2,1)}) custom-call(bf16[84,84,4,224]{3,2,1,0:T(4,128)(2,1)} %bitcast.92, ...), custom_call_target="tpu_custom_call", output_to_operand_aliasing={{0}: (3, {}), {1}: (4, {}), {2}: (5, {})} | custom-call | flops 600000000 | tf_op jit(solution)/shard_map/pallas_call | solution.py:217
  46.4 11.3 %shard_map.259 = (bf16[576,2304]{1,0:T(8,128)(2,1)}, bf16[576,2304]{1,0:T(8,128)(2,1)}) custom-call(bf16[2,640,2560]{2,1,0:T(8,128)(2,1)} %get-tuple-element.103.r0_ref.r1_ref.a_ref, bf16[2,640,2560]{2,1,0:T(8,128)(2,1)} %get-tuple-element.103.r0_ref.r1_ref.a_ref, bf16[192,1024]{1,0:T(8,128)(2,1)} %get-tuple-element.104.t2_ref, ...), custom_call_target="tpu_custom_call" | custom-call | flops 500000000 | tf_op jit(solution)/shard_map/pallas_call | solution.py:243
  57.8 9.2 %shard_map.260 = (bf16[3136,256]{1,0:T(8,128)(2,1)}, bf16[3136,256]{1,0:T(8,128)(2,1)}) custom-call(bf16[576,2304]{1,0:T(8,128)(2,1)} %get-tuple-element.106.r0_ref.r1_ref.r2_ref.a_ref, bf16[576,2304]{1,0:T(8,128)(2,1)} %get-tuple-element.106.r0_ref.r1_ref.r2_ref.a_ref, bf16[576,2304]{1,0:T(8,128)(2,1)} %get-tuple-element.106.r0_ref.r1_ref.r2_ref.a_ref, ...), custom_call_target="tpu_custom_call" | custom-call | flops 500000000 | tf_op jit(solution)/shard_map/pallas_call | solution.py:267
  67.0 0.6 broadcast_select_fusion
  67.6 3.6 %convolution_bitcast_fusion.1.pd_ref = f32[512,256]{1,0:T(8,128)} fusion(bf16[3136,256]{1,0:T(8,128)(2,1)} %get-tuple-element.108.a_ref, bf16[1,3136,512]{2,1,0:T(8,128)(2,1)S(1)} %copy-done.3), kind=kOutput, calls=%fused_computation.5 | convolution fusion | flops 822083584 | bytes 5341184 | tf_op jit(solution)/shard_map/dot_general | solution.py:952
  71.2 2.9 %shard_map.261 = (bf16[512,256]{1,0:T(8,128)(2,1)}, bf16[512,256]{1,0:T(8,128)(2,1)}, f32[51,224]{1,0:T(8,128)}, bf16[51,224]{1,0:T(8,128)(2,1)}) custom-call(f32[512,256]{1,0:T(8,128)} %convolution_bitcast_fusion.1.pd_ref, bf16[1,512]{1,0:T(2,128)(2,1)} %bd_ref.1, bf16[918,512]{1,0:T(8,128)(2,1)} %bitcast.102, bf16[1,918]{1,0:T(2,128)(2,1)} %bh_ref.1, ...), custom_call_target="tpu_custom_call" | custom-call | flops 250000000 | tf_op jit(solution)/shard_map/pallas_call | solution.py:300
  74.1 1.3 collective-permute-start
  75.4 0.7 pad_add_fusion.flag_ref
  76.1 4.0 %collective-permute-done.cho_ref = bf16[51,224]{1,0:T(8,128)(2,1)S(1)} collective-permute-done((bf16[51,224]{1,0:T(8,128)(2,1)}, bf16[51,224]{1,0:T(8,128)(2,1)S(1)}, u32[]{:S(2)}, u32[]{:S(2)}) %collective-permute-start) | collective-permute-done | bytes 22880 | tf_op jit(solution)/shard_map/ppermute | solution.py:956
  80.1 0.6 copy-done.19
  80.7 2.8 %shard_map.262 = (f32[1,224]{1,0:T(1,128)}, bf16[918,256]{1,0:T(8,128)(2,1)}, f32[918,1]{1,0:T(8,128)}) custom-call(bf16[51,224]{1,0:T(8,128)(2,1)} %copy-done.19, s32[1,224]{1,0:T(1,128)} %bitcast.118, s32[51,224]{1,0:T(8,128)} %bitcast.116, f32[51,224]{1,0:T(8,128)} %bitcast.117, f32[51,224]{1,0:T(8,128)} %get-tuple-element.110.lp_ref, s32[1,224]{1,0:T(1,128)} %bitcast.111), custom_call_target="tpu_custom_call" | custom-call | flops 250000000 | tf_op jit(solution)/shard_map/pallas_call | solution.py:337
  83.5 2.3 fusion.10
  85.8 8.1 %shard_map.264 = (bf16[8,2,512,128]{3,2,1,0:T(8,128)(2,1)}, bf16[8,2,512,128]{3,2,1,0:T(8,128)(2,1)}) custom-call(s32[4]{0:T(128)} %pad_add_fusion.flag_ref, bf16[3136,256]{1,0:T(8,128)(2,1)} %get-tuple-element.108.a_ref, bf16[512,256]{1,0:T(8,128)(2,1)} %get-tuple-element.119.rd_ref, bf16[918,256]{1,0:T(8,128)(2,1)} %get-tuple-element.111.rh_ref, ...), custom_call_target="tpu_custom_call" | custom-call | flops 500000000 | tf_op jit(solution)/shard_map/pallas_call | solution.py:580
  93.9 2.7 %collective-permute-start.5 = (bf16[2,2,1120,128]{3,2,1,0:T(8,128)(2,1)}, bf16[2,2,1120,128]{3,2,1,0:T(8,128)(2,1)}, u32[]{:S(2)}, u32[]{:S(2)}) collective-permute-start(bf16[2,2,1120,128]{3,2,1,0:T(8,128)(2,1)} %get-tuple-element.126), channel_id=1, source_target_pairs={{0,16},{1,17},{2,18},{3,19},{4,20},{5,21},{6,22},{7,23},{8,24},{9,... | collective-permute-start | bytes 3440648 | tf_op jit(solution)/shard_map/ppermute | solution.py:855
  96.6 0.9 copy.44.refs_8_
  97.5 6.7 %shard_map.263 = (bf16[3136,256]{1,0:T(8,128)(2,1)}, f32[64,256]{1,0:T(8,128)}) custom-call(bf16[3136,512]{1,0:T(8,128)(2,1)} %bitcast.97, bf16[512,256]{1,0:T(8,128)(2,1)} %get-tuple-element.119.rd_ref, bf16[3136,256]{1,0:T(8,128)(2,1)} %get-tuple-element.113.s_ref), custom_call_target="tpu_custom_call" | custom-call | flops 1000000000 | tf_op jit(solution)/shard_map/pallas_call | solution.py:359
  104.2 1.3 copy-done.4
  105.5 2.8 %add_convert_fusion = bf16[8,2,512,128]{3,2,1,0:T(8,128)(2,1)S(1)} fusion(bf16[8,2,512,128]{3,2,1,0:T(8,128)(2,1)} %copy-done.4, bf16[8,2,512,128]{3,2,1,0:T(8,128)(2,1)} %get-tuple-element.139), kind=kLoop, calls=%fused_computation | loop fusion | flops 4194304 | bytes 6291456 | tf_op jit(solution)/shard_map/convert_element_type | solution.py:864
  108.3 1.0 dynamic-slice_bitcast_fusion
  109.4 1.5 collective-permute-start.6
  110.9 11.2 %shard_map.265 = (bf16[576,2304]{1,0:T(8,128)(2,1)}, bf16[6,1008,128]{2,1,0:T(8,128)(2,1)}, f32[64,256]{1,0:T(8,128)}) custom-call(bf16[3136,256]{1,0:T(8,128)(2,1)} %get-tuple-element.142.r3_ref.r_ref, bf16[576,1344]{1,0:T(8,128)(2,1)} %get-tuple-element.123.t_ref, bf16[576,2304]{1,0:T(8,128)(2,1)} %get-tuple-element.124.s_ref), custom_call_target="tpu_custom_call" | custom-call | flops 5500000256 | tf_op jit(solution)/shard_map/pallas_call | solution.py:391
  122.0 3.7 %collective-permute-start.8 = (bf16[6,1008,128]{2,1,0:T(8,128)(2,1)}, bf16[6,1008,128]{2,1,0:T(8,128)(2,1)S(1)}, u32[]{:S(2)}, u32[]{:S(2)}) collective-permute-start(bf16[6,1008,128]{2,1,0:T(8,128)(2,1)} %get-tuple-element.146), channel_id=1, source_target_pairs={{0,16},{1,17},{2,18},{3,19},{4,20},{5,21},{6,22},{7,23},{8,24},{9,... | collective-permute-start | bytes 4644872 | tf_op jit(solution)/shard_map/ppermute | solution.py:855
  125.7 4.5 %shard_map.266 = (bf16[2,640,2560]{2,1,0:T(8,128)(2,1)}, bf16[2,2,1120,128]{3,2,1,0:T(8,128)(2,1)}, f32[32,256]{1,0:T(8,128)}) custom-call(bf16[576,2304]{1,0:T(8,128)(2,1)} %get-tuple-element.141.cur_ref.prev_ref.r_ref, bf16[576,2304]{1,0:T(8,128)(2,1)} %get-tuple-element.141.cur_ref.prev_ref.r_ref, bf16[640,768]{1,0:T(8,128)(2,1)} %get-tuple-element.128.t_ref, ...), custom_call_target="tpu_custom_call" | custom-call | flops 2000000000 | tf_op jit(solution)/shard_map/pallas_call | solution.py:450
  130.2 4.6 %shard_map.267 = (bf16[2,640,2560]{2,1,0:T(8,128)(2,1)}, bf16[2,2,1120,128]{3,2,1,0:T(8,128)(2,1)}, f32[32,256]{1,0:T(8,128)}) custom-call(bf16[576,2304]{1,0:T(8,128)(2,1)} %get-tuple-element.141.cur_ref.prev_ref.r_ref, bf16[576,2304]{1,0:T(8,128)(2,1)} %get-tuple-element.141.cur_ref.prev_ref.r_ref, ...), custom_call_target="tpu_custom_call", output_to_operand_aliasing={{0}: (4, {})} | custom-call | flops 2000000000 | tf_op jit(solution)/shard_map/pallas_call | solution.py:450
  134.8 8.6 %shard_map.268 = (bf16[2,640,2560]{2,1,0:T(8,128)(2,1)}, f32[32,256]{1,0:T(8,128)}) custom-call(bf16[576,2304]{1,0:T(8,128)(2,1)} %get-tuple-element.141.cur_ref.prev_ref.r_ref, bf16[576,2304]{1,0:T(8,128)(2,1)} %get-tuple-element.141.cur_ref.prev_ref.r_ref, bf16[640,768]{1,0:T(8,128)(2,1)} %get-tuple-element.128.t_ref, ...), custom_call_target="tpu_custom_call", output_to_operand_aliasing={{0}: (4, {})} | custom-call | flops 6000000000 | tf_op jit(solution)/shard_map/pallas_call | solution.py:450
  143.4 1.5 fusion
  144.9 1.0 copy-done.1
  145.9 1.6 collective-permute-start.7
  147.5 6.9 %shard_map.271.refs_7_ = f32[64,576]{1,0:T(8,128)} custom-call(bf16[576,2304]{1,0:T(8,128)(2,1)} %get-tuple-element.106.r0_ref.r1_ref.r2_ref.a_ref, bf16[3136,256]{1,0:T(8,128)(2,1)} %get-tuple-element.142.r3_ref.r_ref), custom_call_target="tpu_custom_call" | custom-call | flops 3500000000 | tf_op jit(solution)/shard_map/pallas_call | solution.py:611
  154.4 11.3 %shard_map.270.refs_6_ = f32[512,64]{1,0:T(8,128)} custom-call(bf16[2,640,2560]{2,1,0:T(8,128)(2,1)} %get-tuple-element.103.r0_ref.r1_ref.a_ref, bf16[576,2304]{1,0:T(8,128)(2,1)} %get-tuple-element.141.cur_ref.prev_ref.r_ref), custom_call_target="tpu_custom_call" | custom-call | flops 5500000256 | tf_op jit(solution)/shard_map/pallas_call | solution.py:636
  165.8 2.3 collective-permute-start.9
  168.1 0.1 fusion.2
  168.3 2.6 collective-permute-start.15
  170.9 13.6 %shard_map.269.refs_5_ = f32[256,32]{1,0:T(8,128)} custom-call(bf16[4,336,5376]{2,1,0:T(8,128)(2,1)} %get-tuple-element.137.x_ref.n_ref, bf16[4,336,5376]{2,1,0:T(8,128)(2,1)} %get-tuple-element.137.x_ref.n_ref, bf16[2,640,2560]{2,1,0:T(8,128)(2,1)} %get-tuple-element.140.r_ref.own_ref), custom_call_target="tpu_custom_call" | custom-call | flops 7000000000 | tf_op jit(solution)/shard_map/pallas_call | solution.py:685
  184.7 1.3 collective-permute-start.16
  186.0 2.7 %shard_map.272 = bf16[768,128]{1,0:T(8,128)(2,1)} custom-call(s32[4]{0:T(128)} %pad_add_fusion.flag_ref, f32[32,256]{1,0:T(8,128)} %get-tuple-element.130.refs_0_, f32[32,256]{1,0:T(8,128)} %get-tuple-element.132.refs_1_, f32[32,256]{1,0:T(8,128)} %get-tuple-element.134.refs_2_, f32[64,256]{1,0:T(8,128)} %get-tuple-element.135.refs_3_, ...), custom_call_target="tpu_custom_call" | custom-call | flops 1500000000 | tf_op jit(solution)/shard_map/pallas_call | solution.py:757
  188.7 5.5 %collective-permute-done.16 = bf16[512,128]{1,0:T(8,128)(2,1)S(1)} collective-permute-done((bf16[512,128]{1,0:T(8,128)(2,1)S(1)}, bf16[512,128]{1,0:T(8,128)(2,1)S(1)}, u32[]{:S(2)}, u32[]{:S(2)}) %collective-permute-start.16) | collective-permute-done | bytes 131104 | tf_op jit(solution)/shard_map/ppermute | solution.py:855
  194.2 2.6 collective-permute-start.17
  196.9 4.6 %collective-permute-start.19 = (bf16[2,2,1120,128]{3,2,1,0:T(8,128)(2,1)S(1)}, bf16[2,2,1120,128]{3,2,1,0:T(8,128)(2,1)S(1)}, u32[]{:S(2)}, u32[]{:S(2)}) collective-permute-start(bf16[2,2,1120,128]{3,2,1,0:T(8,128)(2,1)S(1)} %copy-done.13), channel_id=1, source_target_pairs={{0,16},{1,17},{2,18},{3,19},{4,20},{5,21},{6,22},{7,23},{8,24},{9,... | collective-permute-start | bytes 3440648 | tf_op jit(solution)/shard_map/ppermute | solution.py:855
  201.5 2.3 shard_map.273
  203.9 0.5 collective-permute-start.18
  204.5 1.6 collective-permute-start.11
  206.1 7.4 %shard_map.274 = (bf16[84,84,2,224]{3,2,1,0:T(2,128)(2,1)}, bf16[640,256]{1,0:T(8,128)(2,1)}) custom-call(s32[4]{0:T(128)} %pad_add_fusion.flag_ref, bf16[2,640,2560]{2,1,0:T(8,128)(2,1)} %get-tuple-element.140.r_ref.own_ref, bf16[6,1008,128]{2,1,0:T(8,128)(2,1)} %copy-done, bf16[6,1008,128]{2,1,0:T(8,128)(2,1)} %copy-done, ...), custom_call_target="tpu_custom_call" | custom-call | flops 6000000000 | tf_op jit(solution)/shard_map/pallas_call | solution.py:546
  213.6 10.8 %collective-permute-done.19.rest_0_ = bf16[2,2,1120,128]{3,2,1,0:T(8,128)(2,1)S(1)} collective-permute-done((bf16[2,2,1120,128]{3,2,1,0:T(8,128)(2,1)S(1)}, bf16[2,2,1120,128]{3,2,1,0:T(8,128)(2,1)S(1)}, u32[]{:S(2)}, u32[]{:S(2)}) %collective-permute-start.19) | collective-permute-done | bytes 1146912 | tf_op jit(solution)/shard_map/ppermute | solution.py:855
  224.4 1.5 collective-permute-start.20
  226.0 0.5 collective-permute-start.12
  226.5 5.0 %shard_map.275 = (bf16[84,84,2,224]{3,2,1,0:T(2,128)(2,1)}, bf16[640,256]{1,0:T(8,128)(2,1)}) custom-call(s32[4]{0:T(128)} %pad_add_fusion.flag_ref, bf16[2,640,2560]{2,1,0:T(8,128)(2,1)} %get-tuple-element.140.r_ref.own_ref, bf16[6,1008,128]{2,1,0:T(8,128)(2,1)} %copy-done, bf16[6,1008,128]{2,1,0:T(8,128)(2,1)} %copy-done, ...), custom_call_target="tpu_custom_call", output_to_operand_aliasing={{0}: (8, {})} | custom-call | flops 3000000000 | tf_op jit(solution)/shard_map/pallas_call | solution.py:546
  231.5 0.3 collective-permute-done.12
  231.8 0.4 collective-permute-start.13
  232.2 3.5 %collective-permute-done.20 = bf16[4,512,128]{2,1,0:T(8,128)(2,1)S(1)} collective-permute-done((bf16[4,512,128]{2,1,0:T(8,128)(2,1)S(1)}, bf16[4,512,128]{2,1,0:T(8,128)(2,1)S(1)}, u32[]{:S(2)}, u32[]{:S(2)}) %collective-permute-start.20) | collective-permute-done | bytes 524320 | tf_op jit(solution)/shard_map/ppermute | solution.py:860
  235.9 4.7 %collective-permute-done.13 = bf16[768,128]{1,0:T(8,128)(2,1)S(1)} collective-permute-done((bf16[768,128]{1,0:T(8,128)(2,1)S(1)}, bf16[768,128]{1,0:T(8,128)(2,1)S(1)}, u32[]{:S(2)}, u32[]{:S(2)}) %collective-permute-start.13) | collective-permute-done | bytes 196640 | tf_op jit(solution)/shard_map/ppermute | solution.py:860
  240.6 5.6 %collective-permute-start.14 = (bf16[768,128]{1,0:T(8,128)(2,1)S(1)}, bf16[768,128]{1,0:T(8,128)(2,1)S(1)}, u32[]{:S(2)}, u32[]{:S(2)}) collective-permute-start(bf16[768,128]{1,0:T(8,128)(2,1)S(1)} %add_convert_fusion.2.own_ref), channel_id=1, source_target_pairs={{0,16},{1,17},{2,18},{3,19},{4,20},{5,21},{6,22},{7,23},{8,24},{9,... | collective-permute-start | bytes 589832 | tf_op jit(solution)/shard_map/ppermute | solution.py:855
  246.2 4.3 %shard_map.278 = (bf16[84,84,2,224]{3,2,1,0:T(2,128)(2,1)}, bf16[640,256]{1,0:T(8,128)(2,1)}) custom-call(s32[4]{0:T(128)} %pad_add_fusion.flag_ref, bf16[2,640,2560]{2,1,0:T(8,128)(2,1)} %get-tuple-element.140.r_ref.own_ref, bf16[2,2,1120,128]{3,2,1,0:T(8,128)(2,1)} %collective-permute-done.9.rest_0_, ...), custom_call_target="tpu_custom_call", output_to_operand_aliasing={{0}: (5, {})} | custom-call | flops 3000000000 | tf_op jit(solution)/shard_map/pallas_call | solution.py:546
  250.6 0.7 copy-done.15
  251.3 2.0 shard_map.276
  253.2 5.2 %shard_map.279 = (bf16[84,84,2,224]{3,2,1,0:T(2,128)(2,1)}, bf16[640,256]{1,0:T(8,128)(2,1)}) custom-call(s32[4]{0:T(128)} %pad_add_fusion.flag_ref, bf16[2,640,2560]{2,1,0:T(8,128)(2,1)} %get-tuple-element.140.r_ref.own_ref, bf16[2,2,1120,128]{3,2,1,0:T(8,128)(2,1)} %copy-done.5, ...), custom_call_target="tpu_custom_call", output_to_operand_aliasing={{0}: (5, {})} | custom-call | flops 3000000000 | tf_op jit(solution)/shard_map/pallas_call | solution.py:546
  258.4 1.0 copy-done.14
  259.4 6.9 %shard_map.277 = (f32[3136,256]{1,0:T(8,128)}, f32[918,256]{1,0:T(8,128)}) custom-call(s32[4]{0:T(128)} %pad_add_fusion.flag_ref, bf16[8,512,128]{2,1,0:T(8,128)(2,1)} %bitcast.101, bf16[8,512,128]{2,1,0:T(8,128)(2,1)} %copy-done.14), custom_call_target="tpu_custom_call" | custom-call | flops 3500000000 | tf_op jit(solution)/shard_map/pallas_call | solution.py:833
  (66 shorter events, 0.9 us)
Async XLA Ops:
  0.6 4.7 %copy-start.16 = (bf16[1,4,4,32,64]{4,3,2,1,0:T(8,128)(2,1)S(1)}, bf16[1,4,4,32,64]{4,3,2,1,0:T(8,128)(2,1)}, u32[]{:S(2)}) copy-start(bf16[1,4,4,32,64]{4,3,2,1,0:T(8,128)(2,1)} %param.22) | copy-start | bytes 196612
  0.7 9.5 %copy-start.10 = (bf16[1,8,8,4,32]{4,3,2,1,0:T(4,128)(2,1)S(1)}, bf16[1,8,8,4,32]{4,3,2,1,0:T(4,128)(2,1)}, u32[]{:S(2)}) copy-start(bf16[1,8,8,4,32]{4,3,2,1,0:T(4,128)(2,1)} %param.20) | copy-start | bytes 49156
  5.3 19.7 %collective-permute-start.2 = (bf16[4,4,32,64]{3,2,1,0:T(8,128)(2,1)S(1)}, bf16[4,4,32,64]{3,2,1,0:T(8,128)(2,1)S(1)}, u32[]{:S(2)}, u32[]{:S(2)}) collective-permute-start(bf16[4,4,32,64]{3,2,1,0:T(8,128)(2,1)S(1)} %bitcast.115), channel_id=1, source_target_pairs={{0,16},{1,17},{2,18},{3,19},{4,20},{5,21},{6,22},{7,23},{8,24},{9,... | collective-permute-start | bytes 196616 | tf_op jit(solution)/shard_map/ppermute | solution.py:855
  10.2 14.8 %collective-permute-start.1 = (bf16[8,8,2,32]{3,2,1,0:T(2,128)(2,1)S(1)}, bf16[8,8,2,32]{3,2,1,0:T(2,128)(2,1)S(1)}, u32[]{:S(2)}, u32[]{:S(2)}) collective-permute-start(bf16[8,8,2,32]{3,2,1,0:T(2,128)(2,1)S(1)} %slice.28), channel_id=1, source_target_pairs={{0,16},{1,17},{2,18},{3,19},{4,20},{5,21},{6,22},{7,23},{8,24},{9,... | collective-permute-start | bytes 24584 | tf_op jit(solution)/shard_map/ppermute | solution.py:855
  25.0 0.7 copy-start.18
  25.0 0.7 copy-start.17
  25.7 60.1 %collective-permute-start.3 = (bf16[4,2,1120,128]{3,2,1,0:T(8,128)(2,1)}, bf16[4,2,1120,128]{3,2,1,0:T(8,128)(2,1)}, u32[]{:S(2)}, u32[]{:S(2)}) collective-permute-start(bf16[4,2,1120,128]{3,2,1,0:T(8,128)(2,1)} %get-tuple-element.118), channel_id=1, source_target_pairs={{0,16},{1,17},{2,18},{3,19},{4,20},{5,21},{6,22},{7,23},{8,24},{9,... | collective-permute-start | bytes 6881288 | tf_op jit(solution)/shard_map/ppermute | solution.py:855
  57.8 9.2 %copy-start.11 = (s32[224]{0:T(256)S(1)}, s32[224]{0:T(256)}, u32[]{:S(2)}) copy-start(s32[224]{0:T(256)} %param.31) | copy-start | bytes 2692
  57.8 9.2 %copy-start.12 = (s32[224]{0:T(256)S(1)}, s32[224]{0:T(256)}, u32[]{:S(2)}) copy-start(s32[224]{0:T(256)} %param.30) | copy-start | bytes 2692
  57.8 9.8 %copy-start.3 = (bf16[1,3136,512]{2,1,0:T(8,128)(2,1)S(1)}, bf16[1,3136,512]{2,1,0:T(8,128)(2,1)}, u32[]{:S(2)}) copy-start(bf16[1,3136,512]{2,1,0:T(8,128)(2,1)} %param.26) | copy-start | bytes 9633796
  71.2 12.3 %copy-start.7 = (bf16[1,512,918]{1,2,0:T(8,128)(2,1)S(1)}, bf16[1,512,918]{1,2,0:T(8,128)(2,1)}, u32[]{:S(2)}) copy-start(bf16[1,512,918]{1,2,0:T(8,128)(2,1)} %param.28) | copy-start | bytes 2820100
  74.1 6.0 %collective-permute-start = (bf16[51,224]{1,0:T(8,128)(2,1)}, bf16[51,224]{1,0:T(8,128)(2,1)S(1)}, u32[]{:S(2)}, u32[]{:S(2)}) collective-permute-start(bf16[51,224]{1,0:T(8,128)(2,1)} %get-tuple-element.109), channel_id=1, source_target_pairs={{16,0},{17,1},{18,2},{19,3},{20,4},{21,5},{22,6},{23,7},{24,8},{25... | collective-permute-start | bytes 68552 | tf_op jit(solution)/shard_map/ppermute | solution.py:956
  80.1 0.6 copy-start.19
  93.9 10.3 %collective-permute-start.4 = (bf16[8,2,512,128]{3,2,1,0:T(8,128)(2,1)}, bf16[8,2,512,128]{3,2,1,0:T(8,128)(2,1)S(1)}, u32[]{:S(2)}, u32[]{:S(2)}) collective-permute-start(bf16[8,2,512,128]{3,2,1,0:T(8,128)(2,1)} %get-tuple-element.121), channel_id=1, source_target_pairs={{0,1},{1,0},{2,3},{3,2},{4,5},{5,4},{6,7},{7,6},{8,9},{9,8},{10,11... | collective-permute-start | bytes 6291464 | tf_op jit(solution)/shard_map/ppermute | solution.py:860
  93.9 28.1 %collective-permute-start.5 = (bf16[2,2,1120,128]{3,2,1,0:T(8,128)(2,1)}, bf16[2,2,1120,128]{3,2,1,0:T(8,128)(2,1)}, u32[]{:S(2)}, u32[]{:S(2)}) collective-permute-start(bf16[2,2,1120,128]{3,2,1,0:T(8,128)(2,1)} %get-tuple-element.126), channel_id=1, source_target_pairs={{0,16},{1,17},{2,18},{3,19},{4,20},{5,21},{6,22},{7,23},{8,24},{9,... | collective-permute-start | bytes 3440648 | tf_op jit(solution)/shard_map/ppermute | solution.py:855
  104.2 1.3 copy-start.4
  109.4 34.0 %collective-permute-start.6 = (bf16[4,2,512,128]{3,2,1,0:T(8,128)(2,1)}, bf16[4,2,512,128]{3,2,1,0:T(8,128)(2,1)}, u32[]{:S(2)}, u32[]{:S(2)}) collective-permute-start(bf16[4,2,512,128]{3,2,1,0:T(8,128)(2,1)} %dynamic-slice_bitcast_fusion), channel_id=1, source_target_pairs={{0,2},{1,3},{2,0},{3,1},{4,6},{5,7},{6,4},{7,5},{8,10},{9,11},{10,... | collective-permute-start | bytes 3145736 | tf_op jit(solution)/shard_map/ppermute | solution.py:860
  122.0 43.7 %collective-permute-start.8 = (bf16[6,1008,128]{2,1,0:T(8,128)(2,1)}, bf16[6,1008,128]{2,1,0:T(8,128)(2,1)S(1)}, u32[]{:S(2)}, u32[]{:S(2)}) collective-permute-start(bf16[6,1008,128]{2,1,0:T(8,128)(2,1)} %get-tuple-element.146), channel_id=1, source_target_pairs={{0,16},{1,17},{2,18},{3,19},{4,20},{5,21},{6,22},{7,23},{8,24},{9,... | collective-permute-start | bytes 4644872 | tf_op jit(solution)/shard_map/ppermute | solution.py:855
  144.9 1.0 copy-start.1
  145.9 22.2 %collective-permute-start.7 = (bf16[2,2,512,128]{3,2,1,0:T(8,128)(2,1)S(1)}, bf16[2,2,512,128]{3,2,1,0:T(8,128)(2,1)S(1)}, u32[]{:S(2)}, u32[]{:S(2)}) collective-permute-start(bf16[2,2,512,128]{3,2,1,0:T(8,128)(2,1)S(1)} %dynamic-slice_bitcast_fusion.1), channel_id=1, source_target_pairs={{0,4},{1,5},{2,6},{3,7},{4,0},{5,1},{6,2},{7,3},{8,12},{9,13},{10,... | collective-permute-start | bytes 1572872 | tf_op jit(solution)/shard_map/ppermute | solution.py:860
  154.4 13.7 %copy-start.2 = (bf16[4,2,512,128]{3,2,1,0:T(8,128)(2,1)S(1)}, bf16[4,2,512,128]{3,2,1,0:T(8,128)(2,1)}, u32[]{:S(2)}) copy-start(bf16[4,2,512,128]{3,2,1,0:T(8,128)(2,1)} %copy-done.1) | copy-start | bytes 3145732
  165.8 18.8 %copy-start = (bf16[6,1008,128]{2,1,0:T(8,128)(2,1)}, bf16[6,1008,128]{2,1,0:T(8,128)(2,1)S(1)}, u32[]{:S(2)}) copy-start(bf16[6,1008,128]{2,1,0:T(8,128)(2,1)S(1)} %collective-permute-done.8.rest_0_.rest_1_) | copy-start | bytes 4644868
  165.8 31.1 %collective-permute-start.9 = (bf16[2,2,1120,128]{3,2,1,0:T(8,128)(2,1)}, bf16[2,2,1120,128]{3,2,1,0:T(8,128)(2,1)}, u32[]{:S(2)}, u32[]{:S(2)}) collective-permute-start(bf16[2,2,1120,128]{3,2,1,0:T(8,128)(2,1)} %get-tuple-element.147), channel_id=1, source_target_pairs={{0,16},{1,17},{2,18},{3,19},{4,20},{5,21},{6,22},{7,23},{8,24},{9,... | collective-permute-start | bytes 3440648 | tf_op jit(solution)/shard_map/ppermute | solution.py:855
  168.3 16.3 %collective-permute-start.15 = (bf16[1,2,512,128]{3,2,1,0:T(8,128)(2,1)S(1)}, bf16[1,2,512,128]{3,2,1,0:T(8,128)(2,1)S(1)}, u32[]{:S(2)}, u32[]{:S(2)}) collective-permute-start(bf16[1,2,512,128]{3,2,1,0:T(8,128)(2,1)S(1)} %constant_dynamic-slice_fusion), channel_id=1, source_target_pairs={{0,8},{1,9},{2,10},{3,11},{4,12},{5,13},{6,14},{7,15},{8,0},{9,1},... | collective-permute-start | bytes 786440 | tf_op jit(solution)/shard_map/ppermute | solution.py:860
  184.7 9.5 %collective-permute-start.16 = (bf16[512,128]{1,0:T(8,128)(2,1)S(1)}, bf16[512,128]{1,0:T(8,128)(2,1)S(1)}, u32[]{:S(2)}, u32[]{:S(2)}) collective-permute-start(bf16[512,128]{1,0:T(8,128)(2,1)S(1)} %slice_bitcast_fusion), channel_id=1, source_target_pairs={{0,16},{1,17},{2,18},{3,19},{4,20},{5,21},{6,22},{7,23},{8,24},{9,... | collective-permute-start | bytes 393224 | tf_op jit(solution)/shard_map/ppermute | solution.py:855
  186.0 10.9 %copy-start.13 = (bf16[2,2,1120,128]{3,2,1,0:T(8,128)(2,1)S(1)}, bf16[2,2,1120,128]{3,2,1,0:T(8,128)(2,1)}, u32[]{:S(2)}) copy-start(bf16[2,2,1120,128]{3,2,1,0:T(8,128)(2,1)} %get-tuple-element.163) | copy-start | bytes 3440644
  194.2 9.7 %collective-permute-start.17 = (bf16[1,512,128]{2,1,0:T(8,128)(2,1)S(1)}, bf16[1,512,128]{2,1,0:T(8,128)(2,1)S(1)}, u32[]{:S(2)}, u32[]{:S(2)}) collective-permute-start(bf16[1,512,128]{2,1,0:T(8,128)(2,1)S(1)} %get-tuple-element.177), channel_id=1, source_target_pairs={{0,8},{1,9},{2,10},{3,11},{4,12},{5,13},{6,14},{7,15},{8,0},{9,1},... | collective-permute-start | bytes 393224 | tf_op jit(solution)/shard_map/ppermute | solution.py:860
  196.9 7.6 %copy-start.8 = (bf16[768,128]{1,0:T(8,128)(2,1)S(1)}, bf16[768,128]{1,0:T(8,128)(2,1)}, u32[]{:S(2)}) copy-start(bf16[768,128]{1,0:T(8,128)(2,1)} %shard_map.272) | copy-start | bytes 589828
  196.9 27.5 %collective-permute-start.19 = (bf16[2,2,1120,128]{3,2,1,0:T(8,128)(2,1)S(1)}, bf16[2,2,1120,128]{3,2,1,0:T(8,128)(2,1)S(1)}, u32[]{:S(2)}, u32[]{:S(2)}) collective-permute-start(bf16[2,2,1120,128]{3,2,1,0:T(8,128)(2,1)S(1)} %copy-done.13), channel_id=1, source_target_pairs={{0,16},{1,17},{2,18},{3,19},{4,20},{5,21},{6,22},{7,23},{8,24},{9,... | collective-permute-start | bytes 3440648 | tf_op jit(solution)/shard_map/ppermute | solution.py:855
  201.5 3.0 %collective-permute-start.10 = (bf16[768,128]{1,0:T(8,128)(2,1)}, bf16[768,128]{1,0:T(8,128)(2,1)S(1)}, u32[]{:S(2)}, u32[]{:S(2)}) collective-permute-start(bf16[768,128]{1,0:T(8,128)(2,1)} %shard_map.272), channel_id=1, source_target_pairs={{0,1},{1,0},{2,3},{3,2},{4,5},{5,4},{6,7},{7,6},{8,9},{9,8},{10,11... | collective-permute-start | bytes 589832 | tf_op jit(solution)/shard_map/ppermute | solution.py:860
  203.9 9.6 %collective-permute-start.18 = (bf16[2,512,128]{2,1,0:T(8,128)(2,1)S(1)}, bf16[2,512,128]{2,1,0:T(8,128)(2,1)S(1)}, u32[]{:S(2)}, u32[]{:S(2)}) collective-permute-start(bf16[2,512,128]{2,1,0:T(8,128)(2,1)S(1)} %get-tuple-element.179), channel_id=1, source_target_pairs={{0,4},{1,5},{2,6},{3,7},{4,0},{5,1},{6,2},{7,3},{8,12},{9,13},{10,... | collective-permute-start | bytes 786440 | tf_op jit(solution)/shard_map/ppermute | solution.py:860
  204.5 21.4 %collective-permute-start.11 = (bf16[768,128]{1,0:T(8,128)(2,1)S(1)}, bf16[768,128]{1,0:T(8,128)(2,1)S(1)}, u32[]{:S(2)}, u32[]{:S(2)}) collective-permute-start(bf16[768,128]{1,0:T(8,128)(2,1)S(1)} %add_convert_fusion.5), channel_id=1, source_target_pairs={{0,2},{1,3},{2,0},{3,1},{4,6},{5,7},{6,4},{7,5},{8,10},{9,11},{10,... | collective-permute-start | bytes 589832 | tf_op jit(solution)/shard_map/ppermute | solution.py:860
  224.4 7.1 %copy-start.5 = (bf16[2,2,1120,128]{3,2,1,0:T(8,128)(2,1)}, bf16[2,2,1120,128]{3,2,1,0:T(8,128)(2,1)S(1)}, u32[]{:S(2)}) copy-start(bf16[2,2,1120,128]{3,2,1,0:T(8,128)(2,1)S(1)} %collective-permute-done.19.rest_0_) | copy-start | bytes 3440644
  224.4 11.3 %collective-permute-start.20 = (bf16[4,512,128]{2,1,0:T(8,128)(2,1)S(1)}, bf16[4,512,128]{2,1,0:T(8,128)(2,1)S(1)}, u32[]{:S(2)}, u32[]{:S(2)}) collective-permute-start(bf16[4,512,128]{2,1,0:T(8,128)(2,1)S(1)} %bitcast.98), channel_id=1, source_target_pairs={{0,2},{1,3},{2,0},{3,1},{4,6},{5,7},{6,4},{7,5},{8,10},{9,11},{10,... | collective-permute-start | bytes 1572872 | tf_op jit(solution)/shard_map/ppermute | solution.py:860
  226.0 5.7 %collective-permute-start.12 = (bf16[768,128]{1,0:T(8,128)(2,1)S(1)}, bf16[768,128]{1,0:T(8,128)(2,1)S(1)}, u32[]{:S(2)}, u32[]{:S(2)}) collective-permute-start(bf16[768,128]{1,0:T(8,128)(2,1)S(1)} %add_convert_fusion.4), channel_id=1, source_target_pairs={{0,4},{1,5},{2,6},{3,7},{4,0},{5,1},{6,2},{7,3},{8,12},{9,13},{10,... | collective-permute-start | bytes 589832 | tf_op jit(solution)/shard_map/ppermute | solution.py:860
  231.8 8.7 %collective-permute-start.13 = (bf16[768,128]{1,0:T(8,128)(2,1)S(1)}, bf16[768,128]{1,0:T(8,128)(2,1)S(1)}, u32[]{:S(2)}, u32[]{:S(2)}) collective-permute-start(bf16[768,128]{1,0:T(8,128)(2,1)S(1)} %add_convert_fusion.3), channel_id=1, source_target_pairs={{0,8},{1,9},{2,10},{3,11},{4,12},{5,13},{6,14},{7,15},{8,0},{9,1},... | collective-permute-start | bytes 589832 | tf_op jit(solution)/shard_map/ppermute | solution.py:860
  235.8 14.8 %copy-start.6 = (bf16[4,2,512,128]{3,2,1,0:T(8,128)(2,1)}, bf16[4,2,512,128]{3,2,1,0:T(8,128)(2,1)S(1)}, u32[]{:S(2)}) copy-start(bf16[4,2,512,128]{3,2,1,0:T(8,128)(2,1)S(1)} %pad_maximum_fusion) | copy-start | bytes 3145732
  235.8 22.6 %collective-permute-start.21 = (bf16[8,512,128]{2,1,0:T(8,128)(2,1)S(1)}, bf16[8,512,128]{2,1,0:T(8,128)(2,1)S(1)}, u32[]{:S(2)}, u32[]{:S(2)}) collective-permute-start(bf16[8,512,128]{2,1,0:T(8,128)(2,1)S(1)} %bitcast.100), channel_id=1, source_target_pairs={{0,1},{1,0},{2,3},{3,2},{4,5},{5,4},{6,7},{7,6},{8,9},{9,8},{10,11... | collective-permute-start | bytes 3145736 | tf_op jit(solution)/shard_map/ppermute | solution.py:860
  240.6 10.0 %copy-start.9 = (bf16[768,128]{1,0:T(8,128)(2,1)}, bf16[768,128]{1,0:T(8,128)(2,1)S(1)}, u32[]{:S(2)}) copy-start(bf16[768,128]{1,0:T(8,128)(2,1)S(1)} %add_convert_fusion.2.own_ref) | copy-start | bytes 589828
  240.6 10.0 %collective-permute-start.14 = (bf16[768,128]{1,0:T(8,128)(2,1)S(1)}, bf16[768,128]{1,0:T(8,128)(2,1)S(1)}, u32[]{:S(2)}, u32[]{:S(2)}) collective-permute-start(bf16[768,128]{1,0:T(8,128)(2,1)S(1)} %add_convert_fusion.2.own_ref), channel_id=1, source_target_pairs={{0,16},{1,17},{2,18},{3,19},{4,20},{5,21},{6,22},{7,23},{8,24},{9,... | collective-permute-start | bytes 589832 | tf_op jit(solution)/shard_map/ppermute | solution.py:855
  250.6 0.7 copy-start.15
  258.4 1.0 copy-start.14

commit v3 on v2

--- a/solution.py
+++ b/solution.py
@@ -21,7 +21,7 @@
 
 
 def cost(us):
-    return pl.CostEstimate(flops=int(us * 0.5e9), bytes_accessed=0, transcendentals=0)
+    return pl.CostEstimate(flops=int(us * 0.4e9), bytes_accessed=0, transcendentals=0)
 
 
 def call(kernel, out, ins, outs, us, grid=None, scratch=()):
@@ -73,7 +73,7 @@
                 ]
 
 
-def bands_kernel(k1, b1, k2, b2, k3, b3, t1, t2, t3, t3b, t2b, b2c, w1, w2, w3, w3b, w2b):
+def bands_kernel(k1, b1, k2, b2, k3, b3, t1, t2, t3, t3b, t2b, b2c, send, w1, w2, w3, w3b, w2b):
     for ref in (w1, w2, w3, w3b, w2b):
         ref[...] = jnp.zeros_like(ref)
 
@@ -84,6 +84,9 @@
         return flat, flat.T, bias.T[:, :1]
 
     _, k1t, b1c = turned(k1, b1)
+    send[:512, :] = k2[...].reshape(512, 64)
+    send[512:, :32] = k1[:, :, 2:, :].astype(F32).reshape(128, 32).astype(BF)
+    send[512:, 32:] = jnp.zeros((128, 32), BF)
     k2n, k2t, b2t = turned(k2, b2)
     k3n, k3t, b3c = turned(k3, b3)
     for jj in range(10):
@@ -111,19 +114,19 @@
     shapes = ((320, 1424), (192, 1024), (448, 1744), (576, 1344), (640, 768))
     return call(
         bands_kernel,
-        tuple(sds(s, BF) for s in shapes) + (sds((192, 1), F32),),
+        tuple(sds(s, BF) for s in shapes) + (sds((192, 1), F32), sds((640, 64), BF)),
         [whole(a.shape) for a in ins],
-        [whole(s) for s in shapes] + [whole((192, 1))],
+        [whole(s) for s in shapes] + [whole((192, 1)), whole((640, 64))],
         scratch=[pltpu.VMEM(s, F32) for s in shapes],
         us=5,
     )(*ins)
 
 
-def band_frames_kernel(flag_ref, k1, k1_got, k2, k2_got, t1b, t2b, w1b, w2b):
+def band_frames_kernel(flag_ref, k1, k2, got, t1b, t2b, w1b, w2b):
     own = flag_ref[0] == 1
     w1b[...] = jnp.zeros_like(w1b)
     w2b[...] = jnp.zeros_like(w2b)
-    half = jnp.where(own, k1[:, :, :2, :].astype(F32), k1_got[...].astype(F32)).reshape(8, 16, 32)
+    half = jnp.where(own, k1[:, :, :2, :].astype(F32).reshape(128, 32), got[512:, :32].astype(F32)).reshape(8, 16, 32)
     for dy in range(8):
         t, row = divmod(dy, 4)
         for j in range(8):
@@ -133,7 +136,7 @@
             w1b[56 * row + 2 * lo : 56 * row + 2 * hi, 256 * t + 32 * j : 256 * t + 32 * j + 32] = half[
                 dy, 2 * d0 : 2 * (d0 + hi - lo), :
             ]
-    second_bands(jnp.where(own, k2[...].astype(F32), k2_got[...].astype(F32)).reshape(512, 64), w2b)
+    second_bands(jnp.where(own, k2[...].astype(F32).reshape(512, 64), got[:512, :].astype(F32)), w2b)
     t1b[...] = w1b[...].astype(BF)
     t2b[...] = (0.5 * w2b[...]).astype(BF)
 
@@ -165,114 +168,138 @@
     return jnp.concatenate([packed[:n], jnp.concatenate(tail + [last], axis=0)], axis=1)
 
 
-def conv1_kernel(rows, start, packs, x_ref, t1_ref, ones_ref, *rest):
+def conv1_kernel(rows, start, packs, first_ref, xa_ref, xb_ref, t1_ref, ones_ref, *rest):
     cells = rest[-1]
-    a_ref, s_ref, xt_ref, p_ref = rest[-5:-1]
-    c = pl.program_id(0) + start
-    slot = lax.rem(c, 2)
-
-    @pl.when(c == start)
+    a_ref, s_ref, xt_ref, p_ref = rest[-5:-1] if start else rest[-6:-2]
+    m = pl.program_id(0) + start
+
+    def relay(ref, slot):
+        for dy in range(4):
+            cells[slot, dy, :, :rows] = ref[dy].reshape(336, rows)
+
+    @pl.when(m == start)
     def _():
         cells[...] = jnp.zeros_like(cells)
-
+        relay(first_ref, 0)
+        if not start:
+            rest[-2][...] = cells[0]
+
+    relay(xa_ref, 1)
+    relay(xb_ref, 2)
+    slopes = []
+    for e in range(2):
+        parts_of = lambda window, e=e: [cells[e + t, dy, window, :] for t in range(2) for dy in range(4)]
+        row = []
+        for g in range(2):
+            half = dot(t1_ref[...], jnp.concatenate(parts_of(pl.ds(160 * g, 176)) + [ones_ref[...]], axis=0))
+            act, slope = act_slope(half)
+            a_ref[e, 320 * g : 320 * g + 320, :] = act.astype(BF)
+            s_ref[e, 320 * g : 320 * g + 320, :] = slope.astype(BF)
+            row.append(slope)
+        slopes.append(row)
+    if not start:
+        for e in range(2):
+            p_ref[0, e] = pack_rows(jnp.concatenate(slopes[e], axis=0), 640).astype(BF)
     for dy in range(4):
-        flat = x_ref[dy].reshape(336, rows)
-        cells[slot, dy, :, :rows] = flat
-        xt_ref[dy, :, :] = cells[slot, dy]
-
-    @pl.when(c > start)
-    def _():
-        slopes = []
-        for g in range(2):
-            window = pl.ds(160 * g, 176)
-            parts = [cells[1 - slot, dy, window, :] for dy in range(4)]
-            parts += [cells[slot, dy, window, :] for dy in range(4)]
-            half = dot(t1_ref[...], jnp.concatenate(parts + [ones_ref[...]], axis=0))
-            act, slope = act_slope(half)
-            a_ref[0, 320 * g : 320 * g + 320, :] = act.astype(BF)
-            s_ref[0, 320 * g : 320 * g + 320, :] = slope.astype(BF)
-            slopes.append(slope)
-        @pl.when(c <= packs)
+        xt_ref[dy, :, :LANES] = cells[1, dy]
+        xt_ref[dy, :, LANES:] = cells[2, dy]
+        cells[0, dy] = cells[2, dy]
+    if start:
+
+        @pl.when(m < packs)
         def _():
-            p_ref[0, 0] = pack_rows(jnp.concatenate(slopes, axis=0), 640).astype(BF)
+            for e in range(2):
+                p_ref[0, e] = pack_rows(s_ref[e].astype(F32), 640).astype(BF)
 
 
 def conv1(xv, t1, ones, start, stop, before):
     rows = xv.shape[3]
-    packs = min(stop, 2 * FAR)
-
-    def place(c):
-        i = jnp.maximum(c - 1 + start, start)
-        return (lax.rem(i, 2), i // 2)
-
-    out = pl.BlockSpec((1, 640, LANES), lambda c: (place(c)[0], 0, place(c)[1]))
-    outs = [out, out, pl.BlockSpec((4, 336, LANES), lambda c: (0, 0, c + start))]
-    shapes = [sds((2, 640, 10 * LANES), BF), sds((2, 640, 10 * LANES), BF), sds((4, 336, 21 * LANES), BF)]
-    def packed_place(c):
-        i = jnp.clip(c - 1, 0, packs - start - 1)
-        return (i // 2, lax.rem(i, 2), 0, 0)
-
-    outs.append(pl.BlockSpec((1, 1, 1120, 128), packed_place))
-    shapes.append(sds(((packs - start) // 2, 2, 1120, 128), BF))
+    packs = min(stop, FAR)
+    cell = lambda f: pl.BlockSpec((4, 84, 4, rows), lambda m: (f(m + start), 0, 0, 0))
+    out = pl.BlockSpec((2, 640, LANES), lambda m: (0, 0, m + start))
+    outs = [
+        out,
+        out,
+        pl.BlockSpec((4, 336, 2 * LANES), lambda m: (0, 0, m + start)),
+        pl.BlockSpec((1, 2, 1120, 128), lambda m: (jnp.minimum(m, packs - start - 1), 0, 0, 0)),
+    ]
+    shapes = [
+        sds((2, 640, 10 * LANES), BF),
+        sds((2, 640, 10 * LANES), BF),
+        sds((4, 336, 20 * LANES), BF),
+        sds((packs - start, 2, 1120, 128), BF),
+    ]
+    if not start:
+        outs.append(whole((4, 336, LANES)))
+        shapes.append(sds((4, 336, LANES), BF))
     return pl.pallas_call(
         functools.partial(conv1_kernel, rows, start, packs),
         out_shape=tuple(shapes),
-        grid=(stop - start + 1,),
-        in_specs=[pl.BlockSpec((4, 84, 4, rows), lambda c: (c + start, 0, 0, 0)), whole((320, 1424)), whole((16, LANES))]
+        grid=(stop - start,),
+        in_specs=[
+            pl.BlockSpec((4, 84, 4, rows), lambda m: (2 * start, 0, 0, 0)),
+            cell(lambda m: 2 * m + 1),
+            cell(lambda m: 2 * m + 2),
+            whole((320, 1424)),
+            whole((16, LANES)),
+        ]
         + [pl.BlockSpec(memory_space=pl.ANY)] * len(before),
         out_specs=outs,
-        scratch_shapes=[pltpu.VMEM((2, 4, 336, LANES), BF)],
-        input_output_aliases={3 + n: n for n in range(len(before))},
+        scratch_shapes=[pltpu.VMEM((3, 4, 336, LANES), BF)],
+        input_output_aliases={5 + n: n for n in range(len(before))},
         compiler_params=pltpu.CompilerParams(vmem_limit_bytes=VMEM_BIG),
-        cost_estimate=cost(0.1 * (stop - start)),
-    )(xv, t1, ones, *before)
-
-
-def conv2_kernel(r0_ref, r1_ref, t2_ref, b2_ref, a_ref, s_ref):
-    for g in range(3):
-        window = pl.ds(192 * g, 256)
-        parts = [r0_ref[0, window, :], r0_ref[1, window, :], r1_ref[0, window, :], r1_ref[1, window, :]]
-        half = dot(t2_ref[...], jnp.concatenate(parts, axis=0)) + b2_ref[...]
+        cost_estimate=cost(0.2 * (stop - start)),
+    )(xv, xv, xv, t1, ones, *before)
+
+
+def conv23_kernel(r0_ref, r1_ref, t2_ref, b2_ref, t3_ref, ones_ref, a2_ref, s2_ref, a3_ref, s3_ref, keep):
+    g = pl.program_id(0)
+
+    def third():
+        window = pl.ds(pl.multiple_of(576 * (g - 3), 64), 1728)
+        half = dot(t3_ref[...], jnp.concatenate([keep[window, :], ones_ref[...]], axis=0))
         act, slope = act_slope(half)
-        a_ref[192 * g : 192 * g + 192, :] = act.astype(BF)
-        s_ref[192 * g : 192 * g + 192, :] = slope.astype(BF)
-
-
-def conv2(a1, t2, b2):
-    out = pl.BlockSpec((576, LANES), lambda i: (0, i))
+        a3_ref[...] = act.astype(BF)
+        s3_ref[...] = slope.astype(BF)
+
+    def second():
+        for n in range(3):
+            window = pl.ds(192 * n, 256)
+            parts = [r0_ref[0, window, :], r0_ref[1, window, :], r1_ref[0, window, :], r1_ref[1, window, :]]
+            half = dot(t2_ref[...], jnp.concatenate(parts, axis=0)) + b2_ref[...]
+            act, slope = act_slope(half)
+            act = act.astype(BF)
+            a2_ref[192 * n : 192 * n + 192, :] = act
+            keep[pl.ds(pl.multiple_of(576 * g + 192 * n, 64), 192), :] = act
+            s2_ref[192 * n : 192 * n + 192, :] = slope.astype(BF)
+
+    @pl.when(g < 3)
+    def _():
+        second()
+
+    @pl.when((g >= 3) & (g < 9))
+    def _():
+        third()
+        second()
+
+    @pl.when(g == 9)
+    def _():
+        third()
+
+
+def conv23(a1, t2, b2, t3, ones):
+    row = lambda t: pl.BlockSpec((2, 640, LANES), lambda g: (0, 0, jnp.minimum(g, 8) + t))
+    out2 = pl.BlockSpec((576, LANES), lambda g: (0, jnp.minimum(g, 8)))
+    out3 = pl.BlockSpec((448, LANES), lambda g: (jnp.maximum(g - 3, 0), 0))
     return call(
-        conv2_kernel,
-        (sds((576, 9 * LANES), BF), sds((576, 9 * LANES), BF)),
-        [
-            pl.BlockSpec((2, 640, LANES), lambda i: (0, 0, i)),
-            pl.BlockSpec((2, 640, LANES), lambda i: (0, 0, i + 1)),
-            whole((192, 1024)),
-            whole((192, 1)),
-        ],
-        [out, out],
-        grid=(9,),
-        us=1,
-    )(a1, a1, t2, b2)
-
-
-def conv3_kernel(r0_ref, r1_ref, r2_ref, t3_ref, ones_ref, a_ref, s_ref):
-    half = dot(t3_ref[...], jnp.concatenate([r0_ref[...], r1_ref[...], r2_ref[...], ones_ref[...]], axis=0))
-    act, slope = act_slope(half)
-    a_ref[...] = act.astype(BF)
-    s_ref[...] = slope.astype(BF)
-
-
-def conv3(a2, t3, ones):
-    out = pl.BlockSpec((448, LANES), lambda i: (i, 0))
-    return call(
-        conv3_kernel,
-        (sds((3136, LANES), BF), sds((3136, LANES), BF)),
-        [pl.BlockSpec((576, LANES), lambda i, u=u: (0, i + u)) for u in range(3)]
-        + [whole((448, 1744)), whole((16, LANES))],
-        [out, out],
-        grid=(7,),
-        us=1,
-    )(a2, a2, a2, t3, ones)
+        conv23_kernel,
+        (sds((576, 9 * LANES), BF), sds((576, 9 * LANES), BF), sds((3136, LANES), BF), sds((3136, LANES), BF)),
+        [row(0), row(1), whole((192, 1024)), whole((192, 1)), whole((448, 1744)), whole((16, LANES))],
+        [out2, out2, out3, out3],
+        us=2,
+        grid=(10,),
+        scratch=[pltpu.VMEM((9 * 576, LANES), BF)],
+    )(a1, a1, t2, b2, t3, ones)
 
 
 def head_kernel(rows, pd_ref, bd_ref, wh_ref, bh_ref, sel_ref, act_ref, slope_ref, lp_ref, cho_ref, lg_ref):
@@ -344,59 +371,73 @@
     )(*ins)
 
 
-def dflat_kernel(w_ref, rd_ref, s_ref, r_ref, b_ref):
-    @pl.when(pl.program_id(0) == 0)
-    def _():
-        b_ref[...] = jnp.zeros_like(b_ref)
-
-    diff = dot(w_ref[...], rd_ref[...]) * (0.5 * s_ref[...].astype(F32))
-    r_ref[...] = diff.astype(BF)
-    b_ref[...] += jnp.sum(diff.reshape(7, 64, LANES), axis=0)
-
-
-def dflat(wd, rd, s3):
-    block = pl.BlockSpec((448, LANES), lambda i: (i, 0))
+def dthird_kernel(w_ref, rd_ref, s3_ref, t_ref, s2_ref, r3_ref, b3_ref, r2_ref, p_ref, b2_ref, keep):
+    g = pl.program_id(0)
+
+    def third():
+        diff = dot(w_ref[...], rd_ref[...]) * (0.5 * s3_ref[...].astype(F32))
+        part = diff.astype(BF)
+        r3_ref[...] = part
+        keep[pl.ds(pl.multiple_of(448 * (g + 2), 64), 448), :] = part
+        b3_ref[...] += jnp.sum(diff.reshape(7, 64, LANES), axis=0)
+
+    def second():
+        window = pl.ds(pl.multiple_of(448 * (g - 1), 64), 1344)
+        diff = dot(t_ref[...], keep[window, :]) * s2_ref[...].astype(F32)
+        r2_ref[...] = diff.astype(BF)
+        b2_ref[...] += jnp.sum(diff.reshape(9, 64, LANES), axis=0)
+        return diff
+
+    def pack(diff):
+        p_ref[0] = pack_rows(diff, 576).astype(BF)
+
+    @pl.when(g == 0)
+    def _():
+        b3_ref[...] = jnp.zeros_like(b3_ref)
+        b2_ref[...] = jnp.zeros_like(b2_ref)
+        keep[:896, :] = jnp.zeros((896, LANES), BF)
+        keep[4032:, :] = jnp.zeros((896, LANES), BF)
+        third()
+
+    @pl.when((g >= 1) & (g < 7))
+    def _():
+        pack(second())
+        third()
+
+    @pl.when((g >= 7) & (g <= FAR))
+    def _():
+        pack(second())
+
+    @pl.when(g > FAR)
+    def _():
+        second()
+
+
+def dthird(wd, rd, s3, t3b, s2):
+    block3 = pl.BlockSpec((448, LANES), lambda g: (jnp.minimum(g, 6), 0))
+    block2 = pl.BlockSpec((576, LANES), lambda g: (0, jnp.maximum(g - 1, 0)))
+    packed = pl.BlockSpec((1, 1008, 128), lambda g: (jnp.clip(g - 1, 0, FAR - 1), 0, 0))
     return call(
-        dflat_kernel,
-        (sds((3136, LANES), BF), sds((64, LANES), F32)),
-        [pl.BlockSpec((448, 512), lambda i: (i, 0)), whole((512, LANES)), block],
-        [block, whole((64, LANES))],
-        grid=(7,),
-        us=2,
-    )(wd, rd, s3)
-
-
-def dconv3_kernel(r3_ref, t_ref, s_ref, r_ref, p_ref, b_ref, pad):
-    p = pl.program_id(0)
-
-    @pl.when(p == 0)
-    def _():
-        b_ref[...] = jnp.zeros_like(b_ref)
-        pad[:896, :] = jnp.zeros((896, LANES), BF)
-        pad[896:4032, :] = r3_ref[...]
-        pad[4032:, :] = jnp.zeros((896, LANES), BF)
-
-    window = pl.ds(pl.multiple_of(448 * p, 64), 1344)
-    diff = dot(t_ref[...], pad[window, :]) * s_ref[...].astype(F32)
-    r_ref[...] = diff.astype(BF)
-    b_ref[...] += jnp.sum(diff.reshape(9, 64, LANES), axis=0)
-
-    @pl.when(p < FAR)
-    def _():
-        p_ref[0] = pack_rows(diff, 576).astype(BF)
-
-
-def dconv3(r3, t3b, s2):
-    block = pl.BlockSpec((576, LANES), lambda p: (0, p))
-    return call(
-        dconv3_kernel,
-        (sds((576, 9 * LANES), BF), sds((FAR, 1008, 128), BF), sds((64, LANES), F32)),
-        [whole((3136, LANES)), whole((576, 1344)), block],
-        [block, pl.BlockSpec((1, 1008, 128), lambda p: (jnp.minimum(p, FAR - 1), 0, 0)), whole((64, LANES))],
-        grid=(9,),
+        dthird_kernel,
+        (
+            sds((3136, LANES), BF),
+            sds((64, LANES), F32),
+            sds((576, 9 * LANES), BF),
+            sds((FAR, 1008, 128), BF),
+            sds((64, LANES), F32),
+        ),
+        [
+            pl.BlockSpec((448, 512), lambda g: (jnp.minimum(g, 6), 0)),
+            whole((512, LANES)),
+            block3,
+            whole((576, 1344)),
+            block2,
+        ],
+        [block3, whole((64, LANES)), block2, packed, whole((64, LANES))],
+        us=1.5,
+        grid=(10,),
         scratch=[pltpu.VMEM((4928, LANES), BF)],
-        us=11,
-    )(r3, t3b, s2)
+    )(wd, rd, s3, t3b, s2)
 
 
 def first_diffs(t, cur, prev):
@@ -412,29 +453,47 @@
 
 
 def dconv2_kernel(first, packs, cur_ref, prev_ref, t_ref, s_ref, *rest):
-    r_ref, b_ref = (rest[-3], rest[-1]) if packs else rest[-2:]
-    m = pl.program_id(0) + first
+    dense = [(ref, n) for ref, (_, size) in zip(rest[-3:-1], NEAR) for n in range(size)] if packs else []
+    r_ref, b_ref = rest[-4 if packs else -2], rest[-1]
+    q = pl.program_id(0)
+    m = 2 * q + first
+    zero = jnp.zeros((576, LANES), BF)
 
     @pl.when(pl.program_id(0) == 0)
     def _():
         b_ref[...] = jnp.zeros_like(b_ref)
 
-    cur = jnp.where(m < 9, cur_ref[...], jnp.zeros((576, LANES), BF))
-    prev = jnp.where(m > 0, prev_ref[...], jnp.zeros((576, LANES), BF))
-    for e, part in enumerate(first_diffs(t_ref[...], cur, prev)):
-        part = part * s_ref[e].astype(F32)
-        r_ref[e] = part.astype(BF)
-        if packs:
-            rest[-2][0, e] = pack_rows(part, 640).astype(BF)
-        b_ref[...] += jnp.sum(part.reshape(20, 32, LANES), axis=0)
-
-
-def dconv2(r2, t2b, s1, first, count, packs, r1):
-    block = pl.BlockSpec((2, 640, LANES), lambda m: (0, 0, m + first))
+    r2 = [
+        jnp.where(m > 0, prev_ref[...], zero),
+        cur_ref[:, :LANES],
+        jnp.where(m < 8, cur_ref[:, LANES:], zero),
+    ]
+    total = b_ref[...]
+    for k in range(2):
+        lanes = slice(LANES * k, LANES * (k + 1))
+        for e, part in enumerate(first_diffs(t_ref[...], r2[k + 1], r2[k])):
+            part = part * s_ref[e, :, lanes].astype(F32)
+            r_ref[e, :, lanes] = part.astype(BF)
+            if packs:
+                value = pack_rows(part, 640).astype(BF)
+                for step in range(packs):
+
+                    @pl.when(q == step)
+                    def _(step=step, k=k, e=e, value=value):
+                        ref, n = dense[2 * step + k]
+                        ref[n, e] = value
+
+            total = total + jnp.sum(part.reshape(20, 32, LANES), axis=0)
+    b_ref[...] = total
+
+
+def dconv2(r2, t2b, s1, first, count, dense, r1):
+    packs = count // 2 if dense else 0
+    block = pl.BlockSpec((2, 640, 2 * LANES), lambda q: (0, 0, q + first // 2))
     ins = [r2, r2, t2b, s1]
     in_specs = [
-        pl.BlockSpec((576, LANES), lambda m: (0, jnp.minimum(m + first, 8))),
-        pl.BlockSpec((576, LANES), lambda m: (0, jnp.maximum(m + first - 1, 0))),
+        pl.BlockSpec((576, 2 * LANES), lambda q: (0, q + first // 2)),
+        pl.BlockSpec((576, LANES), lambda q: (0, jnp.maximum(2 * q + first - 1, 0))),
         whole((640, 768)),
         block,
     ]
@@ -443,14 +502,13 @@
         ins.append(r1)
         in_specs.append(pl.BlockSpec(memory_space=pl.ANY))
         aliases = {4: 0}
-    shapes = [sds((2, 640, 10 * LANES), BF), sds((count, 2, 1120, 128), BF), sds((32, LANES), F32)]
-    outs = [block, pl.BlockSpec((1, 2, 1120, 128), lambda m: (m, 0, 0, 0)), whole((32, LANES))]
-    if not packs:
-        del shapes[1], outs[1]
+    parts = [(size, 2, 1120, 128) for _, size in NEAR] if packs else []
+    shapes = [sds((2, 640, 10 * LANES), BF)] + [sds(p, BF) for p in parts] + [sds((32, LANES), F32)]
+    outs = [block] + [whole(p) for p in parts] + [whole((32, LANES))]
     return pl.pallas_call(
         functools.partial(dconv2_kernel, first, packs),
         out_shape=tuple(shapes),
-        grid=(count,),
+        grid=(count // 2,),
         in_specs=in_specs,
         out_specs=outs,
         input_output_aliases=aliases,
@@ -555,7 +613,7 @@
         ),
         input_output_aliases=aliases,
         compiler_params=pltpu.CompilerParams(vmem_limit_bytes=VMEM_BIG),
-        cost_estimate=cost(3 * count),
+        cost_estimate=cost(0.03 * count),
     )(*ins)
 
 
@@ -596,63 +654,92 @@
     )(flag, a3, rd, rh, h)
 
 
-def wconv3_kernel(a_ref, r_ref, g_ref):
-    acc = jnp.zeros((64, 576), F32)
-    for j in range(7):
-        left = jnp.concatenate(
-            [a_ref[64 * j : 64 * j + 192, LANES * u : LANES * (u + 7)] for u in range(3)], axis=0
-        )
-        right = jnp.concatenate([r_ref[448 * i + 64 * j : 448 * i + 64 * j + 64, :] for i in range(7)], axis=1)
-        acc = acc + dot_nt(right, left)
-    g_ref[...] = acc * (1.0 / LOSS_SCALE)
+def wconv3_kernel(*refs):
+    columns, (r_ref, g_ref, acc) = refs[:4], refs[4:]
+    q = pl.program_id(0)
+
+    @pl.when(q == 0)
+    def _():
+        acc[...] = jnp.zeros_like(acc)
+
+    left = jnp.concatenate([ref[:, LANES * u : LANES * (u + 7)] for u in range(3) for ref in columns], axis=0)
+    last = jnp.where(q < 3, r_ref[:, 64:, :], jnp.zeros((7, 64, LANES), BF))
+    right = jnp.concatenate([jnp.concatenate([r_ref[i, :64], last[i]], axis=0) for i in range(7)], axis=1)
+    acc[...] += dot_nt(left, right)
+
+    @pl.when(q == 3)
+    def _():
+        for u in range(3):
+            for v in range(3):
+                at = 256 * u + 64 * v
+                part = acc[at : at + 64, :64] + acc[at + 64 : at + 128, 64:]
+                g_ref[:, 192 * u + 64 * v : 192 * u + 64 * v + 64] = part.T * (1.0 / LOSS_SCALE)
 
 
 def wconv3(a2, r3):
     return call(
         wconv3_kernel,
         sds((64, 576), F32),
-        [whole(a2.shape), whole(r3.shape)],
+        [pl.BlockSpec((64, 9 * LANES), lambda q, k=k: (jnp.minimum(2 * q + k, 8), 0)) for k in range(4)]
+        + [pl.BlockSpec((7, 128, LANES), lambda q: (0, q, 0))],
         whole((64, 576)),
-        us=7,
-    )(a2, r3)
-
-
-def wconv2_kernel(a_ref, r_ref, g_ref):
-    g_ref[...] = jnp.zeros_like(g_ref)
-
-    def body(j, _):
-        window = pl.ds(pl.multiple_of(64 * j, 64), 128)
-        left = jnp.concatenate(
-            [a_ref[e, window, LANES * t : LANES * (t + 9)] for t in range(2) for e in range(2)], axis=0
-        )
-        g_ref[...] += dot_nt(left, r_ref[pl.ds(pl.multiple_of(64 * j, 64), 64), :])
-        return 0
-
-    lax.fori_loop(0, 9, body, 0)
-    g_ref[...] = g_ref[...] * (1.0 / LOSS_SCALE)
+        us=6,
+        grid=(4,),
+        scratch=[pltpu.VMEM((768, 128), F32)],
+    )(a2, a2, a2, a2, r3.reshape(7, 448, LANES))
+
+
+def wconv2_kernel(a0_ref, a1_ref, r_ref, g_ref, acc):
+    q = pl.program_id(0)
+
+    @pl.when(q == 0)
+    def _():
+        acc[...] = jnp.zeros_like(acc)
+
+    left = jnp.concatenate(
+        [ref[e, :, LANES * t : LANES * (t + 9)] for t in range(2) for e in range(2) for ref in (a0_ref, a1_ref)],
+        axis=0,
+    )
+    last = jnp.where(q < 4, r_ref[64:, :], jnp.zeros((64, 9 * LANES), BF))
+    acc[...] += dot_nt(left, jnp.concatenate([r_ref[:64, :], last], axis=0))
+
+    @pl.when(q == 4)
+    def _():
+        for u in range(4):
+            at = 192 * u
+            g_ref[128 * u : 128 * u + 128, :] = (acc[at : at + 128, :64] + acc[at + 64 : at + 192, 64:]) * (
+                1.0 / LOSS_SCALE
+            )
 
 
 def wconv2(a1, r2):
     return call(
         wconv2_kernel,
         sds((512, 64), F32),
-        [whole(a1.shape), whole(r2.shape)],
+        [
+            pl.BlockSpec((2, 128, 10 * LANES), lambda q: (0, q, 0)),
+            pl.BlockSpec((2, 64, 10 * LANES), lambda q: (0, jnp.minimum(2 * q + 2, 9), 0)),
+            pl.BlockSpec((128, 9 * LANES), lambda q: (q, 0)),
+        ],
         whole((512, 64)),
-        us=11,
-    )(a1, r2)
-
-
-def wconv1_kernel(x_ref, n_ref, r_ref, g_ref, acc):
+        us=8,
+        grid=(5,),
+        scratch=[pltpu.VMEM((768, 128), F32)],
+    )(a1, a1, r2)
+
+
+def wconv1_kernel(x_ref, x0_ref, r_ref, g_ref, acc, before):
     step = pl.program_id(0)
 
     @pl.when(step == 0)
     def _():
         acc[...] = jnp.zeros_like(acc)
+        before[...] = x0_ref[...]
 
     def column(dy, rows, c):
-        if c < 4:
-            return x_ref[dy, rows, LANES * c : LANES * (c + 1)]
-        return n_ref[dy, rows, :]
+        if c:
+            return x_ref[dy, rows, LANES * (c - 1) : LANES * c]
+        return before[dy, rows, :]
 
     total = acc[...]
     for g in range(5):
@@ -671,6 +758,7 @@
         )
         total = total + dot_nt(left, right)
     acc[...] = total
+    before[...] = x_ref[:, :, 3 * LANES :]
 
     @pl.when(step == 4)
     def _():
@@ -681,20 +769,20 @@
             g_ref[32 * dy : 32 * dy + 32, :] = part * (1.0 / LOSS_SCALE)
 
 
-def wconv1(xt, r1):
+def wconv1(xt, x0, r1):
     return call(
         wconv1_kernel,
         sds((256, 32), F32),
         [
             pl.BlockSpec((4, 336, 4 * LANES), lambda s: (0, 0, s)),
-            pl.BlockSpec((4, 336, LANES), lambda s: (0, 0, 4 * s + 4)),
+            whole((4, 336, LANES)),
             pl.BlockSpec((2, 640, 2 * LANES), lambda s: (0, 0, s)),
         ],
         whole((256, 32)),
+        us=14,
         grid=(5,),
-        scratch=[pltpu.VMEM((640, 128), F32)],
-        us=14,
-    )(xt, xt, r1)
+        scratch=[pltpu.VMEM((640, 128), F32), pltpu.VMEM((4, 336, LANES), BF)],
+    )(xt, x0, r1)
 
 
 SMALL_ROWS = 704
@@ -760,7 +848,7 @@
         [pl.BlockSpec(memory_space=pltpu.SMEM)] + [whole(a.shape) for a in ins],
         whole((total, 128)),
         scratch=[pltpu.VMEM((total, 128), F32)],
-        us=3,
+        us=0.1,
     )(flag, *ins)
 
 
@@ -818,32 +906,23 @@
 
 
 def unchunk_kernel(flag_ref, cur_ref, other_ref, d_ref, h_ref):
-    core = flag_ref[1]
-    cur, other = cur_ref[0].astype(F32), other_ref[0].astype(F32)
-    tile0 = jnp.where(core == 0, cur, other)
-    tile1 = jnp.where(core == 0, other, cur)
-    d_ref[:, :128] = tile0[:392]
-    d_ref[:, 128:] = tile1[:392]
-    h_ref[:, :128] = tile0[392:]
-    h_ref[:, 128:] = tile1[392:]
+    core, code = flag_ref[1], flag_ref[3]
+    for k in range(2):
+        block = (2 * pl.program_id(0) + k) ^ code
+        cur, other = cur_ref[block].astype(F32), other_ref[block].astype(F32)
+        for lane, tile in enumerate((jnp.where(core == 0, cur, other), jnp.where(core == 0, other, cur))):
+            d_ref[392 * k : 392 * k + 392, 128 * lane : 128 * lane + 128] = tile[:392]
+            h_ref[120 * k : 120 * k + 120, 128 * lane : 128 * lane + 128] = tile[392:]
 
 
 def unchunk(flag, cur, other):
-    part = pl.BlockSpec((1, 512, 128), lambda i, f: (i ^ f[3], 0, 0))
-    return pl.pallas_call(
+    return call(
         unchunk_kernel,
-        out_shape=(sds((3136, 256), F32), sds((LOGITS, 256), F32)),
-        grid_spec=pltpu.PrefetchScalarGridSpec(
-            num_scalar_prefetch=1,
-            grid=(8,),
-            in_specs=[part, part],
-            out_specs=[
-                pl.BlockSpec((392, 256), lambda i, *_: (i, 0)),
-                pl.BlockSpec((120, 256), lambda i, *_: (i, 0)),
-            ],
-        ),
-        compiler_params=pltpu.CompilerParams(vmem_limit_bytes=VMEM_BIG),
-        cost_estimate=cost(7),
+        (sds((3136, 256), F32), sds((LOGITS, 256), F32)),
+        [pl.BlockSpec(memory_space=pltpu.SMEM), whole(cur.shape), whole(other.shape)],
+        [pl.BlockSpec((784, 256), lambda i: (i, 0)), pl.BlockSpec((240, 256), lambda i: (i, 0))],
+        us=4,
+        grid=(4,),
     )(flag, cur, other)
 
 
@@ -864,26 +943,21 @@
     return (left.astype(F32) + right.astype(F32)).astype(BF)
 
 
-def reduce_chunks(keep, send, me):
+def split_blocks(cur):
     devices = lax.axis_size("batch")
-    got = swap(send, 1)
-    cur = add(keep, got)
-    blocks, spread = devices // 2, devices // 16
+    spread = devices // 16
     if spread > 1:
         cur = cur.reshape(8, 2, spread, 512 // spread, 128).transpose(0, 2, 1, 3, 4)
-        cur = cur.reshape(blocks, 2, 512 // spread, 128)
-    bit = 2
-    arrived = [got]
-    while bit < devices:
-        mine = (me // bit) % 2
-        pairs = cur.reshape((cur.shape[0] // 2, 2) + cur.shape[1:])
-        send = lax.dynamic_index_in_dim(pairs, 1 - mine, axis=1, keepdims=False)
-        keep = lax.dynamic_index_in_dim(pairs, mine, axis=1, keepdims=False)
-        got = swap(send, bit)
-        arrived.append(got)
-        cur = add(keep, got)
-        bit *= 2
-    return cur[0], arrived
+        cur = cur.reshape(devices // 2, 2, 512 // spread, 128)
+    return cur
+
+
+def halve(cur, me, bit):
+    mine = (me // bit) % 2
+    pairs = cur.reshape((cur.shape[0] // 2, 2) + cur.shape[1:])
+    send = lax.dynamic_index_in_dim(pairs, 1 - mine, axis=1, keepdims=False)
+    keep = lax.dynamic_index_in_dim(pairs, mine, axis=1, keepdims=False)
+    return keep, swap(send, bit)
 
 
 def unmix(blocks, code):
@@ -895,18 +969,8 @@
     return blocks
 
 
-def gather_chunks(mine, me, late):
-    devices = lax.axis_size("batch")
-    cur = mine[None]
-    bit = devices // 2
-    while bit > 1:
-        if bit == 2:
-            cur = after(cur, late)
-        other = swap(cur, bit)
-        cur = jnp.stack([cur, other], axis=1).reshape((2 * cur.shape[0],) + cur.shape[1:])
-        bit //= 2
-    other = swap(cur, 1)
-    return cur, other
+def join(cur, other):
+    return jnp.stack([cur, other], axis=1).reshape((2 * cur.shape[0],) + cur.shape[1:])
 
 
 def local(
@@ -938,15 +1002,14 @@
     xv = frames[0].transpose(2, 3, 1, 0)
     k1, k2, k3 = kernel_first[0], kernel_second[0], kernel_third[0]
     ones = jnp.zeros((16, LANES), BF).at[0].set(1)
-    t1, t2, t3, t3b, t2b, b2 = bands(k1, bias_first, k2, bias_second, k3, bias_third)
-
-    k1_got, k2_got = hand(after(k1[:, :, 2:], t1)), hand(after(k2, t1))
-    a1, s1, xt, early = conv1(xv, t1, ones, 0, 2 * EARLY, ())
-    early = hand(after(early, k1_got, k2_got))
-    a1, s1, xt, late = conv1(xv, t1, ones, 2 * EARLY, 20, (a1, s1, xt))
+    t1, t2, t3, t3b, t2b, b2, kernels = bands(k1, bias_first, k2, bias_second, k3, bias_third)
+
+    kernels = hand(kernels)
+    a1, s1, xt, early, x0 = conv1(xv, t1, ones, 0, EARLY, ())
+    early = hand(after(early, kernels))
+    a1, s1, xt, late = conv1(xv, t1, ones, EARLY, 10, (a1, s1, xt))
     late = hand(late)
-    a2, s2 = conv2(a1, t2, b2)
-    a3, s3 = conv3(a2, t3, ones)
+    a2, s2, a3, s3 = conv23(a1, t2, b2, t3, ones)
     wd = dense_weight[0]
     wht = head_weight[0].T
     pd = lax.dot_general(wd, a3, (((0,), (0,)), ((), ())), preferred_element_type=F32)
@@ -962,43 +1025,65 @@
     db = jnp.sum(diff_dense, axis=1, keepdims=True)
 
     keep, send = wdense(flag, a3, after(rd, early), rh, h)
-    chunk, arrived = reduce_chunks(keep, send, me)
-
-    r3, b3g = dflat(wd, rd, s3)
-    r2, r2p, b2g = dconv3(after(r3, arrived[0]), t3b, s2)
+    cur = split_blocks(add(keep, swap(send, 1)))
+    keep, got = halve(cur, me, 2)
+
+    r3, b3g, r2, r2p, b2g = dthird(wd, rd, s3, t3b, s2)
     r2p = hand(r2p)
-    r1, packed, b1s = None, [], []
-    for first, count in NEAR:
-        r1, part, b1g = dconv2(after(r2, late), t2b, s1, first, count, True, r1)
-        packed.append(part)
-        b1s.append(b1g)
-    r1, b1g = dconv2(r2, t2b, s1, 0, FAR, False, r1)
-    b1s.append(b1g)
-    gots = [hand(after(packed[0], r2p))]
-    g3 = wconv3(a2, after(r3, arrived[1]))
-    g2 = wconv2(a1, after(r2, arrived[1]))
-    g1 = wconv1(xt, after(r1, arrived[2]))
-    small = pack(flag, b1s, shards, capacity, b2g, b3g, g1, g2, g3, db, hb, row_loss, owner_shard.T)
-    t1b, t2b_online = band_frames(flag, k1, k1_got, k2, k2_got)
+    r1, near0, near1, b1g = dconv2(r2, t2b, s1, FAR, 10 - FAR, True, None)
+    cur = add(after(keep, b1g), got)
+    keep, far = halve(cur, me, 4)
+    r1, b1g_far = dconv2(after(r2, got, late), t2b, s1, 0, FAR, False, r1)
+    b1s = [b1g, b1g_far]
+    g3 = wconv3(a2, after(r3, b1g_far))
+    bit = 4
+    while 2 * bit < shards:
+        cur = add(after(keep, g3) if bit == 4 else keep, far)
+        bit *= 2
+        keep, far = halve(cur, me, bit)
+    g1 = wconv1(xt, x0, after(r1, g3))
+    chunk = add(after(keep, g1), far)[0]
     far_chunk = hand(chunk[1])
-    gots.append(hand(after(packed[1], arrived[-1], gots[0])))
-    out, edge, outs = None, None, []
-    for first, s1p in ((0, early), (EARLY, late)):
-        out, edge = dframes(flag, r1, (r2p, s1p, t2b_online), t1b, rows, first, s1p.shape[0], edge, out)
-        outs.append(edge)
-    for (first, count), got in zip(NEAR, gots):
-        out, edge = dframes(flag, r1, (got,), t1b, rows, first, count, edge, out)
-        outs.append(edge)
-    small = after(small, gots[0])
-    bit, n = 1, -2
-    while bit < shards:
-        if 0 <= n < 3:
-            small = after(small, outs[n])
-        small = add(small, swap(small, bit))
-        bit, n = 2 * bit, n + 1
-    far_small = hand(small)
+    gots = [hand(after(near0, far))]
+    gots.append(hand(after(near1, gots[0])))
+    t1b, t2b_online = band_frames(after(flag, g1), k1, k2, kernels)
     mine = jnp.where(online, chunk[0], far_chunk)
-    cur, other = gather_chunks(mine, me, gots[1])
+    g2 = wconv2(a1, after(r2, mine, t1b))
+
+    parts = [early, late] + gots
+    firsts = [0, EARLY] + [first for first, _ in NEAR]
+    out, edge = None, None
+
+    def frames_step(n, *waits):
+        extra = (r2p, parts[n], t2b_online) if n < 2 else (parts[n],)
+        return dframes(flag, after(r1, *waits), extra, t1b, rows, firsts[n], parts[n].shape[0], edge, out)
+
+    bit = shards // 2
+    cur = mine[None]
+    part = swap(cur, bit)
+    small = pack(after(flag, part, r2p), b1s, shards, capacity, b2g, b3g, g1, g2, g3, db, hb, row_loss, owner_shard.T)
+    cur = join(cur, part)
+    part = swap(cur, bit // 2)
+    small = add(small, swap(small, 1))
+    got = swap(small, 2)
+    out, edge = frames_step(0, cur, small)
+    cur = join(after(cur, edge), part)
+    small = add(after(small, edge), got)
+    part_y, got_z = swap(cur, bit // 4), swap(small, 4)
+    out, edge = frames_step(1, cur, small, gots[0])
+    small = add(after(small, edge), got_z)
+    got = swap(small, 8)
+    out, edge = frames_step(2, small)
+    cur = join(after(cur, edge), part_y)
+    small = add(after(small, edge), got)
+    lower = 16
+    while lower < shards:
+        small = add(small, swap(small, lower))
+        cur = join(cur, swap(cur, 2 * bit // lower))
+        lower *= 2
+    other = swap(cur, 1)
+    far_small = hand(after(small, gots[1]))
+    out, edge = frames_step(3, cur, small)
     if shards != 16:
         cur, other = (unmix(v, me // 2).reshape(8, 512, 128) for v in (cur, other))
     dense_out, head_out = unchunk(flag, cur, other)

time: 269 us -> 234 us (0.87)
  Pallas kernels: 174 us -> 148 us
  waiting for transfers between devices: 28.8 us -> 22.8 us
  local copies, waits for them, and re-layouts: 7.32 us -> 3.45 us
    pallas_call x7 -> x5, Pallas kernels: 63.6 us -> 47.1 us  [the longest x1 14.5 us: conv23(): call(conv23_kernel, (sds((576, 9 * LANES), BF), sds((576, 9 * LANES), BF)...]
    ppermute x9 -> x8, waiting for transfers between devices: 16.4 us -> 7.28 us  [hand(): return lax.ppermute(value, 'pair', [(0, 1)])]
    pallas_call x2, Pallas kernels: 31.5 us -> 25.5 us  [conv1(): pl.pallas_call(functools.partial(conv1_kernel, rows, start, packs), out_s...]
    unnamed x40 -> x22, local copies, waits for them, and re-layouts: 5.31 us -> 1.33 us
    ppermute x12, waiting for transfers between devices: 8.44 us -> 11.5 us  [swap(): return lax.ppermute(value, 'batch', [(i, i ^ bit) for i in range(devices)])]
    pallas_call x3 -> x2, Pallas kernels: 17.6 us -> 14.9 us  [dconv2(): pl.pallas_call(functools.partial(dconv2_kernel, first, packs), out_shape=...]
    ppermute x9 -> x8, starting transfers between devices: 28.9 us -> 30.8 us  [hand(): return lax.ppermute(value, 'pair', [(0, 1)])]
  transfers between devices with their start and end apart: 22 -> 21, of which waited for: 6 -> 6; matrix products, arithmetic and copies ran while one was open for 5% -> 6% of each run, Pallas kernels for 58% -> 58%
where the time goes in v3:
time: 234 us; the launch traced here: 232 us
  Pallas kernels  148 us (63%)
  starting transfers between devices  44.5 us (19%)
  waiting for transfers between devices  22.8 us (10%)
  other arithmetic  6.41 us (3%)
  matrix products  5.94 us (3%)
  local copies, waits for them, and re-layouts  3.45 us (1%)
    ppermute x8, starting transfers between devices, hand(): return lax.ppermute(value, 'pair', [(0, 1)])  30.8 us
    pallas_call x2, Pallas kernels, conv1(): pl.pallas_call(functools.partial(conv1_kernel, rows, start, packs), out_s...  25.5 us
    pallas_call x4, Pallas kernels, dframes(): pl.pallas_call(functools.partial(dframes_kernel, rows, first, last, far),...  21.9 us
    pallas_call x2, Pallas kernels, dconv2(): pl.pallas_call(functools.partial(dconv2_kernel, first, packs), out_shape=...  14.9 us
    pallas_call x1, Pallas kernels, conv23(): call(conv23_kernel, (sds((576, 9 * LANES), BF), sds((576, 9 * LANES), BF)...  14.5 us
    pallas_call x1, Pallas kernels, wconv1(): call(wconv1_kernel, sds((256, 32), F32), [pl.BlockSpec((4, 336, 4 * LANES...  13.2 us
    pallas_call x1, Pallas kernels, dthird(): call(dthird_kernel, (sds((3136, LANES), BF), sds((64, LANES), F32), sds((...  12.6 us
    ppermute x12, starting transfers between devices, swap(): return lax.ppermute(value, 'batch', [(i, i ^ bit) for i in range(devices)])  12.4 us
  transfers between devices with their start and end apart: 21, of which 6 were waited for; matrix products, arithmetic and copies ran while one was open for 6% of the time, Pallas kernels for 58%

profile of v3, /device:TPU:0, one launch (start us, length us, event | category | flops | bytes accessed | tf_op | source)
XLA Modules:
  0.0 232.4 jit_solution(4072735789518623670)
XLA Ops:
  0.6 4.6 %shard_map.256 = (bf16[320,1424]{1,0:T(8,128)(2,1)}, bf16[192,1024]{1,0:T(8,128)(2,1)}, bf16[448,1744]{1,0:T(8,128)(2,1)}, bf16[576,1344]{1,0:T(8,128)(2,1)}, bf...) custom-call(bf16[8,8,4,32]{3,2,1,0:T(4,128)(2,1)} %bitcast.109, bf16[1,32]{1,0:T(2,128)(2,1)} %b1.1, ...), custom_call_target="tpu_custom_call" | custom-call | flops 2000000000 | tf_op jit(solution)/shard_map/pallas_call | solution.py:115
  5.2 4.8 %collective-permute-start.1 = (bf16[640,64]{1,0:T(8,128)(2,1)}, bf16[640,64]{1,0:T(8,128)(2,1)S(1)}, u32[]{:S(2)}, u32[]{:S(2)}) collective-permute-start(bf16[640,64]{1,0:T(8,128)(2,1)} %get-tuple-element.121), channel_id=1, source_target_pairs={{0,16},{1,17},{2,18},{3,19},{4,20},{5,21},{6,22},{7,23},{8,24},{9,... | collective-permute-start | bytes 245768 | tf_op jit(solution)/shard_map/ppermute | solution.py:934
  10.0 11.0 %shard_map.257 = (bf16[2,640,2560]{2,1,0:T(8,128)(2,1)}, bf16[2,640,2560]{2,1,0:T(8,128)(2,1)}, bf16[4,336,5120]{2,1,0:T(8,128)(2,1)}, bf16[4,2,1120,128]{3,2,1,0:T(8,128)(2,1)}, bf16[4,336,256]{2,1,0:T(8,128)(2,1)}) custom-call(bf16[84,84,4,224]{3,2,1,0:T(4,128)(2,1)} %bitcast.80, bf16[84,84,4,224]{3,2,1,0:T(4,128)(2,1)} %bitcast.81, ...), custom_call_target="tpu_custom_call" | custom-call | flops 320000000 | tf_op jit(solution)/shard_map/pallas_call | solution.py:235
  21.0 2.7 %collective-permute-start.2 = (bf16[4,2,1120,128]{3,2,1,0:T(8,128)(2,1)}, bf16[4,2,1120,128]{3,2,1,0:T(8,128)(2,1)}, u32[]{:S(2)}, u32[]{:S(2)}) collective-permute-start(bf16[4,2,1120,128]{3,2,1,0:T(8,128)(2,1)} %get-tuple-element.122), channel_id=1, source_target_pairs={{0,16},{1,17},{2,18},{3,19},{4,20},{5,21},{6,22},{7,23},{8,24},{9,... | collective-permute-start | bytes 6881288 | tf_op jit(solution)/shard_map/ppermute | solution.py:934
  23.8 14.5 %shard_map.258 = (bf16[2,640,2560]{2,1,0:T(8,128)(2,1)}, bf16[2,640,2560]{2,1,0:T(8,128)(2,1)}, bf16[4,336,5120]{2,1,0:T(8,128)(2,1)}, bf16[2,2,1120,128]{3,2,1,0:T(8,128)(2,1)}) custom-call(bf16[84,84,4,224]{3,2,1,0:T(4,128)(2,1)} %bitcast.83, bf16[84,84,4,224]{3,2,1,0:T(4,128)(2,1)} %bitcast.84, ...), custom_call_target="tpu_custom_call", output_to_operand_aliasing={{0}: (5, {}), {1}: (6, {}), {2}: (7, {})} | custom-call | flops 480000000 | tf_op jit(solution)/shard_map/pallas_call | solution.py:235
  38.3 14.5 %shard_map.259 = (bf16[576,2304]{1,0:T(8,128)(2,1)}, bf16[576,2304]{1,0:T(8,128)(2,1)}, bf16[3136,256]{1,0:T(8,128)(2,1)}, bf16[3136,256]{1,0:T(8,128)(2,1)}) custom-call(bf16[2,640,2560]{2,1,0:T(8,128)(2,1)} %get-tuple-element.111.r0_ref.r1_ref.a0_ref.a1_ref, bf16[2,640,2560]{2,1,0:T(8,128)(2,1)} %get-tuple-element.111.r0_ref.r1_ref.a0_ref.a1_ref, ...), custom_call_target="tpu_custom_call" | custom-call | flops 800000000 | tf_op jit(solution)/shard_map/pallas_call | solution.py:294
  52.8 0.6 broadcast_select_fusion
  53.4 3.6 %convolution_bitcast_fusion.1.pd_ref = f32[512,256]{1,0:T(8,128)} fusion(bf16[3136,256]{1,0:T(8,128)(2,1)} %get-tuple-element.115.a_ref, bf16[1,3136,512]{2,1,0:T(8,128)(2,1)S(1)} %copy-done.1), kind=kOutput, calls=%fused_computation.4 | convolution fusion | flops 822083584 | bytes 5341184 | tf_op jit(solution)/shard_map/dot_general | solution.py:1015
  57.0 2.9 %shard_map.260 = (bf16[512,256]{1,0:T(8,128)(2,1)}, bf16[512,256]{1,0:T(8,128)(2,1)}, f32[51,224]{1,0:T(8,128)}, bf16[51,224]{1,0:T(8,128)(2,1)}) custom-call(f32[512,256]{1,0:T(8,128)} %convolution_bitcast_fusion.1.pd_ref, bf16[1,512]{1,0:T(2,128)(2,1)} %bd_ref.1, bf16[918,512]{1,0:T(8,128)(2,1)} %bitcast.96, bf16[1,918]{1,0:T(2,128)(2,1)} %bh_ref.1, ...), custom_call_target="tpu_custom_call" | custom-call | flops 200000000 | tf_op jit(solution)/shard_map/pallas_call | solution.py:327
  59.9 1.3 collective-permute-start
  61.2 0.7 pad_add_fusion.flag_ref
  61.9 4.0 %collective-permute-done.cho_ref = bf16[51,224]{1,0:T(8,128)(2,1)S(1)} collective-permute-done((bf16[51,224]{1,0:T(8,128)(2,1)}, bf16[51,224]{1,0:T(8,128)(2,1)S(1)}, u32[]{:S(2)}, u32[]{:S(2)}) %collective-permute-start) | collective-permute-done | bytes 22880 | tf_op jit(solution)/shard_map/ppermute | solution.py:1019
  65.8 0.6 copy-done.10
  66.5 2.8 %shard_map.261 = (f32[1,224]{1,0:T(1,128)}, bf16[918,256]{1,0:T(8,128)(2,1)}, f32[918,1]{1,0:T(8,128)}) custom-call(bf16[51,224]{1,0:T(8,128)(2,1)} %copy-done.10, s32[1,224]{1,0:T(1,128)} %bitcast.113, s32[51,224]{1,0:T(8,128)} %bitcast.111, f32[51,224]{1,0:T(8,128)} %bitcast.112, f32[51,224]{1,0:T(8,128)} %get-tuple-element.117.lp_ref, s32[1,224]{1,0:T(1,128)} %bitcast.105), custom_call_target="tpu_custom_call" | custom-call | flops 200000000 | tf_op jit(solution)/shard_map/pallas_call | solution.py:364
  69.3 2.3 %fusion.4 = (f32[512]{0:T(512)S(1)}, bf16[512,256]{1,0:T(8,128)(2,1)}) fusion(bf16[512,256]{1,0:T(8,128)(2,1)} %get-tuple-element.119, bf16[918,256]{1,0:T(8,128)(2,1)} %get-tuple-element.118.rh_ref, bf16[1,512,918]{1,2,0:T(8,128)(2,1)S(1)} %copy-done.4), kind=kOutput, calls=%fused_computation.27 | convolution fusion | flops 241303040 | bytes 1936384 | tf_op jit(solution)/shard_map/dot_general | solution.py:1022
  71.6 0.2 collective-permute-done.2.rest_2_
  71.7 8.1 %shard_map.262 = (bf16[8,2,512,128]{3,2,1,0:T(8,128)(2,1)}, bf16[8,2,512,128]{3,2,1,0:T(8,128)(2,1)}) custom-call(s32[4]{0:T(128)} %pad_add_fusion.flag_ref, bf16[3136,256]{1,0:T(8,128)(2,1)} %get-tuple-element.115.a_ref, bf16[512,256]{1,0:T(8,128)(2,1)} %get-tuple-element.123.rd_ref, bf16[918,256]{1,0:T(8,128)(2,1)} %get-tuple-element.118.rh_ref, ...), custom_call_target="tpu_custom_call" | custom-call | flops 400000000 | tf_op jit(solution)/shard_map/pallas_call | solution.py:638
  79.8 5.4 %collective-permute-start.5 = (bf16[2,2,1120,128]{3,2,1,0:T(8,128)(2,1)}, bf16[2,2,1120,128]{3,2,1,0:T(8,128)(2,1)}, u32[]{:S(2)}, u32[]{:S(2)}) collective-permute-start(bf16[2,2,1120,128]{3,2,1,0:T(8,128)(2,1)} %get-tuple-element.137), channel_id=1, source_target_pairs={{0,16},{1,17},{2,18},{3,19},{4,20},{5,21},{6,22},{7,23},{8,24},{9,... | collective-permute-start | bytes 3440648 | tf_op jit(solution)/shard_map/ppermute | solution.py:934
  85.2 2.1 add_convert_fusion
  87.4 1.1 dynamic-slice_bitcast_fusion.1
  88.5 1.5 collective-permute-start.4
  90.0 12.6 %shard_map.263 = (bf16[3136,256]{1,0:T(8,128)(2,1)}, f32[64,256]{1,0:T(8,128)}, bf16[576,2304]{1,0:T(8,128)(2,1)}, bf16[6,1008,128]{2,1,0:T(8,128)(2,1)}, f32[64,256]{1,0:T(8,128)}) custom-call(bf16[3136,512]{1,0:T(8,128)(2,1)} %bitcast.89, bf16[512,256]{1,0:T(8,128)(2,1)} %get-tuple-element.123.rd_ref, bf16[3136,256]{1,0:T(8,128)(2,1)} %get-tuple-element.127.s3_ref, ...), custom_call_target="tpu_custom_call" | custom-call | flops 600000000 | tf_op jit(solution)/shard_map/pallas_call | solution.py:420
  102.6 3.4 %collective-permute-start.10 = (bf16[6,1008,128]{2,1,0:T(8,128)(2,1)}, bf16[6,1008,128]{2,1,0:T(8,128)(2,1)S(1)}, u32[]{:S(2)}, u32[]{:S(2)}) collective-permute-start(bf16[6,1008,128]{2,1,0:T(8,128)(2,1)} %get-tuple-element.148), channel_id=1, source_target_pairs={{0,16},{1,17},{2,18},{3,19},{4,20},{5,21},{6,22},{7,23},{8,24},{9,... | collective-permute-start | bytes 4644872 | tf_op jit(solution)/shard_map/ppermute | solution.py:934
  106.0 7.4 %shard_map.264 = (bf16[2,640,2560]{2,1,0:T(8,128)(2,1)}, bf16[2,2,1120,128]{3,2,1,0:T(8,128)(2,1)}, bf16[2,2,1120,128]{3,2,1,0:T(8,128)(2,1)}, f32[32,256]{1,0:T(8,128)}) custom-call(bf16[576,2304]{1,0:T(8,128)(2,1)} %get-tuple-element.154.cur_ref.prev_ref.r_ref, bf16[576,2304]{1,0:T(8,128)(2,1)} %get-tuple-element.154.cur_ref.prev_ref.r_ref, ...), custom_call_target="tpu_custom_call" | custom-call | flops 3200000000 | tf_op jit(solution)/shard_map/pallas_call | solution.py:508
  113.4 0.7 collective-permute-done.4
  114.1 1.5 add_convert_fusion.1
  115.6 0.1 dynamic-slice_bitcast_fusion.3
  115.7 1.6 collective-permute-start.6
  117.4 7.5 %shard_map.265 = (bf16[2,640,2560]{2,1,0:T(8,128)(2,1)}, f32[32,256]{1,0:T(8,128)}) custom-call(bf16[576,2304]{1,0:T(8,128)(2,1)} %get-tuple-element.154.cur_ref.prev_ref.r_ref, bf16[576,2304]{1,0:T(8,128)(2,1)} %get-tuple-element.154.cur_ref.prev_ref.r_ref, bf16[640,768]{1,0:T(8,128)(2,1)} %get-tuple-element.131.t_ref, ...), custom_call_target="tpu_custom_call", output_to_operand_aliasing={{0}: (4, {})} | custom-call | flops 4800000000 | tf_op jit(solution)/shard_map/pallas_call | solution.py:508
  124.9 7.0 %shard_map.266.refs_6_ = f32[64,576]{1,0:T(8,128)} custom-call(bf16[576,2304]{1,0:T(8,128)(2,1)} %get-tuple-element.135.refs_0_.refs_1_.refs_2_.refs_3_, bf16[576,2304]{1,0:T(8,128)(2,1)} %get-tuple-element.135.refs_0_.refs_1_.refs_2_.refs_3_, bf16[576,2304]{1,0:T(8,128)(2,1)} %get-tuple-element.135.refs_0_.refs_1_.refs_2_.refs_3_, ...), custom_call_target="tpu_custom_call" | custom-call | flops 2400000000 | tf_op jit(solution)/shard_map/pallas_call | solution.py:680
  131.9 0.1 add_convert_fusion.2
  132.1 2.7 %collective-permute-start.7 = (bf16[1,2,512,128]{3,2,1,0:T(8,128)(2,1)S(1)}, bf16[1,2,512,128]{3,2,1,0:T(8,128)(2,1)S(1)}, u32[]{:S(2)}, u32[]{:S(2)}) collective-permute-start(bf16[1,2,512,128]{3,2,1,0:T(8,128)(2,1)S(1)} %get-tuple-element.197), channel_id=1, source_target_pairs={{0,8},{1,9},{2,10},{3,11},{4,12},{5,13},{6,14},{7,15},{8,0},{9,1},... | collective-permute-start | bytes 786440 | tf_op jit(solution)/shard_map/ppermute | solution.py:939
  134.7 13.2 %shard_map.267.refs_4_ = f32[256,32]{1,0:T(8,128)} custom-call(bf16[4,336,5120]{2,1,0:T(8,128)(2,1)} %get-tuple-element.143.x_ref, bf16[4,336,256]{2,1,0:T(8,128)(2,1)} %get-tuple-element.144.x0_ref, bf16[2,640,2560]{2,1,0:T(8,128)(2,1)} %get-tuple-element.186.r_ref.own_ref), custom_call_target="tpu_custom_call" | custom-call | flops 5600000000 | tf_op jit(solution)/shard_map/pallas_call | solution.py:773
  147.9 0.1 add_convert_fusion.3
  148.0 3.3 %collective-permute-start.8 = (bf16[512,128]{1,0:T(8,128)(2,1)S(1)}, bf16[512,128]{1,0:T(8,128)(2,1)S(1)}, u32[]{:S(2)}, u32[]{:S(2)}) collective-permute-start(bf16[512,128]{1,0:T(8,128)(2,1)S(1)} %slice_bitcast_fusion), channel_id=1, source_target_pairs={{0,16},{1,17},{2,18},{3,19},{4,20},{5,21},{6,22},{7,23},{8,24},{9,... | collective-permute-start | bytes 393224 | tf_op jit(solution)/shard_map/ppermute | solution.py:934
  151.3 0.9 copy.42.refs_7_
  152.1 2.3 %shard_map.268 = (bf16[224,512]{1,0:T(8,128)(2,1)}, bf16[640,768]{1,0:T(8,128)(2,1)}) custom-call(s32[4]{0:T(128)} %pad_add_fusion.flag_ref, bf16[8,8,4,32]{3,2,1,0:T(4,128)(2,1)} %bitcast.110, bf16[4,4,32,64]{3,2,1,0:T(8,128)(2,1)} %bitcast.108, bf16[640,64]{1,0:T(8,128)(2,1)} %copy-done.9), custom_call_target="tpu_custom_call" | custom-call | flops 1200000000 | tf_op jit(solution)/shard_map/pallas_call | solution.py:146
  154.5 2.3 collective-permute-start.14
  156.8 0.4 collective-permute-start.9
  157.2 9.1 %shard_map.269.refs_5_ = f32[512,64]{1,0:T(8,128)} custom-call(bf16[2,640,2560]{2,1,0:T(8,128)(2,1)} %get-tuple-element.111.r0_ref.r1_ref.a0_ref.a1_ref, bf16[2,640,2560]{2,1,0:T(8,128)(2,1)} %get-tuple-element.111.r0_ref.r1_ref.a0_ref.a1_ref, bf16[576,2304]{1,0:T(8,128)(2,1)} %get-tuple-element.154.cur_ref.prev_ref.r_ref), custom_call_target="tpu_custom_call" | custom-call | flops 3200000000 | tf_op jit(solution)/shard_map/pallas_call | solution.py:716
  166.2 3.1 %shard_map.270 = bf16[768,128]{1,0:T(8,128)(2,1)} custom-call(s32[4]{0:T(128)} %pad_add_fusion.flag_ref, f32[32,256]{1,0:T(8,128)} %get-tuple-element.133.refs_0_, f32[32,256]{1,0:T(8,128)} %get-tuple-element.140.refs_1_, f32[64,256]{1,0:T(8,128)} %get-tuple-element.150.refs_2_, f32[64,256]{1,0:T(8,128)} %get-tuple-element.151.refs_3_, ...), custom_call_target="tpu_custom_call" | custom-call | flops 40000000 | tf_op jit(solution)/shard_map/pallas_call | solution.py:845
  169.4 0.8 collective-permute-start.13
  170.2 0.9 collective-permute-done.11
  171.0 1.0 add_convert_fusion.7
  172.0 1.6 collective-permute-start.12
  173.6 7.4 %shard_map.271 = (bf16[84,84,2,224]{3,2,1,0:T(2,128)(2,1)}, bf16[640,256]{1,0:T(8,128)(2,1)}) custom-call(s32[4]{0:T(128)} %pad_add_fusion.flag_ref, bf16[2,640,2560]{2,1,0:T(8,128)(2,1)} %get-tuple-element.186.r_ref.own_ref, bf16[6,1008,128]{2,1,0:T(8,128)(2,1)} %copy-done, bf16[6,1008,128]{2,1,0:T(8,128)(2,1)} %copy-done, ...), custom_call_target="tpu_custom_call" | custom-call | flops 48000000 | tf_op jit(solution)/shard_map/pallas_call | solution.py:604
  181.1 0.6 collective-permute-start.19
  181.6 0.1 add_convert_fusion.6
  181.7 0.8 collective-permute-start.15
  182.5 5.0 %shard_map.272 = (bf16[84,84,2,224]{3,2,1,0:T(2,128)(2,1)}, bf16[640,256]{1,0:T(8,128)(2,1)}) custom-call(s32[4]{0:T(128)} %pad_add_fusion.flag_ref, bf16[2,640,2560]{2,1,0:T(8,128)(2,1)} %get-tuple-element.186.r_ref.own_ref, bf16[6,1008,128]{2,1,0:T(8,128)(2,1)} %copy-done, bf16[6,1008,128]{2,1,0:T(8,128)(2,1)} %copy-done, ...), custom_call_target="tpu_custom_call", output_to_operand_aliasing={{0}: (8, {})} | custom-call | flops 24000000 | tf_op jit(solution)/shard_map/pallas_call | solution.py:604
  187.4 4.6 %collective-permute-start.17 = (bf16[2,2,1120,128]{3,2,1,0:T(8,128)(2,1)}, bf16[2,2,1120,128]{3,2,1,0:T(8,128)(2,1)S(1)}, u32[]{:S(2)}, u32[]{:S(2)}) collective-permute-start(bf16[2,2,1120,128]{3,2,1,0:T(8,128)(2,1)} %get-tuple-element.173), channel_id=1, source_target_pairs={{0,16},{1,17},{2,18},{3,19},{4,20},{5,21},{6,22},{7,23},{8,24},{9,... | collective-permute-start | bytes 3440648 | tf_op jit(solution)/shard_map/ppermute | solution.py:934
  192.0 0.1 add_convert_fusion.5
  192.1 4.3 %shard_map.273 = (bf16[84,84,2,224]{3,2,1,0:T(2,128)(2,1)}, bf16[640,256]{1,0:T(8,128)(2,1)}) custom-call(s32[4]{0:T(128)} %pad_add_fusion.flag_ref, bf16[2,640,2560]{2,1,0:T(8,128)(2,1)} %get-tuple-element.186.r_ref.own_ref, bf16[2,2,1120,128]{3,2,1,0:T(8,128)(2,1)} %collective-permute-done.14.rest_0_, ...), custom_call_target="tpu_custom_call", output_to_operand_aliasing={{0}: (5, {})} | custom-call | flops 24000000 | tf_op jit(solution)/shard_map/pallas_call | solution.py:604
  196.4 0.1 pad_maximum_fusion
  196.6 0.1 collective-permute-start.20
  196.6 2.4 %collective-permute-start.16 = (bf16[768,128]{1,0:T(8,128)(2,1)S(1)}, bf16[768,128]{1,0:T(8,128)(2,1)S(1)}, u32[]{:S(2)}, u32[]{:S(2)}) collective-permute-start(bf16[768,128]{1,0:T(8,128)(2,1)S(1)} %add_convert_fusion.5), channel_id=1, source_target_pairs={{0,8},{1,9},{2,10},{3,11},{4,12},{5,13},{6,14},{7,15},{8,0},{9,1},... | collective-permute-start | bytes 589832 | tf_op jit(solution)/shard_map/ppermute | solution.py:939
  199.1 10.0 %collective-permute-done.16 = bf16[768,128]{1,0:T(8,128)(2,1)S(1)} collective-permute-done((bf16[768,128]{1,0:T(8,128)(2,1)S(1)}, bf16[768,128]{1,0:T(8,128)(2,1)S(1)}, u32[]{:S(2)}, u32[]{:S(2)}) %collective-permute-start.16) | collective-permute-done | bytes 196640 | tf_op jit(solution)/shard_map/ppermute | solution.py:939
  209.1 0.1 add_convert_fusion.4.own_ref
  209.1 7.1 %collective-permute-done.17.rest_0_ = bf16[2,2,1120,128]{3,2,1,0:T(8,128)(2,1)S(1)} collective-permute-done((bf16[2,2,1120,128]{3,2,1,0:T(8,128)(2,1)}, bf16[2,2,1120,128]{3,2,1,0:T(8,128)(2,1)S(1)}, u32[]{:S(2)}, u32[]{:S(2)}) %collective-permute-start.17) | collective-permute-done | bytes 1146912 | tf_op jit(solution)/shard_map/ppermute | solution.py:934
  216.2 4.3 %collective-permute-start.18 = (bf16[768,128]{1,0:T(8,128)(2,1)S(1)}, bf16[768,128]{1,0:T(8,128)(2,1)S(1)}, u32[]{:S(2)}, u32[]{:S(2)}) collective-permute-start(bf16[768,128]{1,0:T(8,128)(2,1)S(1)} %add_convert_fusion.4.own_ref), channel_id=1, source_target_pairs={{0,16},{1,17},{2,18},{3,19},{4,20},{5,21},{6,22},{7,23},{8,24},{9,... | collective-permute-start | bytes 589832 | tf_op jit(solution)/shard_map/ppermute | solution.py:934
  220.5 4.0 %shard_map.275 = (f32[3136,256]{1,0:T(8,128)}, f32[918,256]{1,0:T(8,128)}) custom-call(s32[4]{0:T(128)} %pad_add_fusion.flag_ref, bf16[8,512,128]{2,1,0:T(8,128)(2,1)} %bitcast.94, bf16[8,512,128]{2,1,0:T(8,128)(2,1)} %collective-permute-done.20.other_ref), custom_call_target="tpu_custom_call" | custom-call | flops 1600000000 | tf_op jit(solution)/shard_map/pallas_call | solution.py:919
  224.6 5.2 %shard_map.276 = (bf16[84,84,2,224]{3,2,1,0:T(2,128)(2,1)}, bf16[640,256]{1,0:T(8,128)(2,1)}) custom-call(s32[4]{0:T(128)} %pad_add_fusion.flag_ref, bf16[2,640,2560]{2,1,0:T(8,128)(2,1)} %get-tuple-element.186.r_ref.own_ref, bf16[2,2,1120,128]{3,2,1,0:T(8,128)(2,1)} %copy-done.2, ...), custom_call_target="tpu_custom_call", output_to_operand_aliasing={{0}: (5, {})} | custom-call | flops 24000000 | tf_op jit(solution)/shard_map/pallas_call | solution.py:604
  229.7 0.7 copy-done.8
  230.4 2.0 shard_map.274
  (42 shorter events, 0.2 us)
Async XLA Ops:
  5.2 15.8 %collective-permute-start.1 = (bf16[640,64]{1,0:T(8,128)(2,1)}, bf16[640,64]{1,0:T(8,128)(2,1)S(1)}, u32[]{:S(2)}, u32[]{:S(2)}) collective-permute-start(bf16[640,64]{1,0:T(8,128)(2,1)} %get-tuple-element.121), channel_id=1, source_target_pairs={{0,16},{1,17},{2,18},{3,19},{4,20},{5,21},{6,22},{7,23},{8,24},{9,... | collective-permute-start | bytes 245768 | tf_op jit(solution)/shard_map/ppermute | solution.py:934
  21.0 17.2 %copy-start.9 = (bf16[640,64]{1,0:T(8,128)(2,1)}, bf16[640,64]{1,0:T(8,128)(2,1)S(1)}, u32[]{:S(2)}) copy-start(bf16[640,64]{1,0:T(8,128)(2,1)S(1)} %collective-permute-done.1.got) | copy-start | bytes 245764
  21.0 50.7 %collective-permute-start.2 = (bf16[4,2,1120,128]{3,2,1,0:T(8,128)(2,1)}, bf16[4,2,1120,128]{3,2,1,0:T(8,128)(2,1)}, u32[]{:S(2)}, u32[]{:S(2)}) collective-permute-start(bf16[4,2,1120,128]{3,2,1,0:T(8,128)(2,1)} %get-tuple-element.122), channel_id=1, source_target_pairs={{0,16},{1,17},{2,18},{3,19},{4,20},{5,21},{6,22},{7,23},{8,24},{9,... | collective-permute-start | bytes 6881288 | tf_op jit(solution)/shard_map/ppermute | solution.py:934
  38.2 14.5 %copy-start.6 = (s32[224]{0:T(256)S(1)}, s32[224]{0:T(256)}, u32[]{:S(2)}) copy-start(s32[224]{0:T(256)} %param.31) | copy-start | bytes 2692
  38.3 14.5 %copy-start.7 = (s32[224]{0:T(256)S(1)}, s32[224]{0:T(256)}, u32[]{:S(2)}) copy-start(s32[224]{0:T(256)} %param.30) | copy-start | bytes 2692
  38.3 15.1 %copy-start.1 = (bf16[1,3136,512]{2,1,0:T(8,128)(2,1)S(1)}, bf16[1,3136,512]{2,1,0:T(8,128)(2,1)}, u32[]{:S(2)}) copy-start(bf16[1,3136,512]{2,1,0:T(8,128)(2,1)} %param.26) | copy-start | bytes 9633796
  57.0 12.3 %copy-start.4 = (bf16[1,512,918]{1,2,0:T(8,128)(2,1)S(1)}, bf16[1,512,918]{1,2,0:T(8,128)(2,1)}, u32[]{:S(2)}) copy-start(bf16[1,512,918]{1,2,0:T(8,128)(2,1)} %param.28) | copy-start | bytes 2820100
  59.9 6.0 %collective-permute-start = (bf16[51,224]{1,0:T(8,128)(2,1)}, bf16[51,224]{1,0:T(8,128)(2,1)S(1)}, u32[]{:S(2)}, u32[]{:S(2)}) collective-permute-start(bf16[51,224]{1,0:T(8,128)(2,1)} %get-tuple-element.116), channel_id=1, source_target_pairs={{16,0},{17,1},{18,2},{19,3},{20,4},{21,5},{22,6},{23,7},{24,8},{25... | collective-permute-start | bytes 68552 | tf_op jit(solution)/shard_map/ppermute | solution.py:1019
  65.8 0.6 copy-start.10
  79.8 5.4 %collective-permute-start.3 = (bf16[8,2,512,128]{3,2,1,0:T(8,128)(2,1)}, bf16[8,2,512,128]{3,2,1,0:T(8,128)(2,1)S(1)}, u32[]{:S(2)}, u32[]{:S(2)}) collective-permute-start(bf16[8,2,512,128]{3,2,1,0:T(8,128)(2,1)} %get-tuple-element.126), channel_id=1, source_target_pairs={{0,1},{1,0},{2,3},{3,2},{4,5},{5,4},{6,7},{7,6},{8,9},{9,8},{10,11... | collective-permute-start | bytes 6291464 | tf_op jit(solution)/shard_map/ppermute | solution.py:939
  79.8 33.6 %collective-permute-start.5 = (bf16[2,2,1120,128]{3,2,1,0:T(8,128)(2,1)}, bf16[2,2,1120,128]{3,2,1,0:T(8,128)(2,1)}, u32[]{:S(2)}, u32[]{:S(2)}) collective-permute-start(bf16[2,2,1120,128]{3,2,1,0:T(8,128)(2,1)} %get-tuple-element.137), channel_id=1, source_target_pairs={{0,16},{1,17},{2,18},{3,19},{4,20},{5,21},{6,22},{7,23},{8,24},{9,... | collective-permute-start | bytes 3440648 | tf_op jit(solution)/shard_map/ppermute | solution.py:934
  88.5 25.6 %collective-permute-start.4 = (bf16[4,2,512,128]{3,2,1,0:T(8,128)(2,1)}, bf16[4,2,512,128]{3,2,1,0:T(8,128)(2,1)}, u32[]{:S(2)}, u32[]{:S(2)}) collective-permute-start(bf16[4,2,512,128]{3,2,1,0:T(8,128)(2,1)} %get-tuple-element.191), channel_id=1, source_target_pairs={{0,2},{1,3},{2,0},{3,1},{4,6},{5,7},{6,4},{7,5},{8,10},{9,11},{10,... | collective-permute-start | bytes 3145736 | tf_op jit(solution)/shard_map/ppermute | solution.py:939
  102.6 63.6 %collective-permute-start.10 = (bf16[6,1008,128]{2,1,0:T(8,128)(2,1)}, bf16[6,1008,128]{2,1,0:T(8,128)(2,1)S(1)}, u32[]{:S(2)}, u32[]{:S(2)}) collective-permute-start(bf16[6,1008,128]{2,1,0:T(8,128)(2,1)} %get-tuple-element.148), channel_id=1, source_target_pairs={{0,16},{1,17},{2,18},{3,19},{4,20},{5,21},{6,22},{7,23},{8,24},{9,... | collective-permute-start | bytes 4644872 | tf_op jit(solution)/shard_map/ppermute | solution.py:934
  115.7 16.2 %collective-permute-start.6 = (bf16[2,2,512,128]{3,2,1,0:T(8,128)(2,1)S(1)}, bf16[2,2,512,128]{3,2,1,0:T(8,128)(2,1)S(1)}, u32[]{:S(2)}, u32[]{:S(2)}) collective-permute-start(bf16[2,2,512,128]{3,2,1,0:T(8,128)(2,1)S(1)} %get-tuple-element.193), channel_id=1, source_target_pairs={{0,4},{1,5},{2,6},{3,7},{4,0},{5,1},{6,2},{7,3},{8,12},{9,13},{10,... | collective-permute-start | bytes 1572872 | tf_op jit(solution)/shard_map/ppermute | solution.py:939
  132.1 15.8 %collective-permute-start.7 = (bf16[1,2,512,128]{3,2,1,0:T(8,128)(2,1)S(1)}, bf16[1,2,512,128]{3,2,1,0:T(8,128)(2,1)S(1)}, u32[]{:S(2)}, u32[]{:S(2)}) collective-permute-start(bf16[1,2,512,128]{3,2,1,0:T(8,128)(2,1)S(1)} %get-tuple-element.197), channel_id=1, source_target_pairs={{0,8},{1,9},{2,10},{3,11},{4,12},{5,13},{6,14},{7,15},{8,0},{9,1},... | collective-permute-start | bytes 786440 | tf_op jit(solution)/shard_map/ppermute | solution.py:939
  148.0 8.8 %collective-permute-start.8 = (bf16[512,128]{1,0:T(8,128)(2,1)S(1)}, bf16[512,128]{1,0:T(8,128)(2,1)S(1)}, u32[]{:S(2)}, u32[]{:S(2)}) collective-permute-start(bf16[512,128]{1,0:T(8,128)(2,1)S(1)} %slice_bitcast_fusion), channel_id=1, source_target_pairs={{0,16},{1,17},{2,18},{3,19},{4,20},{5,21},{6,22},{7,23},{8,24},{9,... | collective-permute-start | bytes 393224 | tf_op jit(solution)/shard_map/ppermute | solution.py:934
  154.5 28.0 %collective-permute-start.14 = (bf16[2,2,1120,128]{3,2,1,0:T(8,128)(2,1)}, bf16[2,2,1120,128]{3,2,1,0:T(8,128)(2,1)}, u32[]{:S(2)}, u32[]{:S(2)}) collective-permute-start(bf16[2,2,1120,128]{3,2,1,0:T(8,128)(2,1)} %get-tuple-element.163), channel_id=1, source_target_pairs={{0,16},{1,17},{2,18},{3,19},{4,20},{5,21},{6,22},{7,23},{8,24},{9,... | collective-permute-start | bytes 3440648 | tf_op jit(solution)/shard_map/ppermute | solution.py:934
  156.8 9.5 %collective-permute-start.9 = (bf16[1,512,128]{2,1,0:T(8,128)(2,1)S(1)}, bf16[1,512,128]{2,1,0:T(8,128)(2,1)S(1)}, u32[]{:S(2)}, u32[]{:S(2)}) collective-permute-start(bf16[1,512,128]{2,1,0:T(8,128)(2,1)S(1)} %bitcast.97), channel_id=1, source_target_pairs={{0,8},{1,9},{2,10},{3,11},{4,12},{5,13},{6,14},{7,15},{8,0},{9,1},... | collective-permute-start | bytes 393224 | tf_op jit(solution)/shard_map/ppermute | solution.py:939
  166.2 7.4 %copy-start = (bf16[6,1008,128]{2,1,0:T(8,128)(2,1)}, bf16[6,1008,128]{2,1,0:T(8,128)(2,1)S(1)}, u32[]{:S(2)}) copy-start(bf16[6,1008,128]{2,1,0:T(8,128)(2,1)S(1)} %collective-permute-done.10.rest_0_.rest_1_) | copy-start | bytes 4644868
  169.4 1.7 collective-permute-start.11
  169.4 11.6 %collective-permute-start.13 = (bf16[2,512,128]{2,1,0:T(8,128)(2,1)S(1)}, bf16[2,512,128]{2,1,0:T(8,128)(2,1)S(1)}, u32[]{:S(2)}, u32[]{:S(2)}) collective-permute-start(bf16[2,512,128]{2,1,0:T(8,128)(2,1)S(1)} %maximum_bitcast_fusion), channel_id=1, source_target_pairs={{0,4},{1,5},{2,6},{3,7},{4,0},{5,1},{6,2},{7,3},{8,12},{9,13},{10,... | collective-permute-start | bytes 786440 | tf_op jit(solution)/shard_map/ppermute | solution.py:939
  172.0 9.6 %collective-permute-start.12 = (bf16[768,128]{1,0:T(8,128)(2,1)S(1)}, bf16[768,128]{1,0:T(8,128)(2,1)S(1)}, u32[]{:S(2)}, u32[]{:S(2)}) collective-permute-start(bf16[768,128]{1,0:T(8,128)(2,1)S(1)} %add_convert_fusion.7), channel_id=1, source_target_pairs={{0,2},{1,3},{2,0},{3,1},{4,6},{5,7},{6,4},{7,5},{8,10},{9,11},{10,... | collective-permute-start | bytes 589832 | tf_op jit(solution)/shard_map/ppermute | solution.py:939
  181.1 15.4 %collective-permute-start.19 = (bf16[4,512,128]{2,1,0:T(8,128)(2,1)S(1)}, bf16[4,512,128]{2,1,0:T(8,128)(2,1)S(1)}, u32[]{:S(2)}, u32[]{:S(2)}) collective-permute-start(bf16[4,512,128]{2,1,0:T(8,128)(2,1)S(1)} %bitcast.90), channel_id=1, source_target_pairs={{0,2},{1,3},{2,0},{3,1},{4,6},{5,7},{6,4},{7,5},{8,10},{9,11},{10,... | collective-permute-start | bytes 1572872 | tf_op jit(solution)/shard_map/ppermute | solution.py:939
  181.7 10.3 %collective-permute-start.15 = (bf16[768,128]{1,0:T(8,128)(2,1)S(1)}, bf16[768,128]{1,0:T(8,128)(2,1)S(1)}, u32[]{:S(2)}, u32[]{:S(2)}) collective-permute-start(bf16[768,128]{1,0:T(8,128)(2,1)S(1)} %add_convert_fusion.6), channel_id=1, source_target_pairs={{0,4},{1,5},{2,6},{3,7},{4,0},{5,1},{6,2},{7,3},{8,12},{9,13},{10,... | collective-permute-start | bytes 589832 | tf_op jit(solution)/shard_map/ppermute | solution.py:939
  187.4 28.8 %collective-permute-start.17 = (bf16[2,2,1120,128]{3,2,1,0:T(8,128)(2,1)}, bf16[2,2,1120,128]{3,2,1,0:T(8,128)(2,1)S(1)}, u32[]{:S(2)}, u32[]{:S(2)}) collective-permute-start(bf16[2,2,1120,128]{3,2,1,0:T(8,128)(2,1)} %get-tuple-element.173), channel_id=1, source_target_pairs={{0,16},{1,17},{2,18},{3,19},{4,20},{5,21},{6,22},{7,23},{8,24},{9,... | collective-permute-start | bytes 3440648 | tf_op jit(solution)/shard_map/ppermute | solution.py:934
  196.6 24.0 %copy-start.3 = (bf16[4,2,512,128]{3,2,1,0:T(8,128)(2,1)}, bf16[4,2,512,128]{3,2,1,0:T(8,128)(2,1)S(1)}, u32[]{:S(2)}) copy-start(bf16[4,2,512,128]{3,2,1,0:T(8,128)(2,1)S(1)} %pad_maximum_fusion) | copy-start | bytes 3145732
  196.6 24.0 %collective-permute-start.20 = (bf16[8,512,128]{2,1,0:T(8,128)(2,1)S(1)}, bf16[8,512,128]{2,1,0:T(8,128)(2,1)}, u32[]{:S(2)}, u32[]{:S(2)}) collective-permute-start(bf16[8,512,128]{2,1,0:T(8,128)(2,1)S(1)} %bitcast.93), channel_id=1, source_target_pairs={{0,1},{1,0},{2,3},{3,2},{4,5},{5,4},{6,7},{7,6},{8,9},{9,8},{10,11... | collective-permute-start | bytes 3145736 | tf_op jit(solution)/shard_map/ppermute | solution.py:939
  196.6 12.4 %collective-permute-start.16 = (bf16[768,128]{1,0:T(8,128)(2,1)S(1)}, bf16[768,128]{1,0:T(8,128)(2,1)S(1)}, u32[]{:S(2)}, u32[]{:S(2)}) collective-permute-start(bf16[768,128]{1,0:T(8,128)(2,1)S(1)} %add_convert_fusion.5), channel_id=1, source_target_pairs={{0,8},{1,9},{2,10},{3,11},{4,12},{5,13},{6,14},{7,15},{8,0},{9,1},... | collective-permute-start | bytes 589832 | tf_op jit(solution)/shard_map/ppermute | solution.py:939
  209.1 15.4 %copy-start.5 = (bf16[768,128]{1,0:T(8,128)(2,1)}, bf16[768,128]{1,0:T(8,128)(2,1)S(1)}, u32[]{:S(2)}) copy-start(bf16[768,128]{1,0:T(8,128)(2,1)S(1)} %add_convert_fusion.4.own_ref) | copy-start | bytes 589828
  216.2 8.3 %copy-start.2 = (bf16[2,2,1120,128]{3,2,1,0:T(8,128)(2,1)}, bf16[2,2,1120,128]{3,2,1,0:T(8,128)(2,1)S(1)}, u32[]{:S(2)}) copy-start(bf16[2,2,1120,128]{3,2,1,0:T(8,128)(2,1)S(1)} %collective-permute-done.17.rest_0_) | copy-start | bytes 3440644
  216.2 13.5 %collective-permute-start.18 = (bf16[768,128]{1,0:T(8,128)(2,1)S(1)}, bf16[768,128]{1,0:T(8,128)(2,1)S(1)}, u32[]{:S(2)}, u32[]{:S(2)}) collective-permute-start(bf16[768,128]{1,0:T(8,128)(2,1)S(1)} %add_convert_fusion.4.own_ref), channel_id=1, source_target_pairs={{0,16},{1,17},{2,18},{3,19},{4,20},{5,21},{6,22},{7,23},{8,24},{9,... | collective-permute-start | bytes 589832 | tf_op jit(solution)/shard_map/ppermute | solution.py:934
  229.7 0.7 copy-start.8

commit v4 on v3

--- a/solution.py
+++ b/solution.py
@@ -14,10 +14,11 @@
 LANES = 256
 BF = jnp.bfloat16
 F32 = jnp.float32
-VMEM_BIG = 60 << 20
+VMEM_BIG = 24 << 20
 FAR = 6
-EARLY = 4
-NEAR = ((6, 2), (8, 2))
+EARLY = 3
+ALONE = 1
+NEAR = ((6, 4),)
 
 
 def cost(us):
@@ -41,6 +42,10 @@
     return pl.BlockSpec(shape, lambda *_: (0,) * len(shape))
 
 
+def hbm(value):
+    return pltpu.with_memory_space_constraint(value, pltpu.HBM)
+
+
 def sds(shape, dtype):
     return jax.ShapeDtypeStruct(shape, dtype)
 
@@ -73,22 +78,23 @@
                 ]
 
 
-def bands_kernel(k1, b1, k2, b2, k3, b3, t1, t2, t3, t3b, t2b, b2c, send, w1, w2, w3, w3b, w2b):
-    for ref in (w1, w2, w3, w3b, w2b):
+def turned(kernel, bias=None):
+    flat = kernel[...].astype(F32)
+    flat = flat.reshape(-1, flat.shape[-1])
+    if bias is not None:
+        bias = jnp.broadcast_to(bias[...].astype(F32), (8, flat.shape[1])).T[:, :1]
+    return flat, flat.T, bias
+
+
+def bands_kernel(k1, b1, k2, b2, k3, b3, t1, t2, t3, b2c, send, w1, w2, w3):
+    for ref in (w1, w2, w3):
         ref[...] = jnp.zeros_like(ref)
-
-    def turned(kernel, bias):
-        flat = kernel[...].astype(F32)
-        flat = flat.reshape(-1, flat.shape[-1])
-        bias = jnp.broadcast_to(bias[...].astype(F32), (8, flat.shape[1]))
-        return flat, flat.T, bias.T[:, :1]
-
     _, k1t, b1c = turned(k1, b1)
-    send[:512, :] = k2[...].reshape(512, 64)
+    k2n, k2t, b2t = turned(k2, b2)
+    _, k3t, b3c = turned(k3, b3)
+    send[:512, :] = k2n.astype(BF)
     send[512:, :32] = k1[:, :, 2:, :].astype(F32).reshape(128, 32).astype(BF)
     send[512:, 32:] = jnp.zeros((128, 32), BF)
-    k2n, k2t, b2t = turned(k2, b2)
-    k3n, k3t, b3c = turned(k3, b3)
     for jj in range(10):
         for dy in range(8):
             w1[32 * jj : 32 * jj + 32, 176 * dy + 16 * jj : 176 * dy + 16 * jj + 32] = k1t[:, 32 * dy : 32 * dy + 32]
@@ -100,32 +106,37 @@
     for j in range(7):
         for u in range(3):
             w3[64 * j : 64 * j + 64, 576 * u + 64 * j : 576 * u + 64 * j + 192] = k3t[:, 192 * u : 192 * u + 192]
-            w3b[64 * j : 64 * j + 192, 448 * (2 - u) + 64 * j : 448 * (2 - u) + 64 * j + 64] = k3n[192 * u : 192 * u + 192, :]
         w3[64 * j : 64 * j + 64, 1728:1729] = b3c
-    second_bands(k2n, w2b)
     t1[...] = (0.5 * w1[...]).astype(BF)
     t2[...] = (0.5 * w2[...]).astype(BF)
     t3[...] = (0.5 * w3[...]).astype(BF)
-    t3b[...] = (0.5 * w3b[...]).astype(BF)
-    t2b[...] = (0.5 * w2b[...]).astype(BF)
 
 
 def bands(*ins):
-    shapes = ((320, 1424), (192, 1024), (448, 1744), (576, 1344), (640, 768))
+    shapes = ((320, 1424), (192, 1024), (448, 1744))
     return call(
         bands_kernel,
-        tuple(sds(s, BF) for s in shapes) + (sds((192, 1), F32), sds((640, 64), BF)),
+        (sds(shapes[0], BF), pltpu.HBM(shapes[1], BF), pltpu.HBM(shapes[2], BF), sds((192, 1), F32), pltpu.HBM((640, 64), BF)),
         [whole(a.shape) for a in ins],
         [whole(s) for s in shapes] + [whole((192, 1)), whole((640, 64))],
+        us=3,
         scratch=[pltpu.VMEM(s, F32) for s in shapes],
-        us=5,
-    )(*ins)
-
-
-def band_frames_kernel(flag_ref, k1, k2, got, t1b, t2b, w1b, w2b):
+    )(*[hbm(v) for v in ins])
+
+
+def bands_back_kernel(flag_ref, k1, k2, k3, got, t3b, t2b, t2o, t1b, w3b, w2b, w1b):
     own = flag_ref[0] == 1
-    w1b[...] = jnp.zeros_like(w1b)
-    w2b[...] = jnp.zeros_like(w2b)
+    for ref in (w3b, w2b, w1b):
+        ref[...] = jnp.zeros_like(ref)
+    k3n, k2n = turned(k3)[0], turned(k2)[0]
+    for j in range(7):
+        for u in range(3):
+            w3b[64 * j : 64 * j + 192, 448 * (2 - u) + 64 * j : 448 * (2 - u) + 64 * j + 64] = k3n[192 * u : 192 * u + 192, :]
+    t3b[...] = (0.5 * w3b[...]).astype(BF)
+    second_bands(k2n, w2b)
+    t2b[...] = (0.5 * w2b[...]).astype(BF)
+    second_bands(jnp.where(own, k2n, got[:512, :].astype(F32)), w2b)
+    t2o[...] = (0.5 * w2b[...]).astype(BF)
     half = jnp.where(own, k1[:, :, :2, :].astype(F32).reshape(128, 32), got[512:, :32].astype(F32)).reshape(8, 16, 32)
     for dy in range(8):
         t, row = divmod(dy, 4)
@@ -136,21 +147,19 @@
             w1b[56 * row + 2 * lo : 56 * row + 2 * hi, 256 * t + 32 * j : 256 * t + 32 * j + 32] = half[
                 dy, 2 * d0 : 2 * (d0 + hi - lo), :
             ]
-    second_bands(jnp.where(own, k2[...].astype(F32).reshape(512, 64), got[:512, :].astype(F32)), w2b)
     t1b[...] = w1b[...].astype(BF)
-    t2b[...] = (0.5 * w2b[...]).astype(BF)
-
-
-def band_frames(flag, *ins):
-    shapes = ((224, 512), (640, 768))
+
+
+def bands_back(flag, *ins):
+    shapes = ((576, 1344), (640, 768), (640, 768), (224, 512))
     return call(
-        band_frames_kernel,
-        tuple(sds(s, BF) for s in shapes),
+        bands_back_kernel,
+        tuple(pltpu.HBM(s, BF) for s in shapes),
         [pl.BlockSpec(memory_space=pltpu.SMEM)] + [whole(a.shape) for a in ins],
         [whole(s) for s in shapes],
-        scratch=[pltpu.VMEM(s, F32) for s in shapes],
-        us=3,
-    )(flag, *ins)
+        us=4,
+        scratch=[pltpu.VMEM(s, F32) for s in (shapes[0], shapes[1], shapes[3])],
+    )(flag, *[hbm(v) for v in ins])
 
 
 def pack_rows(part, n):
@@ -224,14 +233,14 @@
         pl.BlockSpec((1, 2, 1120, 128), lambda m: (jnp.minimum(m, packs - start - 1), 0, 0, 0)),
     ]
     shapes = [
-        sds((2, 640, 10 * LANES), BF),
-        sds((2, 640, 10 * LANES), BF),
-        sds((4, 336, 20 * LANES), BF),
-        sds((packs - start, 2, 1120, 128), BF),
+        pltpu.HBM((2, 640, 10 * LANES), BF),
+        pltpu.HBM((2, 640, 10 * LANES), BF),
+        pltpu.HBM((4, 336, 20 * LANES), BF),
+        pltpu.HBM((packs - start, 2, 1120, 128), BF),
     ]
     if not start:
         outs.append(whole((4, 336, LANES)))
-        shapes.append(sds((4, 336, LANES), BF))
+        shapes.append(pltpu.HBM((4, 336, LANES), BF))
     return pl.pallas_call(
         functools.partial(conv1_kernel, rows, start, packs),
         out_shape=tuple(shapes),
@@ -248,8 +257,8 @@
         scratch_shapes=[pltpu.VMEM((3, 4, 336, LANES), BF)],
         input_output_aliases={5 + n: n for n in range(len(before))},
         compiler_params=pltpu.CompilerParams(vmem_limit_bytes=VMEM_BIG),
-        cost_estimate=cost(0.2 * (stop - start)),
-    )(xv, xv, xv, t1, ones, *before)
+        cost_estimate=cost(0.02 * (stop - start)),
+    )(hbm(xv), hbm(xv), hbm(xv), t1, ones, *[hbm(v) for v in before])
 
 
 def conv23_kernel(r0_ref, r1_ref, t2_ref, b2_ref, t3_ref, ones_ref, a2_ref, s2_ref, a3_ref, s3_ref, keep):
@@ -293,13 +302,13 @@
     out3 = pl.BlockSpec((448, LANES), lambda g: (jnp.maximum(g - 3, 0), 0))
     return call(
         conv23_kernel,
-        (sds((576, 9 * LANES), BF), sds((576, 9 * LANES), BF), sds((3136, LANES), BF), sds((3136, LANES), BF)),
+        (pltpu.HBM((576, 9 * LANES), BF), pltpu.HBM((576, 9 * LANES), BF), sds((3136, LANES), BF), pltpu.HBM((3136, LANES), BF)),
         [row(0), row(1), whole((192, 1024)), whole((192, 1)), whole((448, 1744)), whole((16, LANES))],
         [out2, out2, out3, out3],
-        us=2,
+        us=14,
         grid=(10,),
         scratch=[pltpu.VMEM((9 * 576, LANES), BF)],
-    )(a1, a1, t2, b2, t3, ones)
+    )(hbm(a1), hbm(a1), hbm(t2), b2, hbm(t3), ones)
 
 
 def head_kernel(rows, pd_ref, bd_ref, wh_ref, bh_ref, sel_ref, act_ref, slope_ref, lp_ref, cho_ref, lg_ref):
@@ -330,7 +339,7 @@
         [whole(a.shape) for a in ins],
         [whole(o[0]) for o in outs],
         scratch=[pltpu.VMEM((LOGITS, LANES), F32)],
-        us=0.5,
+        us=3,
     )(*ins)
 
 
@@ -367,7 +376,7 @@
         [whole(a.shape) for a in ins],
         [whole(o[0]) for o in outs],
         scratch=[pltpu.VMEM((LOGITS, rows), F32)],
-        us=0.5,
+        us=3,
     )(*ins)
 
 
@@ -423,7 +432,7 @@
             sds((3136, LANES), BF),
             sds((64, LANES), F32),
             sds((576, 9 * LANES), BF),
-            sds((FAR, 1008, 128), BF),
+            pltpu.HBM((FAR, 1008, 128), BF),
             sds((64, LANES), F32),
         ),
         [
@@ -434,10 +443,10 @@
             block2,
         ],
         [block3, whole((64, LANES)), block2, packed, whole((64, LANES))],
-        us=1.5,
+        us=12,
         grid=(10,),
         scratch=[pltpu.VMEM((4928, LANES), BF)],
-    )(wd, rd, s3, t3b, s2)
+    )(hbm(wd), rd, hbm(s3), hbm(t3b), hbm(s2))
 
 
 def first_diffs(t, cur, prev):
@@ -453,7 +462,6 @@
 
 
 def dconv2_kernel(first, packs, cur_ref, prev_ref, t_ref, s_ref, *rest):
-    dense = [(ref, n) for ref, (_, size) in zip(rest[-3:-1], NEAR) for n in range(size)] if packs else []
     r_ref, b_ref = rest[-4 if packs else -2], rest[-1]
     q = pl.program_id(0)
     m = 2 * q + first
@@ -476,21 +484,22 @@
             r_ref[e, :, lanes] = part.astype(BF)
             if packs:
                 value = pack_rows(part, 640).astype(BF)
-                for step in range(packs):
+                for step in range(2):
 
                     @pl.when(q == step)
-                    def _(step=step, k=k, e=e, value=value):
-                        ref, n = dense[2 * step + k]
-                        ref[n, e] = value
+                    def _(at=2 * step + k, e=e, value=value):
+                        if at < ALONE:
+                            rest[-3][at, e] = value
+                        else:
+                            rest[-2][at - ALONE, e] = value
 
             total = total + jnp.sum(part.reshape(20, 32, LANES), axis=0)
     b_ref[...] = total
 
 
-def dconv2(r2, t2b, s1, first, count, dense, r1):
-    packs = count // 2 if dense else 0
+def dconv2(r2, t2b, s1, first, count, packs, r1):
     block = pl.BlockSpec((2, 640, 2 * LANES), lambda q: (0, 0, q + first // 2))
-    ins = [r2, r2, t2b, s1]
+    ins = [r2, r2, hbm(t2b), hbm(s1)]
     in_specs = [
         pl.BlockSpec((576, 2 * LANES), lambda q: (0, q + first // 2)),
         pl.BlockSpec((576, LANES), lambda q: (0, jnp.maximum(2 * q + first - 1, 0))),
@@ -499,11 +508,11 @@
     ]
     aliases = {}
     if r1 is not None:
-        ins.append(r1)
+        ins.append(hbm(r1))
         in_specs.append(pl.BlockSpec(memory_space=pl.ANY))
         aliases = {4: 0}
-    parts = [(size, 2, 1120, 128) for _, size in NEAR] if packs else []
-    shapes = [sds((2, 640, 10 * LANES), BF)] + [sds(p, BF) for p in parts] + [sds((32, LANES), F32)]
+    parts = [(ALONE, 2, 1120, 128), (count - ALONE, 2, 1120, 128)] if packs else []
+    shapes = [pltpu.HBM((2, 640, 10 * LANES), BF)] + [pltpu.HBM(p, BF) for p in parts] + [sds((32, LANES), F32)]
     outs = [block] + [whole(p) for p in parts] + [whole((32, LANES))]
     return pl.pallas_call(
         functools.partial(dconv2_kernel, first, packs),
@@ -513,7 +522,7 @@
         out_specs=outs,
         input_output_aliases=aliases,
         compiler_params=pltpu.CompilerParams(vmem_limit_bytes=VMEM_BIG),
-        cost_estimate=cost(2 * count),
+        cost_estimate=cost(1.5 * count),
     )(*ins)
 
 
@@ -531,89 +540,104 @@
             o_ref[at + dy, 28 * g : 28 * g + 28, :, :] = out[56 * dy : 56 * dy + 56, :rows].reshape(28, 2, rows)
 
 
-def dframes_kernel(rows, first, last, far, flag_ref, own_ref, *rest):
-    edge_ref, pair = rest[-2:]
-    o_ref = rest[-3]
+def dframes_kernel(rows, first, last, far, flag_ref, own_ref, before_ref, *rest):
+    o_ref, edge_ref = rest[-2:]
     own = flag_ref[0] == 1
-    m = pl.program_id(0)
-    t1b = rest[4] if far else rest[1]
-
-    @pl.when(m == 0)
-    def _():
-        edge_ref[...] = jnp.zeros_like(edge_ref) if first == 0 else rest[5 if far else 2][...]
-
-    @pl.when(own)
-    def _():
-        for e in range(2):
-            pair[e] = own_ref[e]
-
-    @pl.when(jnp.logical_not(own))
-    def _():
-        if far:
-            cur = unpack_rows(rest[0][0].astype(F32), 576).astype(BF)
-            prev = unpack_rows(rest[1][0].astype(F32), 576).astype(BF)
-            prev = jnp.where(m + first > 0, prev, jnp.zeros_like(prev))
-            for e, part in enumerate(first_diffs(rest[3][...], cur, prev)):
-                pair[e] = (part * unpack_rows(rest[2][0, e].astype(F32), 640)).astype(BF)
-        else:
-            for e in range(2):
-                pair[e] = unpack_rows(rest[0][0, e].astype(F32), 640).astype(BF)
-
+    q = pl.program_id(0)
+    final = q == pl.num_programs(0) - 1
+    t1b = rest[5] if far else rest[2]
+
+    @pl.when(q == 0)
+    def _():
+        edge_ref[...] = jnp.zeros_like(edge_ref) if first == 0 else rest[6 if far else 3][...]
+
+    def emit(four, before):
+        for n, row in enumerate(four):
+            frame_rows(row, before, t1b[...], o_ref, 4 * n, rows)
+            before = row
+
+    def own_rows():
+        before = before_ref[0]
+        if first == 0:
+            before = jnp.where(q > 0, before, jnp.zeros_like(before))
+        emit([own_ref[e, :, LANES * k : LANES * (k + 1)] for k in range(2) for e in range(2)], before)
+
+    def other_rows():
+        four = []
+        for k in range(2):
+            if far:
+                cur = unpack_rows(rest[0][k].astype(F32), 576).astype(BF)
+                if k == 0:
+                    prev = unpack_rows(rest[1][0].astype(F32), 576).astype(BF)
+                    if first == 0:
+                        prev = jnp.where(q > 0, prev, jnp.zeros_like(prev))
+                for e, part in enumerate(first_diffs(rest[4][...], cur, prev)):
+                    m = 2 * q + k
+                    soon = rest[2][jnp.minimum(m, EARLY - 1), e]
+                    slope = jnp.where(m < EARLY, soon, rest[3][jnp.maximum(m - EARLY, 0), e]).astype(F32)
+                    four.append((part * unpack_rows(slope, 640)).astype(BF))
+                prev = cur
+            else:
+                for e in range(2):
+                    early_part = rest[0][k, e] if k < ALONE else rest[1][k - ALONE, e]
+                    part = jnp.where(q == 0, early_part, rest[1][2 + k - ALONE, e]).astype(F32)
+                    four.append(unpack_rows(part, 640).astype(BF))
+        emit(four, edge_ref[...])
+        edge_ref[...] = four[3]
+
+    more = jnp.logical_not(final) if last else True
+    pl.when(own & more)(own_rows)
+    pl.when(jnp.logical_not(own) & more)(other_rows)
     if last:
-        inside = m < pl.num_programs(0) - 1
-        for e in range(2):
-            pair[e] = jnp.where(inside, pair[e], jnp.zeros((640, LANES), BF))
-    frame_rows(pair[0], edge_ref[...], t1b[...], o_ref, 0, rows)
-    if last:
-
-        @pl.when(inside)
+
+        @pl.when(final)
         def _():
-            frame_rows(pair[1], pair[0], t1b[...], o_ref, 4, rows)
-
-    else:
-        frame_rows(pair[1], pair[0], t1b[...], o_ref, 4, rows)
-    edge_ref[...] = pair[1]
+            frame_rows(jnp.zeros((640, LANES), BF), jnp.where(own, before_ref[0], edge_ref[...]), t1b[...], o_ref, 0, rows)
 
 
 def dframes(flag, own, got, t1b, rows, first, count, edge, out):
-    far = len(got) > 1
+    far = len(got) > 2
     last = first + count == 10
-    at = lambda m: jnp.minimum(m, count - 1)
+    steps = count // 2
+    at = lambda q: jnp.minimum(q, steps - 1)
     fixed = lambda shape: pl.BlockSpec(shape, lambda *_: (0,) * len(shape))
-    ins = [flag, own]
-    in_specs = [pl.BlockSpec((2, 640, LANES), lambda m, *_: (0, 0, at(m) + first))]
+    ins = [flag, hbm(own), hbm(own)]
+    in_specs = [
+        pl.BlockSpec((2, 640, 2 * LANES), lambda q, *_: (0, 0, at(q) + first // 2)),
+        pl.BlockSpec((1, 640, LANES), lambda q, *_: (1, 0, jnp.maximum(2 * q + first - 1, 0))),
+    ]
     if far:
-        r2p, s1p, t2b = got
-        ins += [r2p, r2p, s1p, t2b]
+        r2p, early, late, t2b = got
+        ins += [hbm(v) for v in (r2p, r2p, early, late, t2b)]
         in_specs += [
-            pl.BlockSpec((1, 1008, 128), lambda m, *_: (m + first, 0, 0)),
-            pl.BlockSpec((1, 1008, 128), lambda m, *_: (jnp.maximum(m + first - 1, 0), 0, 0)),
-            pl.BlockSpec((1, 2, 1120, 128), lambda m, *_: (m, 0, 0, 0)),
+            pl.BlockSpec((2, 1008, 128), lambda q, *_: (q + first // 2, 0, 0)),
+            pl.BlockSpec((1, 1008, 128), lambda q, *_: (jnp.maximum(2 * q + first - 1, 0), 0, 0)),
+            fixed(early.shape),
+            fixed(late.shape),
             fixed((640, 768)),
         ]
     else:
-        ins.append(got[0])
-        in_specs.append(pl.BlockSpec((1, 2, 1120, 128), lambda m, *_: (at(m), 0, 0, 0)))
-    ins.append(t1b)
+        ins += [hbm(v) for v in got]
+        in_specs += [fixed(v.shape) for v in got]
+    ins.append(hbm(t1b))
     in_specs.append(fixed((224, 512)))
     aliases = {}
     if first:
-        ins += [edge, out]
+        ins += [edge, hbm(out)]
         in_specs += [fixed((640, LANES)), pl.BlockSpec(memory_space=pl.ANY)]
         aliases = {len(ins) - 1: 0}
     return pl.pallas_call(
         functools.partial(dframes_kernel, rows, first, last, far),
-        out_shape=(sds((84, 84, 2, rows), BF), sds((640, LANES), BF)),
+        out_shape=(pltpu.HBM((84, 84, 2, rows), BF), sds((640, LANES), BF)),
         grid_spec=pltpu.PrefetchScalarGridSpec(
             num_scalar_prefetch=1,
-            grid=(count + 1 if last else count,),
+            grid=(steps + 1 if last else steps,),
             in_specs=in_specs,
-            out_specs=[pl.BlockSpec((8, 84, 2, rows), lambda m, *_: (m + first, 0, 0, 0)), fixed((640, LANES))],
-            scratch_shapes=[pltpu.VMEM((2, 640, LANES), BF)],
+            out_specs=[pl.BlockSpec((16, 84, 2, rows), lambda q, *_: (q + first // 2, 0, 0, 0)), fixed((640, LANES))],
         ),
         input_output_aliases=aliases,
         compiler_params=pltpu.CompilerParams(vmem_limit_bytes=VMEM_BIG),
-        cost_estimate=cost(0.03 * count),
+        cost_estimate=cost(1.5 * count),
     )(*ins)
 
 
@@ -650,7 +674,7 @@
             out_specs=[out, out],
         ),
         compiler_params=pltpu.CompilerParams(vmem_limit_bytes=VMEM_BIG),
-        cost_estimate=cost(1),
+        cost_estimate=cost(8),
     )(flag, a3, rd, rh, h)
 
 
@@ -683,10 +707,10 @@
         [pl.BlockSpec((64, 9 * LANES), lambda q, k=k: (jnp.minimum(2 * q + k, 8), 0)) for k in range(4)]
         + [pl.BlockSpec((7, 128, LANES), lambda q: (0, q, 0))],
         whole((64, 576)),
-        us=6,
+        us=7,
         grid=(4,),
         scratch=[pltpu.VMEM((768, 128), F32)],
-    )(a2, a2, a2, a2, r3.reshape(7, 448, LANES))
+    )(hbm(a2), hbm(a2), hbm(a2), hbm(a2), r3.reshape(7, 448, LANES))
 
 
 def wconv2_kernel(a0_ref, a1_ref, r_ref, g_ref, acc):
@@ -722,10 +746,10 @@
             pl.BlockSpec((128, 9 * LANES), lambda q: (q, 0)),
         ],
         whole((512, 64)),
-        us=8,
+        us=9,
         grid=(5,),
         scratch=[pltpu.VMEM((768, 128), F32)],
-    )(a1, a1, r2)
+    )(hbm(a1), hbm(a1), r2)
 
 
 def wconv1_kernel(x_ref, x0_ref, r_ref, g_ref, acc, before):
@@ -779,10 +803,10 @@
             pl.BlockSpec((2, 640, 2 * LANES), lambda s: (0, 0, s)),
         ],
         whole((256, 32)),
-        us=14,
+        us=13,
         grid=(5,),
         scratch=[pltpu.VMEM((640, 128), F32), pltpu.VMEM((4, 336, LANES), BF)],
-    )(xt, x0, r1)
+    )(hbm(xt), hbm(x0), hbm(r1))
 
 
 SMALL_ROWS = 704
@@ -848,7 +872,7 @@
         [pl.BlockSpec(memory_space=pltpu.SMEM)] + [whole(a.shape) for a in ins],
         whole((total, 128)),
         scratch=[pltpu.VMEM((total, 128), F32)],
-        us=0.1,
+        us=3,
     )(flag, *ins)
 
 
@@ -1002,7 +1026,7 @@
     xv = frames[0].transpose(2, 3, 1, 0)
     k1, k2, k3 = kernel_first[0], kernel_second[0], kernel_third[0]
     ones = jnp.zeros((16, LANES), BF).at[0].set(1)
-    t1, t2, t3, t3b, t2b, b2, kernels = bands(k1, bias_first, k2, bias_second, k3, bias_third)
+    t1, t2, t3, b2, kernels = bands(k1, bias_first, k2, bias_second, k3, bias_third)
 
     kernels = hand(kernels)
     a1, s1, xt, early, x0 = conv1(xv, t1, ones, 0, EARLY, ())
@@ -1017,7 +1041,8 @@
     sel = jnp.where(online, taken, greedy_actions[None, :])
     h, sd, lp, cho = head(pd, dense_bias, wht, head_bias, sel)
     cho = lax.ppermute(cho, "pair", [(1, 0)])
-    row_loss, rh, hb = loss(cho, done_flags[None, :], bin_lower.T, bin_fraction.T, lp, taken)
+    t3b, t2b, t2b_online, t1b = bands_back(after(flag, lp), k1, k2, k3, kernels)
+    row_loss, rh, hb = loss(after(cho, t1b), done_flags[None, :], bin_lower.T, bin_fraction.T, lp, taken)
 
     diff_dense = lax.dot_general(wht, rh, (((0,), (0,)), ((), ())), preferred_element_type=F32)
     diff_dense = diff_dense * (0.5 * sd.astype(F32))
@@ -1044,46 +1069,34 @@
     g1 = wconv1(xt, x0, after(r1, g3))
     chunk = add(after(keep, g1), far)[0]
     far_chunk = hand(chunk[1])
-    gots = [hand(after(near0, far))]
-    gots.append(hand(after(near1, gots[0])))
-    t1b, t2b_online = band_frames(after(flag, g1), k1, k2, kernels)
+    near0 = hand(after(near0, far))
+    near1 = hand(after(near1, far))
     mine = jnp.where(online, chunk[0], far_chunk)
-    g2 = wconv2(a1, after(r2, mine, t1b))
-
-    parts = [early, late] + gots
-    firsts = [0, EARLY] + [first for first, _ in NEAR]
-    out, edge = None, None
-
-    def frames_step(n, *waits):
-        extra = (r2p, parts[n], t2b_online) if n < 2 else (parts[n],)
-        return dframes(flag, after(r1, *waits), extra, t1b, rows, firsts[n], parts[n].shape[0], edge, out)
-
-    bit = shards // 2
+    g2 = wconv2(a1, after(r2, chunk))
+
     cur = mine[None]
     part = swap(cur, bit)
     small = pack(after(flag, part, r2p), b1s, shards, capacity, b2g, b3g, g1, g2, g3, db, hb, row_loss, owner_shard.T)
+    small = add(small, swap(small, 1))
+    got = swap(small, 2)
     cur = join(cur, part)
     part = swap(cur, bit // 2)
-    small = add(small, swap(small, 1))
-    got = swap(small, 2)
-    out, edge = frames_step(0, cur, small)
+    out, edge = dframes(flag, after(r1, small, cur, near0), (r2p, early, late, t2b_online), t1b, rows, 0, FAR, None, None)
     cur = join(after(cur, edge), part)
     small = add(after(small, edge), got)
-    part_y, got_z = swap(cur, bit // 4), swap(small, 4)
-    out, edge = frames_step(1, cur, small, gots[0])
-    small = add(after(small, edge), got_z)
+    part, got = swap(cur, bit // 4), swap(small, 4)
+    small = add(small, got)
     got = swap(small, 8)
-    out, edge = frames_step(2, small)
-    cur = join(after(cur, edge), part_y)
-    small = add(after(small, edge), got)
+    small = add(after(small, near1), got)
+    cur = join(after(cur, got), part)
     lower = 16
     while lower < shards:
         small = add(small, swap(small, lower))
         cur = join(cur, swap(cur, 2 * bit // lower))
         lower *= 2
     other = swap(cur, 1)
-    far_small = hand(after(small, gots[1]))
-    out, edge = frames_step(3, cur, small)
+    far_small = hand(small)
+    out, edge = dframes(flag, after(r1, cur, small), [near0, near1], t1b, rows, FAR, 10 - FAR, edge, out)
     if shards != 16:
         cur, other = (unmix(v, me // 2).reshape(8, 512, 128) for v in (cur, other))
     dense_out, head_out = unchunk(flag, cur, other)

time: 234 us -> 217 us (0.927)
  Pallas kernels: 148 us -> 127 us
  waiting for transfers between devices: 22.8 us -> 32.7 us
  matrix products: 5.94 us -> 2.05 us
    ppermute x8, waiting for transfers between devices: 7.28 us -> 18.8 us  [hand(): return lax.ppermute(value, 'pair', [(0, 1)])]
    pallas_call x4 -> x2, Pallas kernels: 21.9 us -> 15.5 us  [dframes(): pl.pallas_call(functools.partial(dframes_kernel, rows, first, last, far),...]
    ppermute x1, waiting for transfers between devices: 4 us -> 0.52 us  [local(): cho = lax.ppermute(cho, 'pair', [(1, 0)])]
    pallas_call x1, Pallas kernels: 8.09 us -> 5.08 us  [wdense(): pl.pallas_call(wdense_kernel, out_shape=(sds((8, 2, 512, 128), BF), sds((...]
  transfers between devices with their start and end apart: 21 -> 21, of which waited for: 6 -> 6; matrix products, arithmetic and copies ran while one was open for 6% -> 4% of each run, Pallas kernels for 58% -> 54%
where the time goes in v4:
time: 217 us; the launch traced here: 216 us
  Pallas kernels  127 us (59%)
  starting transfers between devices  45.6 us (21%)
  waiting for transfers between devices  32.7 us (15%)
  other arithmetic  4.36 us (2%)
  local copies, waits for them, and re-layouts  2.94 us (1%)
    ppermute x8, starting transfers between devices, hand(): return lax.ppermute(value, 'pair', [(0, 1)])  31.9 us
    pallas_call x2, Pallas kernels, conv1(): pl.pallas_call(functools.partial(conv1_kernel, rows, start, packs), out_s...  25.6 us
    ppermute x8, waiting for transfers between devices, hand(): return lax.ppermute(value, 'pair', [(0, 1)])  18.8 us
    pallas_call x2, Pallas kernels, dframes(): pl.pallas_call(functools.partial(dframes_kernel, rows, first, last, far),...  15.5 us
    pallas_call x1, Pallas kernels, conv23(): call(conv23_kernel, (pltpu.HBM((576, 9 * LANES), BF), pltpu.HBM((576, 9 *...  14.2 us
    pallas_call x2, Pallas kernels, dconv2(): pl.pallas_call(functools.partial(dconv2_kernel, first, packs), out_shape=...  14 us
    ppermute x12, waiting for transfers between devices, swap(): return lax.ppermute(value, 'batch', [(i, i ^ bit) for i in range(devices)])  13.4 us
    pallas_call x1, Pallas kernels, wconv1(): call(wconv1_kernel, sds((256, 32), F32), [pl.BlockSpec((4, 336, 4 * LANES...  12.5 us
  transfers between devices with their start and end apart: 21, of which 6 were waited for; matrix products, arithmetic and copies ran while one was open for 4% of the time, Pallas kernels for 54%

profile of v4, /device:TPU:0, one launch (start us, length us, event | category | flops | bytes accessed | tf_op | source)
XLA Modules:
  0.0 215.8 jit_solution(12545317021534547414)
XLA Ops:
  0.7 3.0 %shard_map.256 = (bf16[320,1424]{1,0:T(8,128)(2,1)S(1)}, bf16[192,1024]{1,0:T(8,128)(2,1)}, bf16[448,1744]{1,0:T(8,128)(2,1)}, f32[192,1]{1,0:T(8,128)S(1)}, bf16[640,64]{1,0:T(8,128)(2,1)}) custom-call(bf16[8,8,4,32]{3,2,1,0:T(4,128)(2,1)} %bitcast.117, bf16[1,32]{1,0:T(2,128)(2,1)} %b1.1, bf16[4,4,32,64]{3,2,1,0:T(8,128)(2,1)} %bitcast.115, ...), custom_call_target="tpu_custom_call" | custom-call | flops 1200000000 | tf_op jit(solution)/shard_map/pallas_call | solution.py:117
  3.7 4.8 %collective-permute-start.1 = (bf16[640,64]{1,0:T(8,128)(2,1)}, bf16[640,64]{1,0:T(8,128)(2,1)S(1)}, u32[]{:S(2)}, u32[]{:S(2)}) collective-permute-start(bf16[640,64]{1,0:T(8,128)(2,1)} %get-tuple-element.111), channel_id=1, source_target_pairs={{0,16},{1,17},{2,18},{3,19},{4,20},{5,21},{6,22},{7,23},{8,24},{9,... | collective-permute-start | bytes 245768 | tf_op jit(solution)/shard_map/ppermute | solution.py:958
  8.6 9.1 %shard_map.257 = (bf16[2,640,2560]{2,1,0:T(8,128)(2,1)}, bf16[2,640,2560]{2,1,0:T(8,128)(2,1)}, bf16[4,336,5120]{2,1,0:T(8,128)(2,1)}, bf16[3,2,1120,128]{3,2,1,0:T(8,128)(2,1)}, bf16[4,336,256]{2,1,0:T(8,128)(2,1)}) custom-call(bf16[84,84,4,224]{3,2,1,0:T(4,128)(2,1)} %bitcast.96, bf16[84,84,4,224]{3,2,1,0:T(4,128)(2,1)} %bitcast.97, ...), custom_call_target="tpu_custom_call" | custom-call | flops 24000000 | tf_op jit(solution)/shard_map/pallas_call | solution.py:244
  17.7 2.5 %collective-permute-start.2 = (bf16[3,2,1120,128]{3,2,1,0:T(8,128)(2,1)}, bf16[3,2,1120,128]{3,2,1,0:T(8,128)(2,1)}, u32[]{:S(2)}, u32[]{:S(2)}) collective-permute-start(bf16[3,2,1120,128]{3,2,1,0:T(8,128)(2,1)} %get-tuple-element.117), channel_id=1, source_target_pairs={{0,16},{1,17},{2,18},{3,19},{4,20},{5,21},{6,22},{7,23},{8,24},{9,... | collective-permute-start | bytes 5160968 | tf_op jit(solution)/shard_map/ppermute | solution.py:958
  20.2 16.5 %shard_map.258 = (bf16[2,640,2560]{2,1,0:T(8,128)(2,1)}, bf16[2,640,2560]{2,1,0:T(8,128)(2,1)}, bf16[4,336,5120]{2,1,0:T(8,128)(2,1)}, bf16[3,2,1120,128]{3,2,1,0:T(8,128)(2,1)}) custom-call(bf16[84,84,4,224]{3,2,1,0:T(4,128)(2,1)} %bitcast.99, bf16[84,84,4,224]{3,2,1,0:T(4,128)(2,1)} %bitcast.100, ...), custom_call_target="tpu_custom_call", output_to_operand_aliasing={{0}: (5, {}), {1}: (6, {}), {2}: (7, {})} | custom-call | flops 56000000 | tf_op jit(solution)/shard_map/pallas_call | solution.py:244
  36.7 14.2 %shard_map.259 = (bf16[576,2304]{1,0:T(8,128)(2,1)}, bf16[576,2304]{1,0:T(8,128)(2,1)}, bf16[3136,256]{1,0:T(8,128)(2,1)S(1)}, bf16[3136,256]{1,0:T(8,128)(2,1)}) custom-call(bf16[2,640,2560]{2,1,0:T(8,128)(2,1)} %get-tuple-element.103.r0_ref.r1_ref.a0_ref.a1_ref, bf16[2,640,2560]{2,1,0:T(8,128)(2,1)} %get-tuple-element.103.r0_ref.r1_ref.a0_ref.a1_ref, ...), custom_call_target="tpu_custom_call" | custom-call | flops 5600000000 | tf_op jit(solution)/shard_map/pallas_call | solution.py:303
  51.0 1.4 convolution_bitcast_fusion.1.pd_ref
  52.4 0.3 copy-done.2
  52.7 0.8 shard_map.260
  53.5 1.3 collective-permute-start
  54.9 0.1 pad_add_fusion.flag_ref
  54.9 3.8 %shard_map.261 = (bf16[576,1344]{1,0:T(8,128)(2,1)}, bf16[640,768]{1,0:T(8,128)(2,1)}, bf16[640,768]{1,0:T(8,128)(2,1)}, bf16[224,512]{1,0:T(8,128)(2,1)}) custom-call(s32[4]{0:T(128)S(1)} %pad_add_fusion.flag_ref, bf16[8,8,4,32]{3,2,1,0:T(4,128)(2,1)} %bitcast.118, bf16[4,4,32,64]{3,2,1,0:T(8,128)(2,1)} %bitcast.116, bf16[3,3,64,64]{3,2,1,0:T(8,128)(2,1)} %bitcast.114, ...), custom_call_target="tpu_custom_call" | custom-call | flops 1600000000 | tf_op jit(solution)/shard_map/pallas_call | solution.py:155
  58.8 0.5 collective-permute-done.cho_ref
  59.3 1.0 shard_map.262
  60.4 0.6 fusion.6
  61.0 0.8 copy-done.10
  61.8 5.1 %shard_map.263 = (bf16[8,2,512,128]{3,2,1,0:T(8,128)(2,1)S(1)}, bf16[8,2,512,128]{3,2,1,0:T(8,128)(2,1)}) custom-call(s32[4]{0:T(128)S(1)} %pad_add_fusion.flag_ref, bf16[3136,256]{1,0:T(8,128)(2,1)S(1)} %copy-done.10, bf16[512,256]{1,0:T(8,128)(2,1)S(1)} %get-tuple-element.118.rd_ref, bf16[918,256]{1,0:T(8,128)(2,1)S(1)} %get-tuple-element.114.rh_ref, ...), custom_call_target="tpu_custom_call" | custom-call | flops 3200000000 | tf_op jit(solution)/shard_map/pallas_call | solution.py:662
  66.9 5.3 %collective-permute-start.5 = (bf16[3,2,1120,128]{3,2,1,0:T(8,128)(2,1)}, bf16[3,2,1120,128]{3,2,1,0:T(8,128)(2,1)}, u32[]{:S(2)}, u32[]{:S(2)}) collective-permute-start(bf16[3,2,1120,128]{3,2,1,0:T(8,128)(2,1)} %get-tuple-element.132), channel_id=1, source_target_pairs={{0,16},{1,17},{2,18},{3,19},{4,20},{5,21},{6,22},{7,23},{8,24},{9,... | collective-permute-start | bytes 5160968 | tf_op jit(solution)/shard_map/ppermute | solution.py:958
  72.1 2.1 add_convert_fusion
  74.3 1.2 dynamic-slice_bitcast_fusion.1
  75.4 1.5 collective-permute-start.4
  76.9 11.8 %shard_map.264 = (bf16[3136,256]{1,0:T(8,128)(2,1)S(1)}, f32[64,256]{1,0:T(8,128)S(1)}, bf16[576,2304]{1,0:T(8,128)(2,1)S(1)}, bf16[6,1008,128]{2,1,0:T(8,128)(2,1)}, f32[64,256]{1,0:T(8,128)S(1)}) custom-call(bf16[3136,512]{1,0:T(8,128)(2,1)} %bitcast.112, bf16[512,256]{1,0:T(8,128)(2,1)S(1)} %get-tuple-element.118.rd_ref, ...), custom_call_target="tpu_custom_call" | custom-call | flops 4800000000 | tf_op jit(solution)/shard_map/pallas_call | solution.py:429
  88.8 4.4 %collective-permute-start.10 = (bf16[6,1008,128]{2,1,0:T(8,128)(2,1)}, bf16[6,1008,128]{2,1,0:T(8,128)(2,1)}, u32[]{:S(2)}, u32[]{:S(2)}) collective-permute-start(bf16[6,1008,128]{2,1,0:T(8,128)(2,1)} %get-tuple-element.143), channel_id=1, source_target_pairs={{0,16},{1,17},{2,18},{3,19},{4,20},{5,21},{6,22},{7,23},{8,24},{9,... | collective-permute-start | bytes 4644872 | tf_op jit(solution)/shard_map/ppermute | solution.py:958
  93.2 7.1 %shard_map.265 = (bf16[2,640,2560]{2,1,0:T(8,128)(2,1)}, bf16[1,2,1120,128]{3,2,1,0:T(8,128)(2,1)}, bf16[3,2,1120,128]{3,2,1,0:T(8,128)(2,1)}, f32[32,256]{1,0:T(8,128)S(1)}) custom-call(bf16[576,2304]{1,0:T(8,128)(2,1)S(1)} %get-tuple-element.133.cur_ref.prev_ref.r_ref, bf16[576,2304]{1,0:T(8,128)(2,1)S(1)} %get-tuple-element.133.cur_ref.prev_ref.r_ref, ...), custom_call_target="tpu_custom_call" | custom-call | flops 2400000000 | tf_op jit(solution)/shard_map/pallas_call | solution.py:517
  100.2 8.8 %collective-permute-done.5.rest_3_ = bf16[3,2,1120,128]{3,2,1,0:T(8,128)(2,1)} collective-permute-done((bf16[3,2,1120,128]{3,2,1,0:T(8,128)(2,1)}, bf16[3,2,1120,128]{3,2,1,0:T(8,128)(2,1)}, u32[]{:S(2)}, u32[]{:S(2)}) %collective-permute-start.5) | collective-permute-done | bytes 1720352 | tf_op jit(solution)/shard_map/ppermute | solution.py:958
  109.1 1.5 add_convert_fusion.1
  110.6 0.1 dynamic-slice_bitcast_fusion.3
  110.7 1.6 collective-permute-start.6
  112.3 7.0 %shard_map.266 = (bf16[2,640,2560]{2,1,0:T(8,128)(2,1)}, f32[32,256]{1,0:T(8,128)S(1)}) custom-call(bf16[576,2304]{1,0:T(8,128)(2,1)S(1)} %get-tuple-element.133.cur_ref.prev_ref.r_ref, bf16[576,2304]{1,0:T(8,128)(2,1)S(1)} %get-tuple-element.133.cur_ref.prev_ref.r_ref, bf16[640,768]{1,0:T(8,128)(2,1)} %get-tuple-element.126.t_ref, ...), custom_call_target="tpu_custom_call", output_to_operand_aliasing={{0}: (4, {})} | custom-call | flops 3600000000 | tf_op jit(solution)/shard_map/pallas_call | solution.py:517
  119.3 6.2 %shard_map.267.refs_6_ = f32[64,576]{1,0:T(8,128)S(1)} custom-call(bf16[576,2304]{1,0:T(8,128)(2,1)} %get-tuple-element.130.refs_0_.refs_1_.refs_2_.refs_3_, bf16[576,2304]{1,0:T(8,128)(2,1)} %get-tuple-element.130.refs_0_.refs_1_.refs_2_.refs_3_, bf16[576,2304]{1,0:T(8,128)(2,1)} %get-tuple-element.130.refs_0_.refs_1_.refs_2_.refs_3_, ...), custom_call_target="tpu_custom_call" | custom-call | flops 2800000000 | tf_op jit(solution)/shard_map/pallas_call | solution.py:704
  125.5 0.1 add_convert_fusion.2
  125.7 2.6 %collective-permute-start.7 = (bf16[1,2,512,128]{3,2,1,0:T(8,128)(2,1)S(1)}, bf16[1,2,512,128]{3,2,1,0:T(8,128)(2,1)S(1)}, u32[]{:S(2)}, u32[]{:S(2)}) collective-permute-start(bf16[1,2,512,128]{3,2,1,0:T(8,128)(2,1)S(1)} %get-tuple-element.181), channel_id=1, source_target_pairs={{0,8},{1,9},{2,10},{3,11},{4,12},{5,13},{6,14},{7,15},{8,0},{9,1},... | collective-permute-start | bytes 786440 | tf_op jit(solution)/shard_map/ppermute | solution.py:963
  128.4 12.5 %shard_map.268.refs_4_ = f32[256,32]{1,0:T(8,128)S(1)} custom-call(bf16[4,336,5120]{2,1,0:T(8,128)(2,1)} %get-tuple-element.138.x_ref, bf16[4,336,256]{2,1,0:T(8,128)(2,1)} %get-tuple-element.139.x0_ref, bf16[2,640,2560]{2,1,0:T(8,128)(2,1)} %get-tuple-element.170.r_ref.own_ref.before_ref), custom_call_target="tpu_custom_call" | custom-call | flops 5200000000 | tf_op jit(solution)/shard_map/pallas_call | solution.py:797
  140.9 0.1 add_convert_fusion.3
  141.0 4.4 %collective-permute-start.8 = (bf16[512,128]{1,0:T(8,128)(2,1)S(1)}, bf16[512,128]{1,0:T(8,128)(2,1)S(1)}, u32[]{:S(2)}, u32[]{:S(2)}) collective-permute-start(bf16[512,128]{1,0:T(8,128)(2,1)S(1)} %slice_bitcast_fusion), channel_id=1, source_target_pairs={{0,16},{1,17},{2,18},{3,19},{4,20},{5,21},{6,22},{7,23},{8,24},{9,... | collective-permute-start | bytes 393224 | tf_op jit(solution)/shard_map/ppermute | solution.py:958
  145.4 1.3 collective-permute-start.12
  146.8 2.5 %collective-permute-done.8 = bf16[512,128]{1,0:T(8,128)(2,1)S(1)} collective-permute-done((bf16[512,128]{1,0:T(8,128)(2,1)S(1)}, bf16[512,128]{1,0:T(8,128)(2,1)S(1)}, u32[]{:S(2)}, u32[]{:S(2)}) %collective-permute-start.8) | collective-permute-done | bytes 131104 | tf_op jit(solution)/shard_map/ppermute | solution.py:958
  149.3 0.4 collective-permute-start.9
  149.7 7.9 %shard_map.269.refs_5_ = f32[512,64]{1,0:T(8,128)S(1)} custom-call(bf16[2,640,2560]{2,1,0:T(8,128)(2,1)} %get-tuple-element.103.r0_ref.r1_ref.a0_ref.a1_ref, bf16[2,640,2560]{2,1,0:T(8,128)(2,1)} %get-tuple-element.103.r0_ref.r1_ref.a0_ref.a1_ref, bf16[576,2304]{1,0:T(8,128)(2,1)S(1)} %get-tuple-element.133.cur_ref.prev_ref.r_ref), custom_call_target="tpu_custom_call" | custom-call | flops 3600000000 | tf_op jit(solution)/shard_map/pallas_call | solution.py:740
  157.6 0.1 copy.40.refs_7_
  157.8 1.0 shard_map.270
  158.8 0.1 collective-permute-start.11
  158.9 0.3 copy-done.15
  159.3 4.7 %collective-permute-start.15 = (bf16[3,2,1120,128]{3,2,1,0:T(8,128)(2,1)S(1)}, bf16[3,2,1120,128]{3,2,1,0:T(8,128)(2,1)S(1)}, u32[]{:S(2)}, u32[]{:S(2)}) collective-permute-start(bf16[3,2,1120,128]{3,2,1,0:T(8,128)(2,1)S(1)} %copy-done.15), channel_id=1, source_target_pairs={{0,16},{1,17},{2,18},{3,19},{4,20},{5,21},{6,22},{7,23},{8,24},{9,... | collective-permute-start | bytes 5160968 | tf_op jit(solution)/shard_map/ppermute | solution.py:958
  164.0 1.4 collective-permute-start.18
  165.4 0.1 add_convert_fusion.7
  165.5 1.6 collective-permute-start.13
  167.1 9.4 %shard_map.271 = (bf16[84,84,2,224]{3,2,1,0:T(2,128)(2,1)}, bf16[640,256]{1,0:T(8,128)(2,1)S(1)}) custom-call(s32[4]{0:T(128)S(1)} %pad_add_fusion.flag_ref, bf16[2,640,2560]{2,1,0:T(8,128)(2,1)} %get-tuple-element.170.r_ref.own_ref.before_ref, bf16[2,640,2560]{2,1,0:T(8,128)(2,1)} %get-tuple-element.170.r_ref.own_ref.before_ref, ...), custom_call_target="tpu_custom_call" | custom-call | flops 3600000000 | tf_op jit(solution)/shard_map/pallas_call | solution.py:629
  176.5 0.1 add_convert_fusion.6
  176.5 0.8 collective-permute-start.14
  177.3 0.1 pad_maximum_fusion.1
  177.4 0.6 collective-permute-start.19
  177.9 4.8 %collective-permute-done.14 = bf16[768,128]{1,0:T(8,128)(2,1)S(1)} collective-permute-done((bf16[768,128]{1,0:T(8,128)(2,1)S(1)}, bf16[768,128]{1,0:T(8,128)(2,1)S(1)}, u32[]{:S(2)}, u32[]{:S(2)}) %collective-permute-start.14) | collective-permute-done | bytes 196640 | tf_op jit(solution)/shard_map/ppermute | solution.py:963
  182.7 0.1 add_convert_fusion.5
  182.8 1.8 collective-permute-start.16
  184.5 8.6 %collective-permute-done.16 = bf16[768,128]{1,0:T(8,128)(2,1)S(1)} collective-permute-done((bf16[768,128]{1,0:T(8,128)(2,1)S(1)}, bf16[768,128]{1,0:T(8,128)(2,1)S(1)}, u32[]{:S(2)}, u32[]{:S(2)}) %collective-permute-start.16) | collective-permute-done | bytes 196640 | tf_op jit(solution)/shard_map/ppermute | solution.py:963
  193.1 0.1 pad_maximum_fusion
  193.2 0.1 collective-permute-start.20
  193.3 7.5 %collective-permute-done.15.rest_1_ = bf16[3,2,1120,128]{3,2,1,0:T(8,128)(2,1)S(1)} collective-permute-done((bf16[3,2,1120,128]{3,2,1,0:T(8,128)(2,1)S(1)}, bf16[3,2,1120,128]{3,2,1,0:T(8,128)(2,1)S(1)}, u32[]{:S(2)}, u32[]{:S(2)}) %collective-permute-start.15) | collective-permute-done | bytes 1720352 | tf_op jit(solution)/shard_map/ppermute | solution.py:958
  200.8 0.1 add_convert_fusion.4.own_ref
  200.8 4.4 %collective-permute-start.17 = (bf16[768,128]{1,0:T(8,128)(2,1)S(1)}, bf16[768,128]{1,0:T(8,128)(2,1)S(1)}, u32[]{:S(2)}, u32[]{:S(2)}) collective-permute-start(bf16[768,128]{1,0:T(8,128)(2,1)S(1)} %add_convert_fusion.4.own_ref), channel_id=1, source_target_pairs={{0,16},{1,17},{2,18},{3,19},{4,20},{5,21},{6,22},{7,23},{8,24},{9,... | collective-permute-start | bytes 589832 | tf_op jit(solution)/shard_map/ppermute | solution.py:958
  205.3 6.1 %shard_map.274 = (bf16[84,84,2,224]{3,2,1,0:T(2,128)(2,1)}, bf16[640,256]{1,0:T(8,128)(2,1)}) custom-call(s32[4]{0:T(128)S(1)} %pad_add_fusion.flag_ref, bf16[2,640,2560]{2,1,0:T(8,128)(2,1)} %get-tuple-element.170.r_ref.own_ref.before_ref, bf16[2,640,2560]{2,1,0:T(8,128)(2,1)} %get-tuple-element.170.r_ref.own_ref.before_ref, ...), custom_call_target="tpu_custom_call", output_to_operand_aliasing={{0}: (7, {})} | custom-call | flops 2400000000 | tf_op jit(solution)/shard_map/pallas_call | solution.py:629
  211.3 1.5 shard_map.272
  212.8 3.0 %shard_map.273 = (f32[3136,256]{1,0:T(8,128)}, f32[918,256]{1,0:T(8,128)}) custom-call(s32[4]{0:T(128)S(1)} %pad_add_fusion.flag_ref, bf16[8,512,128]{2,1,0:T(8,128)(2,1)S(1)} %bitcast.88, bf16[8,512,128]{2,1,0:T(8,128)(2,1)S(1)} %collective-permute-done.20.other_ref), custom_call_target="tpu_custom_call" | custom-call | flops 1600000000 | tf_op jit(solution)/shard_map/pallas_call | solution.py:943
  (52 shorter events, 0.2 us)
Async XLA Ops:
  0.6 7.9 %copy-start = (bf16[16,256]{1,0:T(8,128)(2,1)S(1)}, bf16[16,256]{1,0:T(8,128)(2,1)}, u32[]{:S(2)}) copy-start(bf16[16,256]{1,0:T(8,128)(2,1)} %constant.120.clone.1.ones_ref) | copy-start | bytes 24580
  3.7 14.0 %collective-permute-start.1 = (bf16[640,64]{1,0:T(8,128)(2,1)}, bf16[640,64]{1,0:T(8,128)(2,1)S(1)}, u32[]{:S(2)}, u32[]{:S(2)}) collective-permute-start(bf16[640,64]{1,0:T(8,128)(2,1)} %get-tuple-element.111), channel_id=1, source_target_pairs={{0,16},{1,17},{2,18},{3,19},{4,20},{5,21},{6,22},{7,23},{8,24},{9,... | collective-permute-start | bytes 245768 | tf_op jit(solution)/shard_map/ppermute | solution.py:958
  8.5 11.7 %copy-start.1 = (s32[224]{0:T(256)S(1)}, s32[224]{0:T(256)}, u32[]{:S(2)}) copy-start(s32[224]{0:T(256)} %param.30) | copy-start | bytes 2692
  8.6 11.7 %copy-start.13 = (s32[224]{0:T(256)S(1)}, s32[224]{0:T(256)}, u32[]{:S(2)}) copy-start(s32[224]{0:T(256)} %param.31) | copy-start | bytes 2692
  17.7 19.1 %copy-start.16 = (bf16[640,64]{1,0:T(8,128)(2,1)}, bf16[640,64]{1,0:T(8,128)(2,1)S(1)}, u32[]{:S(2)}) copy-start(bf16[640,64]{1,0:T(8,128)(2,1)S(1)} %collective-permute-done.1.got) | copy-start | bytes 245764
  17.7 43.3 %collective-permute-start.2 = (bf16[3,2,1120,128]{3,2,1,0:T(8,128)(2,1)}, bf16[3,2,1120,128]{3,2,1,0:T(8,128)(2,1)}, u32[]{:S(2)}, u32[]{:S(2)}) collective-permute-start(bf16[3,2,1120,128]{3,2,1,0:T(8,128)(2,1)} %get-tuple-element.117), channel_id=1, source_target_pairs={{0,16},{1,17},{2,18},{3,19},{4,20},{5,21},{6,22},{7,23},{8,24},{9,... | collective-permute-start | bytes 5160968 | tf_op jit(solution)/shard_map/ppermute | solution.py:958
  36.7 14.2 %copy-start.14 = (bf16[1,3136,512]{2,1,0:T(8,128)(2,1)S(1)}, bf16[1,3136,512]{2,1,0:T(8,128)(2,1)}, u32[]{:S(2)}) copy-start(bf16[1,3136,512]{2,1,0:T(8,128)(2,1)} %param.26) | copy-start | bytes 9633796
  50.9 1.5 copy-start.9
  51.0 1.8 copy-start.2
  51.0 1.8 copy-start.5
  51.0 1.8 copy-start.6
  53.5 5.8 %collective-permute-start = (bf16[51,224]{1,0:T(8,128)(2,1)S(1)}, bf16[51,224]{1,0:T(8,128)(2,1)S(1)}, u32[]{:S(2)}, u32[]{:S(2)}) collective-permute-start(bf16[51,224]{1,0:T(8,128)(2,1)S(1)} %get-tuple-element.108), channel_id=1, source_target_pairs={{16,0},{17,1},{18,2},{19,3},{20,4},{21,5},{22,6},{23,7},{24,8},{25... | collective-permute-start | bytes 68552 | tf_op jit(solution)/shard_map/ppermute | solution.py:1043
  54.9 4.4 %copy-start.3 = (s32[224,51]{0,1:T(8,128)S(1)}, s32[224,51]{0,1:T(8,128)}, u32[]{:S(2)}) copy-start(s32[224,51]{0,1:T(8,128)} %param.33) | copy-start | bytes 137092
  54.9 4.4 %copy-start.4 = (f32[224,51]{0,1:T(8,128)S(1)}, f32[224,51]{0,1:T(8,128)}, u32[]{:S(2)}) copy-start(f32[224,51]{0,1:T(8,128)} %param.34) | copy-start | bytes 137092
  54.9 4.4 %copy-start.7 = (s32[224]{0:T(256)S(1)}, s32[224]{0:T(256)}, u32[]{:S(2)}) copy-start(s32[224]{0:T(256)} %param.32) | copy-start | bytes 2692
  60.4 1.4 copy-start.10
  66.9 5.3 %collective-permute-start.3 = (bf16[8,2,512,128]{3,2,1,0:T(8,128)(2,1)}, bf16[8,2,512,128]{3,2,1,0:T(8,128)(2,1)}, u32[]{:S(2)}, u32[]{:S(2)}) collective-permute-start(bf16[8,2,512,128]{3,2,1,0:T(8,128)(2,1)} %get-tuple-element.121), channel_id=1, source_target_pairs={{0,1},{1,0},{2,3},{3,2},{4,5},{5,4},{6,7},{7,6},{8,9},{9,8},{10,11... | collective-permute-start | bytes 6291464 | tf_op jit(solution)/shard_map/ppermute | solution.py:963
  66.9 42.2 %collective-permute-start.5 = (bf16[3,2,1120,128]{3,2,1,0:T(8,128)(2,1)}, bf16[3,2,1120,128]{3,2,1,0:T(8,128)(2,1)}, u32[]{:S(2)}, u32[]{:S(2)}) collective-permute-start(bf16[3,2,1120,128]{3,2,1,0:T(8,128)(2,1)} %get-tuple-element.132), channel_id=1, source_target_pairs={{0,16},{1,17},{2,18},{3,19},{4,20},{5,21},{6,22},{7,23},{8,24},{9,... | collective-permute-start | bytes 5160968 | tf_op jit(solution)/shard_map/ppermute | solution.py:958
  75.4 33.6 %collective-permute-start.4 = (bf16[4,2,512,128]{3,2,1,0:T(8,128)(2,1)}, bf16[4,2,512,128]{3,2,1,0:T(8,128)(2,1)}, u32[]{:S(2)}, u32[]{:S(2)}) collective-permute-start(bf16[4,2,512,128]{3,2,1,0:T(8,128)(2,1)} %get-tuple-element.175), channel_id=1, source_target_pairs={{0,2},{1,3},{2,0},{3,1},{4,6},{5,7},{6,4},{7,5},{8,10},{9,11},{10,... | collective-permute-start | bytes 3145736 | tf_op jit(solution)/shard_map/ppermute | solution.py:963
  88.8 69.0 %collective-permute-start.10 = (bf16[6,1008,128]{2,1,0:T(8,128)(2,1)}, bf16[6,1008,128]{2,1,0:T(8,128)(2,1)}, u32[]{:S(2)}, u32[]{:S(2)}) collective-permute-start(bf16[6,1008,128]{2,1,0:T(8,128)(2,1)} %get-tuple-element.143), channel_id=1, source_target_pairs={{0,16},{1,17},{2,18},{3,19},{4,20},{5,21},{6,22},{7,23},{8,24},{9,... | collective-permute-start | bytes 4644872 | tf_op jit(solution)/shard_map/ppermute | solution.py:958
  110.7 14.8 %collective-permute-start.6 = (bf16[2,2,512,128]{3,2,1,0:T(8,128)(2,1)S(1)}, bf16[2,2,512,128]{3,2,1,0:T(8,128)(2,1)S(1)}, u32[]{:S(2)}, u32[]{:S(2)}) collective-permute-start(bf16[2,2,512,128]{3,2,1,0:T(8,128)(2,1)S(1)} %get-tuple-element.177), channel_id=1, source_target_pairs={{0,4},{1,5},{2,6},{3,7},{4,0},{5,1},{6,2},{7,3},{8,12},{9,13},{10,... | collective-permute-start | bytes 1572872 | tf_op jit(solution)/shard_map/ppermute | solution.py:963
  125.7 15.2 %collective-permute-start.7 = (bf16[1,2,512,128]{3,2,1,0:T(8,128)(2,1)S(1)}, bf16[1,2,512,128]{3,2,1,0:T(8,128)(2,1)S(1)}, u32[]{:S(2)}, u32[]{:S(2)}) collective-permute-start(bf16[1,2,512,128]{3,2,1,0:T(8,128)(2,1)S(1)} %get-tuple-element.181), channel_id=1, source_target_pairs={{0,8},{1,9},{2,10},{3,11},{4,12},{5,13},{6,14},{7,15},{8,0},{9,1},... | collective-permute-start | bytes 786440 | tf_op jit(solution)/shard_map/ppermute | solution.py:963
  141.0 8.2 %collective-permute-start.8 = (bf16[512,128]{1,0:T(8,128)(2,1)S(1)}, bf16[512,128]{1,0:T(8,128)(2,1)S(1)}, u32[]{:S(2)}, u32[]{:S(2)}) collective-permute-start(bf16[512,128]{1,0:T(8,128)(2,1)S(1)} %slice_bitcast_fusion), channel_id=1, source_target_pairs={{0,16},{1,17},{2,18},{3,19},{4,20},{5,21},{6,22},{7,23},{8,24},{9,... | collective-permute-start | bytes 393224 | tf_op jit(solution)/shard_map/ppermute | solution.py:958
  145.4 21.6 %collective-permute-start.12 = (bf16[1,2,1120,128]{3,2,1,0:T(8,128)(2,1)}, bf16[1,2,1120,128]{3,2,1,0:T(8,128)(2,1)S(1)}, u32[]{:S(2)}, u32[]{:S(2)}) collective-permute-start(bf16[1,2,1120,128]{3,2,1,0:T(8,128)(2,1)} %get-tuple-element.150), channel_id=1, source_target_pairs={{0,16},{1,17},{2,18},{3,19},{4,20},{5,21},{6,22},{7,23},{8,24},{9,... | collective-permute-start | bytes 1720328 | tf_op jit(solution)/shard_map/ppermute | solution.py:958
  149.3 8.5 %copy-start.8 = (s32[224,1]{0,1:T(1,128)S(1)}, s32[224,1]{0,1:T(1,128)}, u32[]{:S(2)}) copy-start(s32[224,1]{0,1:T(1,128)} %param.35) | copy-start | bytes 2692
  149.3 8.5 %collective-permute-start.9 = (bf16[1,512,128]{2,1,0:T(8,128)(2,1)S(1)}, bf16[1,512,128]{2,1,0:T(8,128)(2,1)S(1)}, u32[]{:S(2)}, u32[]{:S(2)}) collective-permute-start(bf16[1,512,128]{2,1,0:T(8,128)(2,1)S(1)} %get-tuple-element.183), channel_id=1, source_target_pairs={{0,8},{1,9},{2,10},{3,11},{4,12},{5,13},{6,14},{7,15},{8,0},{9,1},... | collective-permute-start | bytes 393224 | tf_op jit(solution)/shard_map/ppermute | solution.py:963
  157.8 1.5 copy-start.15
  158.8 6.6 %collective-permute-start.11 = (bf16[768,128]{1,0:T(8,128)(2,1)S(1)}, bf16[768,128]{1,0:T(8,128)(2,1)S(1)}, u32[]{:S(2)}, u32[]{:S(2)}) collective-permute-start(bf16[768,128]{1,0:T(8,128)(2,1)S(1)} %shard_map.270), channel_id=1, source_target_pairs={{0,1},{1,0},{2,3},{3,2},{4,5},{5,4},{6,7},{7,6},{8,9},{9,8},{10,11... | collective-permute-start | bytes 589832 | tf_op jit(solution)/shard_map/ppermute | solution.py:963
  159.3 41.5 %collective-permute-start.15 = (bf16[3,2,1120,128]{3,2,1,0:T(8,128)(2,1)S(1)}, bf16[3,2,1120,128]{3,2,1,0:T(8,128)(2,1)S(1)}, u32[]{:S(2)}, u32[]{:S(2)}) collective-permute-start(bf16[3,2,1120,128]{3,2,1,0:T(8,128)(2,1)S(1)} %copy-done.15), channel_id=1, source_target_pairs={{0,16},{1,17},{2,18},{3,19},{4,20},{5,21},{6,22},{7,23},{8,24},{9,... | collective-permute-start | bytes 5160968 | tf_op jit(solution)/shard_map/ppermute | solution.py:958
  164.0 13.3 %collective-permute-start.18 = (bf16[2,512,128]{2,1,0:T(8,128)(2,1)S(1)}, bf16[2,512,128]{2,1,0:T(8,128)(2,1)S(1)}, u32[]{:S(2)}, u32[]{:S(2)}) collective-permute-start(bf16[2,512,128]{2,1,0:T(8,128)(2,1)S(1)} %maximum_bitcast_fusion), channel_id=1, source_target_pairs={{0,4},{1,5},{2,6},{3,7},{4,0},{5,1},{6,2},{7,3},{8,12},{9,13},{10,... | collective-permute-start | bytes 786440 | tf_op jit(solution)/shard_map/ppermute | solution.py:963
  165.5 11.0 %collective-permute-start.13 = (bf16[768,128]{1,0:T(8,128)(2,1)S(1)}, bf16[768,128]{1,0:T(8,128)(2,1)S(1)}, u32[]{:S(2)}, u32[]{:S(2)}) collective-permute-start(bf16[768,128]{1,0:T(8,128)(2,1)S(1)} %add_convert_fusion.7), channel_id=1, source_target_pairs={{0,2},{1,3},{2,0},{3,1},{4,6},{5,7},{6,4},{7,5},{8,10},{9,11},{10,... | collective-permute-start | bytes 589832 | tf_op jit(solution)/shard_map/ppermute | solution.py:963
  167.1 9.4 %copy-start.12 = (bf16[1,2,1120,128]{3,2,1,0:T(8,128)(2,1)}, bf16[1,2,1120,128]{3,2,1,0:T(8,128)(2,1)S(1)}, u32[]{:S(2)}) copy-start(bf16[1,2,1120,128]{3,2,1,0:T(8,128)(2,1)S(1)} %collective-permute-done.12.rest_0_) | copy-start | bytes 1720324
  176.5 6.2 %collective-permute-start.14 = (bf16[768,128]{1,0:T(8,128)(2,1)S(1)}, bf16[768,128]{1,0:T(8,128)(2,1)S(1)}, u32[]{:S(2)}, u32[]{:S(2)}) collective-permute-start(bf16[768,128]{1,0:T(8,128)(2,1)S(1)} %add_convert_fusion.6), channel_id=1, source_target_pairs={{0,4},{1,5},{2,6},{3,7},{4,0},{5,1},{6,2},{7,3},{8,12},{9,13},{10,... | collective-permute-start | bytes 589832 | tf_op jit(solution)/shard_map/ppermute | solution.py:963
  177.4 15.8 %collective-permute-start.19 = (bf16[4,512,128]{2,1,0:T(8,128)(2,1)S(1)}, bf16[4,512,128]{2,1,0:T(8,128)(2,1)S(1)}, u32[]{:S(2)}, u32[]{:S(2)}) collective-permute-start(bf16[4,512,128]{2,1,0:T(8,128)(2,1)S(1)} %bitcast.105), channel_id=1, source_target_pairs={{0,2},{1,3},{2,0},{3,1},{4,6},{5,7},{6,4},{7,5},{8,10},{9,11},{10,... | collective-permute-start | bytes 1572872 | tf_op jit(solution)/shard_map/ppermute | solution.py:963
  182.8 10.4 %collective-permute-start.16 = (bf16[768,128]{1,0:T(8,128)(2,1)S(1)}, bf16[768,128]{1,0:T(8,128)(2,1)S(1)}, u32[]{:S(2)}, u32[]{:S(2)}) collective-permute-start(bf16[768,128]{1,0:T(8,128)(2,1)S(1)} %add_convert_fusion.5), channel_id=1, source_target_pairs={{0,8},{1,9},{2,10},{3,11},{4,12},{5,13},{6,14},{7,15},{8,0},{9,1},... | collective-permute-start | bytes 589832 | tf_op jit(solution)/shard_map/ppermute | solution.py:963
  193.2 19.6 %collective-permute-start.20 = (bf16[8,512,128]{2,1,0:T(8,128)(2,1)S(1)}, bf16[8,512,128]{2,1,0:T(8,128)(2,1)S(1)}, u32[]{:S(2)}, u32[]{:S(2)}) collective-permute-start(bf16[8,512,128]{2,1,0:T(8,128)(2,1)S(1)} %bitcast.87), channel_id=1, source_target_pairs={{0,1},{1,0},{2,3},{3,2},{4,5},{5,4},{6,7},{7,6},{8,9},{9,8},{10,11... | collective-permute-start | bytes 3145736 | tf_op jit(solution)/shard_map/ppermute | solution.py:963
  200.8 4.5 %copy-start.11 = (bf16[3,2,1120,128]{3,2,1,0:T(8,128)(2,1)}, bf16[3,2,1120,128]{3,2,1,0:T(8,128)(2,1)S(1)}, u32[]{:S(2)}) copy-start(bf16[3,2,1120,128]{3,2,1,0:T(8,128)(2,1)S(1)} %collective-permute-done.15.rest_1_) | copy-start | bytes 5160964
  200.8 10.5 %collective-permute-start.17 = (bf16[768,128]{1,0:T(8,128)(2,1)S(1)}, bf16[768,128]{1,0:T(8,128)(2,1)S(1)}, u32[]{:S(2)}, u32[]{:S(2)}) collective-permute-start(bf16[768,128]{1,0:T(8,128)(2,1)S(1)} %add_convert_fusion.4.own_ref), channel_id=1, source_target_pairs={{0,16},{1,17},{2,18},{3,19},{4,20},{5,21},{6,22},{7,23},{8,24},{9,... | collective-permute-start | bytes 589832 | tf_op jit(solution)/shard_map/ppermute | solution.py:958

commit v5 on v4

--- a/solution.py
+++ b/solution.py
@@ -617,9 +617,9 @@
             fixed((640, 768)),
         ]
     else:
-        ins += [hbm(v) for v in got]
+        ins += got
         in_specs += [fixed(v.shape) for v in got]
-    ins.append(hbm(t1b))
+    ins.append(t1b)
     in_specs.append(fixed((224, 512)))
     aliases = {}
     if first:
@@ -710,7 +710,7 @@
         us=7,
         grid=(4,),
         scratch=[pltpu.VMEM((768, 128), F32)],
-    )(hbm(a2), hbm(a2), hbm(a2), hbm(a2), r3.reshape(7, 448, LANES))
+    )(a2, a2, a2, a2, r3.reshape(7, 448, LANES))
 
 
 def wconv2_kernel(a0_ref, a1_ref, r_ref, g_ref, acc):

time: 217 us -> 215 us (level)
  transfers between devices with their start and end apart: 21 -> 21, of which waited for: 6 -> 6; matrix products, arithmetic and copies ran while one was open for 4% -> 4% of each run, Pallas kernels for 54% -> 53%
where the time goes in v5:
time: 215 us; the launch traced here: 214 us
  Pallas kernels  125 us (58%)
  starting transfers between devices  46.2 us (21%)
  waiting for transfers between devices  32.3 us (15%)
  other arithmetic  4.36 us (2%)
  local copies, waits for them, and re-layouts  2.94 us (1%)
    ppermute x8, starting transfers between devices, hand(): return lax.ppermute(value, 'pair', [(0, 1)])  31.8 us
    pallas_call x2, Pallas kernels, conv1(): pl.pallas_call(functools.partial(conv1_kernel, rows, start, packs), out_s...  25.6 us
    ppermute x8, waiting for transfers between devices, hand(): return lax.ppermute(value, 'pair', [(0, 1)])  18.7 us
    pallas_call x2, Pallas kernels, dframes(): pl.pallas_call(functools.partial(dframes_kernel, rows, first, last, far),...  14.6 us
    pallas_call x1, Pallas kernels, conv23(): call(conv23_kernel, (pltpu.HBM((576, 9 * LANES), BF), pltpu.HBM((576, 9 *...  14.2 us
    pallas_call x2, Pallas kernels, dconv2(): pl.pallas_call(functools.partial(dconv2_kernel, first, packs), out_shape=...  14.2 us
    ppermute x12, waiting for transfers between devices, swap(): return lax.ppermute(value, 'batch', [(i, i ^ bit) for i in range(devices)])  13.1 us
    ppermute x12, starting transfers between devices, swap(): return lax.ppermute(value, 'batch', [(i, i ^ bit) for i in range(devices)])  13.1 us
  transfers between devices with their start and end apart: 21, of which 6 were waited for; matrix products, arithmetic and copies ran while one was open for 4% of the time, Pallas kernels for 53%

profile of v5, /device:TPU:0, one launch (start us, length us, event | category | flops | bytes accessed | tf_op | source)
XLA Modules:
  0.0 213.6 jit_solution(13371456017438006695)
XLA Ops:
  0.7 3.0 %shard_map.256 = (bf16[320,1424]{1,0:T(8,128)(2,1)S(1)}, bf16[192,1024]{1,0:T(8,128)(2,1)}, bf16[448,1744]{1,0:T(8,128)(2,1)}, f32[192,1]{1,0:T(8,128)S(1)}, bf16[640,64]{1,0:T(8,128)(2,1)}) custom-call(bf16[8,8,4,32]{3,2,1,0:T(4,128)(2,1)} %bitcast.117, bf16[1,32]{1,0:T(2,128)(2,1)} %b1.1, bf16[4,4,32,64]{3,2,1,0:T(8,128)(2,1)} %bitcast.115, ...), custom_call_target="tpu_custom_call" | custom-call | flops 1200000000 | tf_op jit(solution)/shard_map/pallas_call | solution.py:117
  3.7 4.8 %collective-permute-start.1 = (bf16[640,64]{1,0:T(8,128)(2,1)}, bf16[640,64]{1,0:T(8,128)(2,1)S(1)}, u32[]{:S(2)}, u32[]{:S(2)}) collective-permute-start(bf16[640,64]{1,0:T(8,128)(2,1)} %get-tuple-element.111), channel_id=1, source_target_pairs={{0,16},{1,17},{2,18},{3,19},{4,20},{5,21},{6,22},{7,23},{8,24},{9,... | collective-permute-start | bytes 245768 | tf_op jit(solution)/shard_map/ppermute | solution.py:958
  8.6 9.1 %shard_map.257 = (bf16[2,640,2560]{2,1,0:T(8,128)(2,1)}, bf16[2,640,2560]{2,1,0:T(8,128)(2,1)}, bf16[4,336,5120]{2,1,0:T(8,128)(2,1)}, bf16[3,2,1120,128]{3,2,1,0:T(8,128)(2,1)}, bf16[4,336,256]{2,1,0:T(8,128)(2,1)}) custom-call(bf16[84,84,4,224]{3,2,1,0:T(4,128)(2,1)} %bitcast.96, bf16[84,84,4,224]{3,2,1,0:T(4,128)(2,1)} %bitcast.97, ...), custom_call_target="tpu_custom_call" | custom-call | flops 24000000 | tf_op jit(solution)/shard_map/pallas_call | solution.py:244
  17.7 2.5 %collective-permute-start.2 = (bf16[3,2,1120,128]{3,2,1,0:T(8,128)(2,1)}, bf16[3,2,1120,128]{3,2,1,0:T(8,128)(2,1)}, u32[]{:S(2)}, u32[]{:S(2)}) collective-permute-start(bf16[3,2,1120,128]{3,2,1,0:T(8,128)(2,1)} %get-tuple-element.117), channel_id=1, source_target_pairs={{0,16},{1,17},{2,18},{3,19},{4,20},{5,21},{6,22},{7,23},{8,24},{9,... | collective-permute-start | bytes 5160968 | tf_op jit(solution)/shard_map/ppermute | solution.py:958
  20.2 16.5 %shard_map.258 = (bf16[2,640,2560]{2,1,0:T(8,128)(2,1)}, bf16[2,640,2560]{2,1,0:T(8,128)(2,1)}, bf16[4,336,5120]{2,1,0:T(8,128)(2,1)}, bf16[3,2,1120,128]{3,2,1,0:T(8,128)(2,1)}) custom-call(bf16[84,84,4,224]{3,2,1,0:T(4,128)(2,1)} %bitcast.99, bf16[84,84,4,224]{3,2,1,0:T(4,128)(2,1)} %bitcast.100, ...), custom_call_target="tpu_custom_call", output_to_operand_aliasing={{0}: (5, {}), {1}: (6, {}), {2}: (7, {})} | custom-call | flops 56000000 | tf_op jit(solution)/shard_map/pallas_call | solution.py:244
  36.7 14.2 %shard_map.259 = (bf16[576,2304]{1,0:T(8,128)(2,1)}, bf16[576,2304]{1,0:T(8,128)(2,1)}, bf16[3136,256]{1,0:T(8,128)(2,1)S(1)}, bf16[3136,256]{1,0:T(8,128)(2,1)}) custom-call(bf16[2,640,2560]{2,1,0:T(8,128)(2,1)} %get-tuple-element.103.r0_ref.r1_ref.a0_ref.a1_ref, bf16[2,640,2560]{2,1,0:T(8,128)(2,1)} %get-tuple-element.103.r0_ref.r1_ref.a0_ref.a1_ref, ...), custom_call_target="tpu_custom_call" | custom-call | flops 5600000000 | tf_op jit(solution)/shard_map/pallas_call | solution.py:303
  51.0 1.4 convolution_bitcast_fusion.1.pd_ref
  52.4 0.3 copy-done.4
  52.7 0.8 shard_map.260
  53.5 1.3 collective-permute-start
  54.9 0.1 pad_add_fusion.flag_ref
  54.9 3.8 %shard_map.261 = (bf16[576,1344]{1,0:T(8,128)(2,1)}, bf16[640,768]{1,0:T(8,128)(2,1)}, bf16[640,768]{1,0:T(8,128)(2,1)}, bf16[224,512]{1,0:T(8,128)(2,1)}) custom-call(s32[4]{0:T(128)S(1)} %pad_add_fusion.flag_ref, bf16[8,8,4,32]{3,2,1,0:T(4,128)(2,1)} %bitcast.118, bf16[4,4,32,64]{3,2,1,0:T(8,128)(2,1)} %bitcast.116, bf16[3,3,64,64]{3,2,1,0:T(8,128)(2,1)} %bitcast.114, ...), custom_call_target="tpu_custom_call" | custom-call | flops 1600000000 | tf_op jit(solution)/shard_map/pallas_call | solution.py:155
  58.8 0.6 collective-permute-done.cho_ref
  59.3 1.0 shard_map.262
  60.4 0.6 fusion.6
  61.0 0.8 copy-done.12
  61.8 5.1 %shard_map.263 = (bf16[8,2,512,128]{3,2,1,0:T(8,128)(2,1)S(1)}, bf16[8,2,512,128]{3,2,1,0:T(8,128)(2,1)}) custom-call(s32[4]{0:T(128)S(1)} %pad_add_fusion.flag_ref, bf16[3136,256]{1,0:T(8,128)(2,1)S(1)} %copy-done.12, bf16[512,256]{1,0:T(8,128)(2,1)S(1)} %get-tuple-element.118.rd_ref, bf16[918,256]{1,0:T(8,128)(2,1)S(1)} %get-tuple-element.114.rh_ref, ...), custom_call_target="tpu_custom_call" | custom-call | flops 3200000000 | tf_op jit(solution)/shard_map/pallas_call | solution.py:662
  66.9 5.2 %collective-permute-start.5 = (bf16[3,2,1120,128]{3,2,1,0:T(8,128)(2,1)}, bf16[3,2,1120,128]{3,2,1,0:T(8,128)(2,1)}, u32[]{:S(2)}, u32[]{:S(2)}) collective-permute-start(bf16[3,2,1120,128]{3,2,1,0:T(8,128)(2,1)} %get-tuple-element.132), channel_id=1, source_target_pairs={{0,16},{1,17},{2,18},{3,19},{4,20},{5,21},{6,22},{7,23},{8,24},{9,... | collective-permute-start | bytes 5160968 | tf_op jit(solution)/shard_map/ppermute | solution.py:958
  72.1 2.1 %add_convert_fusion = bf16[8,2,512,128]{3,2,1,0:T(8,128)(2,1)S(1)} fusion(bf16[8,2,512,128]{3,2,1,0:T(8,128)(2,1)} %collective-permute-done.3, bf16[8,2,512,128]{3,2,1,0:T(8,128)(2,1)S(1)} %get-tuple-element.120), kind=kLoop, calls=%fused_computation | loop fusion | flops 4194304 | bytes 6291456 | tf_op jit(solution)/shard_map/convert_element_type | solution.py:967
  74.2 1.2 dynamic-slice_bitcast_fusion.1
  75.4 1.5 collective-permute-start.4
  76.9 11.8 %shard_map.264 = (bf16[3136,256]{1,0:T(8,128)(2,1)S(1)}, f32[64,256]{1,0:T(8,128)S(1)}, bf16[576,2304]{1,0:T(8,128)(2,1)S(1)}, bf16[6,1008,128]{2,1,0:T(8,128)(2,1)}, f32[64,256]{1,0:T(8,128)S(1)}) custom-call(bf16[3136,512]{1,0:T(8,128)(2,1)} %bitcast.112, bf16[512,256]{1,0:T(8,128)(2,1)S(1)} %get-tuple-element.118.rd_ref, ...), custom_call_target="tpu_custom_call" | custom-call | flops 4800000000 | tf_op jit(solution)/shard_map/pallas_call | solution.py:429
  88.8 4.4 %collective-permute-start.10 = (bf16[6,1008,128]{2,1,0:T(8,128)(2,1)}, bf16[6,1008,128]{2,1,0:T(8,128)(2,1)}, u32[]{:S(2)}, u32[]{:S(2)}) collective-permute-start(bf16[6,1008,128]{2,1,0:T(8,128)(2,1)} %get-tuple-element.143), channel_id=1, source_target_pairs={{0,16},{1,17},{2,18},{3,19},{4,20},{5,21},{6,22},{7,23},{8,24},{9,... | collective-permute-start | bytes 4644872 | tf_op jit(solution)/shard_map/ppermute | solution.py:958
  93.2 7.1 %shard_map.265 = (bf16[2,640,2560]{2,1,0:T(8,128)(2,1)}, bf16[1,2,1120,128]{3,2,1,0:T(8,128)(2,1)}, bf16[3,2,1120,128]{3,2,1,0:T(8,128)(2,1)}, f32[32,256]{1,0:T(8,128)S(1)}) custom-call(bf16[576,2304]{1,0:T(8,128)(2,1)S(1)} %get-tuple-element.133.cur_ref.prev_ref.r_ref, bf16[576,2304]{1,0:T(8,128)(2,1)S(1)} %get-tuple-element.133.cur_ref.prev_ref.r_ref, ...), custom_call_target="tpu_custom_call" | custom-call | flops 2400000000 | tf_op jit(solution)/shard_map/pallas_call | solution.py:517
  100.2 8.8 %collective-permute-done.5.rest_3_ = bf16[3,2,1120,128]{3,2,1,0:T(8,128)(2,1)} collective-permute-done((bf16[3,2,1120,128]{3,2,1,0:T(8,128)(2,1)}, bf16[3,2,1120,128]{3,2,1,0:T(8,128)(2,1)}, u32[]{:S(2)}, u32[]{:S(2)}) %collective-permute-start.5) | collective-permute-done | bytes 1720352 | tf_op jit(solution)/shard_map/ppermute | solution.py:958
  109.0 1.5 add_convert_fusion.1
  110.5 0.1 dynamic-slice_bitcast_fusion.3
  110.6 1.6 collective-permute-start.6
  112.3 7.1 %shard_map.266 = (bf16[2,640,2560]{2,1,0:T(8,128)(2,1)}, f32[32,256]{1,0:T(8,128)S(1)}) custom-call(bf16[576,2304]{1,0:T(8,128)(2,1)S(1)} %get-tuple-element.133.cur_ref.prev_ref.r_ref, bf16[576,2304]{1,0:T(8,128)(2,1)S(1)} %get-tuple-element.133.cur_ref.prev_ref.r_ref, bf16[640,768]{1,0:T(8,128)(2,1)} %get-tuple-element.126.t_ref, ...), custom_call_target="tpu_custom_call", output_to_operand_aliasing={{0}: (4, {})} | custom-call | flops 3600000000 | tf_op jit(solution)/shard_map/pallas_call | solution.py:517
  119.4 4.6 %shard_map.267.refs_6_ = f32[64,576]{1,0:T(8,128)S(1)} custom-call(bf16[576,2304]{1,0:T(8,128)(2,1)S(1)} %copy-done, bf16[576,2304]{1,0:T(8,128)(2,1)S(1)} %copy-done, bf16[576,2304]{1,0:T(8,128)(2,1)S(1)} %copy-done, bf16[576,2304]{1,0:T(8,128)(2,1)S(1)} %copy-done, bf16[7,448,256]{2,1,0:T(8,128)(2,1)S(1)} %bitcast.86), custom_call_target="tpu_custom_call" | custom-call | flops 2800000000 | tf_op jit(solution)/shard_map/pallas_call | solution.py:704
  124.1 0.1 add_convert_fusion.2
  124.3 2.7 %collective-permute-start.7 = (bf16[1,2,512,128]{3,2,1,0:T(8,128)(2,1)S(1)}, bf16[1,2,512,128]{3,2,1,0:T(8,128)(2,1)S(1)}, u32[]{:S(2)}, u32[]{:S(2)}) collective-permute-start(bf16[1,2,512,128]{3,2,1,0:T(8,128)(2,1)S(1)} %get-tuple-element.181), channel_id=1, source_target_pairs={{0,8},{1,9},{2,10},{3,11},{4,12},{5,13},{6,14},{7,15},{8,0},{9,1},... | collective-permute-start | bytes 786440 | tf_op jit(solution)/shard_map/ppermute | solution.py:963
  126.9 12.5 %shard_map.268.refs_4_ = f32[256,32]{1,0:T(8,128)S(1)} custom-call(bf16[4,336,5120]{2,1,0:T(8,128)(2,1)} %get-tuple-element.138.x_ref, bf16[4,336,256]{2,1,0:T(8,128)(2,1)} %get-tuple-element.139.x0_ref, bf16[2,640,2560]{2,1,0:T(8,128)(2,1)} %get-tuple-element.170.r_ref.own_ref.before_ref), custom_call_target="tpu_custom_call" | custom-call | flops 5200000000 | tf_op jit(solution)/shard_map/pallas_call | solution.py:797
  139.5 0.1 add_convert_fusion.3
  139.6 4.4 %collective-permute-start.8 = (bf16[512,128]{1,0:T(8,128)(2,1)S(1)}, bf16[512,128]{1,0:T(8,128)(2,1)S(1)}, u32[]{:S(2)}, u32[]{:S(2)}) collective-permute-start(bf16[512,128]{1,0:T(8,128)(2,1)S(1)} %slice_bitcast_fusion), channel_id=1, source_target_pairs={{0,16},{1,17},{2,18},{3,19},{4,20},{5,21},{6,22},{7,23},{8,24},{9,... | collective-permute-start | bytes 393224 | tf_op jit(solution)/shard_map/ppermute | solution.py:958
  144.0 1.3 collective-permute-start.12
  145.3 2.5 %collective-permute-done.8 = bf16[512,128]{1,0:T(8,128)(2,1)S(1)} collective-permute-done((bf16[512,128]{1,0:T(8,128)(2,1)S(1)}, bf16[512,128]{1,0:T(8,128)(2,1)S(1)}, u32[]{:S(2)}, u32[]{:S(2)}) %collective-permute-start.8) | collective-permute-done | bytes 131104 | tf_op jit(solution)/shard_map/ppermute | solution.py:958
  147.8 0.5 collective-permute-start.9
  148.3 7.9 %shard_map.269.refs_5_ = f32[512,64]{1,0:T(8,128)S(1)} custom-call(bf16[2,640,2560]{2,1,0:T(8,128)(2,1)} %get-tuple-element.103.r0_ref.r1_ref.a0_ref.a1_ref, bf16[2,640,2560]{2,1,0:T(8,128)(2,1)} %get-tuple-element.103.r0_ref.r1_ref.a0_ref.a1_ref, bf16[576,2304]{1,0:T(8,128)(2,1)S(1)} %get-tuple-element.133.cur_ref.prev_ref.r_ref), custom_call_target="tpu_custom_call" | custom-call | flops 3600000000 | tf_op jit(solution)/shard_map/pallas_call | solution.py:740
  156.3 0.1 copy.40.refs_7_
  156.5 1.0 shard_map.270
  157.5 0.1 collective-permute-start.11
  157.6 0.3 copy-done.15
  157.9 4.7 %collective-permute-start.15 = (bf16[3,2,1120,128]{3,2,1,0:T(8,128)(2,1)S(1)}, bf16[3,2,1120,128]{3,2,1,0:T(8,128)(2,1)S(1)}, u32[]{:S(2)}, u32[]{:S(2)}) collective-permute-start(bf16[3,2,1120,128]{3,2,1,0:T(8,128)(2,1)S(1)} %copy-done.15), channel_id=1, source_target_pairs={{0,16},{1,17},{2,18},{3,19},{4,20},{5,21},{6,22},{7,23},{8,24},{9,... | collective-permute-start | bytes 5160968 | tf_op jit(solution)/shard_map/ppermute | solution.py:958
  162.7 1.8 collective-permute-start.18
  164.5 0.1 add_convert_fusion.7
  164.5 1.6 collective-permute-start.13
  166.1 9.3 %shard_map.271 = (bf16[84,84,2,224]{3,2,1,0:T(2,128)(2,1)}, bf16[640,256]{1,0:T(8,128)(2,1)S(1)}) custom-call(s32[4]{0:T(128)S(1)} %pad_add_fusion.flag_ref, bf16[2,640,2560]{2,1,0:T(8,128)(2,1)} %get-tuple-element.170.r_ref.own_ref.before_ref, bf16[2,640,2560]{2,1,0:T(8,128)(2,1)} %get-tuple-element.170.r_ref.own_ref.before_ref, ...), custom_call_target="tpu_custom_call" | custom-call | flops 3600000000 | tf_op jit(solution)/shard_map/pallas_call | solution.py:629
  175.4 0.1 add_convert_fusion.6
  175.5 0.3 collective-permute-start.14
  175.8 0.1 pad_maximum_fusion.1
  175.9 0.6 collective-permute-start.19
  176.5 5.2 %collective-permute-done.14 = bf16[768,128]{1,0:T(8,128)(2,1)S(1)} collective-permute-done((bf16[768,128]{1,0:T(8,128)(2,1)S(1)}, bf16[768,128]{1,0:T(8,128)(2,1)S(1)}, u32[]{:S(2)}, u32[]{:S(2)}) %collective-permute-start.14) | collective-permute-done | bytes 196640 | tf_op jit(solution)/shard_map/ppermute | solution.py:963
  181.7 0.1 add_convert_fusion.5
  181.7 2.3 %collective-permute-start.16 = (bf16[768,128]{1,0:T(8,128)(2,1)S(1)}, bf16[768,128]{1,0:T(8,128)(2,1)S(1)}, u32[]{:S(2)}, u32[]{:S(2)}) collective-permute-start(bf16[768,128]{1,0:T(8,128)(2,1)S(1)} %add_convert_fusion.5), channel_id=1, source_target_pairs={{0,8},{1,9},{2,10},{3,11},{4,12},{5,13},{6,14},{7,15},{8,0},{9,1},... | collective-permute-start | bytes 589832 | tf_op jit(solution)/shard_map/ppermute | solution.py:963
  184.0 7.9 %collective-permute-done.16 = bf16[768,128]{1,0:T(8,128)(2,1)S(1)} collective-permute-done((bf16[768,128]{1,0:T(8,128)(2,1)S(1)}, bf16[768,128]{1,0:T(8,128)(2,1)S(1)}, u32[]{:S(2)}, u32[]{:S(2)}) %collective-permute-start.16) | collective-permute-done | bytes 196640 | tf_op jit(solution)/shard_map/ppermute | solution.py:963
  191.9 0.1 pad_maximum_fusion
  192.0 0.1 collective-permute-start.20
  192.1 7.3 %collective-permute-done.15.rest_1_ = bf16[3,2,1120,128]{3,2,1,0:T(8,128)(2,1)S(1)} collective-permute-done((bf16[3,2,1120,128]{3,2,1,0:T(8,128)(2,1)S(1)}, bf16[3,2,1120,128]{3,2,1,0:T(8,128)(2,1)S(1)}, u32[]{:S(2)}, u32[]{:S(2)}) %collective-permute-start.15) | collective-permute-done | bytes 1720352 | tf_op jit(solution)/shard_map/ppermute | solution.py:958
  199.4 0.1 add_convert_fusion.4.own_ref
  199.5 4.4 %collective-permute-start.17 = (bf16[768,128]{1,0:T(8,128)(2,1)S(1)}, bf16[768,128]{1,0:T(8,128)(2,1)S(1)}, u32[]{:S(2)}, u32[]{:S(2)}) collective-permute-start(bf16[768,128]{1,0:T(8,128)(2,1)S(1)} %add_convert_fusion.4.own_ref), channel_id=1, source_target_pairs={{0,16},{1,17},{2,18},{3,19},{4,20},{5,21},{6,22},{7,23},{8,24},{9,... | collective-permute-start | bytes 589832 | tf_op jit(solution)/shard_map/ppermute | solution.py:958
  203.9 5.3 %shard_map.274 = (bf16[84,84,2,224]{3,2,1,0:T(2,128)(2,1)}, bf16[640,256]{1,0:T(8,128)(2,1)}) custom-call(s32[4]{0:T(128)S(1)} %pad_add_fusion.flag_ref, bf16[2,640,2560]{2,1,0:T(8,128)(2,1)} %get-tuple-element.170.r_ref.own_ref.before_ref, bf16[2,640,2560]{2,1,0:T(8,128)(2,1)} %get-tuple-element.170.r_ref.own_ref.before_ref, ...), custom_call_target="tpu_custom_call", output_to_operand_aliasing={{0}: (7, {})} | custom-call | flops 2400000000 | tf_op jit(solution)/shard_map/pallas_call | solution.py:629
  209.2 1.5 shard_map.272
  210.7 3.0 %shard_map.273 = (f32[3136,256]{1,0:T(8,128)}, f32[918,256]{1,0:T(8,128)}) custom-call(s32[4]{0:T(128)S(1)} %pad_add_fusion.flag_ref, bf16[8,512,128]{2,1,0:T(8,128)(2,1)S(1)} %bitcast.88, bf16[8,512,128]{2,1,0:T(8,128)(2,1)S(1)} %collective-permute-done.20.other_ref), custom_call_target="tpu_custom_call" | custom-call | flops 1600000000 | tf_op jit(solution)/shard_map/pallas_call | solution.py:943
  (52 shorter events, 0.2 us)
Async XLA Ops:
  0.6 7.9 %copy-start.2 = (bf16[16,256]{1,0:T(8,128)(2,1)S(1)}, bf16[16,256]{1,0:T(8,128)(2,1)}, u32[]{:S(2)}) copy-start(bf16[16,256]{1,0:T(8,128)(2,1)} %constant.120.clone.1.ones_ref) | copy-start | bytes 24580
  3.7 14.0 %collective-permute-start.1 = (bf16[640,64]{1,0:T(8,128)(2,1)}, bf16[640,64]{1,0:T(8,128)(2,1)S(1)}, u32[]{:S(2)}, u32[]{:S(2)}) collective-permute-start(bf16[640,64]{1,0:T(8,128)(2,1)} %get-tuple-element.111), channel_id=1, source_target_pairs={{0,16},{1,17},{2,18},{3,19},{4,20},{5,21},{6,22},{7,23},{8,24},{9,... | collective-permute-start | bytes 245768 | tf_op jit(solution)/shard_map/ppermute | solution.py:958
  8.5 11.7 %copy-start.3 = (s32[224]{0:T(256)S(1)}, s32[224]{0:T(256)}, u32[]{:S(2)}) copy-start(s32[224]{0:T(256)} %param.30) | copy-start | bytes 2692
  8.6 11.7 %copy-start.13 = (s32[224]{0:T(256)S(1)}, s32[224]{0:T(256)}, u32[]{:S(2)}) copy-start(s32[224]{0:T(256)} %param.31) | copy-start | bytes 2692
  17.7 19.1 %copy-start.16 = (bf16[640,64]{1,0:T(8,128)(2,1)}, bf16[640,64]{1,0:T(8,128)(2,1)S(1)}, u32[]{:S(2)}) copy-start(bf16[640,64]{1,0:T(8,128)(2,1)S(1)} %collective-permute-done.1.got) | copy-start | bytes 245764
  17.7 43.3 %collective-permute-start.2 = (bf16[3,2,1120,128]{3,2,1,0:T(8,128)(2,1)}, bf16[3,2,1120,128]{3,2,1,0:T(8,128)(2,1)}, u32[]{:S(2)}, u32[]{:S(2)}) collective-permute-start(bf16[3,2,1120,128]{3,2,1,0:T(8,128)(2,1)} %get-tuple-element.117), channel_id=1, source_target_pairs={{0,16},{1,17},{2,18},{3,19},{4,20},{5,21},{6,22},{7,23},{8,24},{9,... | collective-permute-start | bytes 5160968 | tf_op jit(solution)/shard_map/ppermute | solution.py:958
  36.7 14.2 %copy-start.14 = (bf16[1,3136,512]{2,1,0:T(8,128)(2,1)S(1)}, bf16[1,3136,512]{2,1,0:T(8,128)(2,1)}, u32[]{:S(2)}) copy-start(bf16[1,3136,512]{2,1,0:T(8,128)(2,1)} %param.26) | copy-start | bytes 9633796
  50.9 1.5 copy-start.11
  51.0 1.8 copy-start.4
  51.0 1.8 copy-start.7
  51.0 1.8 copy-start.8
  53.5 5.8 %collective-permute-start = (bf16[51,224]{1,0:T(8,128)(2,1)S(1)}, bf16[51,224]{1,0:T(8,128)(2,1)S(1)}, u32[]{:S(2)}, u32[]{:S(2)}) collective-permute-start(bf16[51,224]{1,0:T(8,128)(2,1)S(1)} %get-tuple-element.108), channel_id=1, source_target_pairs={{16,0},{17,1},{18,2},{19,3},{20,4},{21,5},{22,6},{23,7},{24,8},{25... | collective-permute-start | bytes 68552 | tf_op jit(solution)/shard_map/ppermute | solution.py:1043
  54.9 4.4 %copy-start.5 = (s32[224,51]{0,1:T(8,128)S(1)}, s32[224,51]{0,1:T(8,128)}, u32[]{:S(2)}) copy-start(s32[224,51]{0,1:T(8,128)} %param.33) | copy-start | bytes 137092
  54.9 4.4 %copy-start.6 = (f32[224,51]{0,1:T(8,128)S(1)}, f32[224,51]{0,1:T(8,128)}, u32[]{:S(2)}) copy-start(f32[224,51]{0,1:T(8,128)} %param.34) | copy-start | bytes 137092
  54.9 4.4 %copy-start.9 = (s32[224]{0:T(256)S(1)}, s32[224]{0:T(256)}, u32[]{:S(2)}) copy-start(s32[224]{0:T(256)} %param.32) | copy-start | bytes 2692
  60.4 1.4 copy-start.12
  66.9 5.2 %collective-permute-start.3 = (bf16[8,2,512,128]{3,2,1,0:T(8,128)(2,1)}, bf16[8,2,512,128]{3,2,1,0:T(8,128)(2,1)}, u32[]{:S(2)}, u32[]{:S(2)}) collective-permute-start(bf16[8,2,512,128]{3,2,1,0:T(8,128)(2,1)} %get-tuple-element.121), channel_id=1, source_target_pairs={{0,1},{1,0},{2,3},{3,2},{4,5},{5,4},{6,7},{7,6},{8,9},{9,8},{10,11... | collective-permute-start | bytes 6291464 | tf_op jit(solution)/shard_map/ppermute | solution.py:963
  66.9 42.2 %collective-permute-start.5 = (bf16[3,2,1120,128]{3,2,1,0:T(8,128)(2,1)}, bf16[3,2,1120,128]{3,2,1,0:T(8,128)(2,1)}, u32[]{:S(2)}, u32[]{:S(2)}) collective-permute-start(bf16[3,2,1120,128]{3,2,1,0:T(8,128)(2,1)} %get-tuple-element.132), channel_id=1, source_target_pairs={{0,16},{1,17},{2,18},{3,19},{4,20},{5,21},{6,22},{7,23},{8,24},{9,... | collective-permute-start | bytes 5160968 | tf_op jit(solution)/shard_map/ppermute | solution.py:958
  75.4 33.6 %collective-permute-start.4 = (bf16[4,2,512,128]{3,2,1,0:T(8,128)(2,1)}, bf16[4,2,512,128]{3,2,1,0:T(8,128)(2,1)}, u32[]{:S(2)}, u32[]{:S(2)}) collective-permute-start(bf16[4,2,512,128]{3,2,1,0:T(8,128)(2,1)} %get-tuple-element.175), channel_id=1, source_target_pairs={{0,2},{1,3},{2,0},{3,1},{4,6},{5,7},{6,4},{7,5},{8,10},{9,11},{10,... | collective-permute-start | bytes 3145736 | tf_op jit(solution)/shard_map/ppermute | solution.py:963
  88.8 67.7 %collective-permute-start.10 = (bf16[6,1008,128]{2,1,0:T(8,128)(2,1)}, bf16[6,1008,128]{2,1,0:T(8,128)(2,1)}, u32[]{:S(2)}, u32[]{:S(2)}) collective-permute-start(bf16[6,1008,128]{2,1,0:T(8,128)(2,1)} %get-tuple-element.143), channel_id=1, source_target_pairs={{0,16},{1,17},{2,18},{3,19},{4,20},{5,21},{6,22},{7,23},{8,24},{9,... | collective-permute-start | bytes 4644872 | tf_op jit(solution)/shard_map/ppermute | solution.py:958
  110.6 13.4 %collective-permute-start.6 = (bf16[2,2,512,128]{3,2,1,0:T(8,128)(2,1)S(1)}, bf16[2,2,512,128]{3,2,1,0:T(8,128)(2,1)S(1)}, u32[]{:S(2)}, u32[]{:S(2)}) collective-permute-start(bf16[2,2,512,128]{3,2,1,0:T(8,128)(2,1)S(1)} %get-tuple-element.177), channel_id=1, source_target_pairs={{0,4},{1,5},{2,6},{3,7},{4,0},{5,1},{6,2},{7,3},{8,12},{9,13},{10,... | collective-permute-start | bytes 1572872 | tf_op jit(solution)/shard_map/ppermute | solution.py:963
  112.3 7.1 %copy-start = (bf16[576,2304]{1,0:T(8,128)(2,1)S(1)}, bf16[576,2304]{1,0:T(8,128)(2,1)}, u32[]{:S(2)}) copy-start(bf16[576,2304]{1,0:T(8,128)(2,1)} %get-tuple-element.130.refs_0_.refs_1_.refs_2_.refs_3_) | copy-start | bytes 7962628
  124.3 15.2 %collective-permute-start.7 = (bf16[1,2,512,128]{3,2,1,0:T(8,128)(2,1)S(1)}, bf16[1,2,512,128]{3,2,1,0:T(8,128)(2,1)S(1)}, u32[]{:S(2)}, u32[]{:S(2)}) collective-permute-start(bf16[1,2,512,128]{3,2,1,0:T(8,128)(2,1)S(1)} %get-tuple-element.181), channel_id=1, source_target_pairs={{0,8},{1,9},{2,10},{3,11},{4,12},{5,13},{6,14},{7,15},{8,0},{9,1},... | collective-permute-start | bytes 786440 | tf_op jit(solution)/shard_map/ppermute | solution.py:963
  139.6 8.2 %collective-permute-start.8 = (bf16[512,128]{1,0:T(8,128)(2,1)S(1)}, bf16[512,128]{1,0:T(8,128)(2,1)S(1)}, u32[]{:S(2)}, u32[]{:S(2)}) collective-permute-start(bf16[512,128]{1,0:T(8,128)(2,1)S(1)} %slice_bitcast_fusion), channel_id=1, source_target_pairs={{0,16},{1,17},{2,18},{3,19},{4,20},{5,21},{6,22},{7,23},{8,24},{9,... | collective-permute-start | bytes 393224 | tf_op jit(solution)/shard_map/ppermute | solution.py:958
  144.0 22.2 %collective-permute-start.12 = (bf16[1,2,1120,128]{3,2,1,0:T(8,128)(2,1)}, bf16[1,2,1120,128]{3,2,1,0:T(8,128)(2,1)S(1)}, u32[]{:S(2)}, u32[]{:S(2)}) collective-permute-start(bf16[1,2,1120,128]{3,2,1,0:T(8,128)(2,1)} %get-tuple-element.150), channel_id=1, source_target_pairs={{0,16},{1,17},{2,18},{3,19},{4,20},{5,21},{6,22},{7,23},{8,24},{9,... | collective-permute-start | bytes 1720328 | tf_op jit(solution)/shard_map/ppermute | solution.py:958
  147.8 8.7 %copy-start.10 = (s32[224,1]{0,1:T(1,128)S(1)}, s32[224,1]{0,1:T(1,128)}, u32[]{:S(2)}) copy-start(s32[224,1]{0,1:T(1,128)} %param.35) | copy-start | bytes 2692
  147.8 8.6 %collective-permute-start.9 = (bf16[1,512,128]{2,1,0:T(8,128)(2,1)S(1)}, bf16[1,512,128]{2,1,0:T(8,128)(2,1)S(1)}, u32[]{:S(2)}, u32[]{:S(2)}) collective-permute-start(bf16[1,512,128]{2,1,0:T(8,128)(2,1)S(1)} %get-tuple-element.183), channel_id=1, source_target_pairs={{0,8},{1,9},{2,10},{3,11},{4,12},{5,13},{6,14},{7,15},{8,0},{9,1},... | collective-permute-start | bytes 393224 | tf_op jit(solution)/shard_map/ppermute | solution.py:963
  156.5 1.5 copy-start.15
  156.5 9.7 %copy-start.1 = (bf16[224,512]{1,0:T(8,128)(2,1)S(1)}, bf16[224,512]{1,0:T(8,128)(2,1)}, u32[]{:S(2)}) copy-start(bf16[224,512]{1,0:T(8,128)(2,1)} %get-tuple-element.112.rest_5_.rest_2_) | copy-start | bytes 688132
  157.5 7.0 %collective-permute-start.11 = (bf16[768,128]{1,0:T(8,128)(2,1)S(1)}, bf16[768,128]{1,0:T(8,128)(2,1)S(1)}, u32[]{:S(2)}, u32[]{:S(2)}) collective-permute-start(bf16[768,128]{1,0:T(8,128)(2,1)S(1)} %shard_map.270), channel_id=1, source_target_pairs={{0,1},{1,0},{2,3},{3,2},{4,5},{5,4},{6,7},{7,6},{8,9},{9,8},{10,11... | collective-permute-start | bytes 589832 | tf_op jit(solution)/shard_map/ppermute | solution.py:963
  157.9 41.5 %collective-permute-start.15 = (bf16[3,2,1120,128]{3,2,1,0:T(8,128)(2,1)S(1)}, bf16[3,2,1120,128]{3,2,1,0:T(8,128)(2,1)S(1)}, u32[]{:S(2)}, u32[]{:S(2)}) collective-permute-start(bf16[3,2,1120,128]{3,2,1,0:T(8,128)(2,1)S(1)} %copy-done.15), channel_id=1, source_target_pairs={{0,16},{1,17},{2,18},{3,19},{4,20},{5,21},{6,22},{7,23},{8,24},{9,... | collective-permute-start | bytes 5160968 | tf_op jit(solution)/shard_map/ppermute | solution.py:958
  162.7 13.2 %collective-permute-start.18 = (bf16[2,512,128]{2,1,0:T(8,128)(2,1)S(1)}, bf16[2,512,128]{2,1,0:T(8,128)(2,1)S(1)}, u32[]{:S(2)}, u32[]{:S(2)}) collective-permute-start(bf16[2,512,128]{2,1,0:T(8,128)(2,1)S(1)} %maximum_bitcast_fusion), channel_id=1, source_target_pairs={{0,4},{1,5},{2,6},{3,7},{4,0},{5,1},{6,2},{7,3},{8,12},{9,13},{10,... | collective-permute-start | bytes 786440 | tf_op jit(solution)/shard_map/ppermute | solution.py:963
  164.5 10.9 %collective-permute-start.13 = (bf16[768,128]{1,0:T(8,128)(2,1)S(1)}, bf16[768,128]{1,0:T(8,128)(2,1)S(1)}, u32[]{:S(2)}, u32[]{:S(2)}) collective-permute-start(bf16[768,128]{1,0:T(8,128)(2,1)S(1)} %add_convert_fusion.7), channel_id=1, source_target_pairs={{0,2},{1,3},{2,0},{3,1},{4,6},{5,7},{6,4},{7,5},{8,10},{9,11},{10,... | collective-permute-start | bytes 589832 | tf_op jit(solution)/shard_map/ppermute | solution.py:963
  175.5 6.2 %collective-permute-start.14 = (bf16[768,128]{1,0:T(8,128)(2,1)S(1)}, bf16[768,128]{1,0:T(8,128)(2,1)S(1)}, u32[]{:S(2)}, u32[]{:S(2)}) collective-permute-start(bf16[768,128]{1,0:T(8,128)(2,1)S(1)} %add_convert_fusion.6), channel_id=1, source_target_pairs={{0,4},{1,5},{2,6},{3,7},{4,0},{5,1},{6,2},{7,3},{8,12},{9,13},{10,... | collective-permute-start | bytes 589832 | tf_op jit(solution)/shard_map/ppermute | solution.py:963
  175.9 16.0 %collective-permute-start.19 = (bf16[4,512,128]{2,1,0:T(8,128)(2,1)S(1)}, bf16[4,512,128]{2,1,0:T(8,128)(2,1)S(1)}, u32[]{:S(2)}, u32[]{:S(2)}) collective-permute-start(bf16[4,512,128]{2,1,0:T(8,128)(2,1)S(1)} %bitcast.105), channel_id=1, source_target_pairs={{0,2},{1,3},{2,0},{3,1},{4,6},{5,7},{6,4},{7,5},{8,10},{9,11},{10,... | collective-permute-start | bytes 1572872 | tf_op jit(solution)/shard_map/ppermute | solution.py:963
  181.7 10.2 %collective-permute-start.16 = (bf16[768,128]{1,0:T(8,128)(2,1)S(1)}, bf16[768,128]{1,0:T(8,128)(2,1)S(1)}, u32[]{:S(2)}, u32[]{:S(2)}) collective-permute-start(bf16[768,128]{1,0:T(8,128)(2,1)S(1)} %add_convert_fusion.5), channel_id=1, source_target_pairs={{0,8},{1,9},{2,10},{3,11},{4,12},{5,13},{6,14},{7,15},{8,0},{9,1},... | collective-permute-start | bytes 589832 | tf_op jit(solution)/shard_map/ppermute | solution.py:963
  192.0 18.7 %collective-permute-start.20 = (bf16[8,512,128]{2,1,0:T(8,128)(2,1)S(1)}, bf16[8,512,128]{2,1,0:T(8,128)(2,1)S(1)}, u32[]{:S(2)}, u32[]{:S(2)}) collective-permute-start(bf16[8,512,128]{2,1,0:T(8,128)(2,1)S(1)} %bitcast.87), channel_id=1, source_target_pairs={{0,1},{1,0},{2,3},{3,2},{4,5},{5,4},{6,7},{7,6},{8,9},{9,8},{10,11... | collective-permute-start | bytes 3145736 | tf_op jit(solution)/shard_map/ppermute | solution.py:963
  199.5 9.7 %collective-permute-start.17 = (bf16[768,128]{1,0:T(8,128)(2,1)S(1)}, bf16[768,128]{1,0:T(8,128)(2,1)S(1)}, u32[]{:S(2)}, u32[]{:S(2)}) collective-permute-start(bf16[768,128]{1,0:T(8,128)(2,1)S(1)} %add_convert_fusion.4.own_ref), channel_id=1, source_target_pairs={{0,16},{1,17},{2,18},{3,19},{4,20},{5,21},{6,22},{7,23},{8,24},{9,... | collective-permute-start | bytes 589832 | tf_op jit(solution)/shard_map/ppermute | solution.py:958

commit v6 on v5

--- a/solution.py
+++ b/solution.py
@@ -806,7 +806,7 @@
         us=13,
         grid=(5,),
         scratch=[pltpu.VMEM((640, 128), F32), pltpu.VMEM((4, 336, LANES), BF)],
-    )(hbm(xt), hbm(x0), hbm(r1))
+    )(hbm(xt), x0, hbm(r1))
 
 
 SMALL_ROWS = 704

time: 215 us -> 215 us (level)
  no operation moved by 1% of the time
where the time goes in v6:
time: 215 us; the launch traced here: 214 us
  Pallas kernels  125 us (58%)
  starting transfers between devices  46.6 us (22%)
  waiting for transfers between devices  32.5 us (15%)
  other arithmetic  4.36 us (2%)
  local copies, waits for them, and re-layouts  2.96 us (1%)
    ppermute x8, starting transfers between devices, hand(): return lax.ppermute(value, 'pair', [(0, 1)])  31.9 us
    pallas_call x2, Pallas kernels, conv1(): pl.pallas_call(functools.partial(conv1_kernel, rows, start, packs), out_s...  25.6 us
    ppermute x8, waiting for transfers between devices, hand(): return lax.ppermute(value, 'pair', [(0, 1)])  18.9 us
    pallas_call x2, Pallas kernels, dframes(): pl.pallas_call(functools.partial(dframes_kernel, rows, first, last, far),...  14.5 us
    pallas_call x2, Pallas kernels, dconv2(): pl.pallas_call(functools.partial(dconv2_kernel, first, packs), out_shape=...  14.2 us
    pallas_call x1, Pallas kernels, conv23(): call(conv23_kernel, (pltpu.HBM((576, 9 * LANES), BF), pltpu.HBM((576, 9 *...  14.2 us
    ppermute x12, starting transfers between devices, swap(): return lax.ppermute(value, 'batch', [(i, i ^ bit) for i in range(devices)])  13.4 us
    ppermute x12, waiting for transfers between devices, swap(): return lax.ppermute(value, 'batch', [(i, i ^ bit) for i in range(devices)])  13.1 us
  transfers between devices with their start and end apart: 21, of which 6 were waited for; matrix products, arithmetic and copies ran while one was open for 4% of the time, Pallas kernels for 53%

profile of v6, /device:TPU:0, one launch (start us, length us, event | category | flops | bytes accessed | tf_op | source)
XLA Modules:
  0.0 214.0 jit_solution(11115088512518035977)
XLA Ops:
  0.7 3.0 %shard_map.256 = (bf16[320,1424]{1,0:T(8,128)(2,1)S(1)}, bf16[192,1024]{1,0:T(8,128)(2,1)}, bf16[448,1744]{1,0:T(8,128)(2,1)}, f32[192,1]{1,0:T(8,128)S(1)}, bf16[640,64]{1,0:T(8,128)(2,1)}) custom-call(bf16[8,8,4,32]{3,2,1,0:T(4,128)(2,1)} %bitcast.117, bf16[1,32]{1,0:T(2,128)(2,1)} %b1.1, bf16[4,4,32,64]{3,2,1,0:T(8,128)(2,1)} %bitcast.115, ...), custom_call_target="tpu_custom_call" | custom-call | flops 1200000000 | tf_op jit(solution)/shard_map/pallas_call | solution.py:117
  3.7 4.8 %collective-permute-start.1 = (bf16[640,64]{1,0:T(8,128)(2,1)}, bf16[640,64]{1,0:T(8,128)(2,1)S(1)}, u32[]{:S(2)}, u32[]{:S(2)}) collective-permute-start(bf16[640,64]{1,0:T(8,128)(2,1)} %get-tuple-element.111), channel_id=1, source_target_pairs={{0,16},{1,17},{2,18},{3,19},{4,20},{5,21},{6,22},{7,23},{8,24},{9,... | collective-permute-start | bytes 245768 | tf_op jit(solution)/shard_map/ppermute | solution.py:958
  8.6 9.1 %shard_map.257 = (bf16[2,640,2560]{2,1,0:T(8,128)(2,1)}, bf16[2,640,2560]{2,1,0:T(8,128)(2,1)}, bf16[4,336,5120]{2,1,0:T(8,128)(2,1)}, bf16[3,2,1120,128]{3,2,1,0:T(8,128)(2,1)}, bf16[4,336,256]{2,1,0:T(8,128)(2,1)}) custom-call(bf16[84,84,4,224]{3,2,1,0:T(4,128)(2,1)} %bitcast.96, bf16[84,84,4,224]{3,2,1,0:T(4,128)(2,1)} %bitcast.97, ...), custom_call_target="tpu_custom_call" | custom-call | flops 24000000 | tf_op jit(solution)/shard_map/pallas_call | solution.py:244
  17.7 2.5 %collective-permute-start.2 = (bf16[3,2,1120,128]{3,2,1,0:T(8,128)(2,1)}, bf16[3,2,1120,128]{3,2,1,0:T(8,128)(2,1)}, u32[]{:S(2)}, u32[]{:S(2)}) collective-permute-start(bf16[3,2,1120,128]{3,2,1,0:T(8,128)(2,1)} %get-tuple-element.117), channel_id=1, source_target_pairs={{0,16},{1,17},{2,18},{3,19},{4,20},{5,21},{6,22},{7,23},{8,24},{9,... | collective-permute-start | bytes 5160968 | tf_op jit(solution)/shard_map/ppermute | solution.py:958
  20.2 16.5 %shard_map.258 = (bf16[2,640,2560]{2,1,0:T(8,128)(2,1)}, bf16[2,640,2560]{2,1,0:T(8,128)(2,1)}, bf16[4,336,5120]{2,1,0:T(8,128)(2,1)}, bf16[3,2,1120,128]{3,2,1,0:T(8,128)(2,1)}) custom-call(bf16[84,84,4,224]{3,2,1,0:T(4,128)(2,1)} %bitcast.99, bf16[84,84,4,224]{3,2,1,0:T(4,128)(2,1)} %bitcast.100, ...), custom_call_target="tpu_custom_call", output_to_operand_aliasing={{0}: (5, {}), {1}: (6, {}), {2}: (7, {})} | custom-call | flops 56000000 | tf_op jit(solution)/shard_map/pallas_call | solution.py:244
  36.7 14.2 %shard_map.259 = (bf16[576,2304]{1,0:T(8,128)(2,1)}, bf16[576,2304]{1,0:T(8,128)(2,1)}, bf16[3136,256]{1,0:T(8,128)(2,1)S(1)}, bf16[3136,256]{1,0:T(8,128)(2,1)}) custom-call(bf16[2,640,2560]{2,1,0:T(8,128)(2,1)} %get-tuple-element.103.r0_ref.r1_ref.a0_ref.a1_ref, bf16[2,640,2560]{2,1,0:T(8,128)(2,1)} %get-tuple-element.103.r0_ref.r1_ref.a0_ref.a1_ref, ...), custom_call_target="tpu_custom_call" | custom-call | flops 5600000000 | tf_op jit(solution)/shard_map/pallas_call | solution.py:303
  51.0 1.4 convolution_bitcast_fusion.1.pd_ref
  52.4 0.3 copy-done.5
  52.7 0.8 shard_map.260
  53.5 1.3 collective-permute-start
  54.8 0.1 pad_add_fusion.flag_ref
  54.9 3.8 %shard_map.261 = (bf16[576,1344]{1,0:T(8,128)(2,1)}, bf16[640,768]{1,0:T(8,128)(2,1)}, bf16[640,768]{1,0:T(8,128)(2,1)}, bf16[224,512]{1,0:T(8,128)(2,1)}) custom-call(s32[4]{0:T(128)S(1)} %pad_add_fusion.flag_ref, bf16[8,8,4,32]{3,2,1,0:T(4,128)(2,1)} %bitcast.118, bf16[4,4,32,64]{3,2,1,0:T(8,128)(2,1)} %bitcast.116, bf16[3,3,64,64]{3,2,1,0:T(8,128)(2,1)} %bitcast.114, ...), custom_call_target="tpu_custom_call" | custom-call | flops 1600000000 | tf_op jit(solution)/shard_map/pallas_call | solution.py:155
  58.8 0.5 collective-permute-done.cho_ref
  59.3 1.0 shard_map.262
  60.3 0.6 fusion.6
  61.0 0.8 copy-done.13
  61.8 5.1 %shard_map.263 = (bf16[8,2,512,128]{3,2,1,0:T(8,128)(2,1)S(1)}, bf16[8,2,512,128]{3,2,1,0:T(8,128)(2,1)}) custom-call(s32[4]{0:T(128)S(1)} %pad_add_fusion.flag_ref, bf16[3136,256]{1,0:T(8,128)(2,1)S(1)} %copy-done.13, bf16[512,256]{1,0:T(8,128)(2,1)S(1)} %get-tuple-element.118.rd_ref, bf16[918,256]{1,0:T(8,128)(2,1)S(1)} %get-tuple-element.114.rh_ref, ...), custom_call_target="tpu_custom_call" | custom-call | flops 3200000000 | tf_op jit(solution)/shard_map/pallas_call | solution.py:662
  66.8 5.3 %collective-permute-start.5 = (bf16[3,2,1120,128]{3,2,1,0:T(8,128)(2,1)}, bf16[3,2,1120,128]{3,2,1,0:T(8,128)(2,1)}, u32[]{:S(2)}, u32[]{:S(2)}) collective-permute-start(bf16[3,2,1120,128]{3,2,1,0:T(8,128)(2,1)} %get-tuple-element.132), channel_id=1, source_target_pairs={{0,16},{1,17},{2,18},{3,19},{4,20},{5,21},{6,22},{7,23},{8,24},{9,... | collective-permute-start | bytes 5160968 | tf_op jit(solution)/shard_map/ppermute | solution.py:958
  72.1 2.1 add_convert_fusion
  74.2 1.2 dynamic-slice_bitcast_fusion.1
  75.4 1.5 collective-permute-start.4
  77.0 11.8 %shard_map.264 = (bf16[3136,256]{1,0:T(8,128)(2,1)S(1)}, f32[64,256]{1,0:T(8,128)S(1)}, bf16[576,2304]{1,0:T(8,128)(2,1)S(1)}, bf16[6,1008,128]{2,1,0:T(8,128)(2,1)}, f32[64,256]{1,0:T(8,128)S(1)}) custom-call(bf16[3136,512]{1,0:T(8,128)(2,1)} %bitcast.112, bf16[512,256]{1,0:T(8,128)(2,1)S(1)} %get-tuple-element.118.rd_ref, ...), custom_call_target="tpu_custom_call" | custom-call | flops 4800000000 | tf_op jit(solution)/shard_map/pallas_call | solution.py:429
  88.8 4.4 %collective-permute-start.10 = (bf16[6,1008,128]{2,1,0:T(8,128)(2,1)}, bf16[6,1008,128]{2,1,0:T(8,128)(2,1)}, u32[]{:S(2)}, u32[]{:S(2)}) collective-permute-start(bf16[6,1008,128]{2,1,0:T(8,128)(2,1)} %get-tuple-element.143), channel_id=1, source_target_pairs={{0,16},{1,17},{2,18},{3,19},{4,20},{5,21},{6,22},{7,23},{8,24},{9,... | collective-permute-start | bytes 4644872 | tf_op jit(solution)/shard_map/ppermute | solution.py:958
  93.2 7.0 %shard_map.265 = (bf16[2,640,2560]{2,1,0:T(8,128)(2,1)}, bf16[1,2,1120,128]{3,2,1,0:T(8,128)(2,1)}, bf16[3,2,1120,128]{3,2,1,0:T(8,128)(2,1)}, f32[32,256]{1,0:T(8,128)S(1)}) custom-call(bf16[576,2304]{1,0:T(8,128)(2,1)S(1)} %get-tuple-element.133.cur_ref.prev_ref.r_ref, bf16[576,2304]{1,0:T(8,128)(2,1)S(1)} %get-tuple-element.133.cur_ref.prev_ref.r_ref, ...), custom_call_target="tpu_custom_call" | custom-call | flops 2400000000 | tf_op jit(solution)/shard_map/pallas_call | solution.py:517
  100.2 8.8 %collective-permute-done.5.rest_3_ = bf16[3,2,1120,128]{3,2,1,0:T(8,128)(2,1)} collective-permute-done((bf16[3,2,1120,128]{3,2,1,0:T(8,128)(2,1)}, bf16[3,2,1120,128]{3,2,1,0:T(8,128)(2,1)}, u32[]{:S(2)}, u32[]{:S(2)}) %collective-permute-start.5) | collective-permute-done | bytes 1720352 | tf_op jit(solution)/shard_map/ppermute | solution.py:958
  109.1 1.5 add_convert_fusion.1
  110.6 0.1 dynamic-slice_bitcast_fusion.3
  110.6 1.6 collective-permute-start.6
  112.3 7.2 %shard_map.266 = (bf16[2,640,2560]{2,1,0:T(8,128)(2,1)}, f32[32,256]{1,0:T(8,128)S(1)}) custom-call(bf16[576,2304]{1,0:T(8,128)(2,1)S(1)} %get-tuple-element.133.cur_ref.prev_ref.r_ref, bf16[576,2304]{1,0:T(8,128)(2,1)S(1)} %get-tuple-element.133.cur_ref.prev_ref.r_ref, bf16[640,768]{1,0:T(8,128)(2,1)} %get-tuple-element.126.t_ref, ...), custom_call_target="tpu_custom_call", output_to_operand_aliasing={{0}: (4, {})} | custom-call | flops 3600000000 | tf_op jit(solution)/shard_map/pallas_call | solution.py:517
  119.4 4.6 %shard_map.267.refs_6_ = f32[64,576]{1,0:T(8,128)S(1)} custom-call(bf16[576,2304]{1,0:T(8,128)(2,1)S(1)} %copy-done, bf16[576,2304]{1,0:T(8,128)(2,1)S(1)} %copy-done, bf16[576,2304]{1,0:T(8,128)(2,1)S(1)} %copy-done, bf16[576,2304]{1,0:T(8,128)(2,1)S(1)} %copy-done, bf16[7,448,256]{2,1,0:T(8,128)(2,1)S(1)} %bitcast.86), custom_call_target="tpu_custom_call" | custom-call | flops 2800000000 | tf_op jit(solution)/shard_map/pallas_call | solution.py:704
  124.1 0.1 add_convert_fusion.2
  124.3 2.7 %collective-permute-start.7 = (bf16[1,2,512,128]{3,2,1,0:T(8,128)(2,1)S(1)}, bf16[1,2,512,128]{3,2,1,0:T(8,128)(2,1)S(1)}, u32[]{:S(2)}, u32[]{:S(2)}) collective-permute-start(bf16[1,2,512,128]{3,2,1,0:T(8,128)(2,1)S(1)} %get-tuple-element.181), channel_id=1, source_target_pairs={{0,8},{1,9},{2,10},{3,11},{4,12},{5,13},{6,14},{7,15},{8,0},{9,1},... | collective-permute-start | bytes 786440 | tf_op jit(solution)/shard_map/ppermute | solution.py:963
  127.0 12.4 %shard_map.268.refs_4_ = f32[256,32]{1,0:T(8,128)S(1)} custom-call(bf16[4,336,5120]{2,1,0:T(8,128)(2,1)} %get-tuple-element.138.x_ref, bf16[4,336,256]{2,1,0:T(8,128)(2,1)S(1)} %copy-done.2, bf16[2,640,2560]{2,1,0:T(8,128)(2,1)} %get-tuple-element.170.r_ref.own_ref.before_ref), custom_call_target="tpu_custom_call" | custom-call | flops 5200000000 | tf_op jit(solution)/shard_map/pallas_call | solution.py:797
  139.4 0.1 add_convert_fusion.3
  139.5 4.4 %collective-permute-start.8 = (bf16[512,128]{1,0:T(8,128)(2,1)S(1)}, bf16[512,128]{1,0:T(8,128)(2,1)S(1)}, u32[]{:S(2)}, u32[]{:S(2)}) collective-permute-start(bf16[512,128]{1,0:T(8,128)(2,1)S(1)} %slice_bitcast_fusion), channel_id=1, source_target_pairs={{0,16},{1,17},{2,18},{3,19},{4,20},{5,21},{6,22},{7,23},{8,24},{9,... | collective-permute-start | bytes 393224 | tf_op jit(solution)/shard_map/ppermute | solution.py:958
  143.9 1.3 collective-permute-start.12
  145.2 2.5 %collective-permute-done.8 = bf16[512,128]{1,0:T(8,128)(2,1)S(1)} collective-permute-done((bf16[512,128]{1,0:T(8,128)(2,1)S(1)}, bf16[512,128]{1,0:T(8,128)(2,1)S(1)}, u32[]{:S(2)}, u32[]{:S(2)}) %collective-permute-start.8) | collective-permute-done | bytes 131104 | tf_op jit(solution)/shard_map/ppermute | solution.py:958
  147.7 1.0 collective-permute-start.9
  148.7 7.9 %shard_map.269.refs_5_ = f32[512,64]{1,0:T(8,128)S(1)} custom-call(bf16[2,640,2560]{2,1,0:T(8,128)(2,1)} %get-tuple-element.103.r0_ref.r1_ref.a0_ref.a1_ref, bf16[2,640,2560]{2,1,0:T(8,128)(2,1)} %get-tuple-element.103.r0_ref.r1_ref.a0_ref.a1_ref, bf16[576,2304]{1,0:T(8,128)(2,1)S(1)} %get-tuple-element.133.cur_ref.prev_ref.r_ref), custom_call_target="tpu_custom_call" | custom-call | flops 3600000000 | tf_op jit(solution)/shard_map/pallas_call | solution.py:740
  156.7 0.1 copy.40.refs_7_
  156.9 1.0 shard_map.270
  157.9 0.1 collective-permute-start.11
  158.0 0.3 copy-done.16
  158.3 4.7 %collective-permute-start.15 = (bf16[3,2,1120,128]{3,2,1,0:T(8,128)(2,1)S(1)}, bf16[3,2,1120,128]{3,2,1,0:T(8,128)(2,1)S(1)}, u32[]{:S(2)}, u32[]{:S(2)}) collective-permute-start(bf16[3,2,1120,128]{3,2,1,0:T(8,128)(2,1)S(1)} %copy-done.16), channel_id=1, source_target_pairs={{0,16},{1,17},{2,18},{3,19},{4,20},{5,21},{6,22},{7,23},{8,24},{9,... | collective-permute-start | bytes 5160968 | tf_op jit(solution)/shard_map/ppermute | solution.py:958
  163.1 1.4 collective-permute-start.18
  164.5 0.1 add_convert_fusion.7
  164.5 1.6 collective-permute-start.13
  166.1 9.2 %shard_map.271 = (bf16[84,84,2,224]{3,2,1,0:T(2,128)(2,1)}, bf16[640,256]{1,0:T(8,128)(2,1)S(1)}) custom-call(s32[4]{0:T(128)S(1)} %pad_add_fusion.flag_ref, bf16[2,640,2560]{2,1,0:T(8,128)(2,1)} %get-tuple-element.170.r_ref.own_ref.before_ref, bf16[2,640,2560]{2,1,0:T(8,128)(2,1)} %get-tuple-element.170.r_ref.own_ref.before_ref, ...), custom_call_target="tpu_custom_call" | custom-call | flops 3600000000 | tf_op jit(solution)/shard_map/pallas_call | solution.py:629
  175.4 0.1 add_convert_fusion.6
  175.4 0.7 collective-permute-start.14
  176.2 0.1 pad_maximum_fusion.1
  176.2 0.6 collective-permute-start.19
  176.8 4.8 %collective-permute-done.14 = bf16[768,128]{1,0:T(8,128)(2,1)S(1)} collective-permute-done((bf16[768,128]{1,0:T(8,128)(2,1)S(1)}, bf16[768,128]{1,0:T(8,128)(2,1)S(1)}, u32[]{:S(2)}, u32[]{:S(2)}) %collective-permute-start.14) | collective-permute-done | bytes 196640 | tf_op jit(solution)/shard_map/ppermute | solution.py:963
  181.6 0.1 add_convert_fusion.5
  181.7 2.1 collective-permute-start.16
  183.8 8.3 %collective-permute-done.16 = bf16[768,128]{1,0:T(8,128)(2,1)S(1)} collective-permute-done((bf16[768,128]{1,0:T(8,128)(2,1)S(1)}, bf16[768,128]{1,0:T(8,128)(2,1)S(1)}, u32[]{:S(2)}, u32[]{:S(2)}) %collective-permute-start.16) | collective-permute-done | bytes 196640 | tf_op jit(solution)/shard_map/ppermute | solution.py:963
  192.1 0.1 pad_maximum_fusion
  192.2 0.1 collective-permute-start.20
  192.3 7.6 %collective-permute-done.15.rest_1_ = bf16[3,2,1120,128]{3,2,1,0:T(8,128)(2,1)S(1)} collective-permute-done((bf16[3,2,1120,128]{3,2,1,0:T(8,128)(2,1)S(1)}, bf16[3,2,1120,128]{3,2,1,0:T(8,128)(2,1)S(1)}, u32[]{:S(2)}, u32[]{:S(2)}) %collective-permute-start.15) | collective-permute-done | bytes 1720352 | tf_op jit(solution)/shard_map/ppermute | solution.py:958
  199.8 0.1 add_convert_fusion.4.own_ref
  199.9 4.4 %collective-permute-start.17 = (bf16[768,128]{1,0:T(8,128)(2,1)S(1)}, bf16[768,128]{1,0:T(8,128)(2,1)S(1)}, u32[]{:S(2)}, u32[]{:S(2)}) collective-permute-start(bf16[768,128]{1,0:T(8,128)(2,1)S(1)} %add_convert_fusion.4.own_ref), channel_id=1, source_target_pairs={{0,16},{1,17},{2,18},{3,19},{4,20},{5,21},{6,22},{7,23},{8,24},{9,... | collective-permute-start | bytes 589832 | tf_op jit(solution)/shard_map/ppermute | solution.py:958
  204.3 5.3 %shard_map.274 = (bf16[84,84,2,224]{3,2,1,0:T(2,128)(2,1)}, bf16[640,256]{1,0:T(8,128)(2,1)}) custom-call(s32[4]{0:T(128)S(1)} %pad_add_fusion.flag_ref, bf16[2,640,2560]{2,1,0:T(8,128)(2,1)} %get-tuple-element.170.r_ref.own_ref.before_ref, bf16[2,640,2560]{2,1,0:T(8,128)(2,1)} %get-tuple-element.170.r_ref.own_ref.before_ref, ...), custom_call_target="tpu_custom_call", output_to_operand_aliasing={{0}: (7, {})} | custom-call | flops 2400000000 | tf_op jit(solution)/shard_map/pallas_call | solution.py:629
  209.6 1.5 shard_map.272
  211.1 3.0 %shard_map.273 = (f32[3136,256]{1,0:T(8,128)}, f32[918,256]{1,0:T(8,128)}) custom-call(s32[4]{0:T(128)S(1)} %pad_add_fusion.flag_ref, bf16[8,512,128]{2,1,0:T(8,128)(2,1)S(1)} %bitcast.88, bf16[8,512,128]{2,1,0:T(8,128)(2,1)S(1)} %collective-permute-done.20.other_ref), custom_call_target="tpu_custom_call" | custom-call | flops 1600000000 | tf_op jit(solution)/shard_map/pallas_call | solution.py:943
  (54 shorter events, 0.2 us)
Async XLA Ops:
  0.6 7.9 %copy-start.3 = (bf16[16,256]{1,0:T(8,128)(2,1)S(1)}, bf16[16,256]{1,0:T(8,128)(2,1)}, u32[]{:S(2)}) copy-start(bf16[16,256]{1,0:T(8,128)(2,1)} %constant.120.clone.1.ones_ref) | copy-start | bytes 24580
  3.7 14.0 %collective-permute-start.1 = (bf16[640,64]{1,0:T(8,128)(2,1)}, bf16[640,64]{1,0:T(8,128)(2,1)S(1)}, u32[]{:S(2)}, u32[]{:S(2)}) collective-permute-start(bf16[640,64]{1,0:T(8,128)(2,1)} %get-tuple-element.111), channel_id=1, source_target_pairs={{0,16},{1,17},{2,18},{3,19},{4,20},{5,21},{6,22},{7,23},{8,24},{9,... | collective-permute-start | bytes 245768 | tf_op jit(solution)/shard_map/ppermute | solution.py:958
  8.5 11.7 %copy-start.4 = (s32[224]{0:T(256)S(1)}, s32[224]{0:T(256)}, u32[]{:S(2)}) copy-start(s32[224]{0:T(256)} %param.30) | copy-start | bytes 2692
  8.6 11.7 %copy-start.14 = (s32[224]{0:T(256)S(1)}, s32[224]{0:T(256)}, u32[]{:S(2)}) copy-start(s32[224]{0:T(256)} %param.31) | copy-start | bytes 2692
  17.7 19.0 %copy-start.17 = (bf16[640,64]{1,0:T(8,128)(2,1)}, bf16[640,64]{1,0:T(8,128)(2,1)S(1)}, u32[]{:S(2)}) copy-start(bf16[640,64]{1,0:T(8,128)(2,1)S(1)} %collective-permute-done.1.got) | copy-start | bytes 245764
  17.7 43.3 %collective-permute-start.2 = (bf16[3,2,1120,128]{3,2,1,0:T(8,128)(2,1)}, bf16[3,2,1120,128]{3,2,1,0:T(8,128)(2,1)}, u32[]{:S(2)}, u32[]{:S(2)}) collective-permute-start(bf16[3,2,1120,128]{3,2,1,0:T(8,128)(2,1)} %get-tuple-element.117), channel_id=1, source_target_pairs={{0,16},{1,17},{2,18},{3,19},{4,20},{5,21},{6,22},{7,23},{8,24},{9,... | collective-permute-start | bytes 5160968 | tf_op jit(solution)/shard_map/ppermute | solution.py:958
  36.7 14.2 %copy-start.15 = (bf16[1,3136,512]{2,1,0:T(8,128)(2,1)S(1)}, bf16[1,3136,512]{2,1,0:T(8,128)(2,1)}, u32[]{:S(2)}) copy-start(bf16[1,3136,512]{2,1,0:T(8,128)(2,1)} %param.26) | copy-start | bytes 9633796
  50.9 1.5 copy-start.12
  50.9 1.8 copy-start.5
  50.9 1.8 copy-start.8
  51.0 1.8 copy-start.9
  53.5 5.8 %collective-permute-start = (bf16[51,224]{1,0:T(8,128)(2,1)S(1)}, bf16[51,224]{1,0:T(8,128)(2,1)S(1)}, u32[]{:S(2)}, u32[]{:S(2)}) collective-permute-start(bf16[51,224]{1,0:T(8,128)(2,1)S(1)} %get-tuple-element.108), channel_id=1, source_target_pairs={{16,0},{17,1},{18,2},{19,3},{20,4},{21,5},{22,6},{23,7},{24,8},{25... | collective-permute-start | bytes 68552 | tf_op jit(solution)/shard_map/ppermute | solution.py:1043
  54.9 4.4 %copy-start.6 = (s32[224,51]{0,1:T(8,128)S(1)}, s32[224,51]{0,1:T(8,128)}, u32[]{:S(2)}) copy-start(s32[224,51]{0,1:T(8,128)} %param.33) | copy-start | bytes 137092
  54.9 4.4 %copy-start.7 = (f32[224,51]{0,1:T(8,128)S(1)}, f32[224,51]{0,1:T(8,128)}, u32[]{:S(2)}) copy-start(f32[224,51]{0,1:T(8,128)} %param.34) | copy-start | bytes 137092
  54.9 4.4 %copy-start.10 = (s32[224]{0:T(256)S(1)}, s32[224]{0:T(256)}, u32[]{:S(2)}) copy-start(s32[224]{0:T(256)} %param.32) | copy-start | bytes 2692
  60.3 1.4 copy-start.13
  66.8 5.3 %collective-permute-start.3 = (bf16[8,2,512,128]{3,2,1,0:T(8,128)(2,1)}, bf16[8,2,512,128]{3,2,1,0:T(8,128)(2,1)}, u32[]{:S(2)}, u32[]{:S(2)}) collective-permute-start(bf16[8,2,512,128]{3,2,1,0:T(8,128)(2,1)} %get-tuple-element.121), channel_id=1, source_target_pairs={{0,1},{1,0},{2,3},{3,2},{4,5},{5,4},{6,7},{7,6},{8,9},{9,8},{10,11... | collective-permute-start | bytes 6291464 | tf_op jit(solution)/shard_map/ppermute | solution.py:963
  66.8 42.2 %collective-permute-start.5 = (bf16[3,2,1120,128]{3,2,1,0:T(8,128)(2,1)}, bf16[3,2,1120,128]{3,2,1,0:T(8,128)(2,1)}, u32[]{:S(2)}, u32[]{:S(2)}) collective-permute-start(bf16[3,2,1120,128]{3,2,1,0:T(8,128)(2,1)} %get-tuple-element.132), channel_id=1, source_target_pairs={{0,16},{1,17},{2,18},{3,19},{4,20},{5,21},{6,22},{7,23},{8,24},{9,... | collective-permute-start | bytes 5160968 | tf_op jit(solution)/shard_map/ppermute | solution.py:958
  75.4 33.6 %collective-permute-start.4 = (bf16[4,2,512,128]{3,2,1,0:T(8,128)(2,1)}, bf16[4,2,512,128]{3,2,1,0:T(8,128)(2,1)}, u32[]{:S(2)}, u32[]{:S(2)}) collective-permute-start(bf16[4,2,512,128]{3,2,1,0:T(8,128)(2,1)} %get-tuple-element.175), channel_id=1, source_target_pairs={{0,2},{1,3},{2,0},{3,1},{4,6},{5,7},{6,4},{7,5},{8,10},{9,11},{10,... | collective-permute-start | bytes 3145736 | tf_op jit(solution)/shard_map/ppermute | solution.py:963
  88.8 68.1 %collective-permute-start.10 = (bf16[6,1008,128]{2,1,0:T(8,128)(2,1)}, bf16[6,1008,128]{2,1,0:T(8,128)(2,1)}, u32[]{:S(2)}, u32[]{:S(2)}) collective-permute-start(bf16[6,1008,128]{2,1,0:T(8,128)(2,1)} %get-tuple-element.143), channel_id=1, source_target_pairs={{0,16},{1,17},{2,18},{3,19},{4,20},{5,21},{6,22},{7,23},{8,24},{9,... | collective-permute-start | bytes 4644872 | tf_op jit(solution)/shard_map/ppermute | solution.py:958
  110.6 13.5 %collective-permute-start.6 = (bf16[2,2,512,128]{3,2,1,0:T(8,128)(2,1)S(1)}, bf16[2,2,512,128]{3,2,1,0:T(8,128)(2,1)S(1)}, u32[]{:S(2)}, u32[]{:S(2)}) collective-permute-start(bf16[2,2,512,128]{3,2,1,0:T(8,128)(2,1)S(1)} %get-tuple-element.177), channel_id=1, source_target_pairs={{0,4},{1,5},{2,6},{3,7},{4,0},{5,1},{6,2},{7,3},{8,12},{9,13},{10,... | collective-permute-start | bytes 1572872 | tf_op jit(solution)/shard_map/ppermute | solution.py:963
  112.3 7.2 %copy-start = (bf16[576,2304]{1,0:T(8,128)(2,1)S(1)}, bf16[576,2304]{1,0:T(8,128)(2,1)}, u32[]{:S(2)}) copy-start(bf16[576,2304]{1,0:T(8,128)(2,1)} %get-tuple-element.130.refs_0_.refs_1_.refs_2_.refs_3_) | copy-start | bytes 7962628
  124.1 2.9 %copy-start.2 = (bf16[4,336,256]{2,1,0:T(8,128)(2,1)S(1)}, bf16[4,336,256]{2,1,0:T(8,128)(2,1)}, u32[]{:S(2)}) copy-start(bf16[4,336,256]{2,1,0:T(8,128)(2,1)} %get-tuple-element.139.x0_ref) | copy-start | bytes 2064388
  124.3 15.1 %collective-permute-start.7 = (bf16[1,2,512,128]{3,2,1,0:T(8,128)(2,1)S(1)}, bf16[1,2,512,128]{3,2,1,0:T(8,128)(2,1)S(1)}, u32[]{:S(2)}, u32[]{:S(2)}) collective-permute-start(bf16[1,2,512,128]{3,2,1,0:T(8,128)(2,1)S(1)} %get-tuple-element.181), channel_id=1, source_target_pairs={{0,8},{1,9},{2,10},{3,11},{4,12},{5,13},{6,14},{7,15},{8,0},{9,1},... | collective-permute-start | bytes 786440 | tf_op jit(solution)/shard_map/ppermute | solution.py:963
  139.5 8.2 %collective-permute-start.8 = (bf16[512,128]{1,0:T(8,128)(2,1)S(1)}, bf16[512,128]{1,0:T(8,128)(2,1)S(1)}, u32[]{:S(2)}, u32[]{:S(2)}) collective-permute-start(bf16[512,128]{1,0:T(8,128)(2,1)S(1)} %slice_bitcast_fusion), channel_id=1, source_target_pairs={{0,16},{1,17},{2,18},{3,19},{4,20},{5,21},{6,22},{7,23},{8,24},{9,... | collective-permute-start | bytes 393224 | tf_op jit(solution)/shard_map/ppermute | solution.py:958
  143.9 22.3 %collective-permute-start.12 = (bf16[1,2,1120,128]{3,2,1,0:T(8,128)(2,1)}, bf16[1,2,1120,128]{3,2,1,0:T(8,128)(2,1)S(1)}, u32[]{:S(2)}, u32[]{:S(2)}) collective-permute-start(bf16[1,2,1120,128]{3,2,1,0:T(8,128)(2,1)} %get-tuple-element.150), channel_id=1, source_target_pairs={{0,16},{1,17},{2,18},{3,19},{4,20},{5,21},{6,22},{7,23},{8,24},{9,... | collective-permute-start | bytes 1720328 | tf_op jit(solution)/shard_map/ppermute | solution.py:958
  147.7 9.1 %copy-start.11 = (s32[224,1]{0,1:T(1,128)S(1)}, s32[224,1]{0,1:T(1,128)}, u32[]{:S(2)}) copy-start(s32[224,1]{0,1:T(1,128)} %param.35) | copy-start | bytes 2692
  147.7 9.1 %collective-permute-start.9 = (bf16[1,512,128]{2,1,0:T(8,128)(2,1)S(1)}, bf16[1,512,128]{2,1,0:T(8,128)(2,1)S(1)}, u32[]{:S(2)}, u32[]{:S(2)}) collective-permute-start(bf16[1,512,128]{2,1,0:T(8,128)(2,1)S(1)} %get-tuple-element.183), channel_id=1, source_target_pairs={{0,8},{1,9},{2,10},{3,11},{4,12},{5,13},{6,14},{7,15},{8,0},{9,1},... | collective-permute-start | bytes 393224 | tf_op jit(solution)/shard_map/ppermute | solution.py:963
  156.9 1.5 copy-start.16
  156.9 9.3 %copy-start.1 = (bf16[224,512]{1,0:T(8,128)(2,1)S(1)}, bf16[224,512]{1,0:T(8,128)(2,1)}, u32[]{:S(2)}) copy-start(bf16[224,512]{1,0:T(8,128)(2,1)} %get-tuple-element.112.rest_5_.rest_2_) | copy-start | bytes 688132
  157.9 6.6 %collective-permute-start.11 = (bf16[768,128]{1,0:T(8,128)(2,1)S(1)}, bf16[768,128]{1,0:T(8,128)(2,1)S(1)}, u32[]{:S(2)}, u32[]{:S(2)}) collective-permute-start(bf16[768,128]{1,0:T(8,128)(2,1)S(1)} %shard_map.270), channel_id=1, source_target_pairs={{0,1},{1,0},{2,3},{3,2},{4,5},{5,4},{6,7},{7,6},{8,9},{9,8},{10,11... | collective-permute-start | bytes 589832 | tf_op jit(solution)/shard_map/ppermute | solution.py:963
  158.3 41.5 %collective-permute-start.15 = (bf16[3,2,1120,128]{3,2,1,0:T(8,128)(2,1)S(1)}, bf16[3,2,1120,128]{3,2,1,0:T(8,128)(2,1)S(1)}, u32[]{:S(2)}, u32[]{:S(2)}) collective-permute-start(bf16[3,2,1120,128]{3,2,1,0:T(8,128)(2,1)S(1)} %copy-done.16), channel_id=1, source_target_pairs={{0,16},{1,17},{2,18},{3,19},{4,20},{5,21},{6,22},{7,23},{8,24},{9,... | collective-permute-start | bytes 5160968 | tf_op jit(solution)/shard_map/ppermute | solution.py:958
  163.1 13.1 %collective-permute-start.18 = (bf16[2,512,128]{2,1,0:T(8,128)(2,1)S(1)}, bf16[2,512,128]{2,1,0:T(8,128)(2,1)S(1)}, u32[]{:S(2)}, u32[]{:S(2)}) collective-permute-start(bf16[2,512,128]{2,1,0:T(8,128)(2,1)S(1)} %maximum_bitcast_fusion), channel_id=1, source_target_pairs={{0,4},{1,5},{2,6},{3,7},{4,0},{5,1},{6,2},{7,3},{8,12},{9,13},{10,... | collective-permute-start | bytes 786440 | tf_op jit(solution)/shard_map/ppermute | solution.py:963
  164.5 10.8 %collective-permute-start.13 = (bf16[768,128]{1,0:T(8,128)(2,1)S(1)}, bf16[768,128]{1,0:T(8,128)(2,1)S(1)}, u32[]{:S(2)}, u32[]{:S(2)}) collective-permute-start(bf16[768,128]{1,0:T(8,128)(2,1)S(1)} %add_convert_fusion.7), channel_id=1, source_target_pairs={{0,2},{1,3},{2,0},{3,1},{4,6},{5,7},{6,4},{7,5},{8,10},{9,11},{10,... | collective-permute-start | bytes 589832 | tf_op jit(solution)/shard_map/ppermute | solution.py:963
  175.4 6.2 %collective-permute-start.14 = (bf16[768,128]{1,0:T(8,128)(2,1)S(1)}, bf16[768,128]{1,0:T(8,128)(2,1)S(1)}, u32[]{:S(2)}, u32[]{:S(2)}) collective-permute-start(bf16[768,128]{1,0:T(8,128)(2,1)S(1)} %add_convert_fusion.6), channel_id=1, source_target_pairs={{0,4},{1,5},{2,6},{3,7},{4,0},{5,1},{6,2},{7,3},{8,12},{9,13},{10,... | collective-permute-start | bytes 589832 | tf_op jit(solution)/shard_map/ppermute | solution.py:963
  176.2 15.8 %collective-permute-start.19 = (bf16[4,512,128]{2,1,0:T(8,128)(2,1)S(1)}, bf16[4,512,128]{2,1,0:T(8,128)(2,1)S(1)}, u32[]{:S(2)}, u32[]{:S(2)}) collective-permute-start(bf16[4,512,128]{2,1,0:T(8,128)(2,1)S(1)} %bitcast.105), channel_id=1, source_target_pairs={{0,2},{1,3},{2,0},{3,1},{4,6},{5,7},{6,4},{7,5},{8,10},{9,11},{10,... | collective-permute-start | bytes 1572872 | tf_op jit(solution)/shard_map/ppermute | solution.py:963
  181.7 10.4 %collective-permute-start.16 = (bf16[768,128]{1,0:T(8,128)(2,1)S(1)}, bf16[768,128]{1,0:T(8,128)(2,1)S(1)}, u32[]{:S(2)}, u32[]{:S(2)}) collective-permute-start(bf16[768,128]{1,0:T(8,128)(2,1)S(1)} %add_convert_fusion.5), channel_id=1, source_target_pairs={{0,8},{1,9},{2,10},{3,11},{4,12},{5,13},{6,14},{7,15},{8,0},{9,1},... | collective-permute-start | bytes 589832 | tf_op jit(solution)/shard_map/ppermute | solution.py:963
  192.2 18.9 %collective-permute-start.20 = (bf16[8,512,128]{2,1,0:T(8,128)(2,1)S(1)}, bf16[8,512,128]{2,1,0:T(8,128)(2,1)S(1)}, u32[]{:S(2)}, u32[]{:S(2)}) collective-permute-start(bf16[8,512,128]{2,1,0:T(8,128)(2,1)S(1)} %bitcast.87), channel_id=1, source_target_pairs={{0,1},{1,0},{2,3},{3,2},{4,5},{5,4},{6,7},{7,6},{8,9},{9,8},{10,11... | collective-permute-start | bytes 3145736 | tf_op jit(solution)/shard_map/ppermute | solution.py:963
  199.9 9.7 %collective-permute-start.17 = (bf16[768,128]{1,0:T(8,128)(2,1)S(1)}, bf16[768,128]{1,0:T(8,128)(2,1)S(1)}, u32[]{:S(2)}, u32[]{:S(2)}) collective-permute-start(bf16[768,128]{1,0:T(8,128)(2,1)S(1)} %add_convert_fusion.4.own_ref), channel_id=1, source_target_pairs={{0,16},{1,17},{2,18},{3,19},{4,20},{5,21},{6,22},{7,23},{8,24},{9,... | collective-permute-start | bytes 589832 | tf_op jit(solution)/shard_map/ppermute | solution.py:958
